TPU v7x, 32 devices: a whole 2x2x4 slice. The times are simulated.
32 devices in a mesh: shard: 4 (over y, x), ctx: 4 (over z), tp: 2 (over core).
Axes of the slice: x: 2, y: 2, z: 4, core: 2. Of those that a mesh axis runs over, the one named last changes fastest.
Arguments:
- tokens: bfloat16 [6144, 2048], P(('shard', 'ctx')), may hold values from -6 to 6
- lengths: int32 [4, 3], P('shard'), may hold values from 1 to 1024, 1536 in all within a row
- w_qkv: bfloat16 [1, 2048, 3, 2048], P(None, ('shard', 'ctx'), None, 'tp'), may hold values from -0.125 to 0.125
- b_qkv: bfloat16 [1, 3, 32, 64], P(None, None, 'tp', ('shard', 'ctx')), may hold values from -1.1953125 to 1.1953125
- w_out: bfloat16 [1, 2048, 2048], P(None, 'tp', ('shard', 'ctx')), may hold values from -0.5 to 0.5
- w_gateup: bfloat16 [1, 2048, 2, 5632], P(None, ('shard', 'ctx'), None, 'tp'), may hold values from -0.125 to 0.125
- w_down: bfloat16 [1, 5632, 2048], P(None, 'tp', ('shard', 'ctx')), may hold values from -0.078125 to 0.078125
- norm_gain: bfloat16 [1, 2, 2048], P(None, None, ('shard', 'ctx')), may hold values from 0.5 to 1.5
- norm_bias: bfloat16 [1, 2, 2048], P(None, None, ('shard', 'ctx')), may hold values from -1.1953125 to 1.1953125
- cotangent: bfloat16 [6144, 2048], P(('shard', 'ctx')), may hold values from -6 to 6
Outputs:
- output: bfloat16 [6144, 2048], P(('shard', 'ctx'))
- grad_tokens: float32 [6144, 2048], P(('shard', 'ctx'))
- grad_w_qkv: float32 [1, 2048, 3, 2048], P(None, ('shard', 'ctx'), None, 'tp')
- grad_b_qkv: float32 [1, 3, 32, 64], P(None, None, 'tp', ('shard', 'ctx'))
- grad_w_out: float32 [1, 2048, 2048], P(None, 'tp', ('shard', 'ctx'))
- grad_w_gateup: float32 [1, 2048, 2, 5632], P(None, ('shard', 'ctx'), None, 'tp')
- grad_w_down: float32 [1, 5632, 2048], P(None, 'tp', ('shard', 'ctx'))
- grad_norm_gain: float32 [1, 2, 2048], P(None, None, ('shard', 'ctx'))
- grad_norm_bias: float32 [1, 2, 2048], P(None, None, ('shard', 'ctx'))
Inputs may be any that keep to these rules, and one draw needn't show every extreme that they name: Each row holds the lengths of a group's 3 documents; they add up to 1536, and the longest is exactly 1024.
All inputs are finite; a program needn't handle non-finite values.
Results may differ from a plain program's by a relative error of at most 0.019.
Values may be sent and summed in bfloat16 or wider, within the bound.
A program may use at most 256 MiB of HBM per device.

v0:
```python
from functools import partial

import jax
import jax.numpy as jnp
from jax import lax
from jax.sharding import PartitionSpec as P

HEAD = 64
ROT = 16
LAYERS = 1


EPS = 1e-05
NEG = -1e30
BASE = 10000.0


def doc_table(lengths_row, row_ids):
    doc_ends = jnp.cumsum(lengths_row, dtype=jnp.int32)
    doc_begin = doc_ends - lengths_row
    doc_ids = jnp.sum(
        (row_ids[:, None] >= doc_ends[None, :]).astype(jnp.int32), axis=1, dtype=jnp.int32
    )
    numbers = jnp.arange(lengths_row.shape[0], dtype=jnp.int32)
    onehot = (doc_ids[:, None] == numbers[None, :]).astype(jnp.int32)
    places = row_ids - jnp.sum(onehot * doc_begin[None, :], axis=1, dtype=jnp.int32)
    return (doc_ids, places)


def angles(places):
    half_rot = ROT // 2
    frequency = BASE ** (-2.0 * jnp.arange(half_rot, dtype=jnp.float32) / ROT)
    phases = places.astype(jnp.float32)[:, None] * frequency[None, :]
    return (jnp.cos(phases), jnp.sin(phases))


def rotate(values, cosine_table, sine_table, direction):
    half_rot = ROT // 2
    cosine = cosine_table[:, None, :]
    sine_part = sine_table[:, None, :]
    leading = values[..., :half_rot]
    trailing = values[..., half_rot:ROT]
    return jnp.concatenate(
        (
            leading * cosine - direction * trailing * sine_part,
            trailing * cosine + direction * leading * sine_part,
            values[..., ROT:],
        ),
        axis=-1,
    )


def layer_norm(values, gain, shift):
    center = values - jnp.mean(values, axis=-1, keepdims=True)
    inverse = lax.rsqrt(jnp.mean(center * center, axis=-1, keepdims=True) + EPS)
    normal = center * inverse
    return (normal * gain + shift, normal, inverse)


def norm_back(gradient, normal, inverse, gain):
    scaled = gradient * gain
    centered = (
        scaled
        - jnp.mean(scaled, axis=-1, keepdims=True)
        - normal * jnp.mean(scaled * normal, axis=-1, keepdims=True)
    )
    return (inverse * centered, jnp.sum(gradient * normal, axis=0), jnp.sum(gradient, axis=0))


def attend_keys(carried, key_block, first_row, queries, query_docs, query_rows, lengths_row):
    running_max, running_sum, weighted = carried
    block_size = key_block.shape[0]
    local_heads = queries.shape[1]
    key_rows = first_row + jnp.arange(block_size, dtype=jnp.int32)
    key_docs, unused = doc_table(lengths_row, key_rows)
    key_rot = key_block[:, 0].reshape(block_size, local_heads, HEAD)
    key_val = key_block[:, 1].reshape(block_size, local_heads, HEAD)
    scores = jnp.einsum(
        "qhe,khe->hqk", queries, key_rot, preferred_element_type=jnp.float32
    ) * HEAD ** (-0.5)
    allowed = (
        (query_docs[:, None] == key_docs[None, :]) & (key_rows[None, :] <= query_rows[:, None])
    )[None]
    masked = jnp.where(allowed, scores, NEG)
    new_max = jnp.maximum(running_max, jnp.max(masked, axis=-1))
    exp_scores = jnp.where(allowed, jnp.exp(masked - new_max[..., None]), 0.0)
    factor = jnp.exp(running_max - new_max)
    running_sum = running_sum * factor + jnp.sum(exp_scores, axis=-1)
    weighted = weighted * factor[..., None] + jnp.einsum(
        "hqk,khe->hqe", exp_scores.astype(jnp.bfloat16), key_val, preferred_element_type=jnp.float32
    )
    return (new_max, running_sum, weighted)


def fold_keys(carried, shard_piece, first_row, queries, query_docs, query_rows, lengths_row):
    row_count = shard_piece.shape[0]
    block_size = 512
    blocks = shard_piece.reshape(row_count // block_size, block_size, 2, shard_piece.shape[2])
    offsets = block_size * jnp.arange(row_count // block_size, dtype=jnp.int32)
    last_query = query_rows[-1]

    def fold_advance(running, inputs):
        key_block, offset = inputs

        def fold_active(current):
            return attend_keys(
                current, key_block, offset, queries, query_docs, query_rows, lengths_row
            )

        def fold_passive(current):
            return current

        return (lax.cond(offset <= last_query, fold_active, fold_passive, running), None)

    carried, unused = lax.scan(fold_advance, carried, (blocks, offsets))
    return carried


def attend_back(
    queries, grad_heads, row_delta, log_sum, key_all, query_docs, query_rows, lengths_row
):
    row_count = key_all.shape[0]
    block_size = 512
    local_heads = queries.shape[1]
    blocks = key_all.reshape(row_count // block_size, block_size, 2, key_all.shape[2])
    offsets = block_size * jnp.arange(row_count // block_size, dtype=jnp.int32)
    last_query = query_rows[-1]
    scale = HEAD ** (-0.5)

    def attend_advance(grad_query, inputs):
        key_block, offset = inputs

        def attend_active(current):
            key_rows = offset + jnp.arange(block_size, dtype=jnp.int32)
            key_docs, unused = doc_table(lengths_row, key_rows)
            key_rot = key_block[:, 0].reshape(block_size, local_heads, HEAD)
            key_val = key_block[:, 1].reshape(block_size, local_heads, HEAD)
            scores = (
                jnp.einsum("qhe,khe->hqk", queries, key_rot, preferred_element_type=jnp.float32)
                * scale
            )
            allowed = (
                (query_docs[:, None] == key_docs[None, :])
                & (key_rows[None, :] <= query_rows[:, None])
            )[None]
            exp_scores = jnp.exp(jnp.where(allowed, scores - log_sum[..., None], NEG))
            grad_probs = jnp.einsum(
                "qhe,khe->hqk", grad_heads, key_val, preferred_element_type=jnp.float32
            )
            grad_scores = (exp_scores * (grad_probs - row_delta[..., None])).astype(jnp.bfloat16)
            new_grad = (
                current
                + jnp.einsum(
                    "hqk,khe->qhe", grad_scores, key_rot, preferred_element_type=jnp.float32
                )
                * scale
            )
            grad_key = (
                jnp.einsum("hqk,qhe->khe", grad_scores, queries, preferred_element_type=jnp.float32)
                * scale
            )
            grad_val = jnp.einsum(
                "hqk,qhe->khe",
                exp_scores.astype(jnp.bfloat16),
                grad_heads,
                preferred_element_type=jnp.float32,
            )
            return (
                new_grad,
                jnp.stack((grad_key, grad_val), axis=1).reshape(block_size, 2, local_heads * HEAD),
            )

        def attend_passive(current):
            return (current, jnp.zeros((block_size, 2, local_heads * HEAD), jnp.float32))

        return lax.cond(offset <= last_query, attend_active, attend_passive, grad_query)

    start_grad = jnp.zeros(queries.shape, jnp.float32)
    grad_query, grad_blocks = lax.scan(attend_advance, start_grad, (blocks, offsets))
    return (grad_query, grad_blocks.reshape(row_count, 2, key_all.shape[2]))


def body(tokens, lengths, w_qkv, b_qkv, w_out, w_gateup, w_down, norm_gain, norm_bias, cotangent):
    row_count = tokens.shape[0]
    query_rows = lax.axis_index("ctx") * row_count + jnp.arange(row_count, dtype=jnp.int32)
    lengths_row = lengths[0]
    query_docs, places = doc_table(lengths_row, query_rows)
    cosine_table, sine_table = angles(places)
    hidden = tokens.astype(jnp.float32)
    depth = 0
    matrices = (
        lax.all_gather(w_qkv[depth], ("shard", "ctx"), axis=0, tiled=True),
        lax.all_gather(b_qkv[depth], ("shard", "ctx"), axis=2, tiled=True),
        lax.all_gather(w_out[depth], ("shard", "ctx"), axis=1, tiled=True),
        lax.all_gather(w_gateup[depth], ("shard", "ctx"), axis=0, tiled=True),
        lax.all_gather(w_down[depth], ("shard", "ctx"), axis=1, tiled=True),
        lax.all_gather(norm_gain[depth], ("shard", "ctx"), axis=1, tiled=True),
        lax.all_gather(norm_bias[depth], ("shard", "ctx"), axis=1, tiled=True),
    )
    qkv_w, qkv_b, out_w, gate_up_w, down_w, norm_gains, shifts = matrices
    normed_one, normal_one, inverse_one = layer_norm(
        hidden, norm_gains[0].astype(jnp.float32), shifts[0].astype(jnp.float32)
    )
    normed_one = normed_one.astype(jnp.bfloat16)
    projected = jnp.einsum(
        "td,dce->tce", normed_one, qkv_w, preferred_element_type=jnp.float32
    ) + qkv_b.reshape(3, -1).astype(jnp.float32)
    local_heads = projected.shape[2] // HEAD
    queries = rotate(
        projected[:, 0].reshape(row_count, local_heads, HEAD), cosine_table, sine_table, 1.0
    ).astype(jnp.bfloat16)
    key_rot = rotate(
        projected[:, 1].reshape(row_count, local_heads, HEAD), cosine_table, sine_table, 1.0
    ).astype(jnp.bfloat16)
    key_local = jnp.stack(
        (key_rot.reshape(row_count, -1), projected[:, 2].astype(jnp.bfloat16)), axis=1
    )
    start_state = (
        jnp.full((local_heads, row_count), NEG, jnp.float32),
        jnp.zeros((local_heads, row_count), jnp.float32),
        jnp.zeros((local_heads, row_count, HEAD), jnp.float32),
    )
    folder = partial(
        fold_keys,
        queries=queries,
        query_docs=query_docs,
        query_rows=query_rows,
        lengths_row=lengths_row,
    )
    key_all = key_local
    running_max, running_sum, weighted = folder(
        start_state, lax.all_gather(key_local, "ctx", axis=0, tiled=True), jnp.int32(0)
    )
    log_sum = running_max + jnp.log(running_sum)
    mixed = jnp.transpose(weighted / running_sum[..., None], (1, 0, 2))
    heads_low = mixed.reshape(row_count, -1).astype(jnp.bfloat16)
    hidden_mid = hidden + lax.psum(
        jnp.dot(heads_low, out_w, preferred_element_type=jnp.float32).astype(jnp.bfloat16), "tp"
    ).astype(jnp.float32)
    normed_two, normal_two, inverse_two = layer_norm(
        hidden_mid, norm_gains[1].astype(jnp.float32), shifts[1].astype(jnp.float32)
    )
    normed_two = normed_two.astype(jnp.bfloat16)
    gate_up = jnp.einsum("td,dcf->tcf", normed_two, gate_up_w, preferred_element_type=jnp.float32)
    gate_part = gate_up[:, 0]
    up_part = gate_up[:, 1]
    activated = (gate_part * jax.nn.sigmoid(gate_part) * up_part).astype(jnp.bfloat16)
    hidden = hidden_mid + lax.psum(
        jnp.dot(activated, down_w, preferred_element_type=jnp.float32).astype(jnp.bfloat16), "tp"
    ).astype(jnp.float32)
    stored = [
        (
            matrices,
            normed_one,
            normal_one,
            inverse_one,
            queries,
            key_all,
            mixed,
            heads_low,
            log_sum,
            normed_two,
            normal_two,
            inverse_two,
            gate_part,
            up_part,
            activated,
        )
    ]
    gradient = cotangent.astype(jnp.float32)
    collected = [None] * LAYERS
    for depth in reversed(range(LAYERS)):
        (
            matrices,
            normed_one,
            normal_one,
            inverse_one,
            queries,
            key_all,
            mixed,
            heads_low,
            log_sum,
            normed_two,
            normal_two,
            inverse_two,
            gate_part,
            up_part,
            activated,
        ) = stored[depth]
        matrices = (
            lax.all_gather(w_qkv[depth], ("shard", "ctx"), axis=0, tiled=True),
            lax.all_gather(b_qkv[depth], ("shard", "ctx"), axis=2, tiled=True),
            lax.all_gather(w_out[depth], ("shard", "ctx"), axis=1, tiled=True),
            lax.all_gather(w_gateup[depth], ("shard", "ctx"), axis=0, tiled=True),
            lax.all_gather(w_down[depth], ("shard", "ctx"), axis=1, tiled=True),
            lax.all_gather(norm_gain[depth], ("shard", "ctx"), axis=1, tiled=True),
            lax.all_gather(norm_bias[depth], ("shard", "ctx"), axis=1, tiled=True),
        )
        qkv_w, qkv_b, out_w, gate_up_w, down_w, norm_gains, shifts = matrices
        local_heads = queries.shape[1]
        grad_low = gradient.astype(jnp.bfloat16)
        grad_down = jnp.einsum("tf,td->fd", activated, grad_low, preferred_element_type=jnp.float32)
        grad_act = jnp.einsum("td,fd->tf", grad_low, down_w, preferred_element_type=jnp.float32)
        logistic = jax.nn.sigmoid(gate_part)
        grad_gate = grad_act * up_part * logistic * (1.0 + gate_part * (1.0 - logistic))
        grad_up = grad_act * gate_part * logistic
        grad_gate_up = jnp.stack((grad_gate, grad_up), axis=1).astype(jnp.bfloat16)
        grad_gate_up_w = jnp.einsum(
            "td,tcf->dcf", normed_two, grad_gate_up, preferred_element_type=jnp.float32
        )
        grad_normed_two = lax.psum(
            jnp.einsum(
                "tcf,dcf->td", grad_gate_up, gate_up_w, preferred_element_type=jnp.float32
            ).astype(jnp.bfloat16),
            "tp",
        ).astype(jnp.float32)
        grad_norm_two, gain_two, shift_two = norm_back(
            grad_normed_two, normal_two, inverse_two, norm_gains[1].astype(jnp.float32)
        )
        grad_mid = gradient + grad_norm_two
        mid_low = grad_mid.astype(jnp.bfloat16)
        grad_out_w = jnp.einsum("te,td->ed", heads_low, mid_low, preferred_element_type=jnp.float32)
        grad_heads = jnp.einsum(
            "td,ed->te", mid_low, out_w, preferred_element_type=jnp.float32
        ).astype(jnp.bfloat16)
        grad_heads = grad_heads.reshape(row_count, local_heads, HEAD)
        row_delta = jnp.transpose(jnp.sum(grad_heads.astype(jnp.float32) * mixed, axis=-1))
        key_all = lax.all_gather(key_all, "ctx", axis=0, tiled=True)
        grad_query, grad_key_all = attend_back(
            queries, grad_heads, row_delta, log_sum, key_all, query_docs, query_rows, lengths_row
        )
        grad_key_val = lax.psum_scatter(
            grad_key_all.astype(jnp.bfloat16), "ctx", scatter_dimension=0, tiled=True
        ).astype(jnp.float32)
        query_back = rotate(grad_query, cosine_table, sine_table, -1.0).reshape(row_count, -1)
        key_back = rotate(
            grad_key_val[:, 0].reshape(row_count, local_heads, HEAD), cosine_table, sine_table, -1.0
        ).reshape(row_count, -1)
        grad_proj = jnp.stack((query_back, key_back, grad_key_val[:, 1]), axis=1).astype(
            jnp.bfloat16
        )
        grad_bias = jnp.sum(grad_proj.astype(jnp.float32), axis=0).reshape(3, local_heads, HEAD)
        grad_qkv_w = jnp.einsum(
            "td,tce->dce", normed_one, grad_proj, preferred_element_type=jnp.float32
        )
        grad_normed_one = lax.psum(
            jnp.einsum("tce,dce->td", grad_proj, qkv_w, preferred_element_type=jnp.float32).astype(
                jnp.bfloat16
            ),
            "tp",
        ).astype(jnp.float32)
        grad_norm_one, gain_one, shift_one = norm_back(
            grad_normed_one, normal_one, inverse_one, norm_gains[0].astype(jnp.float32)
        )
        gradient = grad_mid + grad_norm_one
        collected[depth] = (
            lax.psum_scatter(grad_qkv_w, ("shard", "ctx"), scatter_dimension=0, tiled=True),
            lax.psum_scatter(grad_bias, ("shard", "ctx"), scatter_dimension=2, tiled=True),
            lax.psum_scatter(grad_out_w, ("shard", "ctx"), scatter_dimension=1, tiled=True),
            lax.psum_scatter(grad_gate_up_w, ("shard", "ctx"), scatter_dimension=0, tiled=True),
            lax.psum_scatter(grad_down, ("shard", "ctx"), scatter_dimension=1, tiled=True),
            lax.psum_scatter(
                jnp.stack((gain_one, gain_two)), ("shard", "ctx"), scatter_dimension=1, tiled=True
            ),
            lax.psum_scatter(
                jnp.stack((shift_one, shift_two)), ("shard", "ctx"), scatter_dimension=1, tiled=True
            ),
        )
    stacks = [jnp.stack([collected[0][member]]) for member in range(7)]
    return (
        hidden.astype(jnp.bfloat16),
        gradient,
        stacks[0],
        stacks[1],
        stacks[2],
        stacks[3],
        stacks[4],
        stacks[5],
        stacks[6],
    )


def solution(mesh):
    return jax.shard_map(
        body,
        mesh=mesh,
        in_specs=(
            P(("shard", "ctx"), None),
            P("shard", None),
            P(None, ("shard", "ctx"), None, "tp"),
            P(None, None, "tp", ("shard", "ctx")),
            P(None, "tp", ("shard", "ctx")),
            P(None, ("shard", "ctx"), None, "tp"),
            P(None, "tp", ("shard", "ctx")),
            P(None, None, ("shard", "ctx")),
            P(None, None, ("shard", "ctx")),
            P(("shard", "ctx"), None),
        ),
        out_specs=(
            P(("shard", "ctx"), None),
            P(("shard", "ctx"), None),
            P(None, ("shard", "ctx"), None, "tp"),
            P(None, None, "tp", ("shard", "ctx")),
            P(None, "tp", ("shard", "ctx")),
            P(None, ("shard", "ctx"), None, "tp"),
            P(None, "tp", ("shard", "ctx")),
            P(None, None, ("shard", "ctx")),
            P(None, None, ("shard", "ctx")),
        ),
        check_vma=False,
    )
```

profile of v0, /device:TPU:9, one launch (start us, length us, event | category | flops | bytes accessed | tf_op | source)
XLA Modules:
  0.0 3471.2 jit_solution(929748074403614084)
XLA Ops:
  8.7 30.8 all-gather.3
  40.5 33.2 all-gather.1
  73.7 29.2 all-gather
  106.8 55.8 %all-gather.15.cloned.1.call-done = bf16[1,2048,3,1024]{3,1,2,0:T(8,128)(2,1)} async-done(((bf16[1,128,3,1024]{3,1,2,0:T(8,128)(2,1)}), bf16[1,2048,3,1024]{3,1,2,0:T(8,128)(2,1)}) %all-gather.15.cloned.1.call-update) | async-done | bytes 12582928 | tf_op jit(solution)/shard_map/all_gather | solution.py:192
  190.1 109.1 %all-gather.13.cloned.1.call-done = bf16[1536,2,1024]{2,0,1:T(8,128)(2,1)} async-done(((bf16[384,2,1024]{2,0,1:T(8,128)(2,1)}), bf16[1536,2,1024]{2,0,1:T(8,128)(2,1)}) %all-gather.13.cloned.1.call-update) | async-done | bytes 6291472 | tf_op jit(solution)/shard_map/all_gather | solution.py:232
  308.1 32.3 while.31
  310.0 13.2 conditional.6
  325.2 13.2 conditional.6
  341.6 48.3 %all-gather.17.cloned.1.call-done = bf16[1,1024,2048]{2,1,0:T(8,128)(2,1)} async-done(((bf16[1,1024,128]{2,1,0:T(8,128)(2,1)}), bf16[1,1024,2048]{2,1,0:T(8,128)(2,1)}) %all-gather.17.cloned.1.call-update) | async-done | bytes 4194320 | tf_op jit(solution)/shard_map/all_gather | solution.py:194
  399.0 18.0 all-reduce.6.cloned.1.call-done
  419.8 250.4 %all-gather.19.cloned.1.call-done = bf16[1,2048,2,2816]{3,1,2,0:T(8,128)(2,1)} async-done(((bf16[1,128,2,2816]{3,1,2,0:T(8,128)(2,1)}), bf16[1,2048,2,2816]{3,1,2,0:T(8,128)(2,1)}) %all-gather.19.cloned.1.call-update) | async-done | bytes 23068688 | tf_op jit(solution)/shard_map/all_gather | solution.py:195
  670.2 16.5 fusion.25
  686.7 167.2 %all-gather.21.cloned.1.call-done = bf16[1,2816,2048]{2,1,0:T(8,128)(2,1)} async-done(((bf16[1,2816,128]{2,1,0:T(8,128)(2,1)}), bf16[1,2816,2048]{2,1,0:T(8,128)(2,1)}) %all-gather.21.cloned.1.call-update) | async-done | bytes 11534352 | tf_op jit(solution)/shard_map/all_gather | solution.py:196
  853.9 13.2 fusion.75
  867.1 15.7 bitcast_convert_fusion.1
  883.1 21.5 all-reduce.8.cloned.1.call-done
  917.6 71.9 %while.32 = (s32[]{:T(128)}, f32[384,16,64]{0,2,1:T(8,128)}, bf16[3,512,2,1024]{1,3,2,0:T(8,128)(2,1)}, s32[3]{0:T(128)S(1)}, s32[]{:T(128)}, /*index=5*/s32[384...) while((s32[]{:T(128)}, f32[384,16,64]{0,2,1:T(8,128)}, ...), condition=%wide.region_26.27_spmd.clone, body=%wide.region_21.26_spmd.clone.sunk | while | flops 2048201600 | bytes 98199944 | solution.py:179
  919.5 30.8 conditional.7
  953.7 30.8 conditional.7
  998.8 10.8 fusion.66
  1010.5 129.9 %reduce-scatter.12.cloned.1.call-done = bf16[384,2,1024]{2,0,1:T(8,128)(2,1)} async-done(((bf16[1536,2,1024]{2,0,1:T(8,128)(2,1)}), bf16[384,2,1024]{2,0,1:T(8,128)(2,1)}) %reduce-scatter.12.cloned.1.call-update) | async-done | bytes 1572880 | tf_op jit(solution)/shard_map/reduce_scatter | solution.py:332
  1148.0 9.8 bitcast_convert_fusion
  1157.9 24.6 all-reduce.10.cloned.1.call-done
  1188.6 20.8 fusion.72
  1217.5 12.7 fusion.102
  1230.9 13.5 fusion.87
  1248.6 61.4 %all-reduce = f32[3,16,64]{1,0,2:T(4,128)S(1)} all-reduce(f32[3,16,64]{1,0,2:T(4,128)S(1)} %copy.125), channel_id=11, replica_groups=mesh['shard'=4,'ctx'=4,'tp'=2] {'shard','ctx'}, use_global_device_ids=true, to_apply=%region_33.34.clone | all-reduce | flops 3072 | bytes 24576
  1317.2 12.6 reduce-scatter.24.cloned.1.call-done
  1331.3 948.8 %reduce-scatter.18.cloned.1.call-done = f32[128,2,2816]{2,0,1:T(8,128)} async-done(((f32[2048,2,2816]{2,0,1:T(8,128)}), f32[128,2,2816]{2,0,1:T(8,128)}) %reduce-scatter.18.cloned.1.call-update) | async-done | bytes 2883600 | tf_op jit(solution)/shard_map/reduce_scatter | solution.py:360
  2285.7 180.0 %reduce-scatter.16.cloned.1.call-done = f32[1024,128]{1,0:T(8,128)} async-done(((f32[1024,2048]{1,0:T(8,128)}), f32[1024,128]{1,0:T(8,128)}) %reduce-scatter.16.cloned.1.call-update) | async-done | bytes 524304 | tf_op jit(solution)/shard_map/reduce_scatter | solution.py:359
  2465.7 477.9 %reduce-scatter.20.cloned.1.call-done = f32[2816,128]{1,0:T(8,128)} async-done(((f32[2816,2048]{1,0:T(8,128)}), f32[2816,128]{1,0:T(8,128)}) %reduce-scatter.20.cloned.1.call-update) | async-done | bytes 1441808 | tf_op jit(solution)/shard_map/reduce_scatter | solution.py:361
  2943.6 520.9 %reduce-scatter.14.cloned.1.call-done = f32[128,3,1024]{2,0,1:T(8,128)} async-done(((f32[2048,3,1024]{2,0,1:T(8,128)}), f32[128,3,1024]{2,0,1:T(8,128)}) %reduce-scatter.14.cloned.1.call-update) | async-done | bytes 1572880 | tf_op jit(solution)/shard_map/reduce_scatter | solution.py:357
  (265 shorter events, 214.8 us)
Async XLA Ops:
  7.2 98.2 %copy-start = (bf16[384,2048]{1,0:T(8,128)(2,1)S(1)}, bf16[384,2048]{1,0:T(8,128)(2,1)}, u32[]{:S(2)}) copy-start(bf16[384,2048]{1,0:T(8,128)(2,1)} %param.18) | copy-start | bytes 4718596
  7.2 155.4 %all-gather.15.cloned.1.call-start = ((), (), s32[]{:S(2)}) async-start(), calls=%async_computation.15 | async-start | bytes 13369344 | tf_op jit(solution)/shard_map/all_gather | solution.py:192
  7.9 291.3 %all-gather.13.cloned.1.call-start = ((), (), s32[]{:S(2)}) async-start(), calls=%async_computation.7 | async-start | bytes 7864320 | tf_op jit(solution)/shard_map/all_gather | solution.py:232
  105.4 65.3 %copy-start.24 = (f32[384]{0:T(512)}, f32[384]{0:T(512)S(1)}, u32[]{:S(2)}) copy-start(f32[384]{0:T(512)S(1)} %broadcast_multiply_fusion.6) | copy-start | bytes 4612
  106.0 64.8 %copy-start.28 = (f32[384]{0:T(512)}, f32[384]{0:T(512)S(1)}, u32[]{:S(2)}) copy-start(f32[384]{0:T(512)S(1)} %add_rsqrt_fusion.1) | copy-start | bytes 4612
  106.7 73.2 %copy-start.22 = (f32[384,8]{0,1:T(8,128)}, f32[384,8]{0,1:T(8,128)S(1)}, u32[]{:S(2)}) copy-start(f32[384,8]{0,1:T(8,128)S(1)} %get-tuple-element.588) | copy-start | bytes 36868
  106.8 64.0 %copy-start.18 = (f32[1,1,2048]{2,1,0:T(1,128)}, f32[1,1,2048]{2,1,0:T(1,128)S(1)}, u32[]{:S(2)}) copy-start(f32[1,1,2048]{2,1,0:T(1,128)S(1)} %get-tuple-element.584) | copy-start | bytes 24580
  106.8 563.5 %copy-start.35 = (f32[1,1,2048]{2,1,0:T(1,128)}, f32[1,1,2048]{2,1,0:T(1,128)S(1)}, u32[]{:S(2)}) copy-start(f32[1,1,2048]{2,1,0:T(1,128)S(1)} %get-tuple-element.585) | copy-start | bytes 24580
  106.8 64.0 %copy-start.16 = (f32[1,1,2048]{2,1,0:T(1,128)}, f32[1,1,2048]{2,1,0:T(1,128)S(1)}, u32[]{:S(2)}) copy-start(f32[1,1,2048]{2,1,0:T(1,128)S(1)} %get-tuple-element.582) | copy-start | bytes 24580
  106.8 801.6 %copy-start.20 = (f32[1,1,2048]{2,1,0:T(1,128)}, f32[1,1,2048]{2,1,0:T(1,128)S(1)}, u32[]{:S(2)}) copy-start(f32[1,1,2048]{2,1,0:T(1,128)S(1)} %get-tuple-element.583) | copy-start | bytes 24580
  186.1 203.8 %all-gather.17.cloned.1.call-start = ((), (), s32[]{:S(2)}) async-start(), calls=%async_computation.16 | async-start | bytes 4456448 | tf_op jit(solution)/shard_map/all_gather | solution.py:194
  186.8 230.2 %all-reduce.6.cloned.1.call-start = ((), (), s32[]{:S(2)}) async-start(), calls=%async_computation.8 | async-start | bytes 3145728 | tf_op jit(solution)/shard_map/psum | solution.py:237
  340.4 54.9 %copy-start.8 = (f32[16,384,64]{1,2,0:T(8,128)}, f32[16,384,64]{1,2,0:T(8,128)S(1)}, u32[]{:S(2)}) copy-start(f32[16,384,64]{1,2,0:T(8,128)S(1)} %get-tuple-element.260) | copy-start | bytes 4718596
  395.3 274.9 %all-gather.19.cloned.1.call-start = ((), (), s32[]{:S(2)}) async-start(), calls=%async_computation.17 | async-start | bytes 24510464 | tf_op jit(solution)/shard_map/all_gather | solution.py:195
  398.0 455.9 %all-gather.21.cloned.1.call-start = ((), (), s32[]{:S(2)}) async-start(), calls=%async_computation.18 | async-start | bytes 12255232 | tf_op jit(solution)/shard_map/all_gather | solution.py:196
  398.6 506.0 %all-reduce.8.cloned.1.call-start = ((), (), s32[]{:S(2)}) async-start(), calls=%async_computation.9 | async-start | bytes 3145728 | tf_op jit(solution)/shard_map/psum | solution.py:311
  419.1 489.4 %copy-start.26 = (f32[384]{0:T(512)}, f32[384]{0:T(512)S(1)}, u32[]{:S(2)}) copy-start(f32[384]{0:T(512)S(1)} %broadcast_multiply_fusion.5) | copy-start | bytes 4612
  419.8 488.6 %copy-start.30 = (f32[384]{0:T(512)}, f32[384]{0:T(512)S(1)}, u32[]{:S(2)}) copy-start(f32[384]{0:T(512)S(1)} %add_rsqrt_fusion) | copy-start | bytes 4612
  882.9 257.5 %reduce-scatter.12.cloned.1.call-start = ((), (), s32[]{:S(2)}) async-start(), calls=%async_computation.10 | async-start | bytes 7864320 | tf_op jit(solution)/shard_map/reduce_scatter | solution.py:332
  998.3 184.1 %all-reduce.10.cloned.1.call-start = ((), (), s32[]{:S(2)}) async-start(), calls=%async_computation.21 | async-start | bytes 6291456 | tf_op jit(solution)/shard_map/psum | solution.py:248
  1157.8 24.7 copy-start.1
  1157.8 24.7 copy-start.17
  1157.8 24.7 copy-start.25
  1157.8 24.7 copy-start.29
  1157.8 27.7 copy-start.34
  1157.8 29.2 copy-start.33
  1157.8 157.9 %reduce-scatter.22.cloned.1.call-start = ((), (), s32[]{:S(2)}) async-start(), calls=%async_computation.19 | async-start | bytes 1114112
  1187.0 142.9 %reduce-scatter.24.cloned.1.call-start = ((), (), s32[]{:S(2)}) async-start(), calls=%async_computation.20 | async-start | bytes 1114112
  1188.5 1091.6 %reduce-scatter.18.cloned.1.call-start = ((), (), s32[]{:S(2)}) async-start(), calls=%async_computation.13 | async-start | bytes 49020928 | tf_op jit(solution)/shard_map/reduce_scatter | solution.py:360
  1209.4 1256.3 %reduce-scatter.16.cloned.1.call-start = ((), (), s32[]{:S(2)}) async-start(), calls=%async_computation.12 | async-start | bytes 8912896 | tf_op jit(solution)/shard_map/reduce_scatter | solution.py:359
  1217.5 1726.1 %reduce-scatter.20.cloned.1.call-start = ((), (), s32[]{:S(2)}) async-start(), calls=%async_computation.14 | async-start | bytes 24510464 | tf_op jit(solution)/shard_map/reduce_scatter | solution.py:361
  1230.2 2234.2 %reduce-scatter.14.cloned.1.call-start = ((), (), s32[]{:S(2)}) async-start(), calls=%async_computation.11 | async-start | bytes 26738688 | tf_op jit(solution)/shard_map/reduce_scatter | solution.py:357
  (25 other events, 115.9 us)
Sparse Core Ops, SparseCore 0:
  10.8 151.7 all-gather.14
  186.2 112.9 all-gather.12
  301.9 87.9 all-gather.16
  395.4 21.5 all-reduce.5
  420.7 249.5 all-gather.18
  673.2 180.7 all-gather.20
  883.0 21.5 all-reduce.7
  998.5 141.8 reduce-scatter.11
  1158.0 24.4 all-reduce.9
  1187.1 64.0 reduce-scatter.21
  1253.4 76.3 reduce-scatter.23
  1332.1 947.8 reduce-scatter.17
  2283.0 182.6 reduce-scatter.15
  2468.5 474.9 reduce-scatter.19
  2946.4 517.9 reduce-scatter.13
where the time goes:
time: 3480 us; the launch traced here: 3470 us
  waiting for transfers between devices  2970 us (85%)
  matrix products  206 us (6%)
  blocking collectives  155 us (4%)
  local copies, waits for them, and re-layouts  74.2 us (2%)
  other arithmetic  43.4 us (1%)
    reduce_scatter x1, waiting for transfers between devices, body(): lax.psum_scatter(grad_gate_up_w, ('shard', 'ctx'), scatter_dimension=0, t...  949 us
    reduce_scatter x1, waiting for transfers between devices, body(): lax.psum_scatter(grad_qkv_w, ('shard', 'ctx'), scatter_dimension=0, tiled...  521 us
    reduce_scatter x1, waiting for transfers between devices, body(): lax.psum_scatter(grad_down, ('shard', 'ctx'), scatter_dimension=1, tiled=...  478 us
    all_gather x1, waiting for transfers between devices, body(): lax.all_gather(w_gateup[depth], ('shard', 'ctx'), axis=0, tiled=True)  250 us
    reduce_scatter x1, waiting for transfers between devices, body(): lax.psum_scatter(grad_out_w, ('shard', 'ctx'), scatter_dimension=1, tiled...  180 us
    all_gather x1, waiting for transfers between devices, body(): lax.all_gather(w_down[depth], ('shard', 'ctx'), axis=1, tiled=True)  167 us
    reduce_scatter x1, waiting for transfers between devices, body(): lax.psum_scatter(grad_key_all.astype(jnp.bfloat16), 'ctx', scatter_dimens...  130 us
    all_gather x1, waiting for transfers between devices, body(): lax.all_gather(key_local, 'ctx', axis=0, tiled=True)  109 us
  transfers between devices with their start and end apart: 15, of which 14 were waited for; matrix products, arithmetic and copies ran while one was open for 4% of the time, Pallas kernels for 0%

commit v1 on v0

v1 whole, which is shorter than its diff:
```python
from functools import partial

import jax
import jax.numpy as jnp
from jax import lax
from jax.experimental import pallas as pl
from jax.experimental.pallas import tpu as pltpu
from jax.sharding import PartitionSpec as P

HEAD = 64
ROT = 16
EPS = 1e-05
NEG = -1e30
BASE = 10000.0
BF = jnp.bfloat16
F32 = jnp.float32
BLK = 256


def mm(a, b, ca, cb):
    return lax.dot_general(a, b, (((ca,), (cb,)), ((), ())), preferred_element_type=F32)


def turn(x, cos, lo, hi):
    n = x.shape[-1]
    return x * cos + pltpu.roll(x, n - ROT // 2, 1) * lo + pltpu.roll(x, ROT // 2, 1) * hi


def attend_kernel(
    first_ref, q_ref, k_ref, v_ref, cos_ref, lo_ref, hi_ref, begin_ref,
    qo_ref, ko_ref, vo_ref, o_ref, lse_ref, vt_ref,
):
    rows = q_ref.shape[0]
    nb = rows // BLK
    lane = lax.broadcasted_iota(jnp.int32, (BLK, 128), 1)
    left = lane < HEAD
    key_at = lax.broadcasted_iota(jnp.int32, (BLK, BLK), 0)
    query_at = lax.broadcasted_iota(jnp.int32, (1, BLK), 1)

    @pl.loop(0, nb)
    def _(i):
        r = pl.ds(pl.multiple_of(i * BLK, BLK), BLK)
        cos, lo, hi = cos_ref[r, :], lo_ref[r, :], hi_ref[r, :]
        qo_ref[r, :] = turn(q_ref[r, :], cos, lo, hi).astype(BF) * jnp.asarray(HEAD**-0.5, BF)
        ko_ref[r, :] = turn(k_ref[r, :], cos, lo, hi).astype(BF)
        v = v_ref[r, :]
        vo_ref[r, :] = v.astype(BF)
        vt_ref[:, r] = v.T.astype(BF)

    @pl.loop(0, nb)
    def _(i):
        r = pl.ds(pl.multiple_of(i * BLK, BLK), BLK)
        q = qo_ref[r, :]
        zero = jnp.zeros_like(q)
        qs = (jnp.where(left, q, zero), jnp.where(left, zero, q))
        begin = begin_ref[0:1, r]
        here = query_at + i * BLK

        def step(j, carry):
            w = pl.ds(pl.multiple_of(j * BLK, BLK), BLK)
            k, vt = ko_ref[w, :], vt_ref[:, w]
            key = key_at + j * BLK
            seen = (key <= here) & (key >= begin)
            out = []
            for h in range(2):
                m, l, acc = carry[h]
                s = jnp.where(seen, mm(k, qs[h], 1, 1), NEG)
                top = jnp.maximum(m, jnp.max(s, axis=0, keepdims=True))
                fade = jnp.exp(m - top)
                e = jnp.exp(s - top)
                out.append(
                    (top, l * fade + jnp.sum(e, axis=0, keepdims=True), acc * fade + mm(vt, e.astype(BF), 1, 0))
                )
            return tuple(out)

        start = (
            jnp.full((1, BLK), NEG, F32), jnp.zeros((1, BLK), F32), jnp.zeros((128, BLK), F32)
        )
        done = lax.fori_loop(first_ref[i], i + 1, step, (start, start))
        parts = []
        for h in range(2):
            m, l, acc = done[h]
            parts.append((acc / l).T)
            lse_ref[0, h : h + 1, r] = m + jnp.log(l)
        o_ref[r, :] = jnp.where(left, parts[0], parts[1]).astype(BF)


def attend(qkv, tables, begin, first):
    rows, wide = qkv.shape
    pairs = wide // 3 // 128
    cos, lo, hi = tables
    full = pl.BlockSpec((rows, 128), lambda j, *_: (0, 0))

    def col(base):
        return pl.BlockSpec((rows, 128), lambda j, *_: (0, base + j))

    half = jax.ShapeDtypeStruct((rows, wide // 3), BF)
    return pl.pallas_call(
        attend_kernel,
        grid_spec=pltpu.PrefetchScalarGridSpec(
            num_scalar_prefetch=1,
            grid=(pairs,),
            in_specs=[
                col(0), col(pairs), col(2 * pairs), full, full, full,
                pl.BlockSpec((1, rows), lambda j, *_: (0, 0)),
            ],
            out_specs=[col(0)] * 4 + [pl.BlockSpec((1, 2, rows), lambda j, *_: (j, 0, 0))],
            scratch_shapes=[pltpu.VMEM((128, rows), BF)],
        ),
        out_shape=[half] * 4 + [jax.ShapeDtypeStruct((pairs, 2, rows), F32)],
        compiler_params=pltpu.CompilerParams(vmem_limit_bytes=48 << 20),
        cost_estimate=pl.CostEstimate(
            flops=4 * rows * rows * wide // 3, bytes_accessed=rows * wide * 8, transcendentals=0
        ),
        name="attend",
    )(first, qkv, qkv, qkv, cos, lo, hi, begin)


def attend_back_kernel(
    first_ref, q_ref, k_ref, v_ref, o_ref, do_ref, lse_ref, cos_ref, lo_ref, hi_ref, begin_ref,
    out_ref, kt_ref, dk_ref, dv_ref,
):
    rows = q_ref.shape[0]
    nb = rows // BLK
    pair, pairs = pl.program_id(0), pl.num_programs(0)
    lane = lax.broadcasted_iota(jnp.int32, (BLK, 128), 1)
    left = lane < HEAD
    key_at = lax.broadcasted_iota(jnp.int32, (BLK, BLK), 0)
    query_at = lax.broadcasted_iota(jnp.int32, (1, BLK), 1)

    def column(base):
        return pl.ds(pl.multiple_of((base * pairs + pair) * 128, 128), 128)

    @pl.loop(0, nb)
    def _(i):
        r = pl.ds(pl.multiple_of(i * BLK, BLK), BLK)
        kt_ref[:, r] = k_ref[r, :].astype(F32).T.astype(BF)
        dk_ref[r, :] = jnp.zeros((BLK, 128), F32)
        dv_ref[r, :] = jnp.zeros((BLK, 128), F32)

    @pl.loop(0, nb)
    def _(i):
        r = pl.ds(pl.multiple_of(i * BLK, BLK), BLK)
        q, do = q_ref[r, :], do_ref[r, :]
        zero = jnp.zeros_like(q)
        qs = (jnp.where(left, q, zero), jnp.where(left, zero, q))
        dos = (jnp.where(left, do, zero), jnp.where(left, zero, do))
        prod = (do.astype(F32) * o_ref[r, :].astype(F32)).T
        deltas = (
            jnp.sum(prod[:HEAD], axis=0, keepdims=True), jnp.sum(prod[HEAD:], axis=0, keepdims=True)
        )
        lses = (lse_ref[0, 0:1, r], lse_ref[0, 1:2, r])
        begin = begin_ref[0:1, r]
        here = query_at + i * BLK

        def step(j, carry):
            w = pl.ds(pl.multiple_of(j * BLK, BLK), BLK)
            k, v, kt = k_ref[w, :], v_ref[w, :], kt_ref[:, w]
            key = key_at + j * BLK
            seen = (key <= here) & (key >= begin)
            out = []
            dk = dv = None
            for h in range(2):
                prob = jnp.exp(jnp.where(seen, mm(k, qs[h], 1, 1) - lses[h], NEG))
                ds = (prob * (mm(v, dos[h], 1, 1) - deltas[h])).astype(BF)
                out.append(carry[h] + mm(kt, ds, 1, 0))
                dk_h, dv_h = mm(ds, qs[h], 1, 0), mm(prob.astype(BF), dos[h], 1, 0)
                dk, dv = (dk_h, dv_h) if h == 0 else (dk + dk_h, dv + dv_h)
            dk_ref[w, :] += dk
            dv_ref[w, :] += dv
            return tuple(out)

        start = jnp.zeros((128, BLK), F32)
        a, b = lax.fori_loop(first_ref[i], i + 1, step, (start, start))
        dq = jnp.where(left, a.T, b.T) * (HEAD**-0.5)
        out_ref[r, column(0)] = turn(dq, cos_ref[r, :], -lo_ref[r, :], -hi_ref[r, :]).astype(BF)

    @pl.loop(0, nb)
    def _(i):
        r = pl.ds(pl.multiple_of(i * BLK, BLK), BLK)
        out_ref[r, column(1)] = turn(dk_ref[r, :], cos_ref[r, :], -lo_ref[r, :], -hi_ref[r, :]).astype(BF)
        out_ref[r, column(2)] = dv_ref[r, :].astype(BF)


def attend_back(q, k, v, o, do, lse, tables, begin, first):
    rows, wide = q.shape
    pairs = wide // 128
    cos, lo, hi = tables
    full = pl.BlockSpec((rows, 128), lambda j, *_: (0, 0))
    col = pl.BlockSpec((rows, 128), lambda j, *_: (0, j))
    return pl.pallas_call(
        attend_back_kernel,
        grid_spec=pltpu.PrefetchScalarGridSpec(
            num_scalar_prefetch=1,
            grid=(pairs,),
            in_specs=[
                col, col, col, col, col, pl.BlockSpec((1, 2, rows), lambda j, *_: (j, 0, 0)),
                full, full, full, pl.BlockSpec((1, rows), lambda j, *_: (0, 0)),
            ],
            out_specs=pl.BlockSpec((rows, 3 * wide), lambda j, *_: (0, 0)),
            scratch_shapes=[
                pltpu.VMEM((128, rows), BF), pltpu.VMEM((rows, 128), F32), pltpu.VMEM((rows, 128), F32)
            ],
        ),
        out_shape=jax.ShapeDtypeStruct((rows, 3 * wide), BF),
        compiler_params=pltpu.CompilerParams(vmem_limit_bytes=48 << 20),
        cost_estimate=pl.CostEstimate(
            flops=10 * rows * rows * wide, bytes_accessed=rows * wide * 16, transcendentals=0
        ),
        name="attend_back",
    )(first, q, k, v, o, do, lse, cos, lo, hi, begin)


def doc_tables(lengths_row, rows):
    row_ids = jnp.arange(rows, dtype=jnp.int32)
    ends = jnp.cumsum(lengths_row, dtype=jnp.int32)
    begins = ends - lengths_row
    inside = (row_ids[:, None] >= begins[None, :]) & (row_ids[:, None] < ends[None, :])
    begin = jnp.sum(jnp.where(inside, begins[None, :], 0), axis=1, dtype=jnp.int32)
    half = ROT // 2
    freq = BASE ** (-2.0 * jnp.arange(half, dtype=F32) / ROT)
    phase = (row_ids - begin).astype(F32)[:, None] * freq[None, :]
    cos, sin = jnp.cos(phase), jnp.sin(phase)
    rest = jnp.ones((rows, HEAD - ROT), F32)
    none = jnp.zeros((rows, half), F32)
    cos_t = jnp.concatenate((cos, cos, rest), axis=1)
    lo_t = jnp.concatenate((-sin, none, 0 * rest), axis=1)
    hi_t = jnp.concatenate((none, sin, 0 * rest), axis=1)
    tables = tuple(jnp.concatenate((t, t), axis=1) for t in (cos_t, lo_t, hi_t))
    return begin, tables


def layer_norm(values, gain, shift):
    center = values - jnp.mean(values, axis=-1, keepdims=True)
    inverse = lax.rsqrt(jnp.mean(center * center, axis=-1, keepdims=True) + EPS)
    normal = center * inverse
    return (normal * gain + shift, normal, inverse)


def norm_back(gradient, normal, inverse, gain):
    scaled = gradient * gain
    centered = (
        scaled
        - jnp.mean(scaled, axis=-1, keepdims=True)
        - normal * jnp.mean(scaled * normal, axis=-1, keepdims=True)
    )
    return (inverse * centered, jnp.sum(gradient * normal, axis=0), jnp.sum(gradient, axis=0))


def make_body(S, C, T):
    assert S == C

    def body(tokens, lengths, w_qkv, b_qkv, w_out, w_gateup, w_down, norm_gain, norm_bias, cotangent):
        p, z, c = lax.axis_index("shard"), lax.axis_index("ctx"), lax.axis_index("tp")
        R, D = tokens.shape
        m = R // (S * T)
        nb = D // (S * C)
        L = R * C

        def permute(x):
            return x.reshape(x.shape[0], S, C, nb).swapaxes(1, 2).reshape(x.shape)

        def unpermute(x):
            return x.reshape(x.shape[0], C, S, nb).swapaxes(1, 2).reshape(x.shape)

        def to_plane(x):
            mine = lax.dynamic_index_in_dim(x.reshape(S, T, m, D), c, 1, keepdims=False)
            moved = lax.all_to_all(mine, "shard", 0, 0, tiled=True)
            moved = lax.all_to_all(moved, "ctx", 0, 0, tiled=True)
            return permute(moved.reshape(C * m, D))

        def from_plane(x):
            x = unpermute(x).reshape(C, m, D)
            x = lax.all_to_all(x, "ctx", 0, 0, tiled=True)
            x = lax.all_to_all(x, "shard", 0, 0, tiled=True)
            x = lax.all_gather(x, "tp", axis=0)
            return x.swapaxes(0, 1).reshape(R, D)

        def gather(x):
            x = lax.all_gather(x, ("shard", "tp"), axis=0, tiled=True)
            return x.reshape(S * T, C, m, D).swapaxes(0, 1).reshape(L, D)

        def scatter(x):
            x = x.astype(BF).reshape(C, S * T, m, D).swapaxes(0, 1).reshape(L, D)
            return lax.psum_scatter(x, ("shard", "tp"), scatter_dimension=0, tiled=True).astype(F32)

        def fetch(w):
            n = w.shape[2]
            w = lax.all_to_all(w, "shard", 0, 0, tiled=True)
            return lax.all_gather(w.reshape(S * nb, n), "ctx", axis=0, tiled=True)

        def give(g):
            n = g.shape[1]
            g = lax.psum_scatter(g.astype(BF), "ctx", scatter_dimension=0, tiled=True)
            return lax.all_to_all(g.reshape(S, nb, n), "shard", 0, 0, tiled=True).astype(F32)

        hn = w_qkv.shape[3] // S
        fn = w_gateup.shape[3] // S
        heads = hn // HEAD

        small = jnp.concatenate(
            (
                norm_gain[0].astype(F32).reshape(-1),
                norm_bias[0].astype(F32).reshape(-1),
                b_qkv[0].astype(F32).reshape(-1),
                lengths[0].astype(F32),
            )
        )
        small = lax.all_gather(small, ("ctx", "shard"), axis=0)
        gains = small[:, : 2 * nb].reshape(C * S, 2, nb).swapaxes(0, 1).reshape(2, D)
        shifts = small[:, 2 * nb : 4 * nb].reshape(C * S, 2, nb).swapaxes(0, 1).reshape(2, D)
        nbias = b_qkv[0].size
        bias = small[:, 4 * nb : 4 * nb + nbias].reshape(C, S, 3, S * heads, -1)
        bias = lax.dynamic_slice_in_dim(bias, p * heads, heads, 3)
        bias = bias.transpose(2, 3, 1, 0, 4).reshape(1, 3 * hn)
        lengths_row = lax.dynamic_index_in_dim(
            small[:S, 4 * nb + nbias :], z, 0, keepdims=False
        ).astype(jnp.int32)

        begin, tables = doc_tables(lengths_row, L)
        first = begin[::BLK] // BLK
        begin = begin[None, :]

        tok = to_plane(tokens)
        wq = fetch(w_qkv[0].reshape(nb, 3, S, hn).transpose(2, 0, 1, 3).reshape(S, nb, 3 * hn))
        wo = fetch(w_out[0].reshape(S, hn, nb).swapaxes(1, 2))
        wg = fetch(w_gateup[0].reshape(nb, 2, S, fn).transpose(2, 0, 1, 3).reshape(S, nb, 2 * fn))
        wd = fetch(w_down[0].reshape(S, fn, nb).swapaxes(1, 2))

        hidden = tok.astype(F32)
        n1, normal1, inverse1 = layer_norm(hidden, gains[0], shifts[0])
        n1 = gather(n1.astype(BF))
        qkv = mm(n1, wq, 1, 0) + bias
        q, k, v, o, lse = attend(qkv, tables, begin, first)
        mid = hidden + scatter(mm(o, wo, 1, 1))
        n2, normal2, inverse2 = layer_norm(mid, gains[1], shifts[1])
        n2 = gather(n2.astype(BF))
        gu = mm(n2, wg, 1, 0)
        gate, up = gu[:, :fn], gu[:, fn:]
        logistic = jax.nn.sigmoid(gate)
        act = (gate * logistic * up).astype(BF)
        out = mid + scatter(mm(act, wd, 1, 1))
        out = from_plane(out.astype(BF))

        grad_own = to_plane(cotangent)
        gb = gather(grad_own)
        gw_down = give(mm(gb, act, 0, 0))
        dact = mm(gb, wd, 1, 0)
        dgate = dact * up * logistic * (1.0 + gate * (1.0 - logistic))
        dup = dact * gate * logistic
        dgu = jnp.concatenate((dgate, dup), axis=1).astype(BF)
        gw_gateup = give(mm(n2, dgu, 0, 0))
        dn2 = scatter(mm(dgu, wg, 1, 1))
        dmid, gain2, shift2 = norm_back(dn2, normal2, inverse2, gains[1])
        dmid = grad_own.astype(F32) + dmid
        gb1 = gather(dmid.astype(BF))
        gw_out = give(mm(gb1, o, 0, 0))
        do = mm(gb1, wo, 1, 0).astype(BF)
        dqkv = attend_back(q, k, v, o, do, lse, tables, begin, first)
        gbias = jnp.sum(dqkv.astype(F32), axis=0)
        gw_qkv = give(mm(n1, dqkv, 0, 0))
        dn1 = scatter(mm(dqkv, wq, 1, 1))
        dtok, gain1, shift1 = norm_back(dn1, normal1, inverse1, gains[0])
        gtok = from_plane((dmid + dtok).astype(BF)).astype(F32)

        slots = jnp.zeros((T * S, 3 * hn), F32)
        slots = lax.dynamic_update_slice(slots, gbias[None], (c * S + p, 0))
        sums = lax.psum(
            jnp.concatenate((gain1, gain2, shift1, shift2, slots.reshape(-1))), ("shard", "ctx", "tp")
        )
        norms = lax.dynamic_index_in_dim(
            sums[: 4 * D].reshape(4, C * S, nb), z * S + p, 1, keepdims=False
        )
        slots = lax.dynamic_index_in_dim(sums[4 * D :].reshape(T, S, 3, heads, S * C, -1), c, 0, keepdims=False)
        slots = lax.dynamic_index_in_dim(slots, p * C + z, 3, keepdims=False)
        gbias = slots.swapaxes(0, 1).reshape(3, S * heads, -1)

        return (
            out,
            gtok,
            gw_qkv.reshape(S, nb, 3, hn).transpose(1, 2, 0, 3).reshape(w_qkv.shape),
            gbias[None],
            gw_out.swapaxes(1, 2).reshape(w_out.shape),
            gw_gateup.reshape(S, nb, 2, fn).transpose(1, 2, 0, 3).reshape(w_gateup.shape),
            gw_down.swapaxes(1, 2).reshape(w_down.shape),
            norms[:2][None],
            norms[2:][None],
        )

    return body


def solution(mesh):
    both = ("shard", "ctx")
    specs = (
        P(None, both, None, "tp"),
        P(None, None, "tp", both),
        P(None, "tp", both),
        P(None, both, None, "tp"),
        P(None, "tp", both),
        P(None, None, both),
        P(None, None, both),
    )
    return jax.shard_map(
        make_body(mesh.shape["shard"], mesh.shape["ctx"], mesh.shape["tp"]),
        mesh=mesh,
        in_specs=(P(both, None), P("shard", None)) + specs + (P(both, None),),
        out_specs=(P(both, None), P(both, None)) + specs,
        check_vma=False,
    )
```

time: 3480 us -> 1260 us (0.36)
  waiting for transfers between devices: 2970 us -> 637 us
  matrix products: 206 us -> 111 us
  blocking collectives: 155 us -> 236 us
  Pallas kernels: 0 us -> 70.9 us
  starting transfers between devices: 1.95 us -> 41.2 us
    reduce_scatter x5 -> x8, waiting for transfers between devices: 2260 us -> 282 us  [the longest x4 190 us: scatter(): lax.psum_scatter(x, ('shard', 'tp'), scatter_dimension=0, tiled=True)]
    all_gather x5 -> x10, waiting for transfers between devices: 631 us -> 297 us  [the longest x4 201 us: fetch(): return lax.all_gather(w.reshape(S * nb, n), 'ctx', axis=0, tiled=True)]
    all_to_all x0 -> x6, blocking collectives: none -> 135 us  [the longest x3 56.7 us: fetch(): w = lax.all_to_all(w, 'shard', 0, 0, tiled=True)]
    dot_general x26 -> x12, matrix products: 206 us -> 111 us  [mm(): lax.dot_general(a, b, (((ca,), (cb,)), ((), ())), preferred_element_type=...]
    all_gather x3 -> x0, blocking collectives: 93.2 us -> none  [the longest x1 33.2 us: body(): lax.all_gather(norm_bias[depth], ('shard', 'ctx'), axis=1, tiled=True)]
    pallas_call x0 -> x2, Pallas kernels: none -> 70.9 us  [the longest x1 37.9 us: attend_back(): pl.pallas_call(attend_back_kernel, grid_spec=pltpu.PrefetchScalarGridSpec...]
    psum x3 -> x0, waiting for transfers between devices: 64.1 us -> none  [the longest x1 24.6 us: body(): lax.psum(jnp.dot(activated, down_w, preferred_element_type=jnp.float32).a...]
    all_to_all x0 -> x10, waiting for transfers between devices: none -> 57.1 us  [the longest x1 29 us: from_plane(): x = lax.all_to_all(x, 'ctx', 0, 0, tiled=True)]
  transfers between devices with their start and end apart: 15 -> 28, of which waited for: 14 -> 19; matrix products, arithmetic and copies ran while one was open for 4% -> 15% of each run, Pallas kernels for 0% -> 6%
where the time goes in v1:
time: 1260 us; the launch traced here: 1250 us
  waiting for transfers between devices  637 us (51%)
  blocking collectives  236 us (19%)
  matrix products  111 us (9%)
  local copies, waits for them, and re-layouts  106 us (8%)
  Pallas kernels  70.9 us (6%)
  starting transfers between devices  41.2 us (3%)
  other arithmetic  28.4 us (2%)
  between operations  16 us (1%)
    all_gather x4, waiting for transfers between devices, fetch(): return lax.all_gather(w.reshape(S * nb, n), 'ctx', axis=0, tiled=True)  201 us
    reduce_scatter x4, waiting for transfers between devices, scatter(): lax.psum_scatter(x, ('shard', 'tp'), scatter_dimension=0, tiled=True)  190 us
    dot_general x12, matrix products, mm(): lax.dot_general(a, b, (((ca,), (cb,)), ((), ())), preferred_element_type=...  111 us
    all_gather x4, waiting for transfers between devices, gather(): x = lax.all_gather(x, ('shard', 'tp'), axis=0, tiled=True)  95.9 us
    reduce_scatter x4, waiting for transfers between devices, give(): g = lax.psum_scatter(g.astype(BF), 'ctx', scatter_dimension=0, tiled=True)  91.6 us
    unnamed x1, blocking collectives  61.4 us
    all_to_all x3, blocking collectives, fetch(): w = lax.all_to_all(w, 'shard', 0, 0, tiled=True)  56.7 us
    all_to_all x1, blocking collectives, from_plane(): x = lax.all_to_all(x, 'ctx', 0, 0, tiled=True)  42.1 us
  transfers between devices with their start and end apart: 28, of which 19 were waited for; matrix products, arithmetic and copies ran while one was open for 15% of the time, Pallas kernels for 6%

profile of v1, /device:TPU:9, one launch (start us, length us, event | category | flops | bytes accessed | tf_op | source)
XLA Modules:
  0.0 1246.2 jit_solution(10711919640466499696)
XLA Ops:
  15.2 8.9 all-to-all-done
  29.1 61.4 %all-reduce = f32[11312]{0:T(1024)S(1)} all-reduce(f32[11312]{0:T(1024)S(1)} %maximum_dynamic-update-slice_fusion), channel_id=2, replica_groups=mesh['shard'=4,'ctx'=4,'tp'=2] {'ctx','shard'}, use_global_device_ids=true, to_apply=%add | all-reduce | flops 11312 | bytes 90496
  97.6 9.8 all_to_all.80
  129.8 31.3 %all-gather.14.cloned.1.call-done = bf16[1536,2048]{1,0:T(8,128)(2,1)} async-done(((bf16[192,2048]{1,0:T(8,128)(2,1)}), bf16[1536,2048]{1,0:T(8,128)(2,1)}) %all-gather.14.cloned.1.call-update) | async-done | bytes 6291472 | tf_op jit(solution)/shard_map/all_gather | solution.py:280
  167.7 56.2 %all-gather.16.cloned.1.call-done = bf16[2048,768]{1,0:T(8,128)(2,1)} async-done(((bf16[512,768]{1,0:T(8,128)(2,1)}), bf16[2048,768]{1,0:T(8,128)(2,1)}) %all-gather.16.cloned.1.call-update) | async-done | bytes 3145744 | tf_op jit(solution)/shard_map/all_gather | solution.py:290
  223.9 9.5 convolution_add_fusion.q_ref.k_ref.v_ref
  233.4 33.0 %attend.1 = (bf16[1536,256]{1,0:T(8,128)(2,1)S(1)}, bf16[1536,256]{1,0:T(8,128)(2,1)S(1)}, bf16[1536,256]{1,0:T(8,128)(2,1)S(1)}, bf16[1536,256]{1,0:T(8,128)(2,1)S(1)}, f32[2,2,1536]{2,1,0:T(2,128)S(1)}) custom-call(s32[6]{0:T(128)S(1)} %and_select_fusion.first_ref, f32[1536,768]{1,0:T(8,128)} %convolution_add_fusion.q_ref.k_ref.v_ref, ...), custom_call_target="tpu_custom_call" | custom-call | flops 2415919104 | bytes 9437184 | tf_op jit(solution)/shard_map/attend/pallas_call | solution.py:98
  276.7 13.2 %all_to_all.81 = bf16[4,48,2048]{2,1,0:T(8,128)(2,1)S(1)} all-to-all(bf16[4,48,2048]{2,1,0:T(8,128)(2,1)S(1)} %dynamic-slice_bitcast_fusion), channel_id=1, replica_groups=mesh['shard'=4,'ctx'=4,'tp'=2] {'shard'}, dimensions={0} | all-to-all | bytes 1572864 | tf_op jit(solution)/shard_map/all_to_all | solution.py:268
  289.9 22.7 %all_to_all.82 = bf16[4,48,2048]{2,1,0:T(8,128)(2,1)} all-to-all(bf16[4,48,2048]{2,1,0:T(8,128)(2,1)S(1)} %all_to_all.81), channel_id=1, replica_groups=mesh['shard'=4,'ctx'=4,'tp'=2] {'ctx'}, dimensions={0} | all-to-all | bytes 1572864 | tf_op jit(solution)/shard_map/all_to_all | solution.py:269
  318.7 19.7 %reduce-scatter.9.cloned.1.call-done = bf16[192,2048]{1,0:T(8,128)(2,1)} async-done(((bf16[1536,2048]{1,0:T(8,128)(2,1)}), bf16[192,2048]{1,0:T(8,128)(2,1)}) %reduce-scatter.9.cloned.1.call-update) | async-done | bytes 786448 | tf_op jit(solution)/shard_map/reduce_scatter | solution.py:285
  349.2 25.3 %all_to_all.83 = bf16[4,128,1408]{1,2,0:T(8,128)(2,1)} all-to-all(bf16[4,128,1408]{1,2,0:T(8,128)(2,1)S(1)} %bitcast.184), channel_id=1, replica_groups=mesh['shard'=4,'ctx'=4,'tp'=2] {'shard'}, dimensions={0} | all-to-all | bytes 2883584 | tf_op jit(solution)/shard_map/all_to_all | solution.py:289
  377.1 21.5 %all_to_all.84 = bf16[4,128,704]{1,2,0:T(8,128)(2,1)S(1)} all-to-all(bf16[4,128,704]{1,2,0:T(8,128)(2,1)} %bitcast.200), channel_id=1, replica_groups=mesh['shard'=4,'ctx'=4,'tp'=2] {'shard'}, dimensions={0} | all-to-all | bytes 1441792 | tf_op jit(solution)/shard_map/all_to_all | solution.py:289
  408.4 41.6 %all-gather.20.cloned.1.call-done = bf16[1536,2048]{1,0:T(8,128)(2,1)} async-done(((bf16[192,2048]{1,0:T(8,128)(2,1)}), bf16[1536,2048]{1,0:T(8,128)(2,1)}) %all-gather.20.cloned.1.call-update) | async-done | bytes 6291472 | tf_op jit(solution)/shard_map/all_gather | solution.py:280
  456.5 99.3 %all-gather.22.cloned.1.call-done = bf16[2048,1408]{1,0:T(8,128)(2,1)} async-done(((bf16[512,1408]{1,0:T(8,128)(2,1)}), bf16[2048,1408]{1,0:T(8,128)(2,1)}) %all-gather.22.cloned.1.call-update) | async-done | bytes 5767184 | tf_op jit(solution)/shard_map/all_gather | solution.py:290
  555.7 15.1 %fusion.30 = f32[1536,1408]{0,1:T(8,128)} fusion(bf16[1536,2048]{1,0:T(8,128)(2,1)} %bitcast.170, bf16[2048,1408]{1,0:T(8,128)(2,1)} %all-gather.22.cloned.1.call-done), kind=kOutput, calls=%fused_computation.104 | convolution fusion | flops 8858370048 | bytes 20709376 | tf_op jit(solution)/shard_map/dot_general | solution.py:21
  570.9 45.1 %all-gather.24.cloned.1.call-done = bf16[2048,704]{0,1:T(8,128)(2,1)} async-done(((bf16[512,704]{0,1:T(8,128)(2,1)}), bf16[2048,704]{0,1:T(8,128)(2,1)}) %all-gather.24.cloned.1.call-update) | async-done | bytes 2883600 | tf_op jit(solution)/shard_map/all_gather | solution.py:290
  615.9 14.5 %multiply_convert_fusion.1 = (bf16[1536,704]{0,1:T(8,128)(2,1)S(1)}, bf16[1536,704]{0,1:T(8,128)(2,1)}, bf16[1536,704]{0,1:T(8,128)(2,1)}) fusion(f32[1536,1408]{0,1:T(8,128)} %fusion.30, bf16[1536,2048]{1,0:T(8,128)(2,1)} %bitcast.172, bf16[2048,704]{0,1:T(8,128)(2,1)} %all-gather.24.cloned.1.call-done), kind=kOutput, calls=%fused_computation.8 | convolution fusion | flops 4446486528 | bytes 24313856 | tf_op jit(solution)/shard_map/dot_general | solution.py:21
  630.5 12.3 convolution_convert_fusion.3
  657.2 51.8 %reduce-scatter.13.cloned.1.call-done = bf16[192,2048]{1,0:T(8,128)(2,1)} async-done(((bf16[1536,2048]{1,0:T(8,128)(2,1)}), bf16[192,2048]{1,0:T(8,128)(2,1)}) %reduce-scatter.13.cloned.1.call-update) | async-done | bytes 786448 | tf_op jit(solution)/shard_map/reduce_scatter | solution.py:285
  711.4 62.5 %reduce-scatter.11.cloned.1.call-done = bf16[192,2048]{1,0:T(8,128)(2,1)} async-done(((bf16[1536,2048]{1,0:T(8,128)(2,1)}), bf16[192,2048]{1,0:T(8,128)(2,1)}) %reduce-scatter.11.cloned.1.call-update) | async-done | bytes 786448 | tf_op jit(solution)/shard_map/reduce_scatter | solution.py:285
  778.5 9.6 convolution_convert_fusion.6
  788.2 15.3 %convolution_convert_fusion.2 = bf16[2048,1408]{1,0:T(8,128)(2,1)} fusion(bf16[1536,2048]{1,0:T(8,128)(2,1)} %bitcast.171, bf16[1536,704]{0,1:T(8,128)(2,1)} %get-tuple-element.86, bf16[1536,704]{0,1:T(8,128)(2,1)} %copy-done.39), kind=kOutput, calls=%fused_computation.2 | convolution fusion | flops 8869904384 | bytes 16384000 | tf_op jit(solution)/shard_map/dot_general | solution.py:21
  803.6 21.0 %all-gather.28.cloned.1.call-done = bf16[1536,2048]{1,0:T(8,128)(2,1)} async-done(((bf16[192,2048]{1,0:T(8,128)(2,1)}), bf16[1536,2048]{1,0:T(8,128)(2,1)}) %all-gather.28.cloned.1.call-update) | async-done | bytes 6291472 | tf_op jit(solution)/shard_map/all_gather | solution.py:280
  831.4 37.9 %attend_back.1 = bf16[1536,768]{1,0:T(8,128)(2,1)} custom-call(s32[6]{0:T(128)S(1)} %and_select_fusion.first_ref, bf16[1536,256]{1,0:T(8,128)(2,1)S(1)} %copy-done.4, bf16[1536,256]{1,0:T(8,128)(2,1)S(1)} %copy-done.6, bf16[1536,256]{1,0:T(8,128)(2,1)S(1)} %copy-done.8, bf16[1536,256]{1,0:T(8,128)(2,1)S(1)} %get-tuple-element.14.o_ref, ...), custom_call_target="tpu_custom_call" | custom-call | flops 6039797760 | bytes 6291456 | tf_op jit(solution)/shard_map/attend_back/pallas_call | solution.py:191
  886.1 9.5 convolution_convert_fusion.5
  911.5 42.1 %all_to_all.85 = bf16[4,48,2048]{2,1,0:T(8,128)(2,1)} all-to-all(bf16[4,48,2048]{2,1,0:T(8,128)(2,1)S(1)} %reshape_reshape.10), channel_id=1, replica_groups=mesh['shard'=4,'ctx'=4,'tp'=2] {'ctx'}, dimensions={0} | all-to-all | bytes 1572864 | tf_op jit(solution)/shard_map/all_to_all | solution.py:274
  957.1 47.5 %reduce-scatter.21.cloned.1.call-done = bf16[512,1408]{1,0:T(8,128)(2,1)} async-done(((bf16[2048,1408]{1,0:T(8,128)(2,1)}), bf16[512,1408]{1,0:T(8,128)(2,1)}) %reduce-scatter.21.cloned.1.call-update) | async-done | bytes 1441808 | tf_op jit(solution)/shard_map/reduce_scatter | solution.py:294
  1012.6 56.4 %reduce-scatter.15.cloned.1.call-done = bf16[192,2048]{1,0:T(8,128)(2,1)} async-done(((bf16[1536,2048]{1,0:T(8,128)(2,1)}), bf16[192,2048]{1,0:T(8,128)(2,1)}) %reduce-scatter.15.cloned.1.call-update) | async-done | bytes 786448 | tf_op jit(solution)/shard_map/reduce_scatter | solution.py:285
  1082.1 29.0 %all-to-all-done.10 = bf16[4,48,2048]{2,1,0:T(8,128)(2,1)} async-done(((bf16[4,48,2048]{2,1,0:T(8,128)(2,1)}), bf16[4,48,2048]{2,1,0:T(8,128)(2,1)}, u32[]{:S(2)}, u32[]{:S(2)}) %all-to-all-start.10) | async-done | bytes 786464 | tf_op jit(solution)/shard_map/all_to_all | solution.py:274
  1114.6 10.3 all-to-all-done.11
  1129.6 44.0 %reduce-scatter.17.cloned.1.call-done = bf16[512,768]{1,0:T(8,128)(2,1)} async-done(((bf16[2048,768]{1,0:T(8,128)(2,1)}), bf16[512,768]{1,0:T(8,128)(2,1)}) %reduce-scatter.17.cloned.1.call-update) | async-done | bytes 786448 | tf_op jit(solution)/shard_map/reduce_scatter | solution.py:294
  1193.8 39.4 %psum.7 = f32[14336]{0:T(1024)S(1)} all-reduce(f32[14336]{0:T(1024)S(1)} %constant_dynamic-update-slice_fusion), channel_id=1, replica_groups=mesh['shard'=4,'ctx'=4,'tp'=2] {'shard','ctx','tp'}, use_global_device_ids=true, to_apply=%region_20.21 | all-reduce | flops 14336 | bytes 114688 | tf_op jit(solution)/shard_map/psum | solution.py:368
  (260 shorter events, 213.2 us)
Async XLA Ops:
  9.5 14.6 %all-to-all-start = ((bf16[4,48,2048]{2,1,0:T(8,128)(2,1)}), bf16[4,48,2048]{2,1,0:T(8,128)(2,1)}, u32[]{:S(2)}, u32[]{:S(2)}) async-start(bf16[4,48,2048]{2,1,0:T(8,128)(2,1)} %dynamic-slice_bitcast_fusion.1), calls=%async_computation | async-start | bytes 1572864 | tf_op jit(solution)/shard_map/all_to_all | solution.py:268
  24.1 66.7 %all-to-all-start.1 = ((bf16[4,48,2048]{2,1,0:T(8,128)(2,1)}), bf16[4,48,2048]{2,1,0:T(8,128)(2,1)S(1)}, u32[]{:S(2)}, u32[]{:S(2)}) async-start(bf16[4,48,2048]{2,1,0:T(8,128)(2,1)} %all-to-all-done), calls=%async_computation.1 | async-start | bytes 1572864 | tf_op jit(solution)/shard_map/all_to_all | solution.py:269
  28.9 132.2 %all-gather.14.cloned.1.call-start = ((), (), s32[]{:S(2)}) async-start(), calls=%async_computation.24 | async-start | bytes 7077888 | tf_op jit(solution)/shard_map/all_gather | solution.py:280
  96.8 127.1 %all-gather.16.cloned.1.call-start = ((), (), s32[]{:S(2)}) async-start(), calls=%async_computation.25 | async-start | bytes 3932160 | tf_op jit(solution)/shard_map/all_gather | solution.py:290
  108.6 8.5 all-to-all-start.3
  112.1 157.0 %all-gather.18.cloned.1.call-start = ((), (), s32[]{:S(2)}) async-start(), calls=%async_computation.26 | async-start | bytes 1310720 | tf_op jit(solution)/shard_map/all_gather | solution.py:290
  118.0 220.4 %reduce-scatter.9.cloned.1.call-start = ((), (), s32[]{:S(2)}) async-start(), calls=%async_computation.27 | async-start | bytes 7077888 | tf_op jit(solution)/shard_map/reduce_scatter | solution.py:285
  125.7 107.7 %copy-start.2 = (f32[1536,128]{1,0:T(8,128)}, f32[1536,128]{1,0:T(8,128)S(1)}, u32[]{:S(2)}) copy-start(f32[1536,128]{1,0:T(8,128)S(1)} %concatenate.28.hi_ref) | copy-start | bytes 2359300
  275.4 126.3 %all-gather.26.cloned.1.call-start = ((), (), s32[]{:S(2)}) async-start(), calls=%async_computation.32 | async-start | bytes 7077888 | tf_op jit(solution)/shard_map/all_gather | solution.py:280
  318.6 131.3 %all-gather.20.cloned.1.call-start = ((), (), s32[]{:S(2)}) async-start(), calls=%async_computation.28 | async-start | bytes 7077888 | tf_op jit(solution)/shard_map/all_gather | solution.py:280
  342.7 213.1 %all-gather.22.cloned.1.call-start = ((), (), s32[]{:S(2)}) async-start(), calls=%async_computation.29 | async-start | bytes 7208960 | tf_op jit(solution)/shard_map/all_gather | solution.py:290
  377.0 238.9 %all-gather.24.cloned.1.call-start = ((), (), s32[]{:S(2)}) async-start(), calls=%async_computation.30 | async-start | bytes 3604480 | tf_op jit(solution)/shard_map/all_gather | solution.py:290
  399.6 309.4 %reduce-scatter.13.cloned.1.call-start = ((), (), s32[]{:S(2)}) async-start(), calls=%async_computation.33 | async-start | bytes 7077888 | tf_op jit(solution)/shard_map/reduce_scatter | solution.py:285
  646.1 127.9 %reduce-scatter.11.cloned.1.call-start = ((), (), s32[]{:S(2)}) async-start(), calls=%async_computation.31 | async-start | bytes 7077888 | tf_op jit(solution)/shard_map/reduce_scatter | solution.py:285
  657.1 116.8 %copy-start.13 = (bf16[192,2048]{1,0:T(8,128)(2,1)S(1)}, bf16[192,2048]{1,0:T(8,128)(2,1)}, u32[]{:S(2)}) copy-start(bf16[192,2048]{1,0:T(8,128)(2,1)} %reshape.310) | copy-start | bytes 2359300
  657.1 167.4 %all-gather.28.cloned.1.call-start = ((), (), s32[]{:S(2)}) async-start(), calls=%async_computation.34 | async-start | bytes 7077888 | tf_op jit(solution)/shard_map/all_gather | solution.py:280
  778.4 117.3 %reduce-scatter.23.cloned.1.call-start = ((), (), s32[]{:S(2)}) async-start(), calls=%async_computation.39 | async-start | bytes 3604480 | tf_op jit(solution)/shard_map/reduce_scatter | solution.py:294
  788.1 216.5 %reduce-scatter.21.cloned.1.call-start = ((), (), s32[]{:S(2)}) async-start(), calls=%async_computation.38 | async-start | bytes 7208960 | tf_op jit(solution)/shard_map/reduce_scatter | solution.py:294
  803.5 265.5 %reduce-scatter.15.cloned.1.call-start = ((), (), s32[]{:S(2)}) async-start(), calls=%async_computation.35 | async-start | bytes 7077888 | tf_op jit(solution)/shard_map/reduce_scatter | solution.py:285
  879.6 235.0 %reduce-scatter.19.cloned.1.call-start = ((), (), s32[]{:S(2)}) async-start(), calls=%async_computation.37 | async-start | bytes 1310720 | tf_op jit(solution)/shard_map/reduce_scatter | solution.py:294
  886.1 287.6 %reduce-scatter.17.cloned.1.call-start = ((), (), s32[]{:S(2)}) async-start(), calls=%async_computation.36 | async-start | bytes 3932160 | tf_op jit(solution)/shard_map/reduce_scatter | solution.py:294
  897.9 13.6 %all-to-all-start.15 = ((bf16[4,128,704]{1,2,0:T(8,128)(2,1)}), bf16[4,128,704]{1,2,0:T(8,128)(2,1)S(1)}, u32[]{:S(2)}, u32[]{:S(2)}) async-start(bf16[4,128,704]{1,2,0:T(8,128)(2,1)} %copy_bitcast_fusion.3), calls=%async_computation.23 | async-start | bytes 1441792 | tf_op jit(solution)/shard_map/all_to_all | solution.py:295
  953.6 53.7 %all-to-all-start.7 = ((bf16[4,48,2048]{2,1,0:T(8,128)(2,1)}), bf16[4,48,2048]{2,1,0:T(8,128)(2,1)S(1)}, u32[]{:S(2)}, u32[]{:S(2)}) async-start(bf16[4,48,2048]{2,1,0:T(8,128)(2,1)} %all_to_all.85), calls=%async_computation.9 | async-start | bytes 1572864 | tf_op jit(solution)/shard_map/all_to_all | solution.py:275
  1004.6 64.4 %copy-start.29 = (f32[192]{0:T(256)S(1)}, f32[192]{0:T(256)}, u32[]{:S(2)}) copy-start(f32[192]{0:T(256)} %copy-done.28) | copy-start | bytes 2308
  1004.6 64.4 %copy-start.31 = (f32[192]{0:T(256)S(1)}, f32[192]{0:T(256)}, u32[]{:S(2)}) copy-start(f32[192]{0:T(256)} %copy-done.30) | copy-start | bytes 2308
  1008.1 68.6 %all-to-all-start.14 = ((bf16[4,128,1408]{1,2,0:T(8,128)(2,1)}), bf16[4,128,1408]{1,2,0:T(8,128)(2,1)}, u32[]{:S(2)}, u32[]{:S(2)}) async-start(bf16[4,128,1408]{1,2,0:T(8,128)(2,1)} %copy.204), calls=%async_computation.21 | async-start | bytes 2883584 | tf_op jit(solution)/shard_map/all_to_all | solution.py:295
  1076.8 34.2 %all-to-all-start.10 = ((bf16[4,48,2048]{2,1,0:T(8,128)(2,1)}), bf16[4,48,2048]{2,1,0:T(8,128)(2,1)}, u32[]{:S(2)}, u32[]{:S(2)}) async-start(bf16[4,48,2048]{2,1,0:T(8,128)(2,1)} %reshape_reshape.12), calls=%async_computation.14 | async-start | bytes 1572864 | tf_op jit(solution)/shard_map/all_to_all | solution.py:274
  1081.5 104.6 %all-gather.30.cloned.1.call-start = ((), (), s32[]{:S(2)}) async-start(), calls=%async_computation.40 | async-start | bytes 2359296 | tf_op jit(solution)/shard_map/all_gather | solution.py:276
  1111.0 13.9 %all-to-all-start.11 = ((bf16[4,48,2048]{2,1,0:T(8,128)(2,1)}), bf16[4,48,2048]{2,1,0:T(8,128)(2,1)S(1)}, u32[]{:S(2)}, u32[]{:S(2)}) async-start(bf16[4,48,2048]{2,1,0:T(8,128)(2,1)} %all-to-all-done.10), calls=%async_computation.15 | async-start | bytes 1572864 | tf_op jit(solution)/shard_map/all_to_all | solution.py:275
  1124.9 51.0 %all-to-all-start.13 = ((bf16[4,128,256]{2,1,0:T(8,128)(2,1)}), bf16[4,128,256]{2,1,0:T(8,128)(2,1)S(1)}, u32[]{:S(2)}, u32[]{:S(2)}) async-start(bf16[4,128,256]{2,1,0:T(8,128)(2,1)} %bitcast.203), calls=%async_computation.19 | async-start | bytes 524288 | tf_op jit(solution)/shard_map/all_to_all | solution.py:295
  1128.3 107.1 %all-gather.32.cloned.1.call-start = ((), (), s32[]{:S(2)}) async-start(), calls=%async_computation.41 | async-start | bytes 2359296 | tf_op jit(solution)/shard_map/all_gather | solution.py:276
  1175.9 14.8 %all-to-all-start.12 = ((bf16[4,128,768]{1,2,0:T(8,128)(2,1)}), bf16[4,128,768]{1,2,0:T(8,128)(2,1)}, u32[]{:S(2)}, u32[]{:S(2)}) async-start(bf16[4,128,768]{1,2,0:T(8,128)(2,1)} %copy.200), calls=%async_computation.17 | async-start | bytes 1572864 | tf_op jit(solution)/shard_map/all_to_all | solution.py:295
  (36 other events, 556.4 us)
Sparse Core Ops, SparseCore 0:
  96.9 64.1 all-gather.13
  163.2 60.6 all-gather.15
  226.0 28.7 all-gather.17
  275.5 62.8 reduce-scatter.8
  340.3 61.4 all-gather.25
  404.2 45.6 all-gather.19
  452.2 103.5 all-gather.21
  558.0 57.9 all-gather.23
  646.2 62.7 reduce-scatter.12
  712.2 61.7 reduce-scatter.10
  778.5 45.9 all-gather.27
  827.3 55.1 reduce-scatter.22
  885.0 119.6 reduce-scatter.20
  1008.2 60.7 reduce-scatter.14
  1071.1 39.6 reduce-scatter.18
  1113.7 59.8 reduce-scatter.16
  1175.1 10.9 all-gather.29
  1187.5 10.9 all-gather.31

commit v2 on v1

--- a/solution.py
+++ b/solution.py
@@ -1,4 +1,4 @@
-from functools import partial
+import functools
 
 import jax
 import jax.numpy as jnp
@@ -15,10 +15,461 @@
 BF = jnp.bfloat16
 F32 = jnp.float32
 BLK = 256
+MESH = pl.DeviceIdType.MESH
+DMA = pltpu.SemaphoreType.DMA
+ANY = pl.BlockSpec(memory_space=pl.ANY)
+IN_VMEM = pl.BlockSpec(memory_space=pltpu.VMEM)
 
 
 def mm(a, b, ca, cb):
     return lax.dot_general(a, b, (((ca,), (cb,)), ((), ())), preferred_element_type=F32)
+
+
+def remote(src, dst, send, recv, where):
+    return pltpu.make_async_remote_copy(
+        src_ref=src, dst_ref=dst, send_sem=send, recv_sem=recv, device_id=where, device_id_type=MESH
+    )
+
+
+def greet(peers):
+    barrier = pltpu.get_barrier_semaphore()
+    for where in peers:
+        pl.semaphore_signal(barrier, inc=1, device_id=where, device_id_type=MESH)
+    pl.semaphore_wait(barrier, len(peers))
+
+
+def comm(kernel, number, **call):
+    return pl.pallas_call(
+        kernel,
+        compiler_params=pltpu.CompilerParams(
+            collective_id=number, has_side_effects=True, vmem_limit_bytes=56 << 20
+        ),
+        **call,
+    )
+
+
+def exchange_kernel(S, C, T, count, small, *refs):
+    ins, refs = refs[:count], refs[count:]
+    if small:
+        tiles, refs = refs[0], refs[1:]
+    outs, refs = refs[:count], refs[count:]
+    if small:
+        got, refs = refs[0], refs[1:]
+    send, recv, own = refs[:3]
+    p, z, c = lax.axis_index("shard"), lax.axis_index("ctx"), lax.axis_index("tp")
+    peers = [{"shard": (p + k) % S} for k in range(1, S)]
+    everyone = [(i, j) for i in range(C) for j in range(S) if i or j]
+    if small:
+        greet(
+            [{"shard": (p + j) % S, "ctx": (z + i) % C} for i, j in everyone] + [{"tp": 1 - c}]
+        )
+    else:
+        greet(peers)
+    copies = []
+    if small:
+        tsend, trecv, bsend, brecv, town = refs[3:]
+        here = pltpu.make_async_copy(tiles.at[z, p], got.at[c, z, p], town)
+        here.start()
+        for at, (i, j) in enumerate(everyone):
+            q, g = (p + j) % S, (z + i) % C
+            copy = remote(
+                tiles.at[g, q], got.at[c, z, p], tsend.at[at], trecv.at[at], {"shard": q, "ctx": g}
+            )
+            copy.start()
+            copies.append((copy, got.at[c, (z - i) % C, (p - j) % S]))
+    moves = []
+    for n in range(count):
+        for k in range(1, S):
+            copy = remote(
+                ins[n].at[(p + k) % S], outs[n].at[p], send.at[n, k - 1], recv.at[n, k - 1], peers[k - 1]
+            )
+            copy.start()
+            moves.append(copy)
+        local = pltpu.make_async_copy(ins[n].at[p], outs[n].at[p], own.at[n])
+        local.start()
+        moves.append(local)
+    if small:
+        here.wait()
+        for copy, _ in copies:
+            copy.wait()
+        back = remote(got.at[c], got.at[c], bsend, brecv, {"tp": 1 - c})
+        back.start()
+        back.wait_send()
+        remote(got.at[1 - c], got.at[1 - c], bsend, brecv, {"tp": 1 - c}).wait_recv()
+    for copy in moves:
+        copy.wait()
+
+
+def exchange(S, C, T, number, arrays, tiles=None):
+    count, small = len(arrays), tiles is not None
+    shapes = [jax.ShapeDtypeStruct(x.shape, x.dtype) for x in arrays]
+    scratch = [DMA((count, S - 1)), DMA((count, S - 1)), DMA((count,))]
+    args = list(arrays)
+    if small:
+        shapes.append(jax.ShapeDtypeStruct((T,) + tiles.shape, tiles.dtype))
+        scratch += [DMA((C * S - 1,)), DMA((C * S - 1,)), DMA, DMA, DMA]
+        args.append(tiles)
+    return comm(
+        functools.partial(exchange_kernel, S, C, T, count, small),
+        number,
+        out_shape=shapes,
+        in_specs=[IN_VMEM] * len(args),
+        out_specs=[ANY] * len(shapes),
+        scratch_shapes=scratch,
+        name="exchange",
+    )(*args)
+
+
+def plane_peers(S):
+    p, c = lax.axis_index("shard"), lax.axis_index("tp")
+    B = S // 2
+    a, b = p // B, p % B
+    rows = [{"shard": a * B + (b + j) % B} for j in range(1, B)]
+    col = {"shard": (1 - a) * B + b}
+    return rows, col, {"tp": 1 - c}
+
+
+def spread_count(S):
+    B = S // 2
+    return 2 * (2 + 2 * (B - 1) + 2 + 2 * (B - 1))
+
+
+def spread(S, own, region, send, recv):
+    p, c = lax.axis_index("shard"), lax.axis_index("tp")
+    B = S // 2
+    a, b = p // B, p % B
+    rows, col, other = plane_peers(S)
+    per = spread_count(S) // 2
+    OWN, ROW, COL, VIA_COL, VIA_ROW = 0, 2, 2 + 2 * (B - 1), 4 + 2 * (B - 1), 4 + 3 * (B - 1)
+    started = []
+
+    def push(q, h, sem, where):
+        view = region(q, h, c)
+        copy = remote(own(h) if q is p else view, view, send.at[sem], recv.at[sem], where)
+        copy.start()
+        started.append(copy)
+
+    def came(q, h, sem, core):
+        view = region(q, h, core)
+        remote(view, view, send.at[sem], recv.at[sem], other).wait_recv()
+
+    for h in range(2):
+        for j in range(1, B):
+            push(p, h, ROW + 2 * (j - 1) + h, rows[j - 1])
+    for h in (1, 0):
+        push(p, h, COL + h, col)
+    for h in range(2):
+        push(p, h, per + OWN + h, other)
+
+    def from_row(j, h):
+        q = a * B + (b - j) % B
+        came(q, h, ROW + 2 * (j - 1) + h, c)
+        push(q, h, per + ROW + 2 * (j - 1) + h, other)
+        return q
+
+    def from_col(h):
+        q = (1 - a) * B + b
+        came(q, h, COL + h, c)
+        push(q, h, per + COL + h, other)
+        return q
+
+    for j in range(1, B):
+        q = from_row(j, 0)
+        push(q, 0, VIA_COL + j - 1, col)
+    q = from_col(1)
+    for j in range(1, B):
+        push(q, 1, VIA_ROW + j - 1, rows[j - 1])
+    for j in range(1, B):
+        from_row(j, 1)
+    from_col(0)
+    for j in range(1, B):
+        q = (1 - a) * B + (b - j) % B
+        came(q, 0, VIA_COL + j - 1, c)
+        push(q, 0, per + VIA_COL + j - 1, other)
+        came(q, 1, VIA_ROW + j - 1, c)
+        push(q, 1, per + VIA_ROW + j - 1, other)
+    for h in range(2):
+        came(p, h, per + OWN + h, 1 - c)
+        came((1 - a) * B + b, h, per + COL + h, 1 - c)
+    for j in range(1, B):
+        for h in range(2):
+            came(a * B + (b - j) % B, h, per + ROW + 2 * (j - 1) + h, 1 - c)
+        q = (1 - a) * B + (b - j) % B
+        came(q, 0, per + VIA_COL + j - 1, 1 - c)
+        came(q, 1, per + VIA_ROW + j - 1, 1 - c)
+    for copy in started:
+        copy.wait_send()
+
+
+def gather_kernel(S, T, x_ref, out_ref, send, recv, own):
+    p, c = lax.axis_index("shard"), lax.axis_index("tp")
+    half = x_ref.shape[0] // 2
+    rows, col, other = plane_peers(S)
+    local = pltpu.make_async_copy(x_ref, out_ref.at[p * T + c], own)
+    local.start()
+    greet(rows + [col, other])
+    spread(
+        S,
+        lambda h: x_ref.at[pl.ds(h * half, half)],
+        lambda q, h, core: out_ref.at[q * T + core, pl.ds(h * half, half)],
+        send,
+        recv,
+    )
+    local.wait()
+
+
+def gather(S, T, number, x):
+    n, D = x.shape
+    out = comm(
+        functools.partial(gather_kernel, S, T),
+        number,
+        out_shape=jax.ShapeDtypeStruct((S * T, n, D), x.dtype),
+        in_specs=[IN_VMEM],
+        out_specs=ANY,
+        scratch_shapes=[DMA((spread_count(S),)), DMA((spread_count(S),)), DMA],
+        name="gather",
+    )(x)
+    return out.reshape(S * T * n, D)
+
+
+def enter_kernel(S, C, T, count, *refs):
+    xs, outs = refs[:count], refs[count : 2 * count]
+    buf, s1, r1, s2, r2, s3, r3, own = refs[2 * count :]
+    p, z, c = lax.axis_index("shard"), lax.axis_index("ctx"), lax.axis_index("tp")
+    n, wide = outs[0].shape[2], outs[0].shape[3] // S
+    rows, col, other = plane_peers(S)
+    mates = [{"shard": (p + k) % S} for k in range(1, S)]
+    line = [{"ctx": (z + k) % C} for k in range(1, C)]
+    greet(mates + line + [other])
+
+    def part(q):
+        return pl.ds(pl.multiple_of(q * wide, 128), wide)
+
+    sends, hops = [], []
+    for t in range(count):
+        mine = pl.ds(pl.multiple_of(c * n, 16), n)
+        local = pltpu.make_async_copy(xs[t].at[mine, part(p)], buf.at[t, p], own.at[t, 0])
+        local.start()
+        hop = [local]
+        for k in range(1, S):
+            copy = remote(
+                xs[t].at[mine, part((p + k) % S)], buf.at[t, p], s1.at[t, k - 1], r1.at[t, k - 1], mates[k - 1]
+            )
+            copy.start()
+            hop.append(copy)
+        hops.append(hop)
+    lines = []
+    for t in range(count):
+        for copy in hops[t]:
+            copy.wait()
+        local = pltpu.make_async_copy(buf.at[t, z], outs[t].at[z, c, :, part(p)], own.at[t, 1])
+        local.start()
+        hop = [local]
+        for k in range(1, C):
+            copy = remote(
+                buf.at[t, (z + k) % C], outs[t].at[z, c, :, part(p)], s2.at[t, k - 1], r2.at[t, k - 1], line[k - 1]
+            )
+            copy.start()
+            hop.append(copy)
+        lines.append(hop)
+    for t in range(count):
+        for copy in lines[t]:
+            copy.wait()
+        out = outs[t]
+
+        def region(q, h, core):
+            return out.at[pl.ds(h * (C // 2), C // 2), core, :, part(q)]
+
+        spread(S, lambda h: region(p, h, c), region, s3.at[t], r3.at[t])
+
+
+def enter(S, C, T, number, arrays):
+    R, D = arrays[0].shape
+    count = len(arrays)
+    outs = comm(
+        functools.partial(enter_kernel, S, C, T, count),
+        number,
+        out_shape=[jax.ShapeDtypeStruct((C, T, R // T, D), x.dtype) for x in arrays],
+        in_specs=[ANY] * count,
+        out_specs=[ANY] * count,
+        scratch_shapes=[
+            pltpu.VMEM((count, S, R // T, D // S), BF),
+            DMA((count, S - 1)), DMA((count, S - 1)), DMA((count, C - 1)), DMA((count, C - 1)),
+            DMA((count, spread_count(S))), DMA((count, spread_count(S))), DMA((count, 2)),
+        ],
+        name="enter",
+    )(*arrays)
+    return [x.reshape(C * R, D) for x in outs]
+
+
+def leave_kernel(S, C, T, x_ref, out_ref, buf, buf2, s1, r1, s2, r2, s3, r3, s4, r4, own):
+    p, z, c = lax.axis_index("shard"), lax.axis_index("ctx"), lax.axis_index("tp")
+    wide = x_ref.shape[1] // S
+    mates = [{"shard": (p + k) % S} for k in range(1, S)]
+    line = [{"ctx": (z + k) % C} for k in range(1, C)]
+    other = {"tp": 1 - c}
+    greet(mates + line + [other])
+
+    def part(q):
+        return pl.ds(pl.multiple_of(q * wide, 128), wide)
+
+    def turn_over(source, target, send, recv, local, extent, me, where):
+        hop = [pltpu.make_async_copy(source(me), target, local)]
+        hop[0].start()
+        for k in range(1, extent):
+            copy = remote(source((me + k) % extent), target, send.at[k - 1], recv.at[k - 1], where[k - 1])
+            copy.start()
+            hop.append(copy)
+        for copy in hop:
+            copy.wait()
+
+    turn_over(lambda q: x_ref.at[:, part(q)], buf.at[p], s1, r1, own.at[0], S, p, mates)
+    turn_over(lambda q: buf.at[q], buf2.at[z], s2, r2, own.at[1], C, z, line)
+    turn_over(lambda q: buf2.at[q], out_ref.at[c, :, part(p)], s3, r3, own.at[2], S, p, mates)
+    copy = remote(out_ref.at[c], out_ref.at[c], s4, r4, other)
+    copy.start()
+    copy.wait_send()
+    remote(out_ref.at[1 - c], out_ref.at[1 - c], s4, r4, other).wait_recv()
+
+
+def leave(S, C, T, number, x):
+    n, D = x.shape
+    out = comm(
+        functools.partial(leave_kernel, S, C, T),
+        number,
+        out_shape=jax.ShapeDtypeStruct((T, n, D), x.dtype),
+        in_specs=[ANY],
+        out_specs=ANY,
+        scratch_shapes=[
+            pltpu.VMEM((S, n, D // S), BF), pltpu.VMEM((C, n, D // S), BF),
+            DMA((S - 1,)), DMA((S - 1,)), DMA((C - 1,)), DMA((C - 1,)), DMA((S - 1,)), DMA((S - 1,)),
+            DMA, DMA, DMA((3,)),
+        ],
+        name="leave",
+    )(x)
+    return out.reshape(T * n, D)
+
+
+CHUNK = 512
+
+
+def scatter_kernel(
+    S, T, x_ref, w_ref, out_ref, away, sib, mine, row1, col1, row2, col2, to_col, to_row,
+    asend, arecv, rsend, rrecv, csend, crecv, fsend, frecv,
+):
+    p, c = lax.axis_index("shard"), lax.axis_index("tp")
+    B = S // 2
+    a, b = p // B, p % B
+    rows, col, other = plane_peers(S)
+    n, D = out_ref.shape
+    half = n // 2
+    steps = D // CHUNK
+    greet(rows + [col, other])
+
+    def chip(e):
+        return ((a + e // B) % 2) * B + (b + e % B) % B
+
+    def product(e, core, store):
+        x = x_ref[chip(e) * T + core]
+
+        def column(j, _):
+            w = pl.ds(pl.multiple_of(j * CHUNK, CHUNK), CHUNK)
+            store(w, mm(x, w_ref[w, :], 1, 1))
+            return 0
+
+        lax.fori_loop(0, steps, column, 0)
+
+    def to_other(e):
+        return remote(away.at[e], sib.at[e], asend.at[e], arecv.at[e], other)
+
+    def first(i, _):
+        e = S - 1 - i
+
+        def store(w, value):
+            away[e, :, w] = value.astype(BF)
+
+        product(e, 1 - c, store)
+        to_other(e).start()
+        return 0
+
+    lax.fori_loop(0, S, first, 0)
+
+    top, low = pl.ds(0, half), pl.ds(half, half)
+    started = []
+
+    def push(src, dst, send, recv, where):
+        copy = remote(src, dst, send, recv, where)
+        copy.start()
+        started.append(copy)
+
+    for e in range(S - 1, -1, -1):
+        to_other(e).wait()
+
+        def store(w, value):
+            value = value + sib[e, :, w].astype(F32)
+            if e:
+                mine[e, :, w] = value.astype(BF)
+            else:
+                out_ref[:, w] = value
+
+        product(e, c, store)
+        j = e % B
+        if e > B:
+            push(mine.at[e, top], row1.at[j - 1, 1], rsend.at[j - 1, 1], rrecv.at[j - 1, 1], rows[j - 1])
+            push(mine.at[e, low], col1.at[j], csend.at[j], crecv.at[j], col)
+        elif e == B:
+            push(mine.at[e, low], col1.at[0], csend.at[0], crecv.at[0], col)
+        elif e:
+            push(mine.at[e, top], row1.at[j - 1, 0], rsend.at[j - 1, 0], rrecv.at[j - 1, 0], rows[j - 1])
+
+    def came(ref, send, recv):
+        remote(ref, ref, send, recv, other).wait_recv()
+
+    total = mine[B, top, :].astype(F32)
+    for j in range(1, B):
+        came(row1.at[j - 1, 1], rsend.at[j - 1, 1], rrecv.at[j - 1, 1])
+        total = total + row1[j - 1, 1].astype(F32)
+    to_col[...] = total.astype(BF)
+    push(to_col, col2, fsend.at[0], frecv.at[0], col)
+    for j in range(1, B):
+        came(col1.at[j], csend.at[j], crecv.at[j])
+        to_row[j - 1] = (mine[j, low, :].astype(F32) + col1[j].astype(F32)).astype(BF)
+        push(to_row.at[j - 1], row2.at[j - 1], fsend.at[j], frecv.at[j], rows[j - 1])
+    came(col1.at[0], csend.at[0], crecv.at[0])
+    upper, lower = out_ref[top, :], out_ref[low, :] + col1[0].astype(F32)
+    for j in range(1, B):
+        came(row1.at[j - 1, 0], rsend.at[j - 1, 0], rrecv.at[j - 1, 0])
+        upper = upper + row1[j - 1, 0].astype(F32)
+    came(col2, fsend.at[0], frecv.at[0])
+    out_ref[top, :] = upper + col2[...].astype(F32)
+    for j in range(1, B):
+        came(row2.at[j - 1], fsend.at[j], frecv.at[j])
+        lower = lower + row2[j - 1].astype(F32)
+    out_ref[low, :] = lower
+    for copy in started:
+        copy.wait_send()
+
+
+def scatter(S, T, number, x, w):
+    L, K = x.shape
+    D = w.shape[0]
+    n, B = L // (S * T), S // 2
+    half = n // 2
+    return comm(
+        functools.partial(scatter_kernel, S, T),
+        number,
+        out_shape=jax.ShapeDtypeStruct((n, D), F32),
+        in_specs=[IN_VMEM, IN_VMEM],
+        out_specs=IN_VMEM,
+        scratch_shapes=[
+            pltpu.VMEM((S, n, D), BF), pltpu.VMEM((S, n, D), BF), pltpu.VMEM((S, n, D), BF),
+            pltpu.VMEM((B - 1, 2, half, D), BF), pltpu.VMEM((B, half, D), BF),
+            pltpu.VMEM((B - 1, half, D), BF), pltpu.VMEM((half, D), BF),
+            pltpu.VMEM((half, D), BF), pltpu.VMEM((B - 1, half, D), BF),
+            DMA((S,)), DMA((S,)), DMA((B - 1, 2)), DMA((B - 1, 2)), DMA((B,)), DMA((B,)), DMA((B,)), DMA((B,)),
+        ],
+        name="scatter",
+    )(x.reshape(S * T, n, K), w)
 
 
 def turn(x, cos, lo, hi):
@@ -247,13 +698,19 @@
     return (inverse * centered, jnp.sum(gradient * normal, axis=0), jnp.sum(gradient, axis=0))
 
 
+def tiles_of(parts, lead):
+    flat = jnp.concatenate([x.astype(F32).reshape(lead + (-1,)) for x in parts], axis=-1)
+    flat = jnp.pad(flat, ((0, 0),) * len(lead) + ((0, 1024 - flat.shape[-1]),))
+    return flat.reshape(lead + (8, 128))
+
+
 def make_body(S, C, T):
     assert S == C
 
     def body(tokens, lengths, w_qkv, b_qkv, w_out, w_gateup, w_down, norm_gain, norm_bias, cotangent):
         p, z, c = lax.axis_index("shard"), lax.axis_index("ctx"), lax.axis_index("tp")
         R, D = tokens.shape
-        m = R // (S * T)
+        n = R // T
         nb = D // (S * C)
         L = R * C
 
@@ -263,128 +720,115 @@
         def unpermute(x):
             return x.reshape(x.shape[0], C, S, nb).swapaxes(1, 2).reshape(x.shape)
 
-        def to_plane(x):
-            mine = lax.dynamic_index_in_dim(x.reshape(S, T, m, D), c, 1, keepdims=False)
-            moved = lax.all_to_all(mine, "shard", 0, 0, tiled=True)
-            moved = lax.all_to_all(moved, "ctx", 0, 0, tiled=True)
-            return permute(moved.reshape(C * m, D))
-
-        def from_plane(x):
-            x = unpermute(x).reshape(C, m, D)
-            x = lax.all_to_all(x, "ctx", 0, 0, tiled=True)
-            x = lax.all_to_all(x, "shard", 0, 0, tiled=True)
-            x = lax.all_gather(x, "tp", axis=0)
-            return x.swapaxes(0, 1).reshape(R, D)
-
-        def gather(x):
-            x = lax.all_gather(x, ("shard", "tp"), axis=0, tiled=True)
-            return x.reshape(S * T, C, m, D).swapaxes(0, 1).reshape(L, D)
-
-        def scatter(x):
-            x = x.astype(BF).reshape(C, S * T, m, D).swapaxes(0, 1).reshape(L, D)
-            return lax.psum_scatter(x, ("shard", "tp"), scatter_dimension=0, tiled=True).astype(F32)
-
-        def fetch(w):
-            n = w.shape[2]
-            w = lax.all_to_all(w, "shard", 0, 0, tiled=True)
-            return lax.all_gather(w.reshape(S * nb, n), "ctx", axis=0, tiled=True)
-
-        def give(g):
-            n = g.shape[1]
+        def own(x):
+            return lax.dynamic_slice_in_dim(x, (p * T + c) * n, n, 0)
+
+        def spread_out(x):
+            return gather(S, T, 4, x)
+
+        def over_ctx(w):
+            return lax.all_gather(w.reshape(S * nb, -1), "ctx", axis=0, tiled=True)
+
+        def sum_ctx(g):
             g = lax.psum_scatter(g.astype(BF), "ctx", scatter_dimension=0, tiled=True)
-            return lax.all_to_all(g.reshape(S, nb, n), "shard", 0, 0, tiled=True).astype(F32)
+            return g.reshape(S, nb, -1)
 
         hn = w_qkv.shape[3] // S
         fn = w_gateup.shape[3] // S
         heads = hn // HEAD
-
-        small = jnp.concatenate(
-            (
-                norm_gain[0].astype(F32).reshape(-1),
-                norm_bias[0].astype(F32).reshape(-1),
-                b_qkv[0].astype(F32).reshape(-1),
-                lengths[0].astype(F32),
-            )
+        nf = HEAD // (S * C)
+
+        tile = tiles_of((norm_gain[0].reshape(-1), norm_bias[0].reshape(-1), b_qkv[0].reshape(-1), lengths[0]), ())
+        wq, small = exchange(
+            S, C, T, 0,
+            [w_qkv[0].reshape(nb, 3, S, hn).transpose(2, 0, 1, 3).reshape(S, nb, 3 * hn)],
+            jnp.broadcast_to(tile, (C, S, 8, 128)),
         )
-        small = lax.all_gather(small, ("ctx", "shard"), axis=0)
-        gains = small[:, : 2 * nb].reshape(C * S, 2, nb).swapaxes(0, 1).reshape(2, D)
-        shifts = small[:, 2 * nb : 4 * nb].reshape(C * S, 2, nb).swapaxes(0, 1).reshape(2, D)
-        nbias = b_qkv[0].size
-        bias = small[:, 4 * nb : 4 * nb + nbias].reshape(C, S, 3, S * heads, -1)
+        wq = over_ctx(wq)
+        wo, wg, wd = exchange(
+            S, C, T, 1,
+            [
+                w_out[0].reshape(S, hn, nb).swapaxes(1, 2),
+                w_gateup[0].reshape(nb, 2, S, fn).transpose(2, 0, 1, 3).reshape(S, nb, 2 * fn),
+                w_down[0].reshape(S, fn, nb).swapaxes(1, 2),
+            ],
+        )
+        wo, wg, wd = over_ctx(wo), over_ctx(wg), over_ctx(wd)
+        tok, gb = enter(S, C, T, 2, [permute(tokens), permute(cotangent)])
+
+        small = lax.dynamic_index_in_dim(small, c, 0, keepdims=False).reshape(C, S, 1024)
+        norms = small[:, :, : 4 * nb].reshape(C * S, 4, nb).swapaxes(0, 1).reshape(4, D)
+        gains, shifts = norms[:2], norms[2:]
+        nbias = 3 * S * heads * nf
+        bias = small[:, :, 4 * nb : 4 * nb + nbias].reshape(C, S, 3, S * heads, nf)
         bias = lax.dynamic_slice_in_dim(bias, p * heads, heads, 3)
         bias = bias.transpose(2, 3, 1, 0, 4).reshape(1, 3 * hn)
+        docs = lengths.shape[1]
         lengths_row = lax.dynamic_index_in_dim(
-            small[:S, 4 * nb + nbias :], z, 0, keepdims=False
+            small[0, :, 4 * nb + nbias : 4 * nb + nbias + docs], z, 0, keepdims=False
         ).astype(jnp.int32)
-
         begin, tables = doc_tables(lengths_row, L)
         first = begin[::BLK] // BLK
         begin = begin[None, :]
 
-        tok = to_plane(tokens)
-        wq = fetch(w_qkv[0].reshape(nb, 3, S, hn).transpose(2, 0, 1, 3).reshape(S, nb, 3 * hn))
-        wo = fetch(w_out[0].reshape(S, hn, nb).swapaxes(1, 2))
-        wg = fetch(w_gateup[0].reshape(nb, 2, S, fn).transpose(2, 0, 1, 3).reshape(S, nb, 2 * fn))
-        wd = fetch(w_down[0].reshape(S, fn, nb).swapaxes(1, 2))
-
-        hidden = tok.astype(F32)
-        n1, normal1, inverse1 = layer_norm(hidden, gains[0], shifts[0])
-        n1 = gather(n1.astype(BF))
+        n1 = layer_norm(tok.astype(F32), gains[0], shifts[0])[0].astype(BF)
+        hidden = own(tok).astype(F32)
+        _, normal1, inverse1 = layer_norm(hidden, gains[0], shifts[0])
         qkv = mm(n1, wq, 1, 0) + bias
         q, k, v, o, lse = attend(qkv, tables, begin, first)
-        mid = hidden + scatter(mm(o, wo, 1, 1))
+        mid = hidden + scatter(S, T, 5, o, wo)
         n2, normal2, inverse2 = layer_norm(mid, gains[1], shifts[1])
-        n2 = gather(n2.astype(BF))
+        n2 = spread_out(n2.astype(BF))
         gu = mm(n2, wg, 1, 0)
         gate, up = gu[:, :fn], gu[:, fn:]
         logistic = jax.nn.sigmoid(gate)
         act = (gate * logistic * up).astype(BF)
-        out = mid + scatter(mm(act, wd, 1, 1))
-        out = from_plane(out.astype(BF))
-
-        grad_own = to_plane(cotangent)
-        gb = gather(grad_own)
-        gw_down = give(mm(gb, act, 0, 0))
+        gw_down = sum_ctx(mm(gb, act, 0, 0))
+
         dact = mm(gb, wd, 1, 0)
         dgate = dact * up * logistic * (1.0 + gate * (1.0 - logistic))
         dup = dact * gate * logistic
         dgu = jnp.concatenate((dgate, dup), axis=1).astype(BF)
-        gw_gateup = give(mm(n2, dgu, 0, 0))
-        dn2 = scatter(mm(dgu, wg, 1, 1))
+        gw_gateup = sum_ctx(mm(n2, dgu, 0, 0))
+        dn2 = scatter(S, T, 6, dgu, wg)
         dmid, gain2, shift2 = norm_back(dn2, normal2, inverse2, gains[1])
-        dmid = grad_own.astype(F32) + dmid
-        gb1 = gather(dmid.astype(BF))
-        gw_out = give(mm(gb1, o, 0, 0))
+        dmid = own(gb).astype(F32) + dmid
+        gb1 = spread_out(dmid.astype(BF))
+        gw_out = sum_ctx(mm(gb1, o, 0, 0))
         do = mm(gb1, wo, 1, 0).astype(BF)
         dqkv = attend_back(q, k, v, o, do, lse, tables, begin, first)
+        gw_qkv = sum_ctx(mm(n1, dqkv, 0, 0))
+        dn1 = scatter(S, T, 7, dqkv, wq)
+        out = mid + scatter(S, T, 8, act, wd)
+        out = leave(S, C, T, 9, unpermute(out.astype(BF)))
+        dtok, gain1, shift1 = norm_back(dn1, normal1, inverse1, gains[0])
+        gtok = leave(S, C, T, 9, unpermute((dmid + dtok).astype(BF))).astype(F32)
+        gw_out, gw_gateup, gw_down = exchange(S, C, T, 1, [gw_out, gw_gateup, gw_down])
+
         gbias = jnp.sum(dqkv.astype(F32), axis=0)
-        gw_qkv = give(mm(n1, dqkv, 0, 0))
-        dn1 = scatter(mm(dqkv, wq, 1, 1))
-        dtok, gain1, shift1 = norm_back(dn1, normal1, inverse1, gains[0])
-        gtok = from_plane((dmid + dtok).astype(BF)).astype(F32)
-
-        slots = jnp.zeros((T * S, 3 * hn), F32)
-        slots = lax.dynamic_update_slice(slots, gbias[None], (c * S + p, 0))
-        sums = lax.psum(
-            jnp.concatenate((gain1, gain2, shift1, shift2, slots.reshape(-1))), ("shard", "ctx", "tp")
+        tiles = tiles_of(
+            (
+                jnp.stack((gain1, gain2, shift1, shift2)).reshape(4, C, S, nb).transpose(1, 2, 0, 3),
+                gbias.reshape(3, heads, S, C, nf).transpose(3, 2, 0, 1, 4),
+            ),
+            (C, S),
         )
-        norms = lax.dynamic_index_in_dim(
-            sums[: 4 * D].reshape(4, C * S, nb), z * S + p, 1, keepdims=False
-        )
-        slots = lax.dynamic_index_in_dim(sums[4 * D :].reshape(T, S, 3, heads, S * C, -1), c, 0, keepdims=False)
-        slots = lax.dynamic_index_in_dim(slots, p * C + z, 3, keepdims=False)
-        gbias = slots.swapaxes(0, 1).reshape(3, S * heads, -1)
+        gw_qkv, small = exchange(S, C, T, 0, [gw_qkv], tiles)
+        small = small.reshape(T, C, S, 1024)
+        norms = jnp.sum(small[..., : 4 * nb], axis=(0, 1, 2)).reshape(1, 4, nb)
+        gbias = lax.dynamic_index_in_dim(small, c, 0, keepdims=False)[..., 4 * nb : 4 * nb + 3 * heads * nf]
+        gbias = jnp.sum(gbias, axis=0).reshape(S, 3, heads, nf).swapaxes(0, 1).reshape(b_qkv.shape)
 
         return (
             out,
             gtok,
-            gw_qkv.reshape(S, nb, 3, hn).transpose(1, 2, 0, 3).reshape(w_qkv.shape),
-            gbias[None],
-            gw_out.swapaxes(1, 2).reshape(w_out.shape),
-            gw_gateup.reshape(S, nb, 2, fn).transpose(1, 2, 0, 3).reshape(w_gateup.shape),
-            gw_down.swapaxes(1, 2).reshape(w_down.shape),
-            norms[:2][None],
-            norms[2:][None],
+            gw_qkv.astype(F32).reshape(S, nb, 3, hn).transpose(1, 2, 0, 3).reshape(w_qkv.shape),
+            gbias,
+            gw_out.astype(F32).swapaxes(1, 2).reshape(w_out.shape),
+            gw_gateup.astype(F32).reshape(S, nb, 2, fn).transpose(1, 2, 0, 3).reshape(w_gateup.shape),
+            gw_down.astype(F32).swapaxes(1, 2).reshape(w_down.shape),
+            norms[:, :2],
+            norms[:, 2:],
         )
 
     return body

time: 1260 us -> 863 us (0.68)
  waiting for transfers between devices: 637 us -> 1.33 us
  Pallas kernels: 70.9 us -> 637 us
  blocking collectives: 236 us -> 0 us
  starting transfers between devices: 41.2 us -> 0.54 us
  matrix products: 111 us -> 80 us
  local copies, waits for them, and re-layouts: 106 us -> 82.8 us
  other arithmetic: 28.4 us -> 44.2 us
    pallas_call x0 -> x13, Pallas kernels: none -> 578 us  [the longest x4 161 us: scatter(): comm(functools.partial(scatter_kernel, S, T), number, out_shape=jax.Shape...]
    all_gather x10 -> x4, waiting for transfers between devices: 297 us -> 0.03 us  [over_ctx(): return lax.all_gather(w.reshape(S * nb, -1), 'ctx', axis=0, tiled=True)]
    reduce_scatter x8 -> x4, waiting for transfers between devices: 282 us -> 0.01 us  [sum_ctx(): g = lax.psum_scatter(g.astype(BF), 'ctx', scatter_dimension=0, tiled=True)]
    all_to_all x6 -> x0, blocking collectives: 135 us -> none  [the longest x3 56.7 us: fetch(): w = lax.all_to_all(w, 'shard', 0, 0, tiled=True)]
    unnamed x1 -> x0, blocking collectives: 61.4 us -> none
    all_to_all x10 -> x0, waiting for transfers between devices: 57.1 us -> none  [the longest x1 29 us: from_plane(): x = lax.all_to_all(x, 'ctx', 0, 0, tiled=True)]
    all_to_all x10 -> x0, starting transfers between devices: 39.8 us -> none  [the longest x4 15.7 us: give(): lax.all_to_all(g.reshape(S, nb, n), 'shard', 0, 0, tiled=True).astype(F32)]
    psum x1 -> x0, blocking collectives: 39.4 us -> none  [body(): lax.psum(jnp.concatenate((gain1, gain2, shift1, shift2, slots.reshape(-1)...]
  transfers between devices with their start and end apart: 28 -> 8, of which waited for: 19 -> 0; matrix products, arithmetic and copies ran while one was open for 15% -> 18% of each run, Pallas kernels for 6% -> 68%
where the time goes in v2:
time: 863 us; the launch traced here: 861 us
  Pallas kernels  637 us (74%)
  local copies, waits for them, and re-layouts  82.8 us (10%)
  matrix products  80 us (9%)
  other arithmetic  44.2 us (5%)
  between operations  15.4 us (2%)
    pallas_call x4, Pallas kernels, scatter(): comm(functools.partial(scatter_kernel, S, T), number, out_shape=jax.Shape...  161 us
    pallas_call x2, Pallas kernels, leave(): comm(functools.partial(leave_kernel, S, C, T), number, out_shape=jax.Shap...  140 us
    pallas_call x1, Pallas kernels, enter(): comm(functools.partial(enter_kernel, S, C, T, count), number, out_shape=[...  115 us
    pallas_call x4, Pallas kernels, exchange(): comm(functools.partial(exchange_kernel, S, C, T, count, small), number, o...  95.7 us
    dot_general x8, matrix products, mm(): lax.dot_general(a, b, (((ca,), (cb,)), ((), ())), preferred_element_type=...  80 us
    pallas_call x2, Pallas kernels, gather(): comm(functools.partial(gather_kernel, S, T), number, out_shape=jax.ShapeD...  65.2 us
    pallas_call x1, Pallas kernels, attend_back(): pl.pallas_call(attend_back_kernel, grid_spec=pltpu.PrefetchScalarGridSpec...  31.7 us
    pallas_call x1, Pallas kernels, attend(): pl.pallas_call(attend_kernel, grid_spec=pltpu.PrefetchScalarGridSpec(num_...  27.1 us
  transfers between devices with their start and end apart: 8, of which 0 were waited for; matrix products, arithmetic and copies ran while one was open for 18% of the time, Pallas kernels for 68%

profile of v2, /device:TPU:9, one launch (start us, length us, event | category | flops | bytes accessed | tf_op | source)
XLA Modules:
  0.0 860.8 jit_solution(18320607590998241806)
XLA Ops:
  12.3 16.4 %exchange.4 = (bf16[4,128,768]{2,1,0:T(8,128)(2,1)}, f32[2,4,4,8,128]{4,3,2,1,0:T(8,128)}) custom-call(bf16[4,128,768]{2,1,0:T(8,128)(2,1)} %copy.114.refs_0_, f32[4,4,8,128]{3,2,1,0:T(8,128)} %broadcast_in_dim.18.refs_1_), custom_call_target="tpu_custom_call" | custom-call | tf_op jit(solution)/shard_map/exchange/pallas_call | solution.py:112
  34.3 31.6 %exchange.5 = (bf16[4,128,256]{2,1,0:T(8,128)(2,1)}, bf16[4,128,1408]{2,1,0:T(8,128)(2,1)}, bf16[4,128,704]{2,1,0:T(8,128)(2,1)}) custom-call(bf16[4,128,256]{2,1,0:T(8,128)(2,1)} %bitcast.148, bf16[4,128,1408]{2,1,0:T(8,128)(2,1)} %copy.121.refs_1_, bf16[4,128,704]{2,1,0:T(8,128)(2,1)} %bitcast.140), custom_call_target="tpu_custom_call" | custom-call | tf_op jit(solution)/shard_map/exchange/pallas_call | solution.py:112
  78.5 115.4 %enter.1 = (bf16[4,2,192,2048]{3,2,1,0:T(8,128)(2,1)}, bf16[4,2,192,2048]{3,2,1,0:T(8,128)(2,1)}) custom-call(bf16[384,2048]{1,0:T(8,128)(2,1)} %reshape.325.refs_0_, bf16[384,2048]{1,0:T(8,128)(2,1)} %reshape.327.refs_1_), custom_call_target="tpu_custom_call" | custom-call | tf_op jit(solution)/shard_map/enter/pallas_call | solution.py:289
  194.0 3.8 convert_reduce_fusion
  201.0 4.3 multiply_sine_fusion
  208.7 3.6 concatenate.36.lo_ref
  217.9 7.7 add_convert_fusion
  225.7 9.9 %convolution_add_fusion.q_ref.k_ref.v_ref = f32[1536,768]{1,0:T(8,128)} fusion(bf16[1536,2048]{1,0:T(8,128)(2,1)} %add_convert_fusion, bf16[2048,768]{1,0:T(8,128)(2,1)} %all-gather.5.cloned.1.call-done.w_ref, f32[768]{0:T(1024)S(1)} %add.120), kind=kOutput, calls=%fused_computation.15 | convolution fusion | flops 4833017856 | bytes 14158848 | tf_op jit(solution)/shard_map/dot_general | solution.py:25
  235.6 27.1 %attend.1 = (bf16[1536,256]{1,0:T(8,128)(2,1)S(1)}, bf16[1536,256]{1,0:T(8,128)(2,1)S(1)}, bf16[1536,256]{1,0:T(8,128)(2,1)S(1)}, bf16[1536,256]{1,0:T(8,128)(2,1)S(1)}, f32[2,2,1536]{2,1,0:T(2,128)S(1)}) custom-call(s32[6]{0:T(128)S(1)} %and_select_fusion.first_ref, f32[1536,768]{1,0:T(8,128)} %convolution_add_fusion.q_ref.k_ref.v_ref, ...), custom_call_target="tpu_custom_call" | custom-call | flops 2415919104 | bytes 9437184 | tf_op jit(solution)/shard_map/attend/pallas_call | solution.py:549
  265.4 35.5 %scatter.4 = f32[192,2048]{1,0:T(8,128)} custom-call(bf16[8,192,256]{2,1,0:T(8,128)(2,1)} %bitcast.115, bf16[2048,256]{1,0:T(8,128)(2,1)} %all-gather.7.cloned.1.call-done.w_ref), custom_call_target="tpu_custom_call" | custom-call | tf_op jit(solution)/shard_map/scatter/pallas_call | solution.py:458
  305.4 32.1 %gather.2 = bf16[8,192,2048]{2,1,0:T(8,128)(2,1)} custom-call(bf16[192,2048]{1,0:T(8,128)(2,1)} %add_convert_fusion.2.x_ref), custom_call_target="tpu_custom_call" | custom-call | tf_op jit(solution)/shard_map/gather/pallas_call | solution.py:223
  337.5 15.1 %fusion.27 = f32[1536,1408]{0,1:T(8,128)} fusion(bf16[1536,2048]{1,0:T(8,128)(2,1)} %bitcast.128, bf16[2048,1408]{1,0:T(8,128)(2,1)} %all-gather.9.cloned.1.call-done.w_ref), kind=kOutput, calls=%fused_computation.98 | convolution fusion | flops 8858370048 | bytes 20709376 | tf_op jit(solution)/shard_map/dot_general | solution.py:25
  352.6 12.6 %multiply_convert_fusion.1 = (bf16[1536,704]{0,1:T(8,128)(2,1)}, bf16[1536,704]{0,1:T(8,128)(2,1)}, bf16[1536,704]{0,1:T(8,128)(2,1)S(1)}) fusion(f32[1536,1408]{0,1:T(8,128)} %fusion.27, bf16[1536,2048]{1,0:T(8,128)(2,1)} %bitcast.165, bf16[2048,704]{1,0:T(8,128)(2,1)} %all-gather.11.cloned.1.call-done.w_ref), kind=kOutput, calls=%fused_computation.12 | convolution fusion | flops 4446486528 | bytes 24313856 | tf_op jit(solution)/shard_map/dot_general | solution.py:25
  366.6 8.9 %convolution_convert_fusion.2 = bf16[2048,704]{0,1:T(8,128)(2,1)} fusion(bf16[1536,704]{0,1:T(8,128)(2,1)S(1)} %get-tuple-element.93, bf16[1536,2048]{1,0:T(8,128)(2,1)} %bitcast.166), kind=kOutput, calls=%fused_computation.17 | convolution fusion | flops 4430626816 | bytes 11337728 | tf_op jit(solution)/shard_map/dot_general | solution.py:25
  375.7 4.4 copy.122
  380.1 4.2 copy.124
  384.2 4.2 copy.125
  388.4 5.7 pad_maximum_fusion.x_ref
  394.2 46.2 %scatter.6 = f32[192,2048]{1,0:T(8,128)} custom-call(bf16[8,192,1408]{2,1,0:T(8,128)(2,1)} %pad_maximum_fusion.x_ref, bf16[2048,1408]{1,0:T(8,128)(2,1)} %all-gather.9.cloned.1.call-done.w_ref), custom_call_target="tpu_custom_call" | custom-call | tf_op jit(solution)/shard_map/scatter/pallas_call | solution.py:458
  440.4 39.4 %scatter.5 = f32[192,2048]{1,0:T(8,128)} custom-call(bf16[8,192,704]{2,1,0:T(8,128)(2,1)} %bitcast.123, bf16[2048,704]{1,0:T(8,128)(2,1)} %all-gather.11.cloned.1.call-done.w_ref), custom_call_target="tpu_custom_call" | custom-call | tf_op jit(solution)/shard_map/scatter/pallas_call | solution.py:458
  484.8 33.1 %gather.3 = bf16[8,192,2048]{2,1,0:T(8,128)(2,1)} custom-call(bf16[192,2048]{1,0:T(8,128)(2,1)} %get-tuple-element.87.x_ref), custom_call_target="tpu_custom_call" | custom-call | tf_op jit(solution)/shard_map/gather/pallas_call | solution.py:223
  518.0 4.7 convolution_convert_fusion.4.do_ref
  522.8 31.7 %attend_back.1 = bf16[1536,768]{1,0:T(8,128)(2,1)} custom-call(s32[6]{0:T(128)S(1)} %and_select_fusion.first_ref, bf16[1536,256]{1,0:T(8,128)(2,1)S(1)} %get-tuple-element.34.q_ref, bf16[1536,256]{1,0:T(8,128)(2,1)S(1)} %copy-done.4, bf16[1536,256]{1,0:T(8,128)(2,1)S(1)} %copy-done.6, bf16[1536,256]{1,0:T(8,128)(2,1)S(1)} %copy-done.2, ...), custom_call_target="tpu_custom_call" | custom-call | flops 6039797760 | bytes 6291456 | tf_op jit(solution)/shard_map/attend_back/pallas_call | solution.py:642
  554.5 8.4 convolution_convert_fusion.1
  563.0 5.8 convolution_convert_fusion.3
  568.9 14.4 %convolution_convert_fusion = bf16[2048,1408]{1,0:T(8,128)(2,1)} fusion(bf16[1536,2048]{1,0:T(8,128)(2,1)} %bitcast.129, bf16[1536,704]{0,1:T(8,128)(2,1)} %get-tuple-element.92, bf16[1536,704]{0,1:T(8,128)(2,1)S(1)} %copy-done.18), kind=kOutput, calls=%fused_computation.5 | convolution fusion | flops 8869904384 | bytes 16384000 | tf_op jit(solution)/shard_map/dot_general | solution.py:25
  586.9 72.8 %leave.2 = bf16[2,192,2048]{2,1,0:T(8,128)(2,1)} custom-call(bf16[192,2048]{1,0:T(8,128)(2,1)} %reshape.344.x_ref), custom_call_target="tpu_custom_call" | custom-call | tf_op jit(solution)/shard_map/leave/pallas_call | solution.py:337
  659.8 40.2 %scatter.7 = f32[192,2048]{1,0:T(8,128)} custom-call(bf16[8,192,768]{2,1,0:T(8,128)(2,1)} %bitcast.122, bf16[2048,768]{1,0:T(8,128)(2,1)} %all-gather.5.cloned.1.call-done.w_ref), custom_call_target="tpu_custom_call" | custom-call | tf_op jit(solution)/shard_map/scatter/pallas_call | solution.py:458
  713.0 67.3 %leave.3 = bf16[2,192,2048]{2,1,0:T(8,128)(2,1)} custom-call(bf16[192,2048]{1,0:T(8,128)(2,1)} %reshape.350.x_ref), custom_call_target="tpu_custom_call" | custom-call | tf_op jit(solution)/shard_map/leave/pallas_call | solution.py:337
  786.0 16.4 %exchange.6 = (bf16[4,128,768]{2,1,0:T(8,128)(2,1)}, f32[2,4,4,8,128]{4,3,2,1,0:T(8,128)}) custom-call(bf16[4,128,768]{2,1,0:T(8,128)(2,1)} %bitcast.151, f32[4,4,8,128]{3,2,1,0:T(8,128)} %reshape.355.refs_1_), custom_call_target="tpu_custom_call" | custom-call | tf_op jit(solution)/shard_map/exchange/pallas_call | solution.py:112
  808.1 31.3 %exchange.7 = (bf16[4,128,256]{2,1,0:T(8,128)(2,1)}, bf16[4,128,1408]{2,1,0:T(8,128)(2,1)}, bf16[4,128,704]{2,1,0:T(8,128)(2,1)}) custom-call(bf16[4,128,256]{2,1,0:T(8,128)(2,1)} %bitcast.155, bf16[4,128,1408]{2,1,0:T(8,128)(2,1)} %bitcast.146, bf16[4,128,704]{2,1,0:T(8,128)(2,1)} %bitcast.139), custom_call_target="tpu_custom_call" | custom-call | tf_op jit(solution)/shard_map/exchange/pallas_call | solution.py:112
  846.7 5.7 copy.137
  (191 shorter events, 85.1 us)
Async XLA Ops:
  7.2 218.5 %all-gather.5.cloned.1.call-start = ((), (), s32[]{:S(2)}) async-start(), calls=%async_computation.4 | async-start | bytes 3932160 | tf_op jit(solution)/shard_map/all_gather | solution.py:730
  8.8 2.8 copy-start.28
  8.8 2.8 copy-start.29
  10.3 18.4 %copy-start.25 = (bf16[1,1024,128]{2,1,0:T(8,128)(2,1)S(1)}, bf16[1,1024,128]{2,1,0:T(8,128)(2,1)}, u32[]{:S(2)}) copy-start(bf16[1,1024,128]{2,1,0:T(8,128)(2,1)} %param.14) | copy-start | bytes 786436
  10.3 19.3 %copy-start.24 = (bf16[1,2816,128]{2,1,0:T(8,128)(2,1)S(1)}, bf16[1,2816,128]{2,1,0:T(8,128)(2,1)}, u32[]{:S(2)}) copy-start(bf16[1,2816,128]{2,1,0:T(8,128)(2,1)} %param.16) | copy-start | bytes 2162692
  11.6 19.2 %copy-start.21 = (bf16[1,128,2,2816]{3,2,1,0:T(2,128)(2,1)S(1)}, bf16[1,128,2,2816]{3,2,1,0:T(2,128)(2,1)}, u32[]{:S(2)}) copy-start(bf16[1,128,2,2816]{3,2,1,0:T(2,128)(2,1)} %param.15) | copy-start | bytes 4325380
  28.7 236.7 %all-gather.7.cloned.1.call-start = ((), (), s32[]{:S(2)}) async-start(), calls=%async_computation.5 | async-start | bytes 1310720 | tf_op jit(solution)/shard_map/all_gather | solution.py:730
  34.3 33.3 %copy-start.27 = (f32[2,4,4,8,128]{4,3,2,1,0:T(8,128)S(1)}, f32[2,4,4,8,128]{4,3,2,1,0:T(8,128)}, u32[]{:S(2)}) copy-start(f32[2,4,4,8,128]{4,3,2,1,0:T(8,128)} %get-tuple-element.27) | copy-start | bytes 393220
  34.3 33.8 %copy-start.20 = (bf16[384,2048]{1,0:T(8,128)(2,1)S(1)}, bf16[384,2048]{1,0:T(8,128)(2,1)}, u32[]{:S(2)}) copy-start(bf16[384,2048]{1,0:T(8,128)(2,1)} %param.10) | copy-start | bytes 4718596
  66.0 271.5 %all-gather.9.cloned.1.call-start = ((), (), s32[]{:S(2)}) async-start(), calls=%async_computation.6 | async-start | bytes 7208960 | tf_op jit(solution)/shard_map/all_gather | solution.py:730
  66.7 285.9 %all-gather.11.cloned.1.call-start = ((), (), s32[]{:S(2)}) async-start(), calls=%async_computation.7 | async-start | bytes 3932160 | tf_op jit(solution)/shard_map/all_gather | solution.py:730
  67.3 716.5 %reduce-scatter.11.cloned.1.call-start = ((), (), s32[]{:S(2)}) async-start(), calls=%async_computation.11 | async-start | bytes 3604480 | tf_op jit(solution)/shard_map/reduce_scatter | solution.py:733
  67.6 2.5 copy-start.26
  194.0 4.6 copy-start.7
  205.4 3.3 copy-start.10
  208.7 26.8 %copy-start = (f32[1536,128]{1,0:T(8,128)}, f32[1536,128]{1,0:T(8,128)S(1)}, u32[]{:S(2)}) copy-start(f32[1536,128]{1,0:T(8,128)S(1)} %concatenate.37.hi_ref) | copy-start | bytes 2359300
  375.6 410.4 %reduce-scatter.5.cloned.1.call-start = ((), (), s32[]{:S(2)}) async-start(), calls=%async_computation.8 | async-start | bytes 3932160 | tf_op jit(solution)/shard_map/reduce_scatter | solution.py:733
  440.3 39.4 %copy-start.9 = (f32[192,2048]{1,0:T(8,128)S(1)}, f32[192,2048]{1,0:T(8,128)}, u32[]{:S(2)}) copy-start(f32[192,2048]{1,0:T(8,128)} %copy-done.8) | copy-start | bytes 4718596
  440.4 39.4 %copy-start.12 = (f32[192,2048]{1,0:T(8,128)S(1)}, f32[192,2048]{1,0:T(8,128)}, u32[]{:S(2)}) copy-start(f32[192,2048]{1,0:T(8,128)} %scatter.6) | copy-start | bytes 4718596
  484.8 33.1 %copy-start.22 = (bf16[2048,256]{1,0:T(8,128)(2,1)S(1)}, bf16[2048,256]{1,0:T(8,128)(2,1)}, u32[]{:S(2)}) copy-start(bf16[2048,256]{1,0:T(8,128)(2,1)} %all-gather.7.cloned.1.call-done.w_ref) | copy-start | bytes 3145732
  518.0 4.8 copy-start.2
  518.0 4.8 copy-start.4
  518.0 4.8 copy-start.6
  518.0 36.5 %slice-start = ((s8[6291456]{0:T(1024)(128)(4,1)}), s8[4194304]{0:T(1024)(128)(4,1)S(1)}, s32[]{:S(2)}) async-start(s8[6291456]{0:T(1024)(128)(4,1)} %bitcast.126), calls=%async_computation.12 | async-start | bytes 8388608
  522.8 31.7 %slice-start.1 = ((s8[6291456]{0:T(1024)(128)(4,1)}), s8[2097152]{0:T(1024)(128)(4,1)S(1)}, s32[]{:S(2)}) async-start(s8[6291456]{0:T(1024)(128)(4,1)} %bitcast.126), calls=%async_computation.13 | async-start | bytes 4194304
  562.9 6.0 copy-start.18
  562.9 245.2 %reduce-scatter.7.cloned.1.call-start = ((), (), s32[]{:S(2)}) async-start(), calls=%async_computation.9 | async-start | bytes 1310720 | tf_op jit(solution)/shard_map/reduce_scatter | solution.py:733
  568.8 239.3 %reduce-scatter.9.cloned.1.call-start = ((), (), s32[]{:S(2)}) async-start(), calls=%async_computation.10 | async-start | bytes 7208960 | tf_op jit(solution)/shard_map/reduce_scatter | solution.py:733
  659.7 42.9 %copy-start.16 = (f32[192,2048]{1,0:T(8,128)S(1)}, f32[192,2048]{1,0:T(8,128)}, u32[]{:S(2)}) copy-start(f32[192,2048]{1,0:T(8,128)} %get-tuple-element.88) | copy-start | bytes 4718596
  700.0 2.6 copy-start.11
  705.3 6.3 copy-start.13
  846.7 5.7 copy-start.15
  (10 other events, 13.7 us)
Sparse Core Ops, SparseCore 0:
  28.8 59.9 all-gather.4
  90.3 47.7 all-gather.6
  139.7 106.0 all-gather.8
  247.2 62.0 all-gather.10
  375.7 57.2 reduce-scatter.10
  563.1 84.4 reduce-scatter.4
  650.4 24.1 reduce-scatter.6
  677.0 121.2 reduce-scatter.8

commit v3 on v1

v3 whole, which is shorter than its diff:
```python
import functools

import jax
import jax.numpy as jnp
import numpy as np
from jax import lax
from jax.experimental import pallas as pl
from jax.experimental.pallas import tpu as pltpu
from jax.sharding import PartitionSpec as P

HEAD = 64
ROT = 16
EPS = 1e-05
NEG = -1e30
BASE = 10000.0
BF = jnp.bfloat16
F32 = jnp.float32
BLK = 256
MESH = pl.DeviceIdType.MESH
DMA = pltpu.SemaphoreType.DMA
ANY = pl.BlockSpec(memory_space=pl.ANY)
IN_VMEM = pl.BlockSpec(memory_space=pltpu.VMEM)


def mm(a, b, ca, cb):
    return lax.dot_general(a, b, (((ca,), (cb,)), ((), ())), preferred_element_type=F32)


def remote(src, dst, send, recv, where):
    return pltpu.make_async_remote_copy(
        src_ref=src, dst_ref=dst, send_sem=send, recv_sem=recv, device_id=where, device_id_type=MESH
    )


def here():
    return lax.axis_index("shard"), lax.axis_index("ctx"), lax.axis_index("tp")


class Riders:
    def __init__(self, S, C, riders):
        self.S, self.C = S, C
        self.axes = [axis for axis, _ in riders]
        self.arrays = [x for _, x in riders]
        self.shapes = [jax.ShapeDtypeStruct(x.shape, x.dtype) for x in self.arrays]
        count, most = len(riders), max(S, C) - 1
        self.scratch = [DMA((count, most)), DMA((count, most)), DMA((count,))] if count else []

    def bind(self, ins, outs, sems):
        self.ins, self.outs, self.sems = ins, outs, sems

    def start(self):
        p, z, c = here()
        self.moves = []
        for n, axis in enumerate(self.axes):
            src, dst = self.ins[n], self.outs[n]
            send, recv, own = self.sems
            if axis == "tp":
                copies = [remote(src, dst, send.at[n, 0], recv.at[n, 0], {"tp": 1 - c})]
            else:
                size, me = (self.S, p) if axis == "shard" else (self.C, z)
                copies = [
                    remote(src.at[(me + k) % size], dst.at[me], send.at[n, k - 1], recv.at[n, k - 1], {axis: (me + k) % size})
                    for k in range(1, size)
                ]
                copies.append(pltpu.make_async_copy(src.at[me], dst.at[me], own.at[n]))
            for copy in copies:
                copy.start()
            self.moves += copies

    def wait(self):
        for copy in self.moves:
            copy.wait()


def greet(S, C, mates=(), line=False, other=False, axes=()):
    p, z, c = here()
    peers = [{"shard": q} for q in ([(p + k) % S for k in range(1, S)] if "shard" in axes else mates)]
    if line or "ctx" in axes:
        peers += [{"ctx": (z + k) % C} for k in range(1, C)]
    if other or "tp" in axes:
        peers.append({"tp": 1 - c})
    barrier = pltpu.get_barrier_semaphore()
    for where in peers:
        pl.semaphore_signal(barrier, inc=1, device_id=where, device_id_type=MESH)
    pl.semaphore_wait(barrier, len(peers))


def comm(kernel, S, C, number, name, args, in_specs, outs, scratch, riders=()):
    ride = Riders(S, C, riders)
    na, nr, no, ns = len(args), len(ride.axes), len(outs), len(scratch)

    def body(*refs):
        ins, refs = refs[:na], refs[na:]
        rins, refs = refs[:nr], refs[nr:]
        os, refs = refs[:no], refs[no:]
        routs, refs = refs[:nr], refs[nr:]
        ride.bind(rins, routs, refs[ns:])
        kernel(ride, ins, os, refs[:ns])

    return pl.pallas_call(
        body,
        out_shape=[shape for shape, _ in outs] + ride.shapes,
        in_specs=list(in_specs) + [IN_VMEM] * nr,
        out_specs=[spec for _, spec in outs] + [ANY] * nr,
        scratch_shapes=list(scratch) + ride.scratch,
        compiler_params=pltpu.CompilerParams(
            collective_id=number, has_side_effects=True, vmem_limit_bytes=56 << 20
        ),
        cost_estimate=pl.CostEstimate(flops=0, bytes_accessed=120_000_000, transcendentals=0),
        name=name,
    )(*args, *ride.arrays)


def exchange(S, C, T, number, riders, tiles=None):
    if tiles is None:

        def plain(ride, ins, outs, scratch):
            greet(S, C, axes=ride.axes)
            ride.start()
            ride.wait()

        return comm(plain, S, C, number, "exchange", [], [], [], [], riders)

    def kernel(ride, ins, outs, scratch):
        (tile,), (got,) = ins, outs
        send, recv, bsend, brecv, own = scratch
        p, z, c = here()
        everyone = [(i, j) for i in range(C) for j in range(S) if i or j]
        barrier = pltpu.get_barrier_semaphore()
        peers = [{"shard": (p + j) % S, "ctx": (z + i) % C} for i, j in everyone] + [{"tp": 1 - c}]
        for where in peers:
            pl.semaphore_signal(barrier, inc=1, device_id=where, device_id_type=MESH)
        pl.semaphore_wait(barrier, len(peers))
        local = pltpu.make_async_copy(tile.at[z, p], got.at[c, z, p], own)
        local.start()
        copies = []
        for at, (where, (i, j)) in enumerate(zip(peers, everyone)):
            q, g = (p + j) % S, (z + i) % C
            copies.append(remote(tile.at[g, q], got.at[c, z, p], send.at[at], recv.at[at], where))
            copies[-1].start()
        ride.start()
        local.wait()
        for copy in copies:
            copy.wait()
        back = remote(got.at[c], got.at[c], bsend, brecv, {"tp": 1 - c})
        back.start()
        back.wait_send()
        remote(got.at[1 - c], got.at[1 - c], bsend, brecv, {"tp": 1 - c}).wait_recv()
        ride.wait()

    count = C * S - 1
    return comm(
        kernel, S, C, number, "exchange", [tiles], [IN_VMEM],
        [(jax.ShapeDtypeStruct((T,) + tiles.shape, tiles.dtype), ANY)],
        [DMA((count,)), DMA((count,)), DMA, DMA, DMA],
        riders,
    )


def plane(S):
    p, _, c = here()
    B = S // 2
    a, b = p // B, p % B
    return a, b, [a * B + (b + j) % B for j in range(1, B)], (1 - a) * B + b


def spread_sems(S):
    count = 4 + 4 * (S // 2 - 1)
    return [DMA((2 * count,)), DMA((2 * count,))]


def spread(S, own, region, send, recv):
    p, _, c = here()
    B = S // 2
    a, b, rows, col = plane(S)
    rows, col, other = [{"shard": q} for q in rows], {"shard": col}, {"tp": 1 - c}
    per = 4 + 4 * (B - 1)
    OWN, ROW, COL, VIA_COL, VIA_ROW = 0, 2, 2 + 2 * (B - 1), 4 + 2 * (B - 1), 4 + 3 * (B - 1)
    started = []

    def push(q, h, sem, where, first=False):
        view = region(q, h, c)
        copy = remote(own(h) if first else view, view, send.at[sem], recv.at[sem], where)
        copy.start()
        started.append(copy)

    def came(q, h, sem, core):
        view = region(q, h, core)
        remote(view, view, send.at[sem], recv.at[sem], other).wait_recv()

    for h in range(2):
        for j in range(1, B):
            push(p, h, ROW + 2 * (j - 1) + h, rows[j - 1], True)
    for h in (1, 0):
        push(p, h, COL + h, col, True)
    for h in range(2):
        push(p, h, per + OWN + h, other, True)

    def from_row(j, h):
        q = a * B + (b - j) % B
        came(q, h, ROW + 2 * (j - 1) + h, c)
        push(q, h, per + ROW + 2 * (j - 1) + h, other)
        return q

    def from_col(h):
        q = (1 - a) * B + b
        came(q, h, COL + h, c)
        push(q, h, per + COL + h, other)
        return q

    for j in range(1, B):
        q = from_row(j, 0)
        push(q, 0, VIA_COL + j - 1, col)
    q = from_col(1)
    for j in range(1, B):
        push(q, 1, VIA_ROW + j - 1, rows[j - 1])
    for j in range(1, B):
        from_row(j, 1)
    from_col(0)
    for j in range(1, B):
        q = (1 - a) * B + (b - j) % B
        came(q, 0, VIA_COL + j - 1, c)
        push(q, 0, per + VIA_COL + j - 1, other)
        came(q, 1, VIA_ROW + j - 1, c)
        push(q, 1, per + VIA_ROW + j - 1, other)
    for h in range(2):
        came(p, h, per + OWN + h, 1 - c)
        came((1 - a) * B + b, h, per + COL + h, 1 - c)
    for j in range(1, B):
        for h in range(2):
            came(a * B + (b - j) % B, h, per + ROW + 2 * (j - 1) + h, 1 - c)
        q = (1 - a) * B + (b - j) % B
        came(q, 0, per + VIA_COL + j - 1, 1 - c)
        came(q, 1, per + VIA_ROW + j - 1, 1 - c)
    for copy in started:
        copy.wait_send()


def gather(S, C, T, number, x, riders=()):
    n, D = x.shape
    half = n // 2

    def kernel(ride, ins, outs, scratch):
        (x_ref,), (out_ref,), (send, recv, own) = ins, outs, scratch
        p, _, c = here()
        _, _, rows, col = plane(S)
        local = pltpu.make_async_copy(x_ref, out_ref.at[p * T + c], own)
        local.start()
        greet(S, C, rows + [col], other=True, axes=ride.axes)
        ride.start()
        spread(
            S,
            lambda h: x_ref.at[pl.ds(h * half, half)],
            lambda q, h, core: out_ref.at[q * T + core, pl.ds(h * half, half)],
            send,
            recv,
        )
        local.wait()
        ride.wait()

    out, *rest = comm(
        kernel, S, C, number, "gather", [x], [IN_VMEM],
        [(jax.ShapeDtypeStruct((S * T, n, D), x.dtype), ANY)], spread_sems(S) + [DMA], riders,
    )
    return [out.reshape(S * T * n, D)] + rest


def gather_columns(S, C, T, number, x, riders=()):
    _, n, wide = x.shape

    def kernel(ride, ins, outs, scratch):
        (x_ref,), (out_ref,), (send, recv, own) = ins, outs, scratch
        p, _, c = here()
        _, _, rows, col = plane(S)

        def region(q, h, core):
            part = pl.ds(pl.multiple_of(q * wide, 128), wide)
            return out_ref.at[pl.ds(h * (C // 2), C // 2), core, :, part]

        local = [
            pltpu.make_async_copy(x_ref.at[pl.ds(h * (C // 2), C // 2)], region(p, h, c), own.at[h]) for h in range(2)
        ]
        for copy in local:
            copy.start()
        greet(S, C, rows + [col], other=True, axes=ride.axes)
        ride.start()
        spread(S, lambda h: x_ref.at[pl.ds(h * (C // 2), C // 2)], region, send, recv)
        for copy in local:
            copy.wait()
        ride.wait()

    out, *rest = comm(
        kernel, S, C, number, "gather_columns", [x], [IN_VMEM],
        [(jax.ShapeDtypeStruct((C, T, n, wide * S), x.dtype), ANY)], spread_sems(S) + [DMA((2,))], riders,
    )
    return [out.reshape(C * T * n, wide * S)] + rest


def enter(S, C, T, number, x, riders=()):
    _, n, wide = x.shape

    def kernel(ride, ins, outs, scratch):
        (x_ref,), (out_ref,) = ins, outs
        buf, s1, r1, s2, r2, own, send, recv = scratch
        p, z, c = here()
        mates = [(p + k) % S for k in range(1, S)]
        line = [(z + k) % C for k in range(1, C)]
        greet(S, C, mates, line=True, other=True, axes=ride.axes)

        def part(q):
            return pl.ds(pl.multiple_of(q * wide, 128), wide)

        hop = [pltpu.make_async_copy(x_ref.at[p], buf.at[p], own.at[0])]
        for k, q in enumerate(mates):
            hop.append(remote(x_ref.at[q], buf.at[p], s1.at[k], r1.at[k], {"shard": q}))
        for copy in hop:
            copy.start()
        ride.start()
        for copy in hop:
            copy.wait()
        hop = [pltpu.make_async_copy(buf.at[z], out_ref.at[z, c, :, part(p)], own.at[1])]
        for k, g in enumerate(line):
            hop.append(remote(buf.at[g], out_ref.at[z, c, :, part(p)], s2.at[k], r2.at[k], {"ctx": g}))
        for copy in hop:
            copy.start()
        for copy in hop:
            copy.wait()

        def region(q, h, core):
            return out_ref.at[pl.ds(h * (C // 2), C // 2), core, :, part(q)]

        spread(S, lambda h: region(p, h, c), region, send, recv)
        ride.wait()

    out, *rest = comm(
        kernel, S, C, number, "enter", [x], [IN_VMEM],
        [(jax.ShapeDtypeStruct((C, T, n, wide * S), x.dtype), ANY)],
        [pltpu.VMEM((S, n, wide), BF), DMA((S - 1,)), DMA((S - 1,)), DMA((C - 1,)), DMA((C - 1,)), DMA((2,))]
        + spread_sems(S),
        riders,
    )
    return [out.reshape(C * T * n, wide * S)] + rest


def leave(S, C, T, number, x, riders=()):
    _, n, wide = x.shape

    def kernel(ride, ins, outs, scratch):
        (x_ref,), (out_ref,) = ins, outs
        buf, buf2, s1, r1, s2, r2, s3, r3, s4, r4, own = scratch
        p, z, c = here()
        mates = [(p + k) % S for k in range(1, S)]
        line = [(z + k) % C for k in range(1, C)]
        other = {"tp": 1 - c}
        greet(S, C, mates, line=True, other=True, axes=ride.axes)

        def turn_over(source, target, send, recv, local, me, axis, peers):
            hop = [pltpu.make_async_copy(source(me), target, local)]
            for k, q in enumerate(peers):
                hop.append(remote(source(q), target, send.at[k], recv.at[k], {axis: q}))
            for copy in hop:
                copy.start()
            return hop

        first = turn_over(lambda q: x_ref.at[q], buf.at[p], s1, r1, own.at[0], p, "shard", mates)
        ride.start()
        for copy in first:
            copy.wait()
        for copy in turn_over(lambda q: buf.at[q], buf2.at[z], s2, r2, own.at[1], z, "ctx", line):
            copy.wait()
        part = pl.ds(pl.multiple_of(p * wide, 128), wide)
        for copy in turn_over(lambda q: buf2.at[q], out_ref.at[c, :, part], s3, r3, own.at[2], p, "shard", mates):
            copy.wait()
        copy = remote(out_ref.at[c], out_ref.at[c], s4, r4, other)
        copy.start()
        copy.wait_send()
        remote(out_ref.at[1 - c], out_ref.at[1 - c], s4, r4, other).wait_recv()
        ride.wait()

    out, *rest = comm(
        kernel, S, C, number, "leave", [x], [IN_VMEM],
        [(jax.ShapeDtypeStruct((T, n, wide * S), x.dtype), ANY)],
        [
            pltpu.VMEM((S, n, wide), BF), pltpu.VMEM((C, n, wide), BF),
            DMA((S - 1,)), DMA((S - 1,)), DMA((C - 1,)), DMA((C - 1,)), DMA((S - 1,)), DMA((S - 1,)),
            DMA, DMA, DMA((3,)),
        ],
        riders,
    )
    return [out.reshape(T * n, wide * S)] + rest


CHUNK = 512


def scatter(S, C, T, number, x, w, riders=()):
    L, K = x.shape
    D = w.shape[0]
    n, B = L // (S * T), S // 2
    half = n // 2
    steps = D // CHUNK

    def kernel(ride, ins, outs, scratch):
        (x_ref, w_ref), (out_ref,) = ins, outs
        away, sib, mine, row1, col1, row2, col2, to_col, to_row = scratch[:9]
        asend, arecv, rsend, rrecv, csend, crecv, fsend, frecv = scratch[9:]
        p, _, c = here()
        a, b, rows, col = plane(S)
        greet(S, C, rows + [col], other=True, axes=ride.axes)
        rows, col, other = [{"shard": q} for q in rows], {"shard": col}, {"tp": 1 - c}
        ride.start()

        def chip(e):
            return ((a + e // B) % 2) * B + (b + e % B) % B

        def product(e, core, store):
            x = x_ref[chip(e) * T + core]

            def column(j, _):
                w = pl.ds(pl.multiple_of(j * CHUNK, CHUNK), CHUNK)
                store(w, mm(x, w_ref[w, :], 1, 1))
                return 0

            lax.fori_loop(0, steps, column, 0)

        def to_other(e):
            return remote(away.at[e], sib.at[e], asend.at[e], arecv.at[e], other)

        def first(i, _):
            e = S - 1 - i

            def store(w, value):
                away[e, :, w] = value.astype(BF)

            product(e, 1 - c, store)
            to_other(e).start()
            return 0

        lax.fori_loop(0, S, first, 0)

        top, low = pl.ds(0, half), pl.ds(half, half)
        started = []

        def push(src, dst, send, recv, where):
            copy = remote(src, dst, send, recv, where)
            copy.start()
            started.append(copy)

        for e in range(S - 1, -1, -1):
            to_other(e).wait()

            def store(w, value):
                value = value + sib[e, :, w].astype(F32)
                if e:
                    mine[e, :, w] = value.astype(BF)
                else:
                    out_ref[:, w] = value

            product(e, c, store)
            j = e % B
            if e > B:
                push(mine.at[e, top], row1.at[j - 1, 1], rsend.at[j - 1, 1], rrecv.at[j - 1, 1], rows[j - 1])
                push(mine.at[e, low], col1.at[j], csend.at[j], crecv.at[j], col)
            elif e == B:
                push(mine.at[e, low], col1.at[0], csend.at[0], crecv.at[0], col)
            elif e:
                push(mine.at[e, top], row1.at[j - 1, 0], rsend.at[j - 1, 0], rrecv.at[j - 1, 0], rows[j - 1])

        def came(ref, send, recv):
            remote(ref, ref, send, recv, other).wait_recv()

        total = mine[B, top, :].astype(F32)
        for j in range(1, B):
            came(row1.at[j - 1, 1], rsend.at[j - 1, 1], rrecv.at[j - 1, 1])
            total = total + row1[j - 1, 1].astype(F32)
        to_col[...] = total.astype(BF)
        push(to_col, col2, fsend.at[0], frecv.at[0], col)
        for j in range(1, B):
            came(col1.at[j], csend.at[j], crecv.at[j])
            to_row[j - 1] = (mine[j, low, :].astype(F32) + col1[j].astype(F32)).astype(BF)
            push(to_row.at[j - 1], row2.at[j - 1], fsend.at[j], frecv.at[j], rows[j - 1])
        came(col1.at[0], csend.at[0], crecv.at[0])
        upper, lower = out_ref[top, :], out_ref[low, :] + col1[0].astype(F32)
        for j in range(1, B):
            came(row1.at[j - 1, 0], rsend.at[j - 1, 0], rrecv.at[j - 1, 0])
            upper = upper + row1[j - 1, 0].astype(F32)
        came(col2, fsend.at[0], frecv.at[0])
        out_ref[top, :] = upper + col2[...].astype(F32)
        for j in range(1, B):
            came(row2.at[j - 1], fsend.at[j], frecv.at[j])
            lower = lower + row2[j - 1].astype(F32)
        out_ref[low, :] = lower
        for copy in started:
            copy.wait_send()
        ride.wait()

    def vm(*shape):
        return pltpu.VMEM(shape, BF)

    return comm(
        kernel, S, C, number, "scatter", [x.reshape(S * T, n, K), w], [IN_VMEM, IN_VMEM],
        [(jax.ShapeDtypeStruct((n, D), F32), IN_VMEM)],
        [
            vm(S, n, D), vm(S, n, D), vm(S, n, D), vm(B - 1, 2, half, D), vm(B, half, D),
            vm(B - 1, half, D), vm(half, D), vm(half, D), vm(B - 1, half, D),
            DMA((S,)), DMA((S,)), DMA((B - 1, 2)), DMA((B - 1, 2)), DMA((B,)), DMA((B,)), DMA((B,)), DMA((B,)),
        ],
        riders,
    )


def turn_tables(rows):
    feature = np.arange(128) % HEAD
    freq = np.where(feature < ROT, BASE ** (-2.0 * (feature % (ROT // 2)) / ROT), 0.0)
    near = np.arange(BLK)[:, None] * freq
    far = np.arange(0, rows, BLK)[:, None] * freq
    return [jnp.asarray(f(x), F32) for x in (near, far) for f in (np.cos, np.sin)]


def turn(x, i, tables, sign):
    cos, sin, cos_far, sin_far = tables
    far_cos, far_sin = cos_far[pl.ds(i, 1), :], sin_far[pl.ds(i, 1), :]
    cos_t = cos[...] * far_cos - sin[...] * far_sin
    sin_t = sin[...] * far_cos + cos[...] * far_sin
    ahead = lax.broadcasted_iota(jnp.int32, x.shape, 1) % HEAD < ROT // 2
    partner = jnp.where(ahead, -pltpu.roll(x, 128 - ROT // 2, 1), pltpu.roll(x, ROT // 2, 1))
    return x * cos_t + partner * (sin_t * sign)


def attend_kernel(
    first_ref, q_ref, k_ref, v_ref, cos_ref, sin_ref, cosf_ref, sinf_ref, begin_ref,
    qo_ref, ko_ref, vo_ref, o_ref, lse_ref, vt_ref,
):
    rows = q_ref.shape[0]
    nb = rows // BLK
    tables = (cos_ref, sin_ref, cosf_ref, sinf_ref)
    lane = lax.broadcasted_iota(jnp.int32, (BLK, 128), 1)
    left = lane < HEAD
    key_at = lax.broadcasted_iota(jnp.int32, (BLK, BLK), 0)
    query_at = lax.broadcasted_iota(jnp.int32, (1, BLK), 1)

    @pl.loop(0, nb)
    def _(i):
        r = pl.ds(pl.multiple_of(i * BLK, BLK), BLK)
        qo_ref[r, :] = turn(q_ref[r, :], i, tables, 1.0).astype(BF) * jnp.asarray(HEAD**-0.5, BF)
        ko_ref[r, :] = turn(k_ref[r, :], i, tables, 1.0).astype(BF)
        v = v_ref[r, :]
        vo_ref[r, :] = v.astype(BF)
        vt_ref[:, r] = v.T.astype(BF)

    @pl.loop(0, nb)
    def _(i):
        r = pl.ds(pl.multiple_of(i * BLK, BLK), BLK)
        q = qo_ref[r, :]
        zero = jnp.zeros_like(q)
        qs = (jnp.where(left, q, zero), jnp.where(left, zero, q))
        begin = begin_ref[0:1, r]
        here = query_at + i * BLK

        def step(j, carry):
            w = pl.ds(pl.multiple_of(j * BLK, BLK), BLK)
            k, vt = ko_ref[w, :], vt_ref[:, w]
            key = key_at + j * BLK
            seen = (key <= here) & (key >= begin)
            out = []
            for h in range(2):
                m, l, acc = carry[h]
                s = jnp.where(seen, mm(k, qs[h], 1, 1), NEG)
                top = jnp.maximum(m, jnp.max(s, axis=0, keepdims=True))
                fade = jnp.exp(m - top)
                e = jnp.exp(s - top)
                out.append(
                    (top, l * fade + jnp.sum(e, axis=0, keepdims=True), acc * fade + mm(vt, e.astype(BF), 1, 0))
                )
            return tuple(out)

        start = (
            jnp.full((1, BLK), NEG, F32), jnp.zeros((1, BLK), F32), jnp.zeros((128, BLK), F32)
        )
        done = lax.fori_loop(first_ref[i], i + 1, step, (start, start))
        parts = []
        for h in range(2):
            m, l, acc = done[h]
            parts.append((acc / l).T)
            lse_ref[0, h : h + 1, r] = m + jnp.log(l)
        o_ref[r, :] = jnp.where(left, parts[0], parts[1]).astype(BF)


def whole(x):
    return pl.BlockSpec(x.shape, lambda j, *_: (0, 0))


def attend(qkv, begin, first):
    rows, wide = qkv.shape
    pairs = wide // 3 // 128
    tables = turn_tables(rows)

    def col(base):
        return pl.BlockSpec((rows, 128), lambda j, *_: (0, base + j))

    half = jax.ShapeDtypeStruct((rows, wide // 3), BF)
    return pl.pallas_call(
        attend_kernel,
        grid_spec=pltpu.PrefetchScalarGridSpec(
            num_scalar_prefetch=1,
            grid=(pairs,),
            in_specs=[
                col(0), col(pairs), col(2 * pairs), *map(whole, tables), whole(begin),
            ],
            out_specs=[col(0)] * 4 + [pl.BlockSpec((1, 2, rows), lambda j, *_: (j, 0, 0))],
            scratch_shapes=[pltpu.VMEM((128, rows), BF)],
        ),
        out_shape=[half] * 4 + [jax.ShapeDtypeStruct((pairs, 2, rows), F32)],
        compiler_params=pltpu.CompilerParams(vmem_limit_bytes=48 << 20),
        cost_estimate=pl.CostEstimate(
            flops=0, bytes_accessed=27 * 3_000_000, transcendentals=0
        ),
        name="attend",
    )(first, qkv, qkv, qkv, *tables, begin)


def attend_back_kernel(
    first_ref, q_ref, k_ref, v_ref, o_ref, do_ref, lse_ref, cos_ref, sin_ref, cosf_ref, sinf_ref, begin_ref,
    out_ref, kt_ref, dk_ref, dv_ref,
):
    rows = q_ref.shape[0]
    nb = rows // BLK
    tables = (cos_ref, sin_ref, cosf_ref, sinf_ref)
    pair, pairs = pl.program_id(0), pl.num_programs(0)
    lane = lax.broadcasted_iota(jnp.int32, (BLK, 128), 1)
    left = lane < HEAD
    key_at = lax.broadcasted_iota(jnp.int32, (BLK, BLK), 0)
    query_at = lax.broadcasted_iota(jnp.int32, (1, BLK), 1)

    def column(base):
        return pl.ds(pl.multiple_of((base * pairs + pair) * 128, 128), 128)

    @pl.loop(0, nb)
    def _(i):
        r = pl.ds(pl.multiple_of(i * BLK, BLK), BLK)
        kt_ref[:, r] = k_ref[r, :].astype(F32).T.astype(BF)
        dk_ref[r, :] = jnp.zeros((BLK, 128), F32)
        dv_ref[r, :] = jnp.zeros((BLK, 128), F32)

    @pl.loop(0, nb)
    def _(i):
        r = pl.ds(pl.multiple_of(i * BLK, BLK), BLK)
        q, do = q_ref[r, :], do_ref[r, :]
        zero = jnp.zeros_like(q)
        qs = (jnp.where(left, q, zero), jnp.where(left, zero, q))
        dos = (jnp.where(left, do, zero), jnp.where(left, zero, do))
        prod = (do.astype(F32) * o_ref[r, :].astype(F32)).T
        deltas = (
            jnp.sum(prod[:HEAD], axis=0, keepdims=True), jnp.sum(prod[HEAD:], axis=0, keepdims=True)
        )
        lses = (lse_ref[0, 0:1, r], lse_ref[0, 1:2, r])
        begin = begin_ref[0:1, r]
        here = query_at + i * BLK

        def step(j, carry):
            w = pl.ds(pl.multiple_of(j * BLK, BLK), BLK)
            k, v, kt = k_ref[w, :], v_ref[w, :], kt_ref[:, w]
            key = key_at + j * BLK
            seen = (key <= here) & (key >= begin)
            out = []
            dk = dv = None
            for h in range(2):
                prob = jnp.exp(jnp.where(seen, mm(k, qs[h], 1, 1) - lses[h], NEG))
                ds = (prob * (mm(v, dos[h], 1, 1) - deltas[h])).astype(BF)
                out.append(carry[h] + mm(kt, ds, 1, 0))
                dk_h, dv_h = mm(ds, qs[h], 1, 0), mm(prob.astype(BF), dos[h], 1, 0)
                dk, dv = (dk_h, dv_h) if h == 0 else (dk + dk_h, dv + dv_h)
            dk_ref[w, :] += dk
            dv_ref[w, :] += dv
            return tuple(out)

        start = jnp.zeros((128, BLK), F32)
        a, b = lax.fori_loop(first_ref[i], i + 1, step, (start, start))
        dq = jnp.where(left, a.T, b.T) * (HEAD**-0.5)
        out_ref[r, column(0)] = turn(dq, i, tables, -1.0).astype(BF)

    @pl.loop(0, nb)
    def _(i):
        r = pl.ds(pl.multiple_of(i * BLK, BLK), BLK)
        out_ref[r, column(1)] = turn(dk_ref[r, :], i, tables, -1.0).astype(BF)
        out_ref[r, column(2)] = dv_ref[r, :].astype(BF)


def attend_back(q, k, v, o, do, lse, begin, first):
    rows, wide = q.shape
    pairs = wide // 128
    tables = turn_tables(rows)
    col = pl.BlockSpec((rows, 128), lambda j, *_: (0, j))
    return pl.pallas_call(
        attend_back_kernel,
        grid_spec=pltpu.PrefetchScalarGridSpec(
            num_scalar_prefetch=1,
            grid=(pairs,),
            in_specs=[
                col, col, col, col, col, pl.BlockSpec((1, 2, rows), lambda j, *_: (j, 0, 0)),
                *map(whole, tables), whole(begin),
            ],
            out_specs=pl.BlockSpec((rows, 3 * wide), lambda j, *_: (0, 0)),
            scratch_shapes=[
                pltpu.VMEM((128, rows), BF), pltpu.VMEM((rows, 128), F32), pltpu.VMEM((rows, 128), F32)
            ],
        ),
        out_shape=jax.ShapeDtypeStruct((rows, 3 * wide), BF),
        compiler_params=pltpu.CompilerParams(vmem_limit_bytes=48 << 20),
        cost_estimate=pl.CostEstimate(
            flops=0, bytes_accessed=32 * 3_000_000, transcendentals=0
        ),
        name="attend_back",
    )(first, q, k, v, o, do, lse, *tables, begin)


def doc_begins(lengths_row, rows):
    row_ids = jnp.arange(rows, dtype=jnp.int32)
    ends = jnp.cumsum(lengths_row, dtype=jnp.int32)
    begins = ends - lengths_row
    inside = (row_ids[:, None] >= begins[None, :]) & (row_ids[:, None] < ends[None, :])
    return jnp.sum(jnp.where(inside, begins[None, :], 0), axis=1, dtype=jnp.int32)


def layer_norm(values, gain, shift):
    center = values - jnp.mean(values, axis=-1, keepdims=True)
    inverse = lax.rsqrt(jnp.mean(center * center, axis=-1, keepdims=True) + EPS)
    normal = center * inverse
    return (normal * gain + shift, normal, inverse)


def norm_back(gradient, normal, inverse, gain):
    scaled = gradient * gain
    centered = (
        scaled
        - jnp.mean(scaled, axis=-1, keepdims=True)
        - normal * jnp.mean(scaled * normal, axis=-1, keepdims=True)
    )
    return (inverse * centered, jnp.sum(gradient * normal, axis=0), jnp.sum(gradient, axis=0))


def tiles_of(parts, lead):
    flat = jnp.concatenate([x.astype(F32).reshape(lead + (-1,)) for x in parts], axis=-1)
    flat = jnp.pad(flat, ((0, 0),) * len(lead) + ((0, 1024 - flat.shape[-1]),))
    return flat.reshape(lead + (8, 128))


def make_body(S, C, T):
    assert S == C

    def body(tokens, lengths, w_qkv, b_qkv, w_out, w_gateup, w_down, norm_gain, norm_bias, cotangent):
        p, z, c = lax.axis_index("shard"), lax.axis_index("ctx"), lax.axis_index("tp")
        R, D = tokens.shape
        n = R // T
        nb = D // (S * C)
        L = R * C

        def to_parts(x):
            return x.reshape(n, S, C, nb).transpose(2, 0, 1, 3).reshape(S, n, D // S)

        def parts(x):
            return x.reshape(n, S, D // S).swapaxes(0, 1)

        def unpermute(x):
            return x.reshape(x.shape[0], C, S, nb).swapaxes(1, 2).reshape(x.shape)

        def own(x):
            return lax.dynamic_slice_in_dim(x, (p * T + c) * n, n, 0)

        def half_of(x):
            return lax.dynamic_slice_in_dim(x, c * n, n, 0)

        def after(x, y):
            return lax.optimization_barrier((x, y))

        def over_ctx(w):
            return lax.all_gather(w.reshape(S * nb, -1), "ctx", axis=0, tiled=True)

        def sum_ctx(g):
            g = lax.psum_scatter(g.astype(BF), "ctx", scatter_dimension=0, tiled=True)
            return g.reshape(S, nb, -1)

        hn = w_qkv.shape[3] // S
        fn = w_gateup.shape[3] // S
        heads = hn // HEAD
        nf = HEAD // (S * C)

        tile = tiles_of((norm_gain[0].reshape(-1), norm_bias[0].reshape(-1), b_qkv[0].reshape(-1), lengths[0]), ())
        small, wq, cot = exchange(
            S, C, T, 0,
            [
                ("shard", w_qkv[0].reshape(nb, 3, S, hn).transpose(2, 0, 1, 3).reshape(S, nb, 3 * hn)),
                ("shard", to_parts(half_of(cotangent))),
            ],
            jnp.broadcast_to(tile, (C, S, 8, 128)),
        )
        wq = over_ctx(wq)
        tok, cot, wo, wg, wd = enter(
            S, C, T, 1, to_parts(half_of(tokens)),
            [
                ("ctx", cot),
                ("shard", w_out[0].reshape(S, hn, nb).swapaxes(1, 2)),
                ("shard", w_gateup[0].reshape(nb, 2, S, fn).transpose(2, 0, 1, 3).reshape(S, nb, 2 * fn)),
                ("shard", w_down[0].reshape(S, fn, nb).swapaxes(1, 2)),
            ],
        )
        wo, wg, wd = over_ctx(wo), over_ctx(wg), over_ctx(wd)

        small = lax.dynamic_index_in_dim(small, c, 0, keepdims=False).reshape(C, S, 1024)
        norms = small[:, :, : 4 * nb].reshape(C * S, 4, nb).swapaxes(0, 1).reshape(4, D)
        gains, shifts = norms[:2], norms[2:]
        nbias = 3 * S * heads * nf
        bias = small[:, :, 4 * nb : 4 * nb + nbias].reshape(C, S, 3, S * heads, nf)
        bias = lax.dynamic_slice_in_dim(bias, p * heads, heads, 3)
        bias = bias.transpose(2, 3, 1, 0, 4).reshape(1, 3 * hn)
        docs = lengths.shape[1]
        lengths_row = lax.dynamic_index_in_dim(
            small[0, :, 4 * nb + nbias : 4 * nb + nbias + docs], z, 0, keepdims=False
        ).astype(jnp.int32)
        begin = doc_begins(lengths_row, L)
        first = begin[::BLK] // BLK
        begin = begin[None, :]

        n1 = layer_norm(tok.astype(F32), gains[0], shifts[0])[0].astype(BF)
        hidden = own(tok).astype(F32)
        _, normal1, inverse1 = layer_norm(hidden, gains[0], shifts[0])
        qkv = mm(n1, wq, 1, 0) + bias
        q, k, v, o, lse = attend(qkv, begin, first)
        (got,) = scatter(S, C, T, 2, o, wo)
        mid = hidden + got
        n2, normal2, inverse2 = layer_norm(mid, gains[1], shifts[1])
        (n2,) = gather(S, C, T, 3, n2.astype(BF))
        cot, n2 = after(cot, n2)
        (gb,) = gather_columns(S, C, T, 4, cot)
        gu = mm(n2, wg, 1, 0)
        gate, up = gu[:, :fn], gu[:, fn:]
        logistic = jax.nn.sigmoid(gate)
        act = (gate * logistic * up).astype(BF)
        gw_down = mm(gb, act, 0, 0).astype(BF)
        wd, gw_down = after(wd, gw_down)
        gw_down = sum_ctx(gw_down)

        dact = mm(gb, wd, 1, 0)
        dgate = dact * up * logistic * (1.0 + gate * (1.0 - logistic))
        dup = dact * gate * logistic
        dgu = jnp.concatenate((dgate, dup), axis=1).astype(BF)
        gw_gateup = mm(n2, dgu, 0, 0).astype(BF)
        act, gw_gateup = after(act, gw_gateup)
        gw_gateup = sum_ctx(gw_gateup)
        (got,) = scatter(S, C, T, 5, act, wd)
        out = parts((mid + got).astype(BF))
        dgu, out = after(dgu, out)
        got, out = scatter(S, C, T, 6, dgu, wg, [("shard", out)])
        dmid, gain2, shift2 = norm_back(got, normal2, inverse2, gains[1])
        dmid = own(gb).astype(F32) + dmid
        gb1, out = gather(S, C, T, 7, dmid.astype(BF), [("ctx", out)])
        gw_out = mm(gb1, o, 0, 0).astype(BF)
        gb1, gw_out = after(gb1, gw_out)
        gw_out = sum_ctx(gw_out)
        do = mm(gb1, wo, 1, 0).astype(BF)
        dqkv = attend_back(q, k, v, o, do, lse, begin, first)
        dqkv, gw_gateup = after(dqkv, gw_gateup)
        gw_qkv = mm(n1, dqkv, 0, 0).astype(BF)
        dqkv, gw_qkv = after(dqkv, gw_qkv)
        gw_qkv = sum_ctx(gw_qkv)
        got, out, gw_gateup, gw_down = scatter(
            S, C, T, 8, dqkv, wq, [("shard", out), ("shard", gw_gateup), ("shard", gw_down)]
        )
        dtok, gain1, shift1 = norm_back(got, normal1, inverse1, gains[0])
        gtok, gw_out, mate = leave(
            S, C, T, 9, parts((dmid + dtok).astype(BF)), [("shard", gw_out), ("tp", out)]
        )
        gtok = unpermute(gtok).astype(F32)
        out = jnp.where(c == 0, jnp.stack((out, mate)), jnp.stack((mate, out)))
        out = unpermute(out.transpose(0, 2, 1, 3).reshape(R, D))

        gbias = jnp.sum(dqkv.astype(F32), axis=0)
        tiles = tiles_of(
            (
                jnp.stack((gain1, gain2, shift1, shift2)).reshape(4, C, S, nb).transpose(1, 2, 0, 3),
                gbias.reshape(3, heads, S, C, nf).transpose(3, 2, 0, 1, 4),
            ),
            (C, S),
        )
        small, gw_qkv = exchange(S, C, T, 10, [("shard", gw_qkv)], tiles)
        small = small.reshape(T, C, S, 1024)
        norms = jnp.sum(small[..., : 4 * nb], axis=(0, 1, 2)).reshape(1, 4, nb)
        gbias = lax.dynamic_index_in_dim(small, c, 0, keepdims=False)[..., 4 * nb : 4 * nb + 3 * heads * nf]
        gbias = jnp.sum(gbias, axis=0).reshape(S, 3, heads, nf).swapaxes(0, 1).reshape(b_qkv.shape)

        return (
            out,
            gtok,
            gw_qkv.astype(F32).reshape(S, nb, 3, hn).transpose(1, 2, 0, 3).reshape(w_qkv.shape),
            gbias,
            gw_out.astype(F32).swapaxes(1, 2).reshape(w_out.shape),
            gw_gateup.astype(F32).reshape(S, nb, 2, fn).transpose(1, 2, 0, 3).reshape(w_gateup.shape),
            gw_down.astype(F32).swapaxes(1, 2).reshape(w_down.shape),
            norms[:, :2],
            norms[:, 2:],
        )

    return body


def solution(mesh):
    both = ("shard", "ctx")
    specs = (
        P(None, both, None, "tp"),
        P(None, None, "tp", both),
        P(None, "tp", both),
        P(None, both, None, "tp"),
        P(None, "tp", both),
        P(None, None, both),
        P(None, None, both),
    )
    return jax.shard_map(
        make_body(mesh.shape["shard"], mesh.shape["ctx"], mesh.shape["tp"]),
        mesh=mesh,
        in_specs=(P(both, None), P("shard", None)) + specs + (P(both, None),),
        out_specs=(P(both, None), P(both, None)) + specs,
        check_vma=False,
    )
```

time: 1260 us -> 778 us (0.62)
  waiting for transfers between devices: 637 us -> 9.82 us
  Pallas kernels: 70.9 us -> 555 us
  blocking collectives: 236 us -> 0 us
  starting transfers between devices: 41.2 us -> 0.49 us
  matrix products: 111 us -> 76.1 us
  local copies, waits for them, and re-layouts: 106 us -> 75.3 us
    pallas_call x0 -> x11, Pallas kernels: none -> 497 us  [comm(): pl.pallas_call(body, out_shape=[shape for shape, _ in outs] + ride.shapes...]
    all_gather x10 -> x4, waiting for transfers between devices: 297 us -> 7.98 us  [over_ctx(): return lax.all_gather(w.reshape(S * nb, -1), 'ctx', axis=0, tiled=True)]
    reduce_scatter x8 -> x4, waiting for transfers between devices: 282 us -> 0.03 us  [sum_ctx(): g = lax.psum_scatter(g.astype(BF), 'ctx', scatter_dimension=0, tiled=True)]
    all_to_all x6 -> x0, blocking collectives: 135 us -> none  [the longest x3 56.7 us: fetch(): w = lax.all_to_all(w, 'shard', 0, 0, tiled=True)]
    unnamed x1 -> x0, blocking collectives: 61.4 us -> none
    all_to_all x10 -> x0, waiting for transfers between devices: 57.1 us -> none  [the longest x1 29 us: from_plane(): x = lax.all_to_all(x, 'ctx', 0, 0, tiled=True)]
    all_to_all x10 -> x0, starting transfers between devices: 39.8 us -> none  [the longest x4 15.7 us: give(): lax.all_to_all(g.reshape(S, nb, n), 'shard', 0, 0, tiled=True).astype(F32)]
    psum x1 -> x0, blocking collectives: 39.4 us -> none  [body(): lax.psum(jnp.concatenate((gain1, gain2, shift1, shift2, slots.reshape(-1)...]
  transfers between devices with their start and end apart: 28 -> 8, of which waited for: 19 -> 1; matrix products, arithmetic and copies ran while one was open for 15% -> 18% of each run, Pallas kernels for 6% -> 67%
where the time goes in v3:
time: 778 us; the launch traced here: 769 us
  Pallas kernels  555 us (71%)
  matrix products  76.1 us (10%)
  local copies, waits for them, and re-layouts  75.3 us (10%)
  other arithmetic  37.7 us (5%)
  between operations  15.2 us (2%)
  waiting for transfers between devices  9.82 us (1%)
    pallas_call x11, Pallas kernels, comm(): pl.pallas_call(body, out_shape=[shape for shape, _ in outs] + ride.shapes...  497 us
    dot_general x8, matrix products, mm(): lax.dot_general(a, b, (((ca,), (cb,)), ((), ())), preferred_element_type=...  76.1 us
    pallas_call x1, Pallas kernels, attend_back(): pl.pallas_call(attend_back_kernel, grid_spec=pltpu.PrefetchScalarGridSpec...  31.2 us
    pallas_call x1, Pallas kernels, attend(): pl.pallas_call(attend_kernel, grid_spec=pltpu.PrefetchScalarGridSpec(num_...  27.1 us
    unnamed x69, local copies, waits for them, and re-layouts  22.5 us
  transfers between devices with their start and end apart: 8, of which 1 were waited for; matrix products, arithmetic and copies ran while one was open for 18% of the time, Pallas kernels for 67%

profile of v3, /device:TPU:9, one launch (start us, length us, event | category | flops | bytes accessed | tf_op | source)
XLA Modules:
  0.0 769.5 jit_solution(14455364104468925107)
XLA Ops:
  16.6 25.1 %exchange.2 = (f32[2,4,4,8,128]{4,3,2,1,0:T(8,128)}, bf16[4,128,768]{2,1,0:T(8,128)(2,1)}, bf16[4,192,512]{2,1,0:T(8,128)(2,1)}) custom-call(f32[4,4,8,128]{3,2,1,0:T(8,128)} %broadcast_in_dim.14.refs_0_, bf16[4,128,768]{2,1,0:T(8,128)(2,1)} %copy.94.refs_1_, bf16[4,192,512]{2,1,0:T(8,128)(2,1)} %reshape.309.refs_2_), custom_call_target="tpu_custom_call" | custom-call | bytes 120000000 | tf_op jit(solution)/shard_map/exchange/pallas_call | solution.py:100
  49.4 111.0 %enter.1 = (bf16[4,2,192,2048]{3,2,1,0:T(8,128)(2,1)}, bf16[4,192,512]{2,1,0:T(8,128)(2,1)}, bf16[4,128,256]{2,1,0:T(8,128)(2,1)}, bf16[4,128,1408]{2,1,0:T(8,128)(2,1)}, bf16[4,128,704]{2,1,0:T(8,128)(2,1)}) custom-call(bf16[4,192,512]{2,1,0:T(8,128)(2,1)} %reshape.313.refs_0_, bf16[4,192,512]{2,1,0:T(8,128)(2,1)} %get-tuple-element.50.refs_1_, ...), custom_call_target="tpu_custom_call" | custom-call | bytes 120000000 | tf_op jit(solution)/shard_map/enter/pallas_call | solution.py:100
  162.5 3.8 convert_reduce_fusion
  171.1 7.7 %add_convert_fusion = bf16[1536,2048]{1,0:T(8,128)(2,1)} fusion(f32[2048]{0:T(1024)S(1)} %bitcast.185, f32[2048]{0:T(1024)S(1)} %bitcast.174, f32[1536]{0:T(1024)S(1)} %rsqrt.28, f32[1536]{0:T(1024)S(1)} %div.52, bf16[4,2,192,2048]{3,2,1,0:T(8,128)(2,1)} %get-tuple-element.51), kind=kLoop, calls=%fused_computation.4 | loop fusion | flops 18874368 | bytes 12611584 | tf_op jit(solution)/shard_map/convert_element_type | solution.py:824
  178.9 9.6 %convolution_add_fusion.q_ref.k_ref.v_ref = f32[1536,768]{1,0:T(8,128)} fusion(bf16[1536,2048]{1,0:T(8,128)(2,1)} %add_convert_fusion, bf16[2048,768]{1,0:T(8,128)(2,1)} %all-gather.5.cloned.1.call-done.refs_1_, f32[768]{0:T(1024)S(1)} %add.123), kind=kOutput, calls=%fused_computation.12 | convolution fusion | flops 4833017856 | bytes 14158848 | tf_op jit(solution)/shard_map/dot_general | solution.py:26
  188.5 27.1 %attend.1 = (bf16[1536,256]{1,0:T(8,128)(2,1)S(1)}, bf16[1536,256]{1,0:T(8,128)(2,1)S(1)}, bf16[1536,256]{1,0:T(8,128)(2,1)S(1)}, bf16[1536,256]{1,0:T(8,128)(2,1)S(1)}, f32[2,2,1536]{2,1,0:T(2,128)S(1)}) custom-call(s32[6]{0:T(128)S(1)} %and_select_fusion.first_ref, f32[1536,768]{1,0:T(8,128)} %convolution_add_fusion.q_ref.k_ref.v_ref, ...), custom_call_target="tpu_custom_call" | custom-call | bytes 81000000 | tf_op jit(solution)/shard_map/attend/pallas_call | solution.py:602
  216.4 35.6 %scatter.4 = f32[192,2048]{1,0:T(8,128)} custom-call(bf16[8,192,256]{2,1,0:T(8,128)(2,1)} %bitcast.127, bf16[2048,256]{1,0:T(8,128)(2,1)} %all-gather.7.cloned.1.call-done.refs_1_), custom_call_target="tpu_custom_call" | custom-call | bytes 120000000 | tf_op jit(solution)/shard_map/scatter/pallas_call | solution.py:100
  256.5 32.1 %gather.2 = bf16[8,192,2048]{2,1,0:T(8,128)(2,1)} custom-call(bf16[192,2048]{1,0:T(8,128)(2,1)} %add_convert_fusion.2.refs_0_), custom_call_target="tpu_custom_call" | custom-call | bytes 120000000 | tf_op jit(solution)/shard_map/gather/pallas_call | solution.py:100
  288.6 32.1 %gather_columns.1 = bf16[4,2,192,2048]{3,2,1,0:T(8,128)(2,1)} custom-call(bf16[4,192,512]{2,1,0:T(8,128)(2,1)} %get-tuple-element.59.refs_0_), custom_call_target="tpu_custom_call" | custom-call | bytes 120000000 | tf_op jit(solution)/shard_map/gather_columns/pallas_call | solution.py:100
  320.7 14.2 %fusion.23 = f32[1536,1408]{0,1:T(8,128)S(1)} fusion(bf16[1536,2048]{1,0:T(8,128)(2,1)} %bitcast.141, bf16[2048,1408]{1,0:T(8,128)(2,1)} %all-gather.11.cloned.1.call-done.refs_1_), kind=kOutput, calls=%fused_computation.91 | convolution fusion | flops 8858370048 | bytes 20709376 | tf_op jit(solution)/shard_map/dot_general | solution.py:26
  336.4 3.0 copy-done.11
  341.7 6.3 convolution_convert_fusion.2
  348.0 7.9 %all-gather.9.cloned.1.call-done.refs_1_ = bf16[2048,704]{1,0:T(8,128)(2,1)} async-done(((bf16[512,704]{1,0:T(8,128)(2,1)}), bf16[2048,704]{1,0:T(8,128)(2,1)}) %all-gather.9.cloned.1.call-update) | async-done | bytes 2883600 | tf_op jit(solution)/shard_map/all_gather | solution.py:777
  355.9 12.5 %multiply_convert_fusion.1 = (bf16[1536,704]{0,1:T(8,128)(2,1)S(1)}, bf16[1536,704]{0,1:T(8,128)(2,1)S(1)}) fusion(f32[1536,1408]{0,1:T(8,128)} %copy-done.11, bf16[1536,2048]{1,0:T(8,128)(2,1)} %bitcast.138, bf16[2048,704]{1,0:T(8,128)(2,1)} %all-gather.9.cloned.1.call-done.refs_1_), kind=kOutput, calls=%fused_computation.9 | convolution fusion | flops 4443242496 | bytes 22151168 | tf_op jit(solution)/shard_map/dot_general | solution.py:26
  370.4 13.7 %convolution_convert_fusion = bf16[2048,1408]{1,0:T(8,128)(2,1)} fusion(bf16[1536,2048]{1,0:T(8,128)(2,1)} %bitcast.142, bf16[1536,704]{0,1:T(8,128)(2,1)S(1)} %get-tuple-element.129, bf16[1536,704]{0,1:T(8,128)(2,1)S(1)} %get-tuple-element.128), kind=kOutput, calls=%fused_computation.5 | convolution fusion | flops 8869904384 | bytes 16384000 | tf_op jit(solution)/shard_map/dot_general | solution.py:26
  384.8 4.4 copy.102
  389.1 40.1 %scatter.5 = f32[192,2048]{1,0:T(8,128)} custom-call(bf16[8,192,704]{2,1,0:T(8,128)(2,1)} %bitcast.137, bf16[2048,704]{1,0:T(8,128)(2,1)} %all-gather.9.cloned.1.call-done.refs_1_), custom_call_target="tpu_custom_call" | custom-call | bytes 120000000 | tf_op jit(solution)/shard_map/scatter/pallas_call | solution.py:100
  434.5 6.5 copy.104
  441.0 47.0 %scatter.6 = (f32[192,2048]{1,0:T(8,128)}, bf16[4,192,512]{2,1,0:T(8,128)(2,1)}) custom-call(bf16[8,192,1408]{2,1,0:T(8,128)(2,1)} %bitcast.133, bf16[2048,1408]{1,0:T(8,128)(2,1)} %all-gather.11.cloned.1.call-done.refs_1_, bf16[4,192,512]{2,1,0:T(8,128)(2,1)} %bitcast.159), custom_call_target="tpu_custom_call" | custom-call | bytes 120000000 | tf_op jit(solution)/shard_map/scatter/pallas_call | solution.py:100
  490.3 3.3 fusion.19
  493.6 45.8 %gather.3 = (bf16[8,192,2048]{2,1,0:T(8,128)(2,1)}, bf16[4,192,512]{2,1,0:T(8,128)(2,1)}) custom-call(bf16[192,2048]{1,0:T(8,128)(2,1)} %get-tuple-element.124.refs_0_, bf16[4,192,512]{2,1,0:T(8,128)(2,1)} %get-tuple-element.68.refs_1_), custom_call_target="tpu_custom_call" | custom-call | bytes 120000000 | tf_op jit(solution)/shard_map/gather/pallas_call | solution.py:100
  539.5 5.7 convolution_convert_fusion.4
  545.3 4.9 convolution_convert_fusion.3.do_ref
  550.1 31.2 %attend_back.1 = bf16[1536,768]{1,0:T(8,128)(2,1)} custom-call(s32[6]{0:T(128)S(1)} %and_select_fusion.first_ref, bf16[1536,256]{1,0:T(8,128)(2,1)S(1)} %get-tuple-element.53.q_ref, bf16[1536,256]{1,0:T(8,128)(2,1)S(1)} %get-tuple-element.54.k_ref, bf16[1536,256]{1,0:T(8,128)(2,1)S(1)} %get-tuple-element.55.v_ref, bf16[1536,256]{1,0:T(8,128)(2,1)S(1)} %copy-done.1, ...), custom_call_target="tpu_custom_call" | custom-call | bytes 96000000 | tf_op jit(solution)/shard_map/attend_back/pallas_call | solution.py:694
  581.3 9.2 %convolution_convert_fusion.1 = bf16[2048,768]{1,0:T(8,128)(2,1)} fusion(bf16[1536,2048]{1,0:T(8,128)(2,1)} %add_convert_fusion, bf16[1536,768]{1,0:T(8,128)(2,1)} %attend_back.1), kind=kOutput, calls=%fused_computation.13 | convolution fusion | flops 4833411072 | bytes 11796480 | tf_op jit(solution)/shard_map/dot_general | solution.py:26
  592.8 65.1 %scatter.7 = (f32[192,2048]{1,0:T(8,128)}, bf16[4,192,512]{2,1,0:T(8,128)(2,1)}, bf16[4,128,1408]{2,1,0:T(8,128)(2,1)}, bf16[4,128,704]{2,1,0:T(8,128)(2,1)}) custom-call(bf16[8,192,768]{2,1,0:T(8,128)(2,1)} %bitcast.132, bf16[2048,768]{1,0:T(8,128)(2,1)} %all-gather.5.cloned.1.call-done.refs_1_, bf16[4,192,512]{2,1,0:T(8,128)(2,1)} %get-tuple-element.75.refs_2_, ...), custom_call_target="tpu_custom_call" | custom-call | bytes 120000000 | tf_op jit(solution)/shard_map/scatter/pallas_call | solution.py:100
  657.9 2.5 fusion.12
  668.8 5.6 copy.120
  676.1 49.7 %leave.1 = (bf16[2,192,2048]{2,1,0:T(8,128)(2,1)}, bf16[4,128,256]{2,1,0:T(8,128)(2,1)}, bf16[4,192,512]{2,1,0:T(8,128)(2,1)}) custom-call(bf16[4,192,512]{2,1,0:T(8,128)(2,1)} %bitcast.149, bf16[4,128,256]{2,1,0:T(8,128)(2,1)} %bitcast.171, bf16[4,192,512]{2,1,0:T(8,128)(2,1)} %get-tuple-element.78.refs_2_), custom_call_target="tpu_custom_call" | custom-call | bytes 120000000 | tf_op jit(solution)/shard_map/leave/pallas_call | solution.py:100
  732.0 4.0 reshape.370
  738.5 5.0 reshape.357
  743.6 13.1 %exchange.3 = (f32[2,4,4,8,128]{4,3,2,1,0:T(8,128)}, bf16[4,128,768]{2,1,0:T(8,128)(2,1)}) custom-call(f32[4,4,8,128]{3,2,1,0:T(8,128)} %reshape.338.refs_0_, bf16[4,128,768]{2,1,0:T(8,128)(2,1)} %bitcast.166), custom_call_target="tpu_custom_call" | custom-call | bytes 120000000 | tf_op jit(solution)/shard_map/exchange/pallas_call | solution.py:100
  (183 shorter events, 69.3 us)
Async XLA Ops:
  7.2 171.7 %all-gather.5.cloned.1.call-start = ((), (), s32[]{:S(2)}) async-start(), calls=%async_computation.4 | async-start | bytes 3932160 | tf_op jit(solution)/shard_map/all_gather | solution.py:777
  8.8 2.9 copy-start.25
  13.8 2.1 copy-start.31
  14.6 27.1 %copy-start.27 = (bf16[1,1024,128]{2,1,0:T(8,128)(2,1)S(1)}, bf16[1,1024,128]{2,1,0:T(8,128)(2,1)}, u32[]{:S(2)}) copy-start(bf16[1,1024,128]{2,1,0:T(8,128)(2,1)} %param.22) | copy-start | bytes 786436
  14.6 28.0 %copy-start.24 = (bf16[1,2816,128]{2,1,0:T(8,128)(2,1)S(1)}, bf16[1,2816,128]{2,1,0:T(8,128)(2,1)}, u32[]{:S(2)}) copy-start(bf16[1,2816,128]{2,1,0:T(8,128)(2,1)} %param.24) | copy-start | bytes 2162692
  15.8 27.9 %copy-start.22 = (bf16[1,128,2,2816]{3,2,1,0:T(2,128)(2,1)S(1)}, bf16[1,128,2,2816]{3,2,1,0:T(2,128)(2,1)}, u32[]{:S(2)}) copy-start(bf16[1,128,2,2816]{3,2,1,0:T(2,128)(2,1)} %param.23) | copy-start | bytes 4325380
  41.7 174.8 %all-gather.7.cloned.1.call-start = ((), (), s32[]{:S(2)}) async-start(), calls=%async_computation.5 | async-start | bytes 1310720 | tf_op jit(solution)/shard_map/all_gather | solution.py:777
  49.4 112.6 %copy-start.29 = (f32[2,4,4,8,128]{4,3,2,1,0:T(8,128)S(1)}, f32[2,4,4,8,128]{4,3,2,1,0:T(8,128)}, u32[]{:S(2)}) copy-start(f32[2,4,4,8,128]{4,3,2,1,0:T(8,128)} %get-tuple-element.49) | copy-start | bytes 393220
  160.5 160.3 %all-gather.11.cloned.1.call-start = ((), (), s32[]{:S(2)}) async-start(), calls=%async_computation.7 | async-start | bytes 7208960 | tf_op jit(solution)/shard_map/all_gather | solution.py:777
  161.2 194.7 %all-gather.9.cloned.1.call-start = ((), (), s32[]{:S(2)}) async-start(), calls=%async_computation.6 | async-start | bytes 3932160 | tf_op jit(solution)/shard_map/all_gather | solution.py:777
  161.8 419.5 %reduce-scatter.5.cloned.1.call-start = ((), (), s32[]{:S(2)}) async-start(), calls=%async_computation.8 | async-start | bytes 7208960 | tf_op jit(solution)/shard_map/reduce_scatter | solution.py:780
  162.1 4.3 copy-start.28
  162.5 4.7 copy-start.6
  178.8 9.7 %copy-start.2 = (f32[256,128]{1,0:T(8,128)S(1)}, f32[256,128]{1,0:T(8,128)}, u32[]{:S(2)}) copy-start(f32[256,128]{1,0:T(8,128)} %constant.86.clone.sin_ref) | copy-start | bytes 393220
  178.8 9.7 %copy-start.3 = (f32[256,128]{1,0:T(8,128)S(1)}, f32[256,128]{1,0:T(8,128)}, u32[]{:S(2)}) copy-start(f32[256,128]{1,0:T(8,128)} %constant.85.clone.cos_ref) | copy-start | bytes 393220
  178.8 9.7 %copy-start.4 = (f32[6,128]{1,0:T(8,128)S(1)}, f32[6,128]{1,0:T(8,128)}, u32[]{:S(2)}) copy-start(f32[6,128]{1,0:T(8,128)} %constant.88.clone.sinf_ref) | copy-start | bytes 9220
  178.8 9.7 %copy-start.5 = (f32[6,128]{1,0:T(8,128)S(1)}, f32[6,128]{1,0:T(8,128)}, u32[]{:S(2)}) copy-start(f32[6,128]{1,0:T(8,128)} %constant.87.clone.cosf_ref) | copy-start | bytes 9220
  335.0 4.4 copy-start.11
  335.0 6.7 copy-start.13
  384.2 206.4 %reduce-scatter.7.cloned.1.call-start = ((), (), s32[]{:S(2)}) async-start(), calls=%async_computation.9 | async-start | bytes 3604480 | tf_op jit(solution)/shard_map/reduce_scatter | solution.py:780
  384.7 291.4 %reduce-scatter.9.cloned.1.call-start = ((), (), s32[]{:S(2)}) async-start(), calls=%async_computation.10 | async-start | bytes 1310720 | tf_op jit(solution)/shard_map/reduce_scatter | solution.py:780
  389.1 40.1 %copy-start.8 = (f32[192,2048]{1,0:T(8,128)S(1)}, f32[192,2048]{1,0:T(8,128)}, u32[]{:S(2)}) copy-start(f32[192,2048]{1,0:T(8,128)} %copy-done.7) | copy-start | bytes 4718596
  429.3 2.7 copy-start.19
  429.3 2.9 copy-start.21
  441.0 47.0 %copy-start.9 = (f32[192,2048]{1,0:T(8,128)S(1)}, f32[192,2048]{1,0:T(8,128)}, u32[]{:S(2)}) copy-start(f32[192,2048]{1,0:T(8,128)} %copy-done.7) | copy-start | bytes 4718596
  488.0 2.3 copy-start.14
  490.3 49.2 %copy-start.1 = (bf16[1536,256]{1,0:T(8,128)(2,1)S(1)}, bf16[1536,256]{1,0:T(8,128)(2,1)}, u32[]{:S(2)}) copy-start(bf16[1536,256]{1,0:T(8,128)(2,1)} %copy-done) | copy-start | bytes 2359300
  545.2 198.3 %reduce-scatter.11.cloned.1.call-start = ((), (), s32[]{:S(2)}) async-start(), calls=%async_computation.11 | async-start | bytes 3932160 | tf_op jit(solution)/shard_map/reduce_scatter | solution.py:780
  657.9 2.6 copy-start.15
  660.6 3.4 copy-start.10
  668.8 5.6 copy-start.23
  674.5 51.3 %copy-start.16 = (bf16[4,192,512]{2,1,0:T(8,128)(2,1)S(1)}, bf16[4,192,512]{2,1,0:T(8,128)(2,1)}, u32[]{:S(2)}) copy-start(bf16[4,192,512]{2,1,0:T(8,128)(2,1)} %get-tuple-element.78.refs_2_) | copy-start | bytes 2359300
  (10 other events, 15.9 us)
Sparse Core Ops, SparseCore 0:
  41.8 92.0 all-gather.4
  160.6 26.4 all-gather.6
  188.6 103.6 all-gather.10
  293.8 62.1 all-gather.8
  384.3 103.3 reduce-scatter.4
  490.5 72.8 reduce-scatter.6
  566.2 24.1 reduce-scatter.8
  592.9 63.9 reduce-scatter.10

commit v4 on v3

--- a/solution.py
+++ b/solution.py
@@ -111,19 +111,10 @@
     )(*args, *ride.arrays)
 
 
-def exchange(S, C, T, number, riders, tiles=None):
-    if tiles is None:
-
-        def plain(ride, ins, outs, scratch):
-            greet(S, C, axes=ride.axes)
-            ride.start()
-            ride.wait()
-
-        return comm(plain, S, C, number, "exchange", [], [], [], [], riders)
-
+def exchange(S, C, T, number, riders, tiles, rows=None):
     def kernel(ride, ins, outs, scratch):
-        (tile,), (got,) = ins, outs
-        send, recv, bsend, brecv, own = scratch
+        tile, got = ins[0], outs[0]
+        send, recv, bsend, brecv, own = scratch[:5]
         p, z, c = here()
         everyone = [(i, j) for i in range(C) for j in range(S) if i or j]
         barrier = pltpu.get_barrier_semaphore()
@@ -131,6 +122,19 @@
         for where in peers:
             pl.semaphore_signal(barrier, inc=1, device_id=where, device_id_type=MESH)
         pl.semaphore_wait(barrier, len(peers))
+
+        def turn_over(source, target, k, axis, size, me):
+            ssem, rsem, local = scratch[5:]
+            hop = [pltpu.make_async_copy(source.at[me], target.at[me], local.at[k])]
+            for j in range(1, size):
+                q = (me + j) % size
+                hop.append(remote(source.at[q], target.at[me], ssem.at[k, j - 1], rsem.at[k, j - 1], {axis: q}))
+            for copy in hop:
+                copy.start()
+            return hop
+
+        if rows is not None:
+            first = turn_over(ins[1], outs[1], 0, "shard", S, p)
         local = pltpu.make_async_copy(tile.at[z, p], got.at[c, z, p], own)
         local.start()
         copies = []
@@ -139,6 +143,10 @@
             copies.append(remote(tile.at[g, q], got.at[c, z, p], send.at[at], recv.at[at], where))
             copies[-1].start()
         ride.start()
+        if rows is not None:
+            for copy in first:
+                copy.wait()
+            second = turn_over(outs[1], outs[2], 1, "ctx", C, z)
         local.wait()
         for copy in copies:
             copy.wait()
@@ -146,15 +154,19 @@
         back.start()
         back.wait_send()
         remote(got.at[1 - c], got.at[1 - c], bsend, brecv, {"tp": 1 - c}).wait_recv()
+        if rows is not None:
+            for copy in second:
+                copy.wait()
         ride.wait()
 
-    count = C * S - 1
-    return comm(
-        kernel, S, C, number, "exchange", [tiles], [IN_VMEM],
-        [(jax.ShapeDtypeStruct((T,) + tiles.shape, tiles.dtype), ANY)],
-        [DMA((count,)), DMA((count,)), DMA, DMA, DMA],
-        riders,
-    )
+    count, most = C * S - 1, max(S, C) - 1
+    args, outs = [tiles], [(jax.ShapeDtypeStruct((T,) + tiles.shape, tiles.dtype), ANY)]
+    scratch = [DMA((count,)), DMA((count,)), DMA, DMA, DMA]
+    if rows is not None:
+        args.append(rows)
+        outs += [(jax.ShapeDtypeStruct(rows.shape, rows.dtype), IN_VMEM)] * 2
+        scratch += [DMA((2, most)), DMA((2, most)), DMA((2,))]
+    return comm(kernel, S, C, number, "exchange", args, [IN_VMEM] * len(args), outs, scratch, riders)
 
 
 def plane(S):
@@ -296,52 +308,6 @@
     return [out.reshape(C * T * n, wide * S)] + rest
 
 
-def enter(S, C, T, number, x, riders=()):
-    _, n, wide = x.shape
-
-    def kernel(ride, ins, outs, scratch):
-        (x_ref,), (out_ref,) = ins, outs
-        buf, s1, r1, s2, r2, own, send, recv = scratch
-        p, z, c = here()
-        mates = [(p + k) % S for k in range(1, S)]
-        line = [(z + k) % C for k in range(1, C)]
-        greet(S, C, mates, line=True, other=True, axes=ride.axes)
-
-        def part(q):
-            return pl.ds(pl.multiple_of(q * wide, 128), wide)
-
-        hop = [pltpu.make_async_copy(x_ref.at[p], buf.at[p], own.at[0])]
-        for k, q in enumerate(mates):
-            hop.append(remote(x_ref.at[q], buf.at[p], s1.at[k], r1.at[k], {"shard": q}))
-        for copy in hop:
-            copy.start()
-        ride.start()
-        for copy in hop:
-            copy.wait()
-        hop = [pltpu.make_async_copy(buf.at[z], out_ref.at[z, c, :, part(p)], own.at[1])]
-        for k, g in enumerate(line):
-            hop.append(remote(buf.at[g], out_ref.at[z, c, :, part(p)], s2.at[k], r2.at[k], {"ctx": g}))
-        for copy in hop:
-            copy.start()
-        for copy in hop:
-            copy.wait()
-
-        def region(q, h, core):
-            return out_ref.at[pl.ds(h * (C // 2), C // 2), core, :, part(q)]
-
-        spread(S, lambda h: region(p, h, c), region, send, recv)
-        ride.wait()
-
-    out, *rest = comm(
-        kernel, S, C, number, "enter", [x], [IN_VMEM],
-        [(jax.ShapeDtypeStruct((C, T, n, wide * S), x.dtype), ANY)],
-        [pltpu.VMEM((S, n, wide), BF), DMA((S - 1,)), DMA((S - 1,)), DMA((C - 1,)), DMA((C - 1,)), DMA((2,))]
-        + spread_sems(S),
-        riders,
-    )
-    return [out.reshape(C * T * n, wide * S)] + rest
-
-
 def leave(S, C, T, number, x, riders=()):
     _, n, wide = x.shape
 
@@ -527,191 +493,170 @@
     return x * cos_t + partner * (sin_t * sign)
 
 
+def two_heads(x, left):
+    zero = jnp.zeros_like(x)
+    return [jnp.where(left, x, zero), jnp.where(left, zero, x)]
+
+
+def block_of(rows):
+    return next(size for size in (512, 256) if rows % size == 0)
+
+
 def attend_kernel(
-    first_ref, q_ref, k_ref, v_ref, cos_ref, sin_ref, cosf_ref, sinf_ref, begin_ref,
+    first_ref, qkv_ref, cos_ref, sin_ref, cosf_ref, sinf_ref, begin_ref,
     qo_ref, ko_ref, vo_ref, o_ref, lse_ref, vt_ref,
 ):
-    rows = q_ref.shape[0]
-    nb = rows // BLK
+    rows, wide = qo_ref.shape
+    pairs, size = wide // 128, block_of(rows)
     tables = (cos_ref, sin_ref, cosf_ref, sinf_ref)
-    lane = lax.broadcasted_iota(jnp.int32, (BLK, 128), 1)
-    left = lane < HEAD
-    key_at = lax.broadcasted_iota(jnp.int32, (BLK, BLK), 0)
-    query_at = lax.broadcasted_iota(jnp.int32, (1, BLK), 1)
-
-    @pl.loop(0, nb)
+    left = lax.broadcasted_iota(jnp.int32, (size, 128), 1) < HEAD
+    key_at = lax.broadcasted_iota(jnp.int32, (size, size), 0)
+    query_at = lax.broadcasted_iota(jnp.int32, (1, size), 1)
+
+    @pl.loop(0, rows // BLK)
     def _(i):
         r = pl.ds(pl.multiple_of(i * BLK, BLK), BLK)
-        qo_ref[r, :] = turn(q_ref[r, :], i, tables, 1.0).astype(BF) * jnp.asarray(HEAD**-0.5, BF)
-        ko_ref[r, :] = turn(k_ref[r, :], i, tables, 1.0).astype(BF)
-        v = v_ref[r, :]
-        vo_ref[r, :] = v.astype(BF)
-        vt_ref[:, r] = v.T.astype(BF)
-
-    @pl.loop(0, nb)
+        for t in range(pairs):
+            w = pl.ds(t * 128, 128)
+            q, k, v = (qkv_ref[r, pl.ds(part * wide + t * 128, 128)] for part in range(3))
+            qo_ref[r, w] = turn(q, i, tables, 1.0).astype(BF) * jnp.asarray(HEAD**-0.5, BF)
+            ko_ref[r, w] = turn(k, i, tables, 1.0).astype(BF)
+            vo_ref[r, w] = v.astype(BF)
+            vt_ref[w, r] = v.T.astype(BF)
+
+    @pl.loop(0, rows // size)
     def _(i):
-        r = pl.ds(pl.multiple_of(i * BLK, BLK), BLK)
-        q = qo_ref[r, :]
-        zero = jnp.zeros_like(q)
-        qs = (jnp.where(left, q, zero), jnp.where(left, zero, q))
+        r = pl.ds(pl.multiple_of(i * size, size), size)
+        qs = sum((two_heads(qo_ref[r, pl.ds(t * 128, 128)], left) for t in range(pairs)), [])
         begin = begin_ref[0:1, r]
-        here = query_at + i * BLK
+        here = query_at + i * size
 
         def step(j, carry):
-            w = pl.ds(pl.multiple_of(j * BLK, BLK), BLK)
-            k, vt = ko_ref[w, :], vt_ref[:, w]
-            key = key_at + j * BLK
+            w = pl.ds(pl.multiple_of(j * size, size), size)
+            key = key_at + j * size
             seen = (key <= here) & (key >= begin)
             out = []
-            for h in range(2):
+            for h in range(2 * pairs):
                 m, l, acc = carry[h]
-                s = jnp.where(seen, mm(k, qs[h], 1, 1), NEG)
+                s = jnp.where(seen, mm(ko_ref[w, pl.ds(h // 2 * 128, 128)], qs[h], 1, 1), NEG)
                 top = jnp.maximum(m, jnp.max(s, axis=0, keepdims=True))
                 fade = jnp.exp(m - top)
                 e = jnp.exp(s - top)
-                out.append(
-                    (top, l * fade + jnp.sum(e, axis=0, keepdims=True), acc * fade + mm(vt, e.astype(BF), 1, 0))
-                )
+                acc = acc * fade + mm(vt_ref[pl.ds(h * HEAD, HEAD), w], e.astype(BF), 1, 0)
+                out.append((top, l * fade + jnp.sum(e, axis=0, keepdims=True), acc))
             return tuple(out)
 
         start = (
-            jnp.full((1, BLK), NEG, F32), jnp.zeros((1, BLK), F32), jnp.zeros((128, BLK), F32)
+            jnp.full((1, size), NEG, F32), jnp.zeros((1, size), F32), jnp.zeros((HEAD, size), F32)
         )
-        done = lax.fori_loop(first_ref[i], i + 1, step, (start, start))
-        parts = []
-        for h in range(2):
-            m, l, acc = done[h]
-            parts.append((acc / l).T)
-            lse_ref[0, h : h + 1, r] = m + jnp.log(l)
-        o_ref[r, :] = jnp.where(left, parts[0], parts[1]).astype(BF)
-
-
-def whole(x):
-    return pl.BlockSpec(x.shape, lambda j, *_: (0, 0))
-
-
-def attend(qkv, begin, first):
-    rows, wide = qkv.shape
-    pairs = wide // 3 // 128
-    tables = turn_tables(rows)
-
-    def col(base):
-        return pl.BlockSpec((rows, 128), lambda j, *_: (0, base + j))
-
-    half = jax.ShapeDtypeStruct((rows, wide // 3), BF)
+        done = lax.fori_loop(first_ref[i], i + 1, step, (start,) * (2 * pairs))
+        for t in range(pairs):
+            both = []
+            for h in (2 * t, 2 * t + 1):
+                m, l, acc = done[h]
+                both.append(acc / l)
+                lse_ref[h : h + 1, r] = m + jnp.log(l)
+            o_ref[r, pl.ds(t * 128, 128)] = jnp.concatenate(both, axis=0).T.astype(BF)
+
+
+def attend(qkv, begin):
+    rows, wide = qkv.shape[0], qkv.shape[1] // 3
+    size = block_of(rows)
+    half = jax.ShapeDtypeStruct((rows, wide), BF)
     return pl.pallas_call(
         attend_kernel,
-        grid_spec=pltpu.PrefetchScalarGridSpec(
-            num_scalar_prefetch=1,
-            grid=(pairs,),
-            in_specs=[
-                col(0), col(pairs), col(2 * pairs), *map(whole, tables), whole(begin),
-            ],
-            out_specs=[col(0)] * 4 + [pl.BlockSpec((1, 2, rows), lambda j, *_: (j, 0, 0))],
-            scratch_shapes=[pltpu.VMEM((128, rows), BF)],
-        ),
-        out_shape=[half] * 4 + [jax.ShapeDtypeStruct((pairs, 2, rows), F32)],
+        in_specs=[pl.BlockSpec(memory_space=pltpu.SMEM)] + [IN_VMEM] * 6,
+        out_specs=[IN_VMEM] * 5,
+        out_shape=[half] * 4 + [jax.ShapeDtypeStruct((wide // HEAD, rows), F32)],
+        scratch_shapes=[pltpu.VMEM((wide, rows), BF)],
         compiler_params=pltpu.CompilerParams(vmem_limit_bytes=48 << 20),
-        cost_estimate=pl.CostEstimate(
-            flops=0, bytes_accessed=27 * 3_000_000, transcendentals=0
-        ),
         name="attend",
-    )(first, qkv, qkv, qkv, *tables, begin)
-
-
-def attend_back_kernel(
-    first_ref, q_ref, k_ref, v_ref, o_ref, do_ref, lse_ref, cos_ref, sin_ref, cosf_ref, sinf_ref, begin_ref,
-    out_ref, kt_ref, dk_ref, dv_ref,
-):
-    rows = q_ref.shape[0]
-    nb = rows // BLK
+    )(begin[0, ::size] // size, qkv, *turn_tables(rows), begin)
+
+
+def attend_back_work(ins, out_ref, scratch):
+    q_ref, k_ref, v_ref, o_ref, do_ref, lse_ref, cos_ref, sin_ref, cosf_ref, sinf_ref, begin_ref = ins
+    kt_ref, dq_ref, dk_ref, dv_ref = scratch
+    rows, wide = q_ref.shape
+    pairs, size = wide // 128, block_of(rows)
     tables = (cos_ref, sin_ref, cosf_ref, sinf_ref)
-    pair, pairs = pl.program_id(0), pl.num_programs(0)
-    lane = lax.broadcasted_iota(jnp.int32, (BLK, 128), 1)
-    left = lane < HEAD
-    key_at = lax.broadcasted_iota(jnp.int32, (BLK, BLK), 0)
-    query_at = lax.broadcasted_iota(jnp.int32, (1, BLK), 1)
-
-    def column(base):
-        return pl.ds(pl.multiple_of((base * pairs + pair) * 128, 128), 128)
-
-    @pl.loop(0, nb)
+    left = lax.broadcasted_iota(jnp.int32, (size, 128), 1) < HEAD
+    key_at = lax.broadcasted_iota(jnp.int32, (size, size), 0)
+    query_at = lax.broadcasted_iota(jnp.int32, (1, size), 1)
+
+    @pl.loop(0, rows // BLK)
     def _(i):
         r = pl.ds(pl.multiple_of(i * BLK, BLK), BLK)
-        kt_ref[:, r] = k_ref[r, :].astype(F32).T.astype(BF)
-        dk_ref[r, :] = jnp.zeros((BLK, 128), F32)
-        dv_ref[r, :] = jnp.zeros((BLK, 128), F32)
-
-    @pl.loop(0, nb)
+        for t in range(pairs):
+            w = pl.ds(t * 128, 128)
+            kt_ref[w, r] = k_ref[r, w].astype(F32).T.astype(BF)
+            dk_ref[r, w] = jnp.zeros((BLK, 128), F32)
+            dv_ref[r, w] = jnp.zeros((BLK, 128), F32)
+
+    @pl.loop(0, rows // size)
+    def _(i):
+        r = pl.ds(pl.multiple_of(i * size, size), size)
+        qs, dos, deltas, lses = [], [], [], []
+        for t in range(pairs):
+            w = pl.ds(t * 128, 128)
+            do = do_ref[r, w]
+            qs += two_heads(q_ref[r, w], left)
+            dos += two_heads(do, left)
+            prod = (do.astype(F32) * o_ref[r, w].astype(F32)).T
+            deltas += [jnp.sum(prod[:HEAD], axis=0, keepdims=True), jnp.sum(prod[HEAD:], axis=0, keepdims=True)]
+            lses += [lse_ref[2 * t : 2 * t + 1, r], lse_ref[2 * t + 1 : 2 * t + 2, r]]
+        begin = begin_ref[0:1, r]
+        here = query_at + i * size
+
+        def step(j, carry):
+            w = pl.ds(pl.multiple_of(j * size, size), size)
+            key = key_at + j * size
+            seen = (key <= here) & (key >= begin)
+            out = []
+            for t in range(pairs):
+                lanes = pl.ds(t * 128, 128)
+                k, v = k_ref[w, lanes], v_ref[w, lanes]
+                dk = dv = None
+                for h in (2 * t, 2 * t + 1):
+                    prob = jnp.exp(jnp.where(seen, mm(k, qs[h], 1, 1) - lses[h], NEG))
+                    ds = (prob * (mm(v, dos[h], 1, 1) - deltas[h])).astype(BF)
+                    out.append(carry[h] + mm(kt_ref[pl.ds(h * HEAD, HEAD), w], ds, 1, 0))
+                    dk_h, dv_h = mm(ds, qs[h], 1, 0), mm(prob.astype(BF), dos[h], 1, 0)
+                    dk, dv = (dk_h, dv_h) if dk is None else (dk + dk_h, dv + dv_h)
+                dk_ref[w, lanes] += dk
+                dv_ref[w, lanes] += dv
+            return tuple(out)
+
+        done = lax.fori_loop(0, i + 1, step, (jnp.zeros((HEAD, size), F32),) * (2 * pairs))
+        for t in range(pairs):
+            both = jnp.concatenate(done[2 * t : 2 * t + 2], axis=0)
+            dq_ref[r, pl.ds(t * 128, 128)] = both.T * (HEAD**-0.5)
+
+    @pl.loop(0, rows // BLK)
     def _(i):
         r = pl.ds(pl.multiple_of(i * BLK, BLK), BLK)
-        q, do = q_ref[r, :], do_ref[r, :]
-        zero = jnp.zeros_like(q)
-        qs = (jnp.where(left, q, zero), jnp.where(left, zero, q))
-        dos = (jnp.where(left, do, zero), jnp.where(left, zero, do))
-        prod = (do.astype(F32) * o_ref[r, :].astype(F32)).T
-        deltas = (
-            jnp.sum(prod[:HEAD], axis=0, keepdims=True), jnp.sum(prod[HEAD:], axis=0, keepdims=True)
-        )
-        lses = (lse_ref[0, 0:1, r], lse_ref[0, 1:2, r])
-        begin = begin_ref[0:1, r]
-        here = query_at + i * BLK
-
-        def step(j, carry):
-            w = pl.ds(pl.multiple_of(j * BLK, BLK), BLK)
-            k, v, kt = k_ref[w, :], v_ref[w, :], kt_ref[:, w]
-            key = key_at + j * BLK
-            seen = (key <= here) & (key >= begin)
-            out = []
-            dk = dv = None
-            for h in range(2):
-                prob = jnp.exp(jnp.where(seen, mm(k, qs[h], 1, 1) - lses[h], NEG))
-                ds = (prob * (mm(v, dos[h], 1, 1) - deltas[h])).astype(BF)
-                out.append(carry[h] + mm(kt, ds, 1, 0))
-                dk_h, dv_h = mm(ds, qs[h], 1, 0), mm(prob.astype(BF), dos[h], 1, 0)
-                dk, dv = (dk_h, dv_h) if h == 0 else (dk + dk_h, dv + dv_h)
-            dk_ref[w, :] += dk
-            dv_ref[w, :] += dv
-            return tuple(out)
-
-        start = jnp.zeros((128, BLK), F32)
-        a, b = lax.fori_loop(first_ref[i], i + 1, step, (start, start))
-        dq = jnp.where(left, a.T, b.T) * (HEAD**-0.5)
-        out_ref[r, column(0)] = turn(dq, i, tables, -1.0).astype(BF)
-
-    @pl.loop(0, nb)
-    def _(i):
-        r = pl.ds(pl.multiple_of(i * BLK, BLK), BLK)
-        out_ref[r, column(1)] = turn(dk_ref[r, :], i, tables, -1.0).astype(BF)
-        out_ref[r, column(2)] = dv_ref[r, :].astype(BF)
-
-
-def attend_back(q, k, v, o, do, lse, begin, first):
+        for t in range(pairs):
+            w = pl.ds(t * 128, 128)
+            for part, value in enumerate((turn(dq_ref[r, w], i, tables, -1.0), turn(dk_ref[r, w], i, tables, -1.0), dv_ref[r, w])):
+                out_ref[r, pl.ds(part * wide + t * 128, 128)] = value.astype(BF)
+
+
+def attend_back(S, C, number, q, k, v, o, do, lse, begin, riders):
     rows, wide = q.shape
-    pairs = wide // 128
-    tables = turn_tables(rows)
-    col = pl.BlockSpec((rows, 128), lambda j, *_: (0, j))
-    return pl.pallas_call(
-        attend_back_kernel,
-        grid_spec=pltpu.PrefetchScalarGridSpec(
-            num_scalar_prefetch=1,
-            grid=(pairs,),
-            in_specs=[
-                col, col, col, col, col, pl.BlockSpec((1, 2, rows), lambda j, *_: (j, 0, 0)),
-                *map(whole, tables), whole(begin),
-            ],
-            out_specs=pl.BlockSpec((rows, 3 * wide), lambda j, *_: (0, 0)),
-            scratch_shapes=[
-                pltpu.VMEM((128, rows), BF), pltpu.VMEM((rows, 128), F32), pltpu.VMEM((rows, 128), F32)
-            ],
-        ),
-        out_shape=jax.ShapeDtypeStruct((rows, 3 * wide), BF),
-        compiler_params=pltpu.CompilerParams(vmem_limit_bytes=48 << 20),
-        cost_estimate=pl.CostEstimate(
-            flops=0, bytes_accessed=32 * 3_000_000, transcendentals=0
-        ),
-        name="attend_back",
-    )(first, q, k, v, o, do, lse, *tables, begin)
+
+    def kernel(ride, ins, outs, scratch):
+        greet(S, C, axes=ride.axes)
+        ride.start()
+        attend_back_work(ins, outs[0], scratch)
+        ride.wait()
+
+    args = [q, k, v, o, do, lse, *turn_tables(rows), begin]
+    return comm(
+        kernel, S, C, number, "attend_back", args, [IN_VMEM] * len(args),
+        [(jax.ShapeDtypeStruct((rows, 3 * wide), BF), IN_VMEM)],
+        [pltpu.VMEM((wide, rows), BF)] + [pltpu.VMEM((rows, wide), F32)] * 3,
+        riders,
+    )
 
 
 def doc_begins(lengths_row, rows):
@@ -786,22 +731,20 @@
         nf = HEAD // (S * C)
 
         tile = tiles_of((norm_gain[0].reshape(-1), norm_bias[0].reshape(-1), b_qkv[0].reshape(-1), lengths[0]), ())
-        small, wq, cot = exchange(
+        small, _, tok, wq = exchange(
             S, C, T, 0,
-            [
-                ("shard", w_qkv[0].reshape(nb, 3, S, hn).transpose(2, 0, 1, 3).reshape(S, nb, 3 * hn)),
-                ("shard", to_parts(half_of(cotangent))),
-            ],
+            [("shard", w_qkv[0].reshape(nb, 3, S, hn).transpose(2, 0, 1, 3).reshape(S, nb, 3 * hn))],
             jnp.broadcast_to(tile, (C, S, 8, 128)),
+            to_parts(half_of(tokens)),
         )
         wq = over_ctx(wq)
-        tok, cot, wo, wg, wd = enter(
-            S, C, T, 1, to_parts(half_of(tokens)),
+        tok, wo, wg, wd, cot = gather_columns(
+            S, C, T, 1, tok,
             [
-                ("ctx", cot),
                 ("shard", w_out[0].reshape(S, hn, nb).swapaxes(1, 2)),
                 ("shard", w_gateup[0].reshape(nb, 2, S, fn).transpose(2, 0, 1, 3).reshape(S, nb, 2 * fn)),
                 ("shard", w_down[0].reshape(S, fn, nb).swapaxes(1, 2)),
+                ("shard", to_parts(half_of(cotangent))),
             ],
         )
         wo, wg, wd = over_ctx(wo), over_ctx(wg), over_ctx(wd)
@@ -818,15 +761,14 @@
             small[0, :, 4 * nb + nbias : 4 * nb + nbias + docs], z, 0, keepdims=False
         ).astype(jnp.int32)
         begin = doc_begins(lengths_row, L)
-        first = begin[::BLK] // BLK
         begin = begin[None, :]
 
         n1 = layer_norm(tok.astype(F32), gains[0], shifts[0])[0].astype(BF)
         hidden = own(tok).astype(F32)
         _, normal1, inverse1 = layer_norm(hidden, gains[0], shifts[0])
         qkv = mm(n1, wq, 1, 0) + bias
-        q, k, v, o, lse = attend(qkv, begin, first)
-        (got,) = scatter(S, C, T, 2, o, wo)
+        q, k, v, o, lse = attend(qkv, begin)
+        got, cot = scatter(S, C, T, 2, o, wo, [("ctx", cot)])
         mid = hidden + got
         n2, normal2, inverse2 = layer_norm(mid, gains[1], shifts[1])
         (n2,) = gather(S, C, T, 3, n2.astype(BF))
@@ -858,14 +800,13 @@
         gb1, gw_out = after(gb1, gw_out)
         gw_out = sum_ctx(gw_out)
         do = mm(gb1, wo, 1, 0).astype(BF)
-        dqkv = attend_back(q, k, v, o, do, lse, begin, first)
-        dqkv, gw_gateup = after(dqkv, gw_gateup)
+        dqkv, gw_gateup, gw_down = attend_back(
+            S, C, 11, q, k, v, o, do, lse, begin, [("shard", gw_gateup), ("shard", gw_down)]
+        )
         gw_qkv = mm(n1, dqkv, 0, 0).astype(BF)
         dqkv, gw_qkv = after(dqkv, gw_qkv)
         gw_qkv = sum_ctx(gw_qkv)
-        got, out, gw_gateup, gw_down = scatter(
-            S, C, T, 8, dqkv, wq, [("shard", out), ("shard", gw_gateup), ("shard", gw_down)]
-        )
+        got, out = scatter(S, C, T, 8, dqkv, wq, [("shard", out)])
         dtok, gain1, shift1 = norm_back(got, normal1, inverse1, gains[0])
         gtok, gw_out, mate = leave(
             S, C, T, 9, parts((dmid + dtok).astype(BF)), [("shard", gw_out), ("tp", out)]

time: 778 us -> 734 us (0.943)
  Pallas kernels: 555 us -> 497 us
  waiting for transfers between devices: 9.82 us -> 19.2 us
    pallas_call x2 -> x1, Pallas kernels: 58.2 us -> 20.2 us  [attend(): pl.pallas_call(attend_kernel, in_specs=[pl.BlockSpec(memory_space=pltpu.S...]
    pallas_call x11 -> x12, Pallas kernels: 497 us -> 477 us  [comm(): pl.pallas_call(body, out_shape=[shape for shape, _ in outs] + ride.shapes...]
    all_gather x4, waiting for transfers between devices: 7.98 us -> 17.9 us  [over_ctx(): return lax.all_gather(w.reshape(S * nb, -1), 'ctx', axis=0, tiled=True)]
    unnamed x69 -> x75, local copies, waits for them, and re-layouts: 22.5 us -> 24.9 us
  transfers between devices with their start and end apart: 8 -> 8, of which waited for: 1 -> 1; matrix products, arithmetic and copies ran while one was open for 18% -> 23% of each run, Pallas kernels for 67% -> 62%
where the time goes in v4:
time: 734 us; the launch traced here: 723 us
  Pallas kernels  497 us (68%)
  local copies, waits for them, and re-layouts  77.2 us (11%)
  matrix products  76.7 us (10%)
  other arithmetic  36.8 us (5%)
  waiting for transfers between devices  19.2 us (3%)
  between operations  15.1 us (2%)
    pallas_call x12, Pallas kernels, comm(): pl.pallas_call(body, out_shape=[shape for shape, _ in outs] + ride.shapes...  477 us
    dot_general x8, matrix products, mm(): lax.dot_general(a, b, (((ca,), (cb,)), ((), ())), preferred_element_type=...  76.7 us
    unnamed x75, local copies, waits for them, and re-layouts  24.9 us
    pallas_call x1, Pallas kernels, attend(): pl.pallas_call(attend_kernel, in_specs=[pl.BlockSpec(memory_space=pltpu.S...  20.2 us
    all_gather x4, waiting for transfers between devices, over_ctx(): return lax.all_gather(w.reshape(S * nb, -1), 'ctx', axis=0, tiled=True)  17.9 us
  transfers between devices with their start and end apart: 8, of which 1 were waited for; matrix products, arithmetic and copies ran while one was open for 23% of the time, Pallas kernels for 62%

profile of v4, /device:TPU:9, one launch (start us, length us, event | category | flops | bytes accessed | tf_op | source)
XLA Modules:
  0.0 723.0 jit_solution(12521048370889919631)
XLA Ops:
  16.6 36.0 %exchange.2 = (f32[2,4,4,8,128]{4,3,2,1,0:T(8,128)}, bf16[4,192,512]{2,1,0:T(8,128)(2,1)}, bf16[4,192,512]{2,1,0:T(8,128)(2,1)}, bf16[4,128,768]{2,1,0:T(8,128)(2,1)}) custom-call(f32[4,4,8,128]{3,2,1,0:T(8,128)} %broadcast_in_dim.14.refs_0_, bf16[4,192,512]{2,1,0:T(8,128)(2,1)} %reshape.308.refs_1_, bf16[4,128,768]{2,1,0:T(8,128)(2,1)} %copy.94.refs_2_), custom_call_target="tpu_custom_call" | custom-call | bytes 120000000 | tf_op jit(solution)/shard_map/exchange/pallas_call | solution.py:100
  60.3 70.5 %gather_columns.2 = (bf16[4,2,192,2048]{3,2,1,0:T(8,128)(2,1)}, bf16[4,128,256]{2,1,0:T(8,128)(2,1)}, bf16[4,128,1408]{2,1,0:T(8,128)(2,1)}, bf16[4,128,704]{2,1,0:T(8,128)(2,1)}, bf16[4,192,512]{2,1,0:T(8,128)(2,1)}) custom-call(bf16[4,192,512]{2,1,0:T(8,128)(2,1)} %get-tuple-element.51.refs_0_, bf16[4,128,256]{2,1,0:T(8,128)(2,1)} %bitcast.171, ...), custom_call_target="tpu_custom_call" | custom-call | bytes 120000000 | tf_op jit(solution)/shard_map/gather_columns/pallas_call | solution.py:100
  132.3 3.8 convert_reduce_fusion
  141.2 8.0 %add_convert_fusion = bf16[1536,2048]{1,0:T(8,128)(2,1)} fusion(f32[2048]{0:T(1024)S(1)} %bitcast.193, f32[2048]{0:T(1024)S(1)} %bitcast.182, f32[1536]{0:T(1024)S(1)} %rsqrt.28, f32[1536]{0:T(1024)S(1)} %div.52, bf16[4,2,192,2048]{3,2,1,0:T(8,128)(2,1)} %get-tuple-element.52), kind=kLoop, calls=%fused_computation.4 | loop fusion | flops 18874368 | bytes 12611584 | tf_op jit(solution)/shard_map/convert_element_type | solution.py:766
  149.3 9.6 %convolution_add_fusion.qkv_ref = f32[1536,768]{1,0:T(8,128)} fusion(bf16[1536,2048]{1,0:T(8,128)(2,1)} %add_convert_fusion, bf16[2048,768]{1,0:T(8,128)(2,1)} %all-gather.5.cloned.1.call-done.refs_1_, f32[768]{0:T(1024)S(1)} %add.123), kind=kOutput, calls=%fused_computation.12 | convolution fusion | flops 4833017856 | bytes 14158848 | tf_op jit(solution)/shard_map/dot_general | solution.py:26
  158.9 20.2 %attend.1 = (bf16[1536,256]{1,0:T(8,128)(2,1)S(1)}, bf16[1536,256]{1,0:T(8,128)(2,1)S(1)}, bf16[1536,256]{1,0:T(8,128)(2,1)S(1)}, bf16[1536,256]{1,0:T(8,128)(2,1)S(1)}, f32[4,1536]{1,0:T(4,128)S(1)}) custom-call(s32[3]{0:T(128)S(1)} %and_select_fusion.first_ref, f32[1536,768]{1,0:T(8,128)} %convolution_add_fusion.qkv_ref, f32[256,128]{1,0:T(8,128)S(1)} %copy-done.6, ...), custom_call_target="tpu_custom_call" | custom-call | tf_op jit(solution)/shard_map/attend/pallas_call | solution.py:566
  183.3 46.0 %scatter.4 = (f32[192,2048]{1,0:T(8,128)}, bf16[4,192,512]{2,1,0:T(8,128)(2,1)}) custom-call(bf16[8,192,256]{2,1,0:T(8,128)(2,1)} %bitcast.135, bf16[2048,256]{1,0:T(8,128)(2,1)} %all-gather.7.cloned.1.call-done.refs_1_, bf16[4,192,512]{2,1,0:T(8,128)(2,1)} %get-tuple-element.59.refs_2_), custom_call_target="tpu_custom_call" | custom-call | bytes 120000000 | tf_op jit(solution)/shard_map/scatter/pallas_call | solution.py:100
  233.0 32.8 %gather.2 = bf16[8,192,2048]{2,1,0:T(8,128)(2,1)} custom-call(bf16[192,2048]{1,0:T(8,128)(2,1)} %add_convert_fusion.2.refs_0_), custom_call_target="tpu_custom_call" | custom-call | bytes 120000000 | tf_op jit(solution)/shard_map/gather/pallas_call | solution.py:100
  265.8 32.1 %gather_columns.3 = bf16[4,2,192,2048]{3,2,1,0:T(8,128)(2,1)} custom-call(bf16[4,192,512]{2,1,0:T(8,128)(2,1)} %get-tuple-element.62.refs_0_), custom_call_target="tpu_custom_call" | custom-call | bytes 120000000 | tf_op jit(solution)/shard_map/gather_columns/pallas_call | solution.py:100
  297.9 14.5 %fusion.23 = f32[1536,1408]{0,1:T(8,128)S(1)} fusion(bf16[1536,2048]{1,0:T(8,128)(2,1)} %bitcast.149, bf16[2048,1408]{1,0:T(8,128)(2,1)} %all-gather.11.cloned.1.call-done.refs_1_), kind=kOutput, calls=%fused_computation.92 | convolution fusion | flops 8858370048 | bytes 20709376 | tf_op jit(solution)/shard_map/dot_general | solution.py:26
  313.9 3.0 copy-done.13
  319.2 5.9 convolution_convert_fusion.2
  325.1 17.9 %all-gather.9.cloned.1.call-done.refs_1_ = bf16[2048,704]{1,0:T(8,128)(2,1)} async-done(((bf16[512,704]{1,0:T(8,128)(2,1)}), bf16[2048,704]{1,0:T(8,128)(2,1)}) %all-gather.9.cloned.1.call-update) | async-done | bytes 2883600 | tf_op jit(solution)/shard_map/all_gather | solution.py:722
  343.2 12.5 %multiply_convert_fusion.1 = (bf16[1536,704]{0,1:T(8,128)(2,1)S(1)}, bf16[1536,704]{0,1:T(8,128)(2,1)S(1)}) fusion(f32[1536,1408]{0,1:T(8,128)} %copy-done.13, bf16[1536,2048]{1,0:T(8,128)(2,1)} %bitcast.146, bf16[2048,704]{1,0:T(8,128)(2,1)} %all-gather.9.cloned.1.call-done.refs_1_), kind=kOutput, calls=%fused_computation.9 | convolution fusion | flops 4443242496 | bytes 22151168 | tf_op jit(solution)/shard_map/dot_general | solution.py:26
  357.7 13.7 %convolution_convert_fusion = bf16[2048,1408]{1,0:T(8,128)(2,1)} fusion(bf16[1536,2048]{1,0:T(8,128)(2,1)} %bitcast.150, bf16[1536,704]{0,1:T(8,128)(2,1)S(1)} %get-tuple-element.131, bf16[1536,704]{0,1:T(8,128)(2,1)S(1)} %get-tuple-element.130), kind=kOutput, calls=%fused_computation.5 | convolution fusion | flops 8869904384 | bytes 16384000 | tf_op jit(solution)/shard_map/dot_general | solution.py:26
  371.7 4.2 copy.102
  375.9 40.4 %scatter.5 = f32[192,2048]{1,0:T(8,128)} custom-call(bf16[8,192,704]{2,1,0:T(8,128)(2,1)} %bitcast.145, bf16[2048,704]{1,0:T(8,128)(2,1)} %all-gather.9.cloned.1.call-done.refs_1_), custom_call_target="tpu_custom_call" | custom-call | bytes 120000000 | tf_op jit(solution)/shard_map/scatter/pallas_call | solution.py:100
  421.3 6.5 copy.104
  427.8 46.2 %scatter.6 = (f32[192,2048]{1,0:T(8,128)}, bf16[4,192,512]{2,1,0:T(8,128)(2,1)}) custom-call(bf16[8,192,1408]{2,1,0:T(8,128)(2,1)} %bitcast.140, bf16[2048,1408]{1,0:T(8,128)(2,1)} %all-gather.11.cloned.1.call-done.refs_1_, bf16[4,192,512]{2,1,0:T(8,128)(2,1)} %bitcast.167), custom_call_target="tpu_custom_call" | custom-call | bytes 120000000 | tf_op jit(solution)/shard_map/scatter/pallas_call | solution.py:100
  476.3 2.8 fusion.19
  479.1 42.6 %gather.3 = (bf16[8,192,2048]{2,1,0:T(8,128)(2,1)}, bf16[4,192,512]{2,1,0:T(8,128)(2,1)}) custom-call(bf16[192,2048]{1,0:T(8,128)(2,1)} %get-tuple-element.126.refs_0_, bf16[4,192,512]{2,1,0:T(8,128)(2,1)} %get-tuple-element.71.refs_1_), custom_call_target="tpu_custom_call" | custom-call | bytes 120000000 | tf_op jit(solution)/shard_map/gather/pallas_call | solution.py:100
  521.8 5.8 convolution_convert_fusion.4
  527.7 5.5 convolution_convert_fusion.3.refs_4_
  535.4 32.1 %attend_back.1 = (bf16[1536,768]{1,0:T(8,128)(2,1)}, bf16[4,128,1408]{2,1,0:T(8,128)(2,1)}, bf16[4,128,704]{2,1,0:T(8,128)(2,1)}) custom-call(bf16[1536,256]{1,0:T(8,128)(2,1)} %copy-done.2, bf16[1536,256]{1,0:T(8,128)(2,1)} %copy-done.3, bf16[1536,256]{1,0:T(8,128)(2,1)} %copy-done.4, bf16[1536,256]{1,0:T(8,128)(2,1)} %copy-done, ...), custom_call_target="tpu_custom_call" | custom-call | bytes 120000000 | tf_op jit(solution)/shard_map/attend_back/pallas_call | solution.py:100
  567.6 9.2 %convolution_convert_fusion.1 = bf16[2048,768]{1,0:T(8,128)(2,1)} fusion(bf16[1536,2048]{1,0:T(8,128)(2,1)} %add_convert_fusion, bf16[1536,768]{1,0:T(8,128)(2,1)} %get-tuple-element.78), kind=kOutput, calls=%fused_computation.13 | convolution fusion | flops 4833411072 | bytes 11796480 | tf_op jit(solution)/shard_map/dot_general | solution.py:26
  576.8 40.7 %scatter.7 = (f32[192,2048]{1,0:T(8,128)}, bf16[4,192,512]{2,1,0:T(8,128)(2,1)}) custom-call(bf16[8,192,768]{2,1,0:T(8,128)(2,1)} %bitcast.144, bf16[2048,768]{1,0:T(8,128)(2,1)} %all-gather.5.cloned.1.call-done.refs_1_, bf16[4,192,512]{2,1,0:T(8,128)(2,1)} %get-tuple-element.79.refs_2_), custom_call_target="tpu_custom_call" | custom-call | bytes 120000000 | tf_op jit(solution)/shard_map/scatter/pallas_call | solution.py:100
  617.5 2.5 fusion.12
  627.8 5.8 copy.120
  635.3 44.3 %leave.1 = (bf16[2,192,2048]{2,1,0:T(8,128)(2,1)}, bf16[4,128,256]{2,1,0:T(8,128)(2,1)}, bf16[4,192,512]{2,1,0:T(8,128)(2,1)}) custom-call(bf16[4,192,512]{2,1,0:T(8,128)(2,1)} %bitcast.157, bf16[4,128,256]{2,1,0:T(8,128)(2,1)} %bitcast.179, bf16[4,192,512]{2,1,0:T(8,128)(2,1)} %get-tuple-element.80.refs_2_), custom_call_target="tpu_custom_call" | custom-call | bytes 120000000 | tf_op jit(solution)/shard_map/leave/pallas_call | solution.py:100
  685.7 3.8 reshape.370
  692.0 5.0 reshape.357
  697.1 13.3 %exchange.3 = (f32[2,4,4,8,128]{4,3,2,1,0:T(8,128)}, bf16[4,128,768]{2,1,0:T(8,128)(2,1)}) custom-call(f32[4,4,8,128]{3,2,1,0:T(8,128)} %reshape.338.refs_0_, bf16[4,128,768]{2,1,0:T(8,128)(2,1)} %bitcast.174), custom_call_target="tpu_custom_call" | custom-call | bytes 120000000 | tf_op jit(solution)/shard_map/exchange/pallas_call | solution.py:100
  (189 shorter events, 70.6 us)
Async XLA Ops:
  7.2 142.1 %all-gather.5.cloned.1.call-start = ((), (), s32[]{:S(2)}) async-start(), calls=%async_computation.4 | async-start | bytes 3932160 | tf_op jit(solution)/shard_map/all_gather | solution.py:722
  8.8 2.9 copy-start.28
  14.6 38.0 %copy-start.30 = (bf16[1,1024,128]{2,1,0:T(8,128)(2,1)S(1)}, bf16[1,1024,128]{2,1,0:T(8,128)(2,1)}, u32[]{:S(2)}) copy-start(bf16[1,1024,128]{2,1,0:T(8,128)(2,1)} %param.22) | copy-start | bytes 786436
  14.6 38.8 %copy-start.27 = (bf16[1,2816,128]{2,1,0:T(8,128)(2,1)S(1)}, bf16[1,2816,128]{2,1,0:T(8,128)(2,1)}, u32[]{:S(2)}) copy-start(bf16[1,2816,128]{2,1,0:T(8,128)(2,1)} %param.24) | copy-start | bytes 2162692
  15.8 38.8 %copy-start.24 = (bf16[1,128,2,2816]{3,2,1,0:T(2,128)(2,1)S(1)}, bf16[1,128,2,2816]{3,2,1,0:T(2,128)(2,1)}, u32[]{:S(2)}) copy-start(bf16[1,128,2,2816]{3,2,1,0:T(2,128)(2,1)} %param.23) | copy-start | bytes 4325380
  52.6 130.7 %all-gather.7.cloned.1.call-start = ((), (), s32[]{:S(2)}) async-start(), calls=%async_computation.5 | async-start | bytes 1310720 | tf_op jit(solution)/shard_map/all_gather | solution.py:722
  60.3 71.9 %copy-start.32 = (f32[2,4,4,8,128]{4,3,2,1,0:T(8,128)S(1)}, f32[2,4,4,8,128]{4,3,2,1,0:T(8,128)}, u32[]{:S(2)}) copy-start(f32[2,4,4,8,128]{4,3,2,1,0:T(8,128)} %get-tuple-element.50) | copy-start | bytes 393220
  130.8 167.1 %all-gather.11.cloned.1.call-start = ((), (), s32[]{:S(2)}) async-start(), calls=%async_computation.7 | async-start | bytes 7208960 | tf_op jit(solution)/shard_map/all_gather | solution.py:722
  131.5 211.4 %all-gather.9.cloned.1.call-start = ((), (), s32[]{:S(2)}) async-start(), calls=%async_computation.6 | async-start | bytes 3932160 | tf_op jit(solution)/shard_map/all_gather | solution.py:722
  132.1 401.0 %reduce-scatter.7.cloned.1.call-start = ((), (), s32[]{:S(2)}) async-start(), calls=%async_computation.9 | async-start | bytes 3604480 | tf_op jit(solution)/shard_map/reduce_scatter | solution.py:725
  132.2 3.9 copy-start.31
  132.3 4.6 copy-start.11
  136.9 2.3 slice-start.1
  136.9 2.4 slice-start
  139.1 19.7 %copy-start.7 = (s32[1,1536]{1,0:T(1,128)}, s32[1,1536]{1,0:T(1,128)S(1)}, u32[]{:S(2)}) copy-start(s32[1,1536]{1,0:T(1,128)S(1)} %broadcast_in_dim.16.begin_ref.refs_10_) | copy-start | bytes 18436
  149.2 9.7 %copy-start.5 = (f32[256,128]{1,0:T(8,128)S(1)}, f32[256,128]{1,0:T(8,128)}, u32[]{:S(2)}) copy-start(f32[256,128]{1,0:T(8,128)} %constant.86.clone.sin_ref.refs_7_) | copy-start | bytes 393220
  149.2 9.7 %copy-start.6 = (f32[256,128]{1,0:T(8,128)S(1)}, f32[256,128]{1,0:T(8,128)}, u32[]{:S(2)}) copy-start(f32[256,128]{1,0:T(8,128)} %constant.85.clone.cos_ref.refs_6_) | copy-start | bytes 393220
  149.2 9.7 %copy-start.9 = (f32[6,128]{1,0:T(8,128)S(1)}, f32[6,128]{1,0:T(8,128)}, u32[]{:S(2)}) copy-start(f32[6,128]{1,0:T(8,128)} %constant.88.clone.sinf_ref.refs_9_) | copy-start | bytes 9220
  149.2 9.7 %copy-start.10 = (f32[6,128]{1,0:T(8,128)S(1)}, f32[6,128]{1,0:T(8,128)}, u32[]{:S(2)}) copy-start(f32[6,128]{1,0:T(8,128)} %constant.87.clone.cosf_ref.refs_8_) | copy-start | bytes 9220
  312.5 4.4 copy-start.13
  312.5 6.7 copy-start.15
  343.0 192.4 %reduce-scatter.5.cloned.1.call-start = ((), (), s32[]{:S(2)}) async-start(), calls=%async_computation.8 | async-start | bytes 7208960 | tf_op jit(solution)/shard_map/reduce_scatter | solution.py:725
  371.4 263.9 %reduce-scatter.9.cloned.1.call-start = ((), (), s32[]{:S(2)}) async-start(), calls=%async_computation.10 | async-start | bytes 1310720 | tf_op jit(solution)/shard_map/reduce_scatter | solution.py:725
  416.3 2.7 copy-start.21
  416.3 2.7 copy-start.23
  476.3 45.4 %copy-start.1 = (bf16[1536,256]{1,0:T(8,128)(2,1)S(1)}, bf16[1536,256]{1,0:T(8,128)(2,1)}, u32[]{:S(2)}) copy-start(bf16[1536,256]{1,0:T(8,128)(2,1)} %copy-done) | copy-start | bytes 2359300
  521.8 5.9 copy-start.25
  527.6 169.4 %reduce-scatter.11.cloned.1.call-start = ((), (), s32[]{:S(2)}) async-start(), calls=%async_computation.11 | async-start | bytes 3932160 | tf_op jit(solution)/shard_map/reduce_scatter | solution.py:725
  617.5 2.6 copy-start.17
  620.1 2.9 copy-start.12
  627.8 5.8 copy-start.26
  633.8 45.9 %copy-start.18 = (bf16[4,192,512]{2,1,0:T(8,128)(2,1)S(1)}, bf16[4,192,512]{2,1,0:T(8,128)(2,1)}, u32[]{:S(2)}) copy-start(bf16[4,192,512]{2,1,0:T(8,128)(2,1)} %get-tuple-element.80.refs_2_) | copy-start | bytes 2359300
  (13 other events, 18.4 us)
Sparse Core Ops, SparseCore 0:
  52.7 61.8 all-gather.4
  130.9 26.5 all-gather.6
  159.1 119.2 all-gather.10
  279.7 63.1 all-gather.8
  345.7 56.6 reduce-scatter.6
  404.6 119.6 reduce-scatter.4
  527.8 26.2 reduce-scatter.8
  576.9 59.4 reduce-scatter.10

commit v5 on v4

--- a/solution.py
+++ b/solution.py
@@ -41,7 +41,9 @@
         self.S, self.C = S, C
         self.axes = [axis for axis, _ in riders]
         self.arrays = [x for _, x in riders]
-        self.shapes = [jax.ShapeDtypeStruct(x.shape, x.dtype) for x in self.arrays]
+        self.shapes = [
+            jax.ShapeDtypeStruct((C,) + x.shape if axis == "all" else x.shape, x.dtype) for axis, x in riders
+        ]
         count, most = len(riders), max(S, C) - 1
         self.scratch = [DMA((count, most)), DMA((count, most)), DMA((count,))] if count else []
 
@@ -56,6 +58,12 @@
             send, recv, own = self.sems
             if axis == "tp":
                 copies = [remote(src, dst, send.at[n, 0], recv.at[n, 0], {"tp": 1 - c})]
+            elif axis == "all":
+                copies = [
+                    remote(src, dst.at[z], send.at[n, k - 1], recv.at[n, k - 1], {"ctx": (z + k) % self.C})
+                    for k in range(1, self.C)
+                ]
+                copies.append(pltpu.make_async_copy(src, dst.at[z], own.at[n]))
             else:
                 size, me = (self.S, p) if axis == "shard" else (self.C, z)
                 copies = [
@@ -75,7 +83,7 @@
 def greet(S, C, mates=(), line=False, other=False, axes=()):
     p, z, c = here()
     peers = [{"shard": q} for q in ([(p + k) % S for k in range(1, S)] if "shard" in axes else mates)]
-    if line or "ctx" in axes:
+    if line or "ctx" in axes or "all" in axes:
         peers += [{"ctx": (z + k) % C} for k in range(1, C)]
     if other or "tp" in axes:
         peers.append({"tp": 1 - c})
@@ -248,35 +256,6 @@
         copy.wait_send()
 
 
-def gather(S, C, T, number, x, riders=()):
-    n, D = x.shape
-    half = n // 2
-
-    def kernel(ride, ins, outs, scratch):
-        (x_ref,), (out_ref,), (send, recv, own) = ins, outs, scratch
-        p, _, c = here()
-        _, _, rows, col = plane(S)
-        local = pltpu.make_async_copy(x_ref, out_ref.at[p * T + c], own)
-        local.start()
-        greet(S, C, rows + [col], other=True, axes=ride.axes)
-        ride.start()
-        spread(
-            S,
-            lambda h: x_ref.at[pl.ds(h * half, half)],
-            lambda q, h, core: out_ref.at[q * T + core, pl.ds(h * half, half)],
-            send,
-            recv,
-        )
-        local.wait()
-        ride.wait()
-
-    out, *rest = comm(
-        kernel, S, C, number, "gather", [x], [IN_VMEM],
-        [(jax.ShapeDtypeStruct((S * T, n, D), x.dtype), ANY)], spread_sems(S) + [DMA], riders,
-    )
-    return [out.reshape(S * T * n, D)] + rest
-
-
 def gather_columns(S, C, T, number, x, riders=()):
     _, n, wide = x.shape
 
@@ -308,17 +287,262 @@
     return [out.reshape(C * T * n, wide * S)] + rest
 
 
-def leave(S, C, T, number, x, riders=()):
-    _, n, wide = x.shape
+CHUNK = 512
+ROWS = 32
+
+
+def sum_scratch(S, n, D):
+    half, B = n // 2, S // 2
+
+    def vm(*shape):
+        return pltpu.VMEM(shape, BF)
+
+    return [
+        vm(S, n, D), vm(S, n, D), vm(S, n, D), vm(B - 1, 2, half, D), vm(B, half, D),
+        vm(B - 1, half, D), vm(half, D), vm(half, D), vm(B - 1, half, D),
+        DMA((S,)), DMA((S,)), DMA((B - 1, 2)), DMA((B - 1, 2)), DMA((B,)), DMA((B,)), DMA((B,)), DMA((B,)),
+    ]
+
+
+def sum_over_plane(S, T, x_ref, w_ref, out_ref, scratch):
+    away, sib, mine, row1, col1, row2, col2, to_col, to_row = scratch[:9]
+    asend, arecv, rsend, rrecv, csend, crecv, fsend, frecv = scratch[9:]
+    n, D = out_ref.shape
+    half, B = n // 2, S // 2
+    _, _, c = here()
+    a, b, rows, col = plane(S)
+    rows, col, other = [{"shard": q} for q in rows], {"shard": col}, {"tp": 1 - c}
+
+    def chip(e):
+        return ((a + e // B) % 2) * B + (b + e % B) % B
+
+    def product(e, core, store):
+        x = x_ref[chip(e) * T + core]
+
+        def column(j, _):
+            w = pl.ds(pl.multiple_of(j * CHUNK, CHUNK), CHUNK)
+            store(w, mm(x, w_ref[w, :], 1, 1))
+            return 0
+
+        lax.fori_loop(0, D // CHUNK, column, 0)
+
+    def to_other(e):
+        return remote(away.at[e], sib.at[e], asend.at[e], arecv.at[e], other)
+
+    def first(i, _):
+        e = S - 1 - i
+
+        def store(w, value):
+            away[e, :, w] = value.astype(BF)
+
+        product(e, 1 - c, store)
+        to_other(e).start()
+        return 0
+
+    lax.fori_loop(0, S, first, 0)
+
+    top, low = pl.ds(0, half), pl.ds(half, half)
+    started = []
+
+    def push(src, dst, send, recv, where):
+        copy = remote(src, dst, send, recv, where)
+        copy.start()
+        started.append(copy)
+
+    for e in range(S - 1, -1, -1):
+        to_other(e).wait()
+
+        def store(w, value):
+            value = value + sib[e, :, w].astype(F32)
+            if e:
+                mine[e, :, w] = value.astype(BF)
+            else:
+                out_ref[:, w] = value
+
+        product(e, c, store)
+        j = e % B
+        if e > B:
+            push(mine.at[e, top], row1.at[j - 1, 1], rsend.at[j - 1, 1], rrecv.at[j - 1, 1], rows[j - 1])
+            push(mine.at[e, low], col1.at[j], csend.at[j], crecv.at[j], col)
+        elif e == B:
+            push(mine.at[e, low], col1.at[0], csend.at[0], crecv.at[0], col)
+        elif e:
+            push(mine.at[e, top], row1.at[j - 1, 0], rsend.at[j - 1, 0], rrecv.at[j - 1, 0], rows[j - 1])
+
+    def came(ref, send, recv):
+        remote(ref, ref, send, recv, other).wait_recv()
+
+    total = mine[B, top, :].astype(F32)
+    for j in range(1, B):
+        came(row1.at[j - 1, 1], rsend.at[j - 1, 1], rrecv.at[j - 1, 1])
+        total = total + row1[j - 1, 1].astype(F32)
+    to_col[...] = total.astype(BF)
+    push(to_col, col2, fsend.at[0], frecv.at[0], col)
+    for j in range(1, B):
+        came(col1.at[j], csend.at[j], crecv.at[j])
+        to_row[j - 1] = (mine[j, low, :].astype(F32) + col1[j].astype(F32)).astype(BF)
+        push(to_row.at[j - 1], row2.at[j - 1], fsend.at[j], frecv.at[j], rows[j - 1])
+    came(col1.at[0], csend.at[0], crecv.at[0])
+    upper, lower = out_ref[top, :], out_ref[low, :] + col1[0].astype(F32)
+    for j in range(1, B):
+        came(row1.at[j - 1, 0], rsend.at[j - 1, 0], rrecv.at[j - 1, 0])
+        upper = upper + row1[j - 1, 0].astype(F32)
+    came(col2, fsend.at[0], frecv.at[0])
+    out_ref[top, :] = upper + col2[...].astype(F32)
+    for j in range(1, B):
+        came(row2.at[j - 1], fsend.at[j], frecv.at[j])
+        lower = lower + row2[j - 1].astype(F32)
+    out_ref[low, :] = lower
+    for copy in started:
+        copy.wait_send()
+
+
+def scatter(S, C, T, number, x, w, riders=()):
+    L, K = x.shape
+    D, n = w.shape[0], L // (S * T)
 
     def kernel(ride, ins, outs, scratch):
-        (x_ref,), (out_ref,) = ins, outs
-        buf, buf2, s1, r1, s2, r2, s3, r3, s4, r4, own = scratch
+        _, _, rows, col = plane(S)
+        greet(S, C, rows + [col], other=True, axes=ride.axes)
+        ride.start()
+        sum_over_plane(S, T, ins[0], ins[1], outs[0], scratch)
+        ride.wait()
+
+    return comm(
+        kernel, S, C, number, "scatter", [x.reshape(S * T, n, K), w], [IN_VMEM, IN_VMEM],
+        [(jax.ShapeDtypeStruct((n, D), F32), IN_VMEM)], sum_scratch(S, n, D), riders,
+    )
+
+
+def row_blocks(n, work):
+    @pl.loop(0, n // ROWS)
+    def _(i):
+        work(pl.ds(pl.multiple_of(i * ROWS, ROWS), ROWS))
+
+
+def norm_of(v):
+    center = v - jnp.mean(v, axis=-1, keepdims=True)
+    inverse = lax.rsqrt(jnp.mean(center * center, axis=-1, keepdims=True) + EPS)
+    return center * inverse, inverse
+
+
+def norm_back(v, g, gain, stats_ref):
+    normal, inverse = norm_of(v)
+    e = g * gain
+    stats_ref[0:1, :] += jnp.sum(g * normal, axis=0, keepdims=True)
+    stats_ref[1:2, :] += jnp.sum(g, axis=0, keepdims=True)
+    return inverse * (
+        e - jnp.mean(e, axis=-1, keepdims=True) - normal * jnp.mean(e * normal, axis=-1, keepdims=True)
+    )
+
+
+def spread_rows(S, T, src, out_ref, send, recv, own):
+    p, _, c = here()
+    half = src.shape[0] // 2
+    local = pltpu.make_async_copy(src, out_ref.at[p * T + c], own)
+    local.start()
+    spread(
+        S,
+        lambda h: src.at[pl.ds(h * half, half)],
+        lambda q, h, core: out_ref.at[q * T + core, pl.ds(h * half, half)],
+        send,
+        recv,
+    )
+    local.wait()
+
+
+def sum_norm_gather(S, C, T, number, x, w, residual, gain, shift, riders=()):
+    L, K = x.shape
+    D, n = w.shape[0], L // (S * T)
+
+    def kernel(ride, ins, outs, scratch):
+        x_ref, w_ref, res_ref, gain_ref, shift_ref = ins
+        v_ref, out_ref = outs
+        acc, low, send, recv, own = scratch[:5]
+        _, _, rows, col = plane(S)
+        greet(S, C, rows + [col], other=True, axes=ride.axes)
+        ride.start()
+        sum_over_plane(S, T, x_ref, w_ref, acc, scratch[5:])
+
+        def work(r):
+            v = res_ref[r, :].astype(F32) + acc[r, :]
+            v_ref[r, :] = v
+            low[r, :] = (norm_of(v)[0] * gain_ref[...] + shift_ref[...]).astype(BF)
+
+        row_blocks(n, work)
+        spread_rows(S, T, low, out_ref, send, recv, own)
+        ride.wait()
+
+    v, out, *rest = comm(
+        kernel, S, C, number, "sum_norm_gather", [x.reshape(S * T, n, K), w, residual, gain, shift], [IN_VMEM] * 5,
+        [(jax.ShapeDtypeStruct((n, D), F32), IN_VMEM), (jax.ShapeDtypeStruct((S * T, n, D), BF), ANY)],
+        [pltpu.VMEM((n, D), F32), pltpu.VMEM((n, D), BF)] + spread_sems(S) + [DMA] + sum_scratch(S, n, D),
+        riders,
+    )
+    return [v, out.reshape(L, D)] + rest
+
+
+def sum_back_gather(S, C, T, number, x, w, v, residual, gain, riders=()):
+    L, K = x.shape
+    D, n = w.shape[0], L // (S * T)
+
+    def kernel(ride, ins, outs, scratch):
+        x_ref, w_ref, in_ref, res_ref, gain_ref = ins
+        v_ref, out_ref, stats = outs
+        acc, low, send, recv, own = scratch[:5]
+        _, _, rows, col = plane(S)
+        greet(S, C, rows + [col], other=True, axes=ride.axes)
+        ride.start()
+        sum_over_plane(S, T, x_ref, w_ref, acc, scratch[5:])
+        stats[...] = jnp.zeros_like(stats)
+
+        def work(r):
+            g = res_ref[r, :].astype(F32) + norm_back(in_ref[r, :], acc[r, :], gain_ref[...], stats)
+            v_ref[r, :] = g
+            low[r, :] = g.astype(BF)
+
+        row_blocks(n, work)
+        spread_rows(S, T, low, out_ref, send, recv, own)
+        ride.wait()
+
+    g, out, stats, *rest = comm(
+        kernel, S, C, number, "sum_back_gather", [x.reshape(S * T, n, K), w, v, residual, gain], [IN_VMEM] * 5,
+        [
+            (jax.ShapeDtypeStruct((n, D), F32), IN_VMEM), (jax.ShapeDtypeStruct((S * T, n, D), BF), ANY),
+            (jax.ShapeDtypeStruct((2, D), F32), IN_VMEM),
+        ],
+        [pltpu.VMEM((n, D), F32), pltpu.VMEM((n, D), BF)] + spread_sems(S) + [DMA] + sum_scratch(S, n, D),
+        riders,
+    )
+    return [g, out.reshape(L, D), stats] + rest
+
+
+def sum_back_leave(S, C, T, number, x, w, v, residual, gain, riders=()):
+    L, K = x.shape
+    D, n = w.shape[0], L // (S * T)
+    wide = D // S
+
+    def kernel(ride, ins, outs, scratch):
+        x_ref, w_ref, in_ref, res_ref, gain_ref = ins
+        out_ref, stats = outs
+        acc, low, buf, buf2, s1, r1, s2, r2, s3, r3, s4, r4, own = scratch[:13]
         p, z, c = here()
         mates = [(p + k) % S for k in range(1, S)]
         line = [(z + k) % C for k in range(1, C)]
         other = {"tp": 1 - c}
         greet(S, C, mates, line=True, other=True, axes=ride.axes)
+        ride.start()
+        sum_over_plane(S, T, x_ref, w_ref, acc, scratch[13:])
+        stats[...] = jnp.zeros_like(stats)
+
+        def work(r):
+            g = res_ref[r, :] + norm_back(in_ref[r, :].astype(F32), acc[r, :], gain_ref[...], stats)
+            low[r, :] = g.astype(BF)
+
+        row_blocks(n, work)
+
+        def part(q):
+            return pl.ds(pl.multiple_of(q * wide, 128), wide)
 
         def turn_over(source, target, send, recv, local, me, axis, peers):
             hop = [pltpu.make_async_copy(source(me), target, local)]
@@ -326,153 +550,29 @@
                 hop.append(remote(source(q), target, send.at[k], recv.at[k], {axis: q}))
             for copy in hop:
                 copy.start()
-            return hop
-
-        first = turn_over(lambda q: x_ref.at[q], buf.at[p], s1, r1, own.at[0], p, "shard", mates)
-        ride.start()
-        for copy in first:
-            copy.wait()
-        for copy in turn_over(lambda q: buf.at[q], buf2.at[z], s2, r2, own.at[1], z, "ctx", line):
-            copy.wait()
-        part = pl.ds(pl.multiple_of(p * wide, 128), wide)
-        for copy in turn_over(lambda q: buf2.at[q], out_ref.at[c, :, part], s3, r3, own.at[2], p, "shard", mates):
-            copy.wait()
+            for copy in hop:
+                copy.wait()
+
+        turn_over(lambda q: low.at[:, part(q)], buf.at[p], s1, r1, own.at[0], p, "shard", mates)
+        turn_over(lambda q: buf.at[q], buf2.at[z], s2, r2, own.at[1], z, "ctx", line)
+        turn_over(lambda q: buf2.at[q], out_ref.at[c, :, part(p)], s3, r3, own.at[2], p, "shard", mates)
         copy = remote(out_ref.at[c], out_ref.at[c], s4, r4, other)
         copy.start()
         copy.wait_send()
         remote(out_ref.at[1 - c], out_ref.at[1 - c], s4, r4, other).wait_recv()
         ride.wait()
 
-    out, *rest = comm(
-        kernel, S, C, number, "leave", [x], [IN_VMEM],
-        [(jax.ShapeDtypeStruct((T, n, wide * S), x.dtype), ANY)],
+    out, stats, *rest = comm(
+        kernel, S, C, number, "sum_back_leave", [x.reshape(S * T, n, K), w, v, residual, gain], [IN_VMEM] * 5,
+        [(jax.ShapeDtypeStruct((T, n, D), BF), ANY), (jax.ShapeDtypeStruct((2, D), F32), IN_VMEM)],
         [
-            pltpu.VMEM((S, n, wide), BF), pltpu.VMEM((C, n, wide), BF),
-            DMA((S - 1,)), DMA((S - 1,)), DMA((C - 1,)), DMA((C - 1,)), DMA((S - 1,)), DMA((S - 1,)),
-            DMA, DMA, DMA((3,)),
-        ],
+            pltpu.VMEM((n, D), F32), pltpu.VMEM((n, D), BF), pltpu.VMEM((S, n, wide), BF), pltpu.VMEM((C, n, wide), BF),
+            DMA((S - 1,)), DMA((S - 1,)), DMA((C - 1,)), DMA((C - 1,)), DMA((S - 1,)), DMA((S - 1,)), DMA, DMA, DMA((3,)),
+        ]
+        + sum_scratch(S, n, D),
         riders,
     )
-    return [out.reshape(T * n, wide * S)] + rest
-
-
-CHUNK = 512
-
-
-def scatter(S, C, T, number, x, w, riders=()):
-    L, K = x.shape
-    D = w.shape[0]
-    n, B = L // (S * T), S // 2
-    half = n // 2
-    steps = D // CHUNK
-
-    def kernel(ride, ins, outs, scratch):
-        (x_ref, w_ref), (out_ref,) = ins, outs
-        away, sib, mine, row1, col1, row2, col2, to_col, to_row = scratch[:9]
-        asend, arecv, rsend, rrecv, csend, crecv, fsend, frecv = scratch[9:]
-        p, _, c = here()
-        a, b, rows, col = plane(S)
-        greet(S, C, rows + [col], other=True, axes=ride.axes)
-        rows, col, other = [{"shard": q} for q in rows], {"shard": col}, {"tp": 1 - c}
-        ride.start()
-
-        def chip(e):
-            return ((a + e // B) % 2) * B + (b + e % B) % B
-
-        def product(e, core, store):
-            x = x_ref[chip(e) * T + core]
-
-            def column(j, _):
-                w = pl.ds(pl.multiple_of(j * CHUNK, CHUNK), CHUNK)
-                store(w, mm(x, w_ref[w, :], 1, 1))
-                return 0
-
-            lax.fori_loop(0, steps, column, 0)
-
-        def to_other(e):
-            return remote(away.at[e], sib.at[e], asend.at[e], arecv.at[e], other)
-
-        def first(i, _):
-            e = S - 1 - i
-
-            def store(w, value):
-                away[e, :, w] = value.astype(BF)
-
-            product(e, 1 - c, store)
-            to_other(e).start()
-            return 0
-
-        lax.fori_loop(0, S, first, 0)
-
-        top, low = pl.ds(0, half), pl.ds(half, half)
-        started = []
-
-        def push(src, dst, send, recv, where):
-            copy = remote(src, dst, send, recv, where)
-            copy.start()
-            started.append(copy)
-
-        for e in range(S - 1, -1, -1):
-            to_other(e).wait()
-
-            def store(w, value):
-                value = value + sib[e, :, w].astype(F32)
-                if e:
-                    mine[e, :, w] = value.astype(BF)
-                else:
-                    out_ref[:, w] = value
-
-            product(e, c, store)
-            j = e % B
-            if e > B:
-                push(mine.at[e, top], row1.at[j - 1, 1], rsend.at[j - 1, 1], rrecv.at[j - 1, 1], rows[j - 1])
-                push(mine.at[e, low], col1.at[j], csend.at[j], crecv.at[j], col)
-            elif e == B:
-                push(mine.at[e, low], col1.at[0], csend.at[0], crecv.at[0], col)
-            elif e:
-                push(mine.at[e, top], row1.at[j - 1, 0], rsend.at[j - 1, 0], rrecv.at[j - 1, 0], rows[j - 1])
-
-        def came(ref, send, recv):
-            remote(ref, ref, send, recv, other).wait_recv()
-
-        total = mine[B, top, :].astype(F32)
-        for j in range(1, B):
-            came(row1.at[j - 1, 1], rsend.at[j - 1, 1], rrecv.at[j - 1, 1])
-            total = total + row1[j - 1, 1].astype(F32)
-        to_col[...] = total.astype(BF)
-        push(to_col, col2, fsend.at[0], frecv.at[0], col)
-        for j in range(1, B):
-            came(col1.at[j], csend.at[j], crecv.at[j])
-            to_row[j - 1] = (mine[j, low, :].astype(F32) + col1[j].astype(F32)).astype(BF)
-            push(to_row.at[j - 1], row2.at[j - 1], fsend.at[j], frecv.at[j], rows[j - 1])
-        came(col1.at[0], csend.at[0], crecv.at[0])
-        upper, lower = out_ref[top, :], out_ref[low, :] + col1[0].astype(F32)
-        for j in range(1, B):
-            came(row1.at[j - 1, 0], rsend.at[j - 1, 0], rrecv.at[j - 1, 0])
-            upper = upper + row1[j - 1, 0].astype(F32)
-        came(col2, fsend.at[0], frecv.at[0])
-        out_ref[top, :] = upper + col2[...].astype(F32)
-        for j in range(1, B):
-            came(row2.at[j - 1], fsend.at[j], frecv.at[j])
-            lower = lower + row2[j - 1].astype(F32)
-        out_ref[low, :] = lower
-        for copy in started:
-            copy.wait_send()
-        ride.wait()
-
-    def vm(*shape):
-        return pltpu.VMEM(shape, BF)
-
-    return comm(
-        kernel, S, C, number, "scatter", [x.reshape(S * T, n, K), w], [IN_VMEM, IN_VMEM],
-        [(jax.ShapeDtypeStruct((n, D), F32), IN_VMEM)],
-        [
-            vm(S, n, D), vm(S, n, D), vm(S, n, D), vm(B - 1, 2, half, D), vm(B, half, D),
-            vm(B - 1, half, D), vm(half, D), vm(half, D), vm(B - 1, half, D),
-            DMA((S,)), DMA((S,)), DMA((B - 1, 2)), DMA((B - 1, 2)), DMA((B,)), DMA((B,)), DMA((B,)), DMA((B,)),
-        ],
-        riders,
-    )
+    return [out.reshape(T * n, D), stats] + rest
 
 
 def turn_tables(rows):
@@ -667,23 +767,6 @@
     return jnp.sum(jnp.where(inside, begins[None, :], 0), axis=1, dtype=jnp.int32)
 
 
-def layer_norm(values, gain, shift):
-    center = values - jnp.mean(values, axis=-1, keepdims=True)
-    inverse = lax.rsqrt(jnp.mean(center * center, axis=-1, keepdims=True) + EPS)
-    normal = center * inverse
-    return (normal * gain + shift, normal, inverse)
-
-
-def norm_back(gradient, normal, inverse, gain):
-    scaled = gradient * gain
-    centered = (
-        scaled
-        - jnp.mean(scaled, axis=-1, keepdims=True)
-        - normal * jnp.mean(scaled * normal, axis=-1, keepdims=True)
-    )
-    return (inverse * centered, jnp.sum(gradient * normal, axis=0), jnp.sum(gradient, axis=0))
-
-
 def tiles_of(parts, lead):
     flat = jnp.concatenate([x.astype(F32).reshape(lead + (-1,)) for x in parts], axis=-1)
     flat = jnp.pad(flat, ((0, 0),) * len(lead) + ((0, 1024 - flat.shape[-1]),))
@@ -731,9 +814,12 @@
         nf = HEAD // (S * C)
 
         tile = tiles_of((norm_gain[0].reshape(-1), norm_bias[0].reshape(-1), b_qkv[0].reshape(-1), lengths[0]), ())
-        small, _, tok, wq = exchange(
+        small, _, tok, wq, wo = exchange(
             S, C, T, 0,
-            [("shard", w_qkv[0].reshape(nb, 3, S, hn).transpose(2, 0, 1, 3).reshape(S, nb, 3 * hn))],
+            [
+                ("shard", w_qkv[0].reshape(nb, 3, S, hn).transpose(2, 0, 1, 3).reshape(S, nb, 3 * hn)),
+                ("shard", w_out[0].reshape(S, hn, nb).swapaxes(1, 2)),
+            ],
             jnp.broadcast_to(tile, (C, S, 8, 128)),
             to_parts(half_of(tokens)),
         )
@@ -741,13 +827,13 @@
         tok, wo, wg, wd, cot = gather_columns(
             S, C, T, 1, tok,
             [
-                ("shard", w_out[0].reshape(S, hn, nb).swapaxes(1, 2)),
+                ("all", wo.reshape(S * nb, hn)),
                 ("shard", w_gateup[0].reshape(nb, 2, S, fn).transpose(2, 0, 1, 3).reshape(S, nb, 2 * fn)),
                 ("shard", w_down[0].reshape(S, fn, nb).swapaxes(1, 2)),
                 ("shard", to_parts(half_of(cotangent))),
             ],
         )
-        wo, wg, wd = over_ctx(wo), over_ctx(wg), over_ctx(wd)
+        wo, wg, wd = wo.reshape(D, hn), over_ctx(wg), over_ctx(wd)
 
         small = lax.dynamic_index_in_dim(small, c, 0, keepdims=False).reshape(C, S, 1024)
         norms = small[:, :, : 4 * nb].reshape(C * S, 4, nb).swapaxes(0, 1).reshape(4, D)
@@ -763,15 +849,11 @@
         begin = doc_begins(lengths_row, L)
         begin = begin[None, :]
 
-        n1 = layer_norm(tok.astype(F32), gains[0], shifts[0])[0].astype(BF)
-        hidden = own(tok).astype(F32)
-        _, normal1, inverse1 = layer_norm(hidden, gains[0], shifts[0])
+        n1 = (norm_of(tok.astype(F32))[0] * gains[0] + shifts[0]).astype(BF)
+        own_tok = own(tok)
         qkv = mm(n1, wq, 1, 0) + bias
         q, k, v, o, lse = attend(qkv, begin)
-        got, cot = scatter(S, C, T, 2, o, wo, [("ctx", cot)])
-        mid = hidden + got
-        n2, normal2, inverse2 = layer_norm(mid, gains[1], shifts[1])
-        (n2,) = gather(S, C, T, 3, n2.astype(BF))
+        mid, n2, cot = sum_norm_gather(S, C, T, 2, o, wo, own_tok, gains[1:], shifts[1:], [("ctx", cot)])
         cot, n2 = after(cot, n2)
         (gb,) = gather_columns(S, C, T, 4, cot)
         gu = mm(n2, wg, 1, 0)
@@ -792,38 +874,34 @@
         (got,) = scatter(S, C, T, 5, act, wd)
         out = parts((mid + got).astype(BF))
         dgu, out = after(dgu, out)
-        got, out = scatter(S, C, T, 6, dgu, wg, [("shard", out)])
-        dmid, gain2, shift2 = norm_back(got, normal2, inverse2, gains[1])
-        dmid = own(gb).astype(F32) + dmid
-        gb1, out = gather(S, C, T, 7, dmid.astype(BF), [("ctx", out)])
+        dmid, gb1, stats2, out = sum_back_gather(
+            S, C, T, 6, dgu, wg, mid, own(gb), gains[1:], [("shard", out)]
+        )
         gw_out = mm(gb1, o, 0, 0).astype(BF)
         gb1, gw_out = after(gb1, gw_out)
         gw_out = sum_ctx(gw_out)
         do = mm(gb1, wo, 1, 0).astype(BF)
-        dqkv, gw_gateup, gw_down = attend_back(
-            S, C, 11, q, k, v, o, do, lse, begin, [("shard", gw_gateup), ("shard", gw_down)]
+        dqkv, gw_gateup, gw_down, out = attend_back(
+            S, C, 11, q, k, v, o, do, lse, begin, [("shard", gw_gateup), ("shard", gw_down), ("ctx", out)]
         )
         gw_qkv = mm(n1, dqkv, 0, 0).astype(BF)
         dqkv, gw_qkv = after(dqkv, gw_qkv)
         gw_qkv = sum_ctx(gw_qkv)
-        got, out = scatter(S, C, T, 8, dqkv, wq, [("shard", out)])
-        dtok, gain1, shift1 = norm_back(got, normal1, inverse1, gains[0])
-        gtok, gw_out, mate = leave(
-            S, C, T, 9, parts((dmid + dtok).astype(BF)), [("shard", gw_out), ("tp", out)]
+        gtok, stats1, gw_out, out = sum_back_leave(
+            S, C, T, 8, dqkv, wq, own_tok, dmid, gains[:1], [("shard", gw_out), ("shard", out)]
         )
         gtok = unpermute(gtok).astype(F32)
-        out = jnp.where(c == 0, jnp.stack((out, mate)), jnp.stack((mate, out)))
-        out = unpermute(out.transpose(0, 2, 1, 3).reshape(R, D))
-
         gbias = jnp.sum(dqkv.astype(F32), axis=0)
         tiles = tiles_of(
             (
-                jnp.stack((gain1, gain2, shift1, shift2)).reshape(4, C, S, nb).transpose(1, 2, 0, 3),
+                jnp.stack((stats1[0], stats2[0], stats1[1], stats2[1])).reshape(4, C, S, nb).transpose(1, 2, 0, 3),
                 gbias.reshape(3, heads, S, C, nf).transpose(3, 2, 0, 1, 4),
             ),
             (C, S),
         )
-        small, gw_qkv = exchange(S, C, T, 10, [("shard", gw_qkv)], tiles)
+        small, gw_qkv, mate = exchange(S, C, T, 10, [("shard", gw_qkv), ("tp", out)], tiles)
+        out = jnp.where(c == 0, jnp.stack((out, mate)), jnp.stack((mate, out)))
+        out = unpermute(out.transpose(0, 2, 1, 3).reshape(R, D))
         small = small.reshape(T, C, S, 1024)
         norms = jnp.sum(small[..., : 4 * nb], axis=(0, 1, 2)).reshape(1, 4, nb)
         gbias = lax.dynamic_index_in_dim(small, c, 0, keepdims=False)[..., 4 * nb : 4 * nb + 3 * heads * nf]

time: 734 us -> 702 us (0.956)
  other arithmetic: 36.8 us -> 21.5 us
  Pallas kernels: 497 us -> 486 us
    reduce_sum x7 -> x2, other arithmetic: 14.1 us -> 5.65 us  [the longest x1 3.84 us: norm_of(): center = v - jnp.mean(v, axis=-1, keepdims=True)]
    pallas_call x12 -> x9, Pallas kernels: 477 us -> 470 us  [comm(): pl.pallas_call(body, out_shape=[shape for shape, _ in outs] + ride.shapes...]
    all_gather x4 -> x3, waiting for transfers between devices: 17.9 us -> 12.6 us  [over_ctx(): return lax.all_gather(w.reshape(S * nb, -1), 'ctx', axis=0, tiled=True)]
    unnamed x75 -> x69, local copies, waits for them, and re-layouts: 24.9 us -> 24.7 us
  transfers between devices with their start and end apart: 8 -> 7, of which waited for: 1 -> 1; matrix products, arithmetic and copies ran while one was open for 23% -> 22% of each run, Pallas kernels for 62% -> 63%
where the time goes in v5:
time: 702 us; the launch traced here: 694 us
  Pallas kernels  486 us (69%)
  local copies, waits for them, and re-layouts  80 us (11%)
  matrix products  77.2 us (11%)
  other arithmetic  21.5 us (3%)
  between operations  15.1 us (2%)
  waiting for transfers between devices  13.4 us (2%)
    pallas_call x9, Pallas kernels, comm(): pl.pallas_call(body, out_shape=[shape for shape, _ in outs] + ride.shapes...  470 us
    dot_general x8, matrix products, mm(): lax.dot_general(a, b, (((ca,), (cb,)), ((), ())), preferred_element_type=...  77.2 us
    unnamed x69, local copies, waits for them, and re-layouts  24.7 us
    pallas_call x1, Pallas kernels, attend(): pl.pallas_call(attend_kernel, in_specs=[pl.BlockSpec(memory_space=pltpu.S...  15.4 us
  transfers between devices with their start and end apart: 7, of which 1 were waited for; matrix products, arithmetic and copies ran while one was open for 22% of the time, Pallas kernels for 63%

profile of v5, /device:TPU:9, one launch (start us, length us, event | category | flops | bytes accessed | tf_op | source)
XLA Modules:
  0.0 693.7 jit_solution(10740533322362514264)
XLA Ops:
  14.3 36.1 %exchange.2 = (f32[2,4,4,8,128]{4,3,2,1,0:T(8,128)}, bf16[4,192,512]{2,1,0:T(8,128)(2,1)}, bf16[4,192,512]{2,1,0:T(8,128)(2,1)}, bf16[4,128,768]{2,1,0:T(8,128)(2,1)}, bf16[4,128,256]{2,1,0:T(8,128)(2,1)}) custom-call(f32[4,4,8,128]{3,2,1,0:T(8,128)} %broadcast_in_dim.14.refs_0_, bf16[4,192,512]{2,1,0:T(8,128)(2,1)} %reshape.260.refs_1_, ...), custom_call_target="tpu_custom_call" | custom-call | bytes 120000000 | tf_op jit(solution)/shard_map/exchange/pallas_call | solution.py:108
  52.5 3.8 copy.99
  58.0 2.3 copy.101
  60.3 67.9 %gather_columns.2 = (bf16[4,2,192,2048]{3,2,1,0:T(8,128)(2,1)}, bf16[4,512,256]{2,1,0:T(8,128)(2,1)}, bf16[4,128,1408]{2,1,0:T(8,128)(2,1)}, bf16[4,128,704]{2,1,0:T(8,128)(2,1)}, bf16[4,192,512]{2,1,0:T(8,128)(2,1)}) custom-call(bf16[4,192,512]{2,1,0:T(8,128)(2,1)} %get-tuple-element.54.refs_0_, bf16[512,256]{1,0:T(8,128)(2,1)} %bitcast.174, ...), custom_call_target="tpu_custom_call" | custom-call | bytes 120000000 | tf_op jit(solution)/shard_map/gather_columns/pallas_call | solution.py:108
  129.3 3.8 convert_reduce_fusion
  139.6 7.7 %add_convert_fusion = bf16[1536,2048]{1,0:T(8,128)(2,1)} fusion(f32[2048]{0:T(1024)S(1)} %get-tuple-element.130, f32[2048]{0:T(1024)S(1)} %get-tuple-element.127, f32[1536]{0:T(1024)S(1)} %rsqrt.12, f32[1536]{0:T(1024)S(1)} %div.28, bf16[4,2,192,2048]{3,2,1,0:T(8,128)(2,1)} %get-tuple-element.56), kind=kLoop, calls=%fused_computation.4 | loop fusion | flops 18874368 | bytes 12611584 | tf_op jit(solution)/shard_map/convert_element_type | solution.py:852
  147.4 10.0 %convolution_add_fusion.qkv_ref = f32[1536,768]{1,0:T(8,128)} fusion(bf16[1536,2048]{1,0:T(8,128)(2,1)} %add_convert_fusion, bf16[2048,768]{1,0:T(8,128)(2,1)} %all-gather.4.cloned.1.call-done.refs_1_, f32[768]{0:T(1024)S(1)} %add.88), kind=kOutput, calls=%fused_computation.12 | convolution fusion | flops 4833017856 | bytes 14158848 | tf_op jit(solution)/shard_map/dot_general | solution.py:26
  157.5 15.4 %attend.1 = (bf16[1536,256]{1,0:T(8,128)(2,1)S(1)}, bf16[1536,256]{1,0:T(8,128)(2,1)S(1)}, bf16[1536,256]{1,0:T(8,128)(2,1)S(1)}, bf16[1536,256]{1,0:T(8,128)(2,1)S(1)}, f32[4,1536]{1,0:T(4,128)S(1)}) custom-call(s32[3]{0:T(128)S(1)} %and_select_fusion.first_ref, f32[1536,768]{1,0:T(8,128)} %convolution_add_fusion.qkv_ref, f32[256,128]{1,0:T(8,128)S(1)} %copy-done.5, ...), custom_call_target="tpu_custom_call" | custom-call | tf_op jit(solution)/shard_map/attend/pallas_call | solution.py:666
  177.1 73.1 %sum_norm_gather.1 = (f32[192,2048]{1,0:T(8,128)}, bf16[8,192,2048]{2,1,0:T(8,128)(2,1)}, bf16[4,192,512]{2,1,0:T(8,128)(2,1)}) custom-call(bf16[8,192,256]{2,1,0:T(8,128)(2,1)} %bitcast.134, bf16[2048,256]{1,0:T(8,128)(2,1)} %bitcast.163, bf16[192,2048]{1,0:T(8,128)(2,1)} %constant_dynamic-slice_fusion.1.refs_2_, f32[1,2048]{1,0:T(1,128)} %bitcast.178, ...), custom_call_target="tpu_custom_call" | custom-call | bytes 120000000 | tf_op jit(solution)/shard_map/sum_norm_gather/pallas_call | solution.py:108
  250.3 32.2 %gather_columns.3 = bf16[4,2,192,2048]{3,2,1,0:T(8,128)(2,1)} custom-call(bf16[4,192,512]{2,1,0:T(8,128)(2,1)} %get-tuple-element.66.refs_0_), custom_call_target="tpu_custom_call" | custom-call | bytes 120000000 | tf_op jit(solution)/shard_map/gather_columns/pallas_call | solution.py:108
  282.4 14.5 %fusion.11 = f32[1536,1408]{0,1:T(8,128)S(1)} fusion(bf16[1536,2048]{1,0:T(8,128)(2,1)} %bitcast.184, bf16[2048,1408]{1,0:T(8,128)(2,1)} %all-gather.8.cloned.1.call-done.refs_1_), kind=kOutput, calls=%fused_computation.66 | convolution fusion | flops 8858370048 | bytes 20709376 | tf_op jit(solution)/shard_map/dot_general | solution.py:26
  298.4 3.0 copy-done.13
  302.9 6.0 convolution_convert_fusion.2
  309.0 12.5 %all-gather.6.cloned.1.call-done.refs_1_ = bf16[2048,704]{1,0:T(8,128)(2,1)} async-done(((bf16[512,704]{1,0:T(8,128)(2,1)}), bf16[2048,704]{1,0:T(8,128)(2,1)}) %all-gather.6.cloned.1.call-update) | async-done | bytes 2883600 | tf_op jit(solution)/shard_map/all_gather | solution.py:805
  321.7 12.5 %multiply_convert_fusion.1 = (bf16[1536,704]{0,1:T(8,128)(2,1)S(1)}, bf16[1536,704]{0,1:T(8,128)(2,1)S(1)}) fusion(f32[1536,1408]{0,1:T(8,128)} %copy-done.13, bf16[1536,2048]{1,0:T(8,128)(2,1)} %bitcast.142, bf16[2048,704]{1,0:T(8,128)(2,1)} %all-gather.6.cloned.1.call-done.refs_1_), kind=kOutput, calls=%fused_computation.9 | convolution fusion | flops 4443242496 | bytes 22151168 | tf_op jit(solution)/shard_map/dot_general | solution.py:26
  336.3 13.7 %convolution_convert_fusion = bf16[2048,1408]{1,0:T(8,128)(2,1)} fusion(bf16[1536,2048]{1,0:T(8,128)(2,1)} %bitcast.185, bf16[1536,704]{0,1:T(8,128)(2,1)S(1)} %get-tuple-element.125, bf16[1536,704]{0,1:T(8,128)(2,1)S(1)} %get-tuple-element.124), kind=kOutput, calls=%fused_computation.5 | convolution fusion | flops 8869904384 | bytes 16384000 | tf_op jit(solution)/shard_map/dot_general | solution.py:26
  352.4 2.4 copy.106
  354.8 40.5 %scatter.1 = f32[192,2048]{1,0:T(8,128)} custom-call(bf16[8,192,704]{2,1,0:T(8,128)(2,1)} %bitcast.141, bf16[2048,704]{1,0:T(8,128)(2,1)} %all-gather.6.cloned.1.call-done.refs_1_), custom_call_target="tpu_custom_call" | custom-call | bytes 120000000 | tf_op jit(solution)/shard_map/scatter/pallas_call | solution.py:108
  398.0 2.3 pad_maximum_fusion
  400.3 6.5 copy.108
  406.8 78.9 %sum_back_gather.1 = (f32[192,2048]{1,0:T(8,128)}, bf16[8,192,2048]{2,1,0:T(8,128)(2,1)}, f32[2,2048]{1,0:T(2,128)}, bf16[4,192,512]{2,1,0:T(8,128)(2,1)}) custom-call(bf16[8,192,1408]{2,1,0:T(8,128)(2,1)} %bitcast.136, bf16[2048,1408]{1,0:T(8,128)(2,1)} %all-gather.8.cloned.1.call-done.refs_1_, f32[192,2048]{1,0:T(8,128)} %get-tuple-element.71.refs_2_, ...), custom_call_target="tpu_custom_call" | custom-call | bytes 120000000 | tf_op jit(solution)/shard_map/sum_back_gather/pallas_call | solution.py:108
  485.8 5.8 convolution_convert_fusion.4
  491.6 5.5 convolution_convert_fusion.3.refs_4_
  497.1 2.3 copy.109
  499.3 36.0 %attend_back.1 = (bf16[1536,768]{1,0:T(8,128)(2,1)}, bf16[4,128,1408]{2,1,0:T(8,128)(2,1)}, bf16[4,128,704]{2,1,0:T(8,128)(2,1)}, bf16[4,192,512]{2,1,0:T(8,128)(2,1)}) custom-call(bf16[1536,256]{1,0:T(8,128)(2,1)} %copy-done.2, bf16[1536,256]{1,0:T(8,128)(2,1)} %copy-done.3, bf16[1536,256]{1,0:T(8,128)(2,1)} %copy-done.4, bf16[1536,256]{1,0:T(8,128)(2,1)} %copy-done, ...), custom_call_target="tpu_custom_call" | custom-call | bytes 120000000 | tf_op jit(solution)/shard_map/attend_back/pallas_call | solution.py:108
  535.3 9.2 %convolution_convert_fusion.1 = bf16[2048,768]{1,0:T(8,128)(2,1)} fusion(bf16[1536,2048]{1,0:T(8,128)(2,1)} %add_convert_fusion, bf16[1536,768]{1,0:T(8,128)(2,1)} %get-tuple-element.82), kind=kOutput, calls=%fused_computation.13 | convolution fusion | flops 4833411072 | bytes 11796480 | tf_op jit(solution)/shard_map/dot_general | solution.py:26
  544.6 90.0 %sum_back_leave.1 = (bf16[2,192,2048]{2,1,0:T(8,128)(2,1)}, f32[2,2048]{1,0:T(2,128)}, bf16[4,128,256]{2,1,0:T(8,128)(2,1)}, bf16[4,192,512]{2,1,0:T(8,128)(2,1)}) custom-call(bf16[8,192,768]{2,1,0:T(8,128)(2,1)} %bitcast.140, bf16[2048,768]{1,0:T(8,128)(2,1)} %all-gather.4.cloned.1.call-done.refs_1_, ...), custom_call_target="tpu_custom_call" | custom-call | bytes 120000000 | tf_op jit(solution)/shard_map/sum_back_leave/pallas_call | solution.py:108
  636.9 3.8 reshape.323
  640.7 2.5 copy.114
  643.2 5.2 reshape.310
  651.9 5.7 copy.124
  660.3 15.6 %exchange.3 = (f32[2,4,4,8,128]{4,3,2,1,0:T(8,128)}, bf16[4,128,768]{2,1,0:T(8,128)(2,1)}, bf16[4,192,512]{2,1,0:T(8,128)(2,1)}) custom-call(f32[4,4,8,128]{3,2,1,0:T(8,128)} %reshape.290.refs_0_, bf16[4,128,768]{2,1,0:T(8,128)(2,1)} %bitcast.168, bf16[4,192,512]{2,1,0:T(8,128)(2,1)} %get-tuple-element.86.refs_2_), custom_call_target="tpu_custom_call" | custom-call | bytes 120000000 | tf_op jit(solution)/shard_map/exchange/pallas_call | solution.py:108
  (164 shorter events, 52.0 us)
Async XLA Ops:
  7.2 3.7 copy-start.28
  7.2 3.9 copy-start.31
  7.2 3.9 copy-start.22
  7.2 140.2 %all-gather.4.cloned.1.call-start = ((), (), s32[]{:S(2)}) async-start(), calls=%async_computation.4 | async-start | bytes 3932160 | tf_op jit(solution)/shard_map/all_gather | solution.py:805
  9.4 3.4 copy-start.25
  9.4 4.2 copy-start.29
  9.4 4.2 copy-start.30
  50.4 232.0 %all-gather.8.cloned.1.call-start = ((), (), s32[]{:S(2)}) async-start(), calls=%async_computation.6 | async-start | bytes 7208960 | tf_op jit(solution)/shard_map/all_gather | solution.py:805
  128.2 193.3 %all-gather.6.cloned.1.call-start = ((), (), s32[]{:S(2)}) async-start(), calls=%async_computation.5 | async-start | bytes 3932160 | tf_op jit(solution)/shard_map/all_gather | solution.py:805
  128.9 368.1 %reduce-scatter.7.cloned.1.call-start = ((), (), s32[]{:S(2)}) async-start(), calls=%async_computation.8 | async-start | bytes 3604480 | tf_op jit(solution)/shard_map/reduce_scatter | solution.py:808
  129.3 4.6 copy-start.11
  133.1 2.6 copy-start.26
  137.4 20.1 %copy-start.7 = (s32[1,1536]{1,0:T(1,128)}, s32[1,1536]{1,0:T(1,128)S(1)}, u32[]{:S(2)}) copy-start(s32[1,1536]{1,0:T(1,128)S(1)} %broadcast_in_dim.16.begin_ref.refs_10_) | copy-start | bytes 18436
  147.4 10.1 %copy-start.5 = (f32[256,128]{1,0:T(8,128)S(1)}, f32[256,128]{1,0:T(8,128)}, u32[]{:S(2)}) copy-start(f32[256,128]{1,0:T(8,128)} %constant.75.clone.cos_ref.refs_6_) | copy-start | bytes 393220
  147.4 10.1 %copy-start.6 = (f32[256,128]{1,0:T(8,128)S(1)}, f32[256,128]{1,0:T(8,128)}, u32[]{:S(2)}) copy-start(f32[256,128]{1,0:T(8,128)} %constant.76.clone.sin_ref.refs_7_) | copy-start | bytes 393220
  147.4 10.1 %copy-start.9 = (f32[6,128]{1,0:T(8,128)S(1)}, f32[6,128]{1,0:T(8,128)}, u32[]{:S(2)}) copy-start(f32[6,128]{1,0:T(8,128)} %constant.77.clone.cosf_ref.refs_8_) | copy-start | bytes 9220
  147.4 10.1 %copy-start.10 = (f32[6,128]{1,0:T(8,128)S(1)}, f32[6,128]{1,0:T(8,128)}, u32[]{:S(2)}) copy-start(f32[6,128]{1,0:T(8,128)} %constant.78.clone.sinf_ref.refs_9_) | copy-start | bytes 9220
  297.0 4.4 copy-start.13
  297.0 5.9 copy-start.14
  321.5 177.8 %reduce-scatter.5.cloned.1.call-start = ((), (), s32[]{:S(2)}) async-start(), calls=%async_computation.7 | async-start | bytes 7208960 | tf_op jit(solution)/shard_map/reduce_scatter | solution.py:808
  350.0 194.6 %reduce-scatter.9.cloned.1.call-start = ((), (), s32[]{:S(2)}) async-start(), calls=%async_computation.9 | async-start | bytes 1310720 | tf_op jit(solution)/shard_map/reduce_scatter | solution.py:808
  354.8 40.5 %copy-start.15 = (f32[192,2048]{1,0:T(8,128)S(1)}, f32[192,2048]{1,0:T(8,128)}, u32[]{:S(2)}) copy-start(f32[192,2048]{1,0:T(8,128)} %get-tuple-element.71.refs_2_) | copy-start | bytes 4718596
  395.2 2.7 copy-start.18
  395.3 2.7 copy-start.20
  406.8 78.9 %copy-start.1 = (bf16[1536,256]{1,0:T(8,128)(2,1)S(1)}, bf16[1536,256]{1,0:T(8,128)(2,1)}, u32[]{:S(2)}) copy-start(bf16[1536,256]{1,0:T(8,128)(2,1)} %copy-done) | copy-start | bytes 2359300
  485.7 5.8 copy-start.21
  491.5 168.7 %reduce-scatter.11.cloned.1.call-start = ((), (), s32[]{:S(2)}) async-start(), calls=%async_computation.10 | async-start | bytes 3932160 | tf_op jit(solution)/shard_map/reduce_scatter | solution.py:808
  535.3 9.2 %copy-start.27 = (f32[2,2048]{1,0:T(2,128)S(1)}, f32[2,2048]{1,0:T(2,128)}, u32[]{:S(2)}) copy-start(f32[2,2048]{1,0:T(2,128)} %get-tuple-element.88) | copy-start | bytes 49156
  544.6 90.9 %copy-start.12 = (bf16[1536,768]{1,0:T(8,128)(2,1)S(1)}, bf16[1536,768]{1,0:T(8,128)(2,1)}, u32[]{:S(2)}) copy-start(bf16[1536,768]{1,0:T(8,128)(2,1)} %get-tuple-element.82) | copy-start | bytes 7077892
  651.9 5.7 copy-start.24
  651.9 6.7 copy-start.23
  657.6 19.4 %copy-start.16 = (bf16[4,192,512]{2,1,0:T(8,128)(2,1)S(1)}, bf16[4,192,512]{2,1,0:T(8,128)(2,1)}, u32[]{:S(2)}) copy-start(bf16[4,192,512]{2,1,0:T(8,128)(2,1)} %get-tuple-element.86.refs_2_) | copy-start | bytes 2359300
  (7 other events, 7.6 us)
Sparse Core Ops, SparseCore 0:
  50.5 82.8 all-gather.3
  135.0 121.6 all-gather.7
  258.3 63.1 all-gather.5
  324.2 56.6 reduce-scatter.6
  383.1 102.7 reduce-scatter.4
  491.7 38.0 reduce-scatter.8
  544.6 59.5 reduce-scatter.10

commit v6 on v5

--- a/solution.py
+++ b/solution.py
@@ -304,7 +304,7 @@
     ]
 
 
-def sum_over_plane(S, T, x_ref, w_ref, out_ref, scratch):
+def sum_over_plane(S, T, x_ref, w_ref, out_ref, scratch, meanwhile=None):
     away, sib, mine, row1, col1, row2, col2, to_col, to_row = scratch[:9]
     asend, arecv, rsend, rrecv, csend, crecv, fsend, frecv = scratch[9:]
     n, D = out_ref.shape
@@ -372,6 +372,8 @@
     def came(ref, send, recv):
         remote(ref, ref, send, recv, other).wait_recv()
 
+    if meanwhile is not None:
+        meanwhile()
     total = mine[B, top, :].astype(F32)
     for j in range(1, B):
         came(row1.at[j - 1, 1], rsend.at[j - 1, 1], rrecv.at[j - 1, 1])
@@ -397,20 +399,33 @@
         copy.wait_send()
 
 
-def scatter(S, C, T, number, x, w, riders=()):
-    L, K = x.shape
-    D, n = w.shape[0], L // (S * T)
+def sum_and_gates(S, C, T, number, act, wd, gb, gu):
+    L, K = act.shape
+    D, n = wd.shape[0], L // (S * T)
 
     def kernel(ride, ins, outs, scratch):
+        act_ref, wd_ref, gb_ref, gu_ref = ins
+        out_ref, dgu_ref = outs
         _, _, rows, col = plane(S)
-        greet(S, C, rows + [col], other=True, axes=ride.axes)
-        ride.start()
-        sum_over_plane(S, T, ins[0], ins[1], outs[0], scratch)
-        ride.wait()
+        greet(S, C, rows + [col], other=True)
+
+        def meanwhile():
+            @pl.loop(0, L // BLK)
+            def _(i):
+                r = pl.ds(pl.multiple_of(i * BLK, BLK), BLK)
+                dact = mm(gb_ref[r, :], wd_ref[...], 1, 0)
+                both = gu_ref[r, :]
+                gate, up = both[:, :K], both[:, K:]
+                s = jax.nn.sigmoid(gate)
+                dgate = dact * up * s * (1.0 + gate * (1.0 - s))
+                dgu_ref[r, :] = jnp.concatenate((dgate, dact * gate * s), axis=1).astype(BF)
+
+        sum_over_plane(S, T, act_ref, wd_ref, out_ref, scratch, meanwhile)
 
     return comm(
-        kernel, S, C, number, "scatter", [x.reshape(S * T, n, K), w], [IN_VMEM, IN_VMEM],
-        [(jax.ShapeDtypeStruct((n, D), F32), IN_VMEM)], sum_scratch(S, n, D), riders,
+        kernel, S, C, number, "sum_and_gates", [act.reshape(S * T, n, K), wd, gb, gu], [IN_VMEM] * 4,
+        [(jax.ShapeDtypeStruct((n, D), F32), IN_VMEM), (jax.ShapeDtypeStruct((L, 2 * K), BF), IN_VMEM)],
+        sum_scratch(S, n, D),
     )
 
 
@@ -517,22 +532,18 @@
     return [g, out.reshape(L, D), stats] + rest
 
 
-def sum_back_leave(S, C, T, number, x, w, v, residual, gain, riders=()):
+def sum_back(S, C, T, number, x, w, v, residual, gain, riders=()):
     L, K = x.shape
     D, n = w.shape[0], L // (S * T)
-    wide = D // S
 
     def kernel(ride, ins, outs, scratch):
         x_ref, w_ref, in_ref, res_ref, gain_ref = ins
-        out_ref, stats = outs
-        acc, low, buf, buf2, s1, r1, s2, r2, s3, r3, s4, r4, own = scratch[:13]
-        p, z, c = here()
-        mates = [(p + k) % S for k in range(1, S)]
-        line = [(z + k) % C for k in range(1, C)]
-        other = {"tp": 1 - c}
-        greet(S, C, mates, line=True, other=True, axes=ride.axes)
+        low, stats = outs
+        acc = scratch[0]
+        _, _, rows, col = plane(S)
+        greet(S, C, rows + [col], other=True, axes=ride.axes)
         ride.start()
-        sum_over_plane(S, T, x_ref, w_ref, acc, scratch[13:])
+        sum_over_plane(S, T, x_ref, w_ref, acc, scratch[1:])
         stats[...] = jnp.zeros_like(stats)
 
         def work(r):
@@ -540,39 +551,101 @@
             low[r, :] = g.astype(BF)
 
         row_blocks(n, work)
+        ride.wait()
+
+    return comm(
+        kernel, S, C, number, "sum_back", [x.reshape(S * T, n, K), w, v, residual, gain], [IN_VMEM] * 5,
+        [(jax.ShapeDtypeStruct((n, D), BF), IN_VMEM), (jax.ShapeDtypeStruct((2, D), F32), IN_VMEM)],
+        [pltpu.VMEM((n, D), F32)] + sum_scratch(S, n, D),
+        riders,
+    )
+
+
+def finish(S, C, T, number, x, stats, bias, riders):
+    n, D = x.shape
+    wide, lines = D // S, bias.shape[1] // 128
+    nb = D // (S * C)
+    count = sum(y.shape[0] for y in stats)
+    tall = -(-(count + lines) // 8) * 8
+    many = C * S - 1
+
+    def kernel(ride, ins, outs, scratch):
+        x_ref, stat_refs, bias_ref = ins[0], ins[1:-1], ins[-1]
+        out_ref, got = outs
+        buf, buf2, tile, s1, r1, s2, r2, s3, r3, s4, r4, own, tsend, trecv, bsend, brecv = scratch
+        p, z, c = here()
+        other = {"tp": 1 - c}
+        everyone = [(i, j) for i in range(C) for j in range(S) if i or j]
+        peers = [{"shard": (p + j) % S, "ctx": (z + i) % C} for i, j in everyone]
+        barrier = pltpu.get_barrier_semaphore()
+        for where in peers + [other]:
+            pl.semaphore_signal(barrier, inc=1, device_id=where, device_id_type=MESH)
+        pl.semaphore_wait(barrier, len(peers) + 1)
 
         def part(q):
             return pl.ds(pl.multiple_of(q * wide, 128), wide)
 
-        def turn_over(source, target, send, recv, local, me, axis, peers):
+        def turn_over(source, target, send, recv, local, size, me, axis):
             hop = [pltpu.make_async_copy(source(me), target, local)]
-            for k, q in enumerate(peers):
-                hop.append(remote(source(q), target, send.at[k], recv.at[k], {axis: q}))
+            for k in range(1, size):
+                q = (me + k) % size
+                hop.append(remote(source(q), target, send.at[k - 1], recv.at[k - 1], {axis: q}))
             for copy in hop:
                 copy.start()
-            for copy in hop:
-                copy.wait()
-
-        turn_over(lambda q: low.at[:, part(q)], buf.at[p], s1, r1, own.at[0], p, "shard", mates)
-        turn_over(lambda q: buf.at[q], buf2.at[z], s2, r2, own.at[1], z, "ctx", line)
-        turn_over(lambda q: buf2.at[q], out_ref.at[c, :, part(p)], s3, r3, own.at[2], p, "shard", mates)
-        copy = remote(out_ref.at[c], out_ref.at[c], s4, r4, other)
-        copy.start()
-        copy.wait_send()
+            return hop
+
+        hop = turn_over(lambda q: x_ref.at[:, part(q)], buf.at[p], s1, r1, own.at[0], S, p, "shard")
+        ride.start()
+        tile[...] = jnp.zeros_like(tile)
+        at = 0
+        for ref in stat_refs:
+            tile[at : at + ref.shape[0], :] = ref[...]
+            at += ref.shape[0]
+        for k in range(lines):
+            for block in range(D // 128):
+                tile[at + k : at + k + 1, pl.ds(block * 128, 128)] = bias_ref[:, pl.ds(k * 128, 128)]
+
+        def columns(g, q):
+            return tile.at[:, pl.ds(pl.multiple_of((g * S + q) * nb // 128 * 128, 128), 128)]
+
+        small = [pltpu.make_async_copy(columns(z, p), got.at[c, z, p], own.at[3])]
+        for k, (where, (i, j)) in enumerate(zip(peers, everyone)):
+            small.append(
+                remote(columns((z + i) % C, (p + j) % S), got.at[c, z, p], tsend.at[k], trecv.at[k], where)
+            )
+        for copy in small:
+            copy.start()
+        for copy in hop:
+            copy.wait()
+        hop = turn_over(lambda q: buf.at[q], buf2.at[z], s2, r2, own.at[1], C, z, "ctx")
+        for copy in small:
+            copy.wait()
+        back = remote(got.at[c], got.at[c], bsend, brecv, other)
+        back.start()
+        for copy in hop:
+            copy.wait()
+        for copy in turn_over(lambda q: buf2.at[q], out_ref.at[c, :, part(p)], s3, r3, own.at[2], S, p, "shard"):
+            copy.wait()
+        last = remote(out_ref.at[c], out_ref.at[c], s4, r4, other)
+        last.start()
+        back.wait_send()
+        remote(got.at[1 - c], got.at[1 - c], bsend, brecv, other).wait_recv()
+        last.wait_send()
         remote(out_ref.at[1 - c], out_ref.at[1 - c], s4, r4, other).wait_recv()
         ride.wait()
 
-    out, stats, *rest = comm(
-        kernel, S, C, number, "sum_back_leave", [x.reshape(S * T, n, K), w, v, residual, gain], [IN_VMEM] * 5,
-        [(jax.ShapeDtypeStruct((T, n, D), BF), ANY), (jax.ShapeDtypeStruct((2, D), F32), IN_VMEM)],
+    args = [x, *stats, bias]
+    out, got, *rest = comm(
+        kernel, S, C, number, "finish", args, [IN_VMEM] * len(args),
+        [(jax.ShapeDtypeStruct((T, n, D), BF), ANY), (jax.ShapeDtypeStruct((T, C, S, tall, 128), F32), ANY)],
         [
-            pltpu.VMEM((n, D), F32), pltpu.VMEM((n, D), BF), pltpu.VMEM((S, n, wide), BF), pltpu.VMEM((C, n, wide), BF),
-            DMA((S - 1,)), DMA((S - 1,)), DMA((C - 1,)), DMA((C - 1,)), DMA((S - 1,)), DMA((S - 1,)), DMA, DMA, DMA((3,)),
-        ]
-        + sum_scratch(S, n, D),
+            pltpu.VMEM((S, n, wide), BF), pltpu.VMEM((C, n, wide), BF), pltpu.VMEM((tall, D), F32),
+            DMA((S - 1,)), DMA((S - 1,)), DMA((C - 1,)), DMA((C - 1,)), DMA((S - 1,)), DMA((S - 1,)),
+            DMA, DMA, DMA((4,)), DMA((many,)), DMA((many,)), DMA, DMA,
+        ],
         riders,
     )
-    return [out.reshape(T * n, D), stats] + rest
+    return [out.reshape(T * n, D), got] + rest
 
 
 def turn_tables(rows):
@@ -674,7 +747,7 @@
     )(begin[0, ::size] // size, qkv, *turn_tables(rows), begin)
 
 
-def attend_back_work(ins, out_ref, scratch):
+def attend_back_work(ins, out_ref, bias_ref, scratch):
     q_ref, k_ref, v_ref, o_ref, do_ref, lse_ref, cos_ref, sin_ref, cosf_ref, sinf_ref, begin_ref = ins
     kt_ref, dq_ref, dk_ref, dv_ref = scratch
     rows, wide = q_ref.shape
@@ -732,13 +805,18 @@
             both = jnp.concatenate(done[2 * t : 2 * t + 2], axis=0)
             dq_ref[r, pl.ds(t * 128, 128)] = both.T * (HEAD**-0.5)
 
+    bias_ref[...] = jnp.zeros_like(bias_ref)
+
     @pl.loop(0, rows // BLK)
     def _(i):
         r = pl.ds(pl.multiple_of(i * BLK, BLK), BLK)
         for t in range(pairs):
             w = pl.ds(t * 128, 128)
             for part, value in enumerate((turn(dq_ref[r, w], i, tables, -1.0), turn(dk_ref[r, w], i, tables, -1.0), dv_ref[r, w])):
-                out_ref[r, pl.ds(part * wide + t * 128, 128)] = value.astype(BF)
+                lanes = pl.ds(part * wide + t * 128, 128)
+                value = value.astype(BF)
+                out_ref[r, lanes] = value
+                bias_ref[:, lanes] += jnp.sum(value.astype(F32), axis=0, keepdims=True)
 
 
 def attend_back(S, C, number, q, k, v, o, do, lse, begin, riders):
@@ -747,13 +825,13 @@
     def kernel(ride, ins, outs, scratch):
         greet(S, C, axes=ride.axes)
         ride.start()
-        attend_back_work(ins, outs[0], scratch)
+        attend_back_work(ins, outs[0], outs[1], scratch)
         ride.wait()
 
     args = [q, k, v, o, do, lse, *turn_tables(rows), begin]
     return comm(
         kernel, S, C, number, "attend_back", args, [IN_VMEM] * len(args),
-        [(jax.ShapeDtypeStruct((rows, 3 * wide), BF), IN_VMEM)],
+        [(jax.ShapeDtypeStruct((rows, 3 * wide), BF), IN_VMEM), (jax.ShapeDtypeStruct((1, 3 * wide), F32), IN_VMEM)],
         [pltpu.VMEM((wide, rows), BF)] + [pltpu.VMEM((rows, wide), F32)] * 3,
         riders,
     )
@@ -864,16 +942,11 @@
         wd, gw_down = after(wd, gw_down)
         gw_down = sum_ctx(gw_down)
 
-        dact = mm(gb, wd, 1, 0)
-        dgate = dact * up * logistic * (1.0 + gate * (1.0 - logistic))
-        dup = dact * gate * logistic
-        dgu = jnp.concatenate((dgate, dup), axis=1).astype(BF)
+        got, dgu = sum_and_gates(S, C, T, 5, act, wd, gb, gu)
         gw_gateup = mm(n2, dgu, 0, 0).astype(BF)
-        act, gw_gateup = after(act, gw_gateup)
+        dgu, gw_gateup = after(dgu, gw_gateup)
         gw_gateup = sum_ctx(gw_gateup)
-        (got,) = scatter(S, C, T, 5, act, wd)
         out = parts((mid + got).astype(BF))
-        dgu, out = after(dgu, out)
         dmid, gb1, stats2, out = sum_back_gather(
             S, C, T, 6, dgu, wg, mid, own(gb), gains[1:], [("shard", out)]
         )
@@ -881,31 +954,24 @@
         gb1, gw_out = after(gb1, gw_out)
         gw_out = sum_ctx(gw_out)
         do = mm(gb1, wo, 1, 0).astype(BF)
-        dqkv, gw_gateup, gw_down, out = attend_back(
+        dqkv, gbias, gw_gateup, gw_down, out = attend_back(
             S, C, 11, q, k, v, o, do, lse, begin, [("shard", gw_gateup), ("shard", gw_down), ("ctx", out)]
         )
         gw_qkv = mm(n1, dqkv, 0, 0).astype(BF)
         dqkv, gw_qkv = after(dqkv, gw_qkv)
         gw_qkv = sum_ctx(gw_qkv)
-        gtok, stats1, gw_out, out = sum_back_leave(
-            S, C, T, 8, dqkv, wq, own_tok, dmid, gains[:1], [("shard", gw_out), ("shard", out)]
+        low, stats1, out = sum_back(S, C, T, 8, dqkv, wq, own_tok, dmid, gains[:1], [("shard", out)])
+        gtok, small, gw_qkv, gw_out, mate = finish(
+            S, C, T, 10, low, [stats1, stats2], gbias, [("shard", gw_qkv), ("shard", gw_out), ("tp", out)]
         )
         gtok = unpermute(gtok).astype(F32)
-        gbias = jnp.sum(dqkv.astype(F32), axis=0)
-        tiles = tiles_of(
-            (
-                jnp.stack((stats1[0], stats2[0], stats1[1], stats2[1])).reshape(4, C, S, nb).transpose(1, 2, 0, 3),
-                gbias.reshape(3, heads, S, C, nf).transpose(3, 2, 0, 1, 4),
-            ),
-            (C, S),
-        )
-        small, gw_qkv, mate = exchange(S, C, T, 10, [("shard", gw_qkv), ("tp", out)], tiles)
         out = jnp.where(c == 0, jnp.stack((out, mate)), jnp.stack((mate, out)))
         out = unpermute(out.transpose(0, 2, 1, 3).reshape(R, D))
-        small = small.reshape(T, C, S, 1024)
-        norms = jnp.sum(small[..., : 4 * nb], axis=(0, 1, 2)).reshape(1, 4, nb)
-        gbias = lax.dynamic_index_in_dim(small, c, 0, keepdims=False)[..., 4 * nb : 4 * nb + 3 * heads * nf]
-        gbias = jnp.sum(gbias, axis=0).reshape(S, 3, heads, nf).swapaxes(0, 1).reshape(b_qkv.shape)
+        norms = lax.dynamic_slice_in_dim(jnp.sum(small[..., :4, :], axis=(0, 1, 2)), (z * S + p) * nb % 128, nb, 1)
+        gbias = lax.dynamic_index_in_dim(small, c, 0, keepdims=False)[:, :, 4 : 4 + 3 * hn // 128]
+        gbias = jnp.sum(gbias, axis=0).reshape(S, 3, heads, S * C, nf)
+        gbias = lax.dynamic_index_in_dim(gbias, p * C + z, 3, keepdims=False)
+        gbias = gbias.swapaxes(0, 1).reshape(b_qkv.shape)
 
         return (
             out,
@@ -915,8 +981,8 @@
             gw_out.astype(F32).swapaxes(1, 2).reshape(w_out.shape),
             gw_gateup.astype(F32).reshape(S, nb, 2, fn).transpose(1, 2, 0, 3).reshape(w_gateup.shape),
             gw_down.astype(F32).swapaxes(1, 2).reshape(w_down.shape),
-            norms[:, :2],
-            norms[:, 2:],
+            jnp.stack((norms[0], norms[2]))[None],
+            jnp.stack((norms[1], norms[3]))[None],
         )
 
     return body

time: 702 us -> 699 us (level)
  matrix products: 77.2 us -> 65.6 us
  waiting for transfers between devices: 13.4 us -> 23.5 us
    dot_general x8 -> x7, matrix products: 77.2 us -> 65.6 us  [mm(): lax.dot_general(a, b, (((ca,), (cb,)), ((), ())), preferred_element_type=...]
    reduce_scatter x4, waiting for transfers between devices: 0.03 us -> 10.2 us  [sum_ctx(): g = lax.psum_scatter(g.astype(BF), 'ctx', scatter_dimension=0, tiled=True)]
    dot_general x0 -> x1, local copies, waits for them, and re-layouts: none -> 9.37 us  [mm(): lax.dot_general(a, b, (((ca,), (cb,)), ((), ())), preferred_element_type=...]
    optimization_barrier x2 -> x0, local copies, waits for them, and re-layouts: 8.91 us -> none  [after(): return lax.optimization_barrier((x, y))]
    unnamed x69 -> x55, local copies, waits for them, and re-layouts: 24.7 us -> 23.7 us
  transfers between devices with their start and end apart: 7 -> 7, of which waited for: 1 -> 3; matrix products, arithmetic and copies ran while one was open for 22% -> 18% of each run, Pallas kernels for 63% -> 58%
where the time goes in v6:
time: 699 us; the launch traced here: 691 us
  Pallas kernels  484 us (69%)
  local copies, waits for them, and re-layouts  81.3 us (12%)
  matrix products  65.6 us (9%)
  waiting for transfers between devices  23.5 us (3%)
  other arithmetic  20.6 us (3%)
  between operations  14.9 us (2%)
    pallas_call x9, Pallas kernels, comm(): pl.pallas_call(body, out_shape=[shape for shape, _ in outs] + ride.shapes...  464 us
    dot_general x7, matrix products, mm(): lax.dot_general(a, b, (((ca,), (cb,)), ((), ())), preferred_element_type=...  65.6 us
    unnamed x55, local copies, waits for them, and re-layouts  23.7 us
    pallas_call x1, Pallas kernels, attend(): pl.pallas_call(attend_kernel, in_specs=[pl.BlockSpec(memory_space=pltpu.S...  20.2 us
  transfers between devices with their start and end apart: 7, of which 3 were waited for; matrix products, arithmetic and copies ran while one was open for 18% of the time, Pallas kernels for 58%

profile of v6, /device:TPU:9, one launch (start us, length us, event | category | flops | bytes accessed | tf_op | source)
XLA Modules:
  0.0 690.8 jit_solution(4690149494136068325)
XLA Ops:
  18.3 36.1 %exchange.1 = (f32[2,4,4,8,128]{4,3,2,1,0:T(8,128)}, bf16[4,192,512]{2,1,0:T(8,128)(2,1)}, bf16[4,192,512]{2,1,0:T(8,128)(2,1)}, bf16[4,128,768]{2,1,0:T(8,128)(2,1)}, bf16[4,128,256]{2,1,0:T(8,128)(2,1)}) custom-call(f32[4,4,8,128]{3,2,1,0:T(8,128)} %broadcast_in_dim.18.refs_0_, bf16[4,192,512]{2,1,0:T(8,128)(2,1)} %reshape.239.refs_1_, ...), custom_call_target="tpu_custom_call" | custom-call | bytes 120000000 | tf_op jit(solution)/shard_map/exchange/pallas_call | solution.py:108
  55.7 3.8 copy.124
  61.2 2.3 reshape.245
  65.0 67.7 %gather_columns.2 = (bf16[4,2,192,2048]{3,2,1,0:T(8,128)(2,1)}, bf16[4,512,256]{2,1,0:T(8,128)(2,1)}, bf16[4,128,1408]{2,1,0:T(8,128)(2,1)}, bf16[4,128,704]{2,1,0:T(8,128)(2,1)}, bf16[4,192,512]{2,1,0:T(8,128)(2,1)}) custom-call(bf16[4,192,512]{2,1,0:T(8,128)(2,1)} %get-tuple-element.56.refs_0_, bf16[512,256]{1,0:T(8,128)(2,1)} %bitcast.167, ...), custom_call_target="tpu_custom_call" | custom-call | bytes 120000000 | tf_op jit(solution)/shard_map/gather_columns/pallas_call | solution.py:108
  134.2 3.8 convert_reduce_fusion
  144.3 7.8 %add_convert_fusion = bf16[1536,2048]{1,0:T(8,128)(2,1)} fusion(f32[2048]{0:T(1024)S(1)} %get-tuple-element.141, f32[2048]{0:T(1024)S(1)} %get-tuple-element.138, f32[1536]{0:T(1024)S(1)} %rsqrt.12, f32[1536]{0:T(1024)S(1)} %div.28, bf16[4,2,192,2048]{3,2,1,0:T(8,128)(2,1)} %get-tuple-element.58), kind=kLoop, calls=%fused_computation.4 | loop fusion | flops 18874368 | bytes 12611584 | tf_op jit(solution)/shard_map/convert_element_type | solution.py:930
  152.2 9.8 %convolution_add_fusion.qkv_ref = f32[1536,768]{1,0:T(8,128)} fusion(bf16[1536,2048]{1,0:T(8,128)(2,1)} %add_convert_fusion, bf16[2048,768]{1,0:T(8,128)(2,1)} %all-gather.4.cloned.1.call-done.refs_1_, f32[768]{0:T(1024)S(1)} %add.94), kind=kOutput, calls=%fused_computation.8 | convolution fusion | flops 4833017856 | bytes 14158848 | tf_op jit(solution)/shard_map/dot_general | solution.py:26
  162.0 20.2 %attend.1 = (bf16[1536,256]{1,0:T(8,128)(2,1)S(1)}, bf16[1536,256]{1,0:T(8,128)(2,1)S(1)}, bf16[1536,256]{1,0:T(8,128)(2,1)S(1)}, bf16[1536,256]{1,0:T(8,128)(2,1)S(1)}, f32[4,1536]{1,0:T(4,128)S(1)}) custom-call(s32[3]{0:T(128)S(1)} %and_select_fusion.first_ref, f32[1536,768]{1,0:T(8,128)} %convolution_add_fusion.qkv_ref, f32[256,128]{1,0:T(8,128)S(1)} %copy-done.6, ...), custom_call_target="tpu_custom_call" | custom-call | tf_op jit(solution)/shard_map/attend/pallas_call | solution.py:739
  186.4 68.2 %sum_norm_gather.1 = (f32[192,2048]{1,0:T(8,128)}, bf16[8,192,2048]{2,1,0:T(8,128)(2,1)}, bf16[4,192,512]{2,1,0:T(8,128)(2,1)}) custom-call(bf16[8,192,256]{2,1,0:T(8,128)(2,1)} %bitcast.129, bf16[2048,256]{1,0:T(8,128)(2,1)} %bitcast.158, bf16[192,2048]{1,0:T(8,128)(2,1)} %constant_dynamic-slice_fusion.1.refs_2_, f32[1,2048]{1,0:T(1,128)} %bitcast.172, ...), custom_call_target="tpu_custom_call" | custom-call | bytes 120000000 | tf_op jit(solution)/shard_map/sum_norm_gather/pallas_call | solution.py:108
  254.7 32.2 %gather_columns.3 = bf16[4,2,192,2048]{3,2,1,0:T(8,128)(2,1)} custom-call(bf16[4,192,512]{2,1,0:T(8,128)(2,1)} %get-tuple-element.71.refs_0_), custom_call_target="tpu_custom_call" | custom-call | bytes 120000000 | tf_op jit(solution)/shard_map/gather_columns/pallas_call | solution.py:108
  286.8 14.2 %fusion.10 = f32[1536,1408]{0,1:T(8,128)S(1)} fusion(bf16[1536,2048]{1,0:T(8,128)(2,1)} %bitcast.177, bf16[2048,1408]{1,0:T(8,128)(2,1)} %all-gather.6.cloned.1.call-done.refs_1_), kind=kOutput, calls=%fused_computation.59 | convolution fusion | flops 8858370048 | bytes 20709376 | tf_op jit(solution)/shard_map/dot_general | solution.py:26
  302.4 3.0 copy-done.12
  307.0 6.0 convolution_convert_fusion.2
  313.0 12.6 %all-gather.8.cloned.1.call-done.refs_1_ = bf16[2048,704]{1,0:T(8,128)(2,1)} async-done(((bf16[512,704]{1,0:T(8,128)(2,1)}), bf16[2048,704]{1,0:T(8,128)(2,1)}) %all-gather.8.cloned.1.call-update) | async-done | bytes 2883600 | tf_op jit(solution)/shard_map/all_gather | solution.py:883
  325.6 9.4 %copy.132.refs_3_ = f32[1536,1408]{1,0:T(8,128)} copy(f32[1536,1408]{0,1:T(8,128)} %copy-done.12) | data formatting | bytes 17301504 | tf_op jit(solution)/shard_map/dot_general | solution.py:26
  335.0 2.4 copy.131
  337.4 46.0 %sum_and_gates.1 = (f32[192,2048]{1,0:T(8,128)}, bf16[1536,1408]{1,0:T(8,128)(2,1)}) custom-call(bf16[8,192,704]{2,1,0:T(8,128)(2,1)} %bitcast.137, bf16[2048,704]{1,0:T(8,128)(2,1)} %all-gather.8.cloned.1.call-done.refs_1_, bf16[1536,2048]{1,0:T(8,128)(2,1)} %bitcast.131, f32[1536,1408]{1,0:T(8,128)} %copy.132.refs_3_), custom_call_target="tpu_custom_call" | custom-call | bytes 120000000 | tf_op jit(solution)/shard_map/sum_and_gates/pallas_call | solution.py:108
  383.5 15.1 %convolution_convert_fusion = bf16[2048,1408]{1,0:T(8,128)(2,1)} fusion(bf16[1536,2048]{1,0:T(8,128)(2,1)} %bitcast.178, bf16[1536,1408]{1,0:T(8,128)(2,1)} %get-tuple-element.74), kind=kOutput, calls=%fused_computation.5 | convolution fusion | flops 8861253632 | bytes 16384000 | tf_op jit(solution)/shard_map/dot_general | solution.py:26
  402.0 80.4 %sum_back_gather.1 = (f32[192,2048]{1,0:T(8,128)}, bf16[8,192,2048]{2,1,0:T(8,128)(2,1)}, f32[2,2048]{1,0:T(2,128)}, bf16[4,192,512]{2,1,0:T(8,128)(2,1)}) custom-call(bf16[8,192,1408]{2,1,0:T(8,128)(2,1)} %bitcast.144, bf16[2048,1408]{1,0:T(8,128)(2,1)} %all-gather.6.cloned.1.call-done.refs_1_, f32[192,2048]{1,0:T(8,128)} %get-tuple-element.75.refs_2_, ...), custom_call_target="tpu_custom_call" | custom-call | bytes 120000000 | tf_op jit(solution)/shard_map/sum_back_gather/pallas_call | solution.py:108
  482.4 5.8 convolution_convert_fusion.4
  488.2 5.5 convolution_convert_fusion.3.refs_4_
  493.7 2.3 copy.134
  496.0 6.0 reduce-scatter.5.cloned.1.call-done
  502.0 43.1 %attend_back.1 = (bf16[1536,768]{1,0:T(8,128)(2,1)}, f32[1,768]{1,0:T(1,128)}, bf16[4,128,1408]{2,1,0:T(8,128)(2,1)}, bf16[4,128,704]{2,1,0:T(8,128)(2,1)}, bf16[4,192,512]{2,1,0:T(8,128)(2,1)}) custom-call(bf16[1536,256]{1,0:T(8,128)(2,1)} %copy-done.2, bf16[1536,256]{1,0:T(8,128)(2,1)} %copy-done.3, bf16[1536,256]{1,0:T(8,128)(2,1)} %copy-done.4, ...), custom_call_target="tpu_custom_call" | custom-call | bytes 120000000 | tf_op jit(solution)/shard_map/attend_back/pallas_call | solution.py:108
  545.2 9.2 %convolution_convert_fusion.1 = bf16[2048,768]{1,0:T(8,128)(2,1)} fusion(bf16[1536,2048]{1,0:T(8,128)(2,1)} %add_convert_fusion, bf16[1536,768]{1,0:T(8,128)(2,1)} %get-tuple-element.84), kind=kOutput, calls=%fused_computation.9 | convolution fusion | flops 4833411072 | bytes 11796480 | tf_op jit(solution)/shard_map/dot_general | solution.py:26
  559.6 5.6 copy.147
  565.2 42.3 %sum_back.1 = (bf16[192,2048]{1,0:T(8,128)(2,1)}, f32[2,2048]{1,0:T(2,128)}, bf16[4,192,512]{2,1,0:T(8,128)(2,1)}) custom-call(bf16[8,192,768]{2,1,0:T(8,128)(2,1)} %bitcast.154, bf16[2048,768]{1,0:T(8,128)(2,1)} %all-gather.4.cloned.1.call-done.refs_1_, bf16[192,2048]{1,0:T(8,128)(2,1)} %constant_dynamic-slice_fusion.1.refs_2_, ...), custom_call_target="tpu_custom_call" | custom-call | bytes 120000000 | tf_op jit(solution)/shard_map/sum_back/pallas_call | solution.py:108
  607.6 4.1 reduce-scatter.9.cloned.1.call-done
  611.7 47.7 %finish.1 = (bf16[2,192,2048]{2,1,0:T(8,128)(2,1)}, f32[2,4,4,16,128]{4,3,2,1,0:T(8,128)}, bf16[4,128,768]{2,1,0:T(8,128)(2,1)}, bf16[4,128,256]{2,1,0:T(8,128)(2,1)}, bf16[4,192,512]{2,1,0:T(8,128)(2,1)}) custom-call(bf16[192,2048]{1,0:T(8,128)(2,1)} %get-tuple-element.88.refs_0_, f32[2,2048]{1,0:T(2,128)} %get-tuple-element.89.refs_1_, ...), custom_call_target="tpu_custom_call" | custom-call | bytes 120000000 | tf_op jit(solution)/shard_map/finish/pallas_call | solution.py:108
  671.3 3.8 reshape.295
  675.1 2.4 copy.137
  677.6 5.0 reshape.282
  (139 shorter events, 51.9 us)
Async XLA Ops:
  7.2 6.2 copy-start.20
  7.2 145.0 %all-gather.4.cloned.1.call-start = ((), (), s32[]{:S(2)}) async-start(), calls=%async_computation.4 | async-start | bytes 3932160 | tf_op jit(solution)/shard_map/all_gather | solution.py:883
  13.4 4.2 copy-start.23
  13.4 4.2 copy-start.24
  15.6 39.0 %copy-start.19 = (bf16[1,2816,128]{2,1,0:T(8,128)(2,1)S(1)}, bf16[1,2816,128]{2,1,0:T(8,128)(2,1)}, u32[]{:S(2)}) copy-start(bf16[1,2816,128]{2,1,0:T(8,128)(2,1)} %param.24) | copy-start | bytes 2162692
  54.5 232.3 %all-gather.6.cloned.1.call-start = ((), (), s32[]{:S(2)}) async-start(), calls=%async_computation.5 | async-start | bytes 7208960 | tf_op jit(solution)/shard_map/all_gather | solution.py:883
  63.8 70.3 %copy-start.22 = (f32[2,4,4,8,128]{4,3,2,1,0:T(8,128)S(1)}, f32[2,4,4,8,128]{4,3,2,1,0:T(8,128)}, u32[]{:S(2)}) copy-start(f32[2,4,4,8,128]{4,3,2,1,0:T(8,128)} %get-tuple-element.55) | copy-start | bytes 393220
  132.7 192.8 %all-gather.8.cloned.1.call-start = ((), (), s32[]{:S(2)}) async-start(), calls=%async_computation.6 | async-start | bytes 3932160 | tf_op jit(solution)/shard_map/all_gather | solution.py:883
  133.5 360.3 %reduce-scatter.7.cloned.1.call-start = ((), (), s32[]{:S(2)}) async-start(), calls=%async_computation.8 | async-start | bytes 3604480 | tf_op jit(solution)/shard_map/reduce_scatter | solution.py:886
  134.1 4.6 copy-start.11
  140.9 21.1 %copy-start.7 = (s32[1,1536]{1,0:T(1,128)}, s32[1,1536]{1,0:T(1,128)S(1)}, u32[]{:S(2)}) copy-start(s32[1,1536]{1,0:T(1,128)S(1)} %broadcast_in_dim.31.begin_ref.refs_10_) | copy-start | bytes 18436
  152.1 9.9 %copy-start.5 = (f32[256,128]{1,0:T(8,128)S(1)}, f32[256,128]{1,0:T(8,128)}, u32[]{:S(2)}) copy-start(f32[256,128]{1,0:T(8,128)} %constant.86.clone.sin_ref.refs_7_) | copy-start | bytes 393220
  152.1 9.9 %copy-start.6 = (f32[256,128]{1,0:T(8,128)S(1)}, f32[256,128]{1,0:T(8,128)}, u32[]{:S(2)}) copy-start(f32[256,128]{1,0:T(8,128)} %constant.85.clone.cos_ref.refs_6_) | copy-start | bytes 393220
  152.1 9.9 %copy-start.9 = (f32[6,128]{1,0:T(8,128)S(1)}, f32[6,128]{1,0:T(8,128)}, u32[]{:S(2)}) copy-start(f32[6,128]{1,0:T(8,128)} %constant.88.clone.sinf_ref.refs_9_) | copy-start | bytes 9220
  152.1 9.9 %copy-start.10 = (f32[6,128]{1,0:T(8,128)S(1)}, f32[6,128]{1,0:T(8,128)}, u32[]{:S(2)}) copy-start(f32[6,128]{1,0:T(8,128)} %constant.87.clone.cosf_ref.refs_8_) | copy-start | bytes 9220
  182.2 0.9 copy-start
  183.1 0.9 copy-start.2
  184.0 0.9 copy-start.3
  184.9 0.9 copy-start.4
  185.8 0.6 copy-start.8
  301.0 4.4 copy-start.12
  301.0 5.9 copy-start.13
  325.6 176.5 %reduce-scatter.5.cloned.1.call-start = ((), (), s32[]{:S(2)}) async-start(), calls=%async_computation.7 | async-start | bytes 7208960 | tf_op jit(solution)/shard_map/reduce_scatter | solution.py:886
  398.5 2.3 copy-start.14
  398.5 2.3 copy-start.15
  398.6 209.0 %reduce-scatter.11.cloned.1.call-start = ((), (), s32[]{:S(2)}) async-start(), calls=%async_computation.10 | async-start | bytes 1310720 | tf_op jit(solution)/shard_map/reduce_scatter | solution.py:886
  402.0 80.4 %copy-start.1 = (bf16[1536,256]{1,0:T(8,128)(2,1)S(1)}, bf16[1536,256]{1,0:T(8,128)(2,1)}, u32[]{:S(2)}) copy-start(bf16[1536,256]{1,0:T(8,128)(2,1)} %copy-done) | copy-start | bytes 2359300
  482.4 5.8 copy-start.16
  488.2 123.5 %reduce-scatter.9.cloned.1.call-start = ((), (), s32[]{:S(2)}) async-start(), calls=%async_computation.9 | async-start | bytes 3932160 | tf_op jit(solution)/shard_map/reduce_scatter | solution.py:886
  545.2 9.3 %copy-start.18 = (bf16[4,128,704]{2,1,0:T(8,128)(2,1)S(1)}, bf16[4,128,704]{2,1,0:T(8,128)(2,1)}, u32[]{:S(2)}) copy-start(bf16[4,128,704]{2,1,0:T(8,128)(2,1)} %get-tuple-element.100) | copy-start | bytes 2162692
  663.6 4.7 copy-start.21
  665.2 4.2 copy-start.17
Sparse Core Ops, SparseCore 0:
  54.6 82.8 all-gather.3
  139.1 121.6 all-gather.5
  262.3 63.1 all-gather.7
  328.3 56.6 reduce-scatter.6
  398.7 103.3 reduce-scatter.4
  504.8 39.8 reduce-scatter.10
  554.6 57.0 reduce-scatter.8

commit v7 on v6

--- a/solution.py
+++ b/solution.py
@@ -399,34 +399,38 @@
         copy.wait_send()
 
 
-def sum_and_gates(S, C, T, number, act, wd, gb, gu):
-    L, K = act.shape
-    D, n = wd.shape[0], L // (S * T)
-
-    def kernel(ride, ins, outs, scratch):
-        act_ref, wd_ref, gb_ref, gu_ref = ins
-        out_ref, dgu_ref = outs
-        _, _, rows, col = plane(S)
-        greet(S, C, rows + [col], other=True)
-
-        def meanwhile():
-            @pl.loop(0, L // BLK)
-            def _(i):
-                r = pl.ds(pl.multiple_of(i * BLK, BLK), BLK)
-                dact = mm(gb_ref[r, :], wd_ref[...], 1, 0)
-                both = gu_ref[r, :]
-                gate, up = both[:, :K], both[:, K:]
-                s = jax.nn.sigmoid(gate)
-                dgate = dact * up * s * (1.0 + gate * (1.0 - s))
-                dgu_ref[r, :] = jnp.concatenate((dgate, dact * gate * s), axis=1).astype(BF)
-
-        sum_over_plane(S, T, act_ref, wd_ref, out_ref, scratch, meanwhile)
-
-    return comm(
-        kernel, S, C, number, "sum_and_gates", [act.reshape(S * T, n, K), wd, gb, gu], [IN_VMEM] * 4,
-        [(jax.ShapeDtypeStruct((n, D), F32), IN_VMEM), (jax.ShapeDtypeStruct((L, 2 * K), BF), IN_VMEM)],
-        sum_scratch(S, n, D),
-    )
+def gates_kernel(n2_ref, wg_ref, gu_ref, act_ref):
+    both = mm(n2_ref[...], wg_ref[...], 1, 0)
+    gu_ref[...] = both
+    width = act_ref.shape[1]
+    gate, up = both[:, :width], both[:, width:]
+    act_ref[...] = (gate * jax.nn.sigmoid(gate) * up).astype(BF)
+
+
+def gates_back_kernel(gb_ref, wd_ref, gu_ref, dgu_ref):
+    dact = mm(gb_ref[...], wd_ref[...], 1, 0)
+    both, width = gu_ref[...], dact.shape[1]
+    gate, up = both[:, :width], both[:, width:]
+    s = jax.nn.sigmoid(gate)
+    dgate = dact * up * s * (1.0 + gate * (1.0 - s))
+    dgu_ref[...] = jnp.concatenate((dgate, dact * gate * s), axis=1).astype(BF)
+
+
+def by_rows(kernel, name, arrays, outs):
+    L = outs[0].shape[0]
+
+    def spec(width):
+        return pl.BlockSpec((BLK, width), lambda i: (i, 0))
+
+    return pl.pallas_call(
+        kernel,
+        grid=(L // BLK,),
+        in_specs=[spec(x.shape[1]) if rows else pl.BlockSpec(x.shape, lambda i: (0, 0)) for rows, x in arrays],
+        out_specs=[spec(x.shape[1]) for x in outs],
+        out_shape=outs,
+        compiler_params=pltpu.CompilerParams(vmem_limit_bytes=48 << 20),
+        name=name,
+    )(*[x for _, x in arrays])
 
 
 def row_blocks(n, work):
@@ -561,18 +565,19 @@
     )
 
 
-def finish(S, C, T, number, x, stats, bias, riders):
+def finish(S, C, T, number, x, y, stats, bias, riders):
     n, D = x.shape
     wide, lines = D // S, bias.shape[1] // 128
     nb = D // (S * C)
-    count = sum(y.shape[0] for y in stats)
+    count = sum(z.shape[0] for z in stats)
     tall = -(-(count + lines) // 8) * 8
     many = C * S - 1
+    pieces = S if ordered(D, S, C) else 1
 
     def kernel(ride, ins, outs, scratch):
-        x_ref, stat_refs, bias_ref = ins[0], ins[1:-1], ins[-1]
-        out_ref, got = outs
-        buf, buf2, tile, s1, r1, s2, r2, s3, r3, s4, r4, own, tsend, trecv, bsend, brecv = scratch
+        x_ref, y_ref, stat_refs, bias_ref = ins[0], ins[1], ins[2:-1], ins[-1]
+        x_out, y_out, got = outs
+        xbuf, xbuf2, ybuf2, tile, send, recv, own, psend, precv, pown, lsend, lrecv, tsend, trecv = scratch
         p, z, c = here()
         other = {"tp": 1 - c}
         everyone = [(i, j) for i in range(C) for j in range(S) if i or j]
@@ -585,16 +590,42 @@
         def part(q):
             return pl.ds(pl.multiple_of(q * wide, 128), wide)
 
-        def turn_over(source, target, send, recv, local, size, me, axis):
-            hop = [pltpu.make_async_copy(source(me), target, local)]
+        def turn_over(source, target, at, size, me, axis):
+            hop = [pltpu.make_async_copy(source(me), target, own.at[at])]
             for k in range(1, size):
                 q = (me + k) % size
-                hop.append(remote(source(q), target, send.at[k - 1], recv.at[k - 1], {axis: q}))
+                hop.append(remote(source(q), target, send.at[at, k - 1], recv.at[at, k - 1], {axis: q}))
             for copy in hop:
                 copy.start()
             return hop
 
-        hop = turn_over(lambda q: x_ref.at[:, part(q)], buf.at[p], s1, r1, own.at[0], S, p, "shard")
+        def arrive(buf, out, at):
+            hop = []
+            for i in range(pieces):
+                src = pl.ds(i * (wide // pieces), wide // pieces)
+                first = (i * C + p) * nb if pieces > 1 else p * wide
+                dst = out.at[c, :, pl.ds(pl.multiple_of(first, 128), wide // pieces)]
+                hop.append(pltpu.make_async_copy(buf.at[p, :, src], dst, pown.at[at, i]))
+                for k in range(1, S):
+                    q = (p + k) % S
+                    hop.append(
+                        remote(buf.at[q, :, src], dst, psend.at[at, k - 1, i], precv.at[at, k - 1, i], {"shard": q})
+                    )
+            for copy in hop:
+                copy.start()
+            return hop
+
+        def both(ref, at):
+            copy = remote(ref.at[c], ref.at[c], lsend.at[at], lrecv.at[at], other)
+            copy.start()
+            return copy
+
+        def settle(ref, at, copy):
+            copy.wait_send()
+            remote(ref.at[1 - c], ref.at[1 - c], lsend.at[at], lrecv.at[at], other).wait_recv()
+
+        x_hop = turn_over(lambda q: x_ref.at[:, part(q)], xbuf.at[p], 0, S, p, "shard")
+        y_hop = turn_over(lambda q: y_ref.at[q], ybuf2.at[z], 1, C, z, "ctx")
         ride.start()
         tile[...] = jnp.zeros_like(tile)
         at = 0
@@ -615,37 +646,48 @@
             )
         for copy in small:
             copy.start()
-        for copy in hop:
+        for copy in x_hop:
             copy.wait()
-        hop = turn_over(lambda q: buf.at[q], buf2.at[z], s2, r2, own.at[1], C, z, "ctx")
+        x_hop = turn_over(lambda q: xbuf.at[q], xbuf2.at[z], 2, C, z, "ctx")
+        for copy in y_hop:
+            copy.wait()
+        y_hop = arrive(ybuf2, y_out, 0)
         for copy in small:
             copy.wait()
-        back = remote(got.at[c], got.at[c], bsend, brecv, other)
-        back.start()
-        for copy in hop:
+        small_last = both(got, 0)
+        for copy in x_hop:
             copy.wait()
-        for copy in turn_over(lambda q: buf2.at[q], out_ref.at[c, :, part(p)], s3, r3, own.at[2], S, p, "shard"):
+        x_hop = arrive(xbuf2, x_out, 1)
+        for copy in y_hop:
             copy.wait()
-        last = remote(out_ref.at[c], out_ref.at[c], s4, r4, other)
-        last.start()
-        back.wait_send()
-        remote(got.at[1 - c], got.at[1 - c], bsend, brecv, other).wait_recv()
-        last.wait_send()
-        remote(out_ref.at[1 - c], out_ref.at[1 - c], s4, r4, other).wait_recv()
+        y_last = both(y_out, 1)
+        for copy in x_hop:
+            copy.wait()
+        x_last = both(x_out, 2)
+        settle(got, 0, small_last)
+        settle(y_out, 1, y_last)
+        settle(x_out, 2, x_last)
         ride.wait()
 
-    args = [x, *stats, bias]
-    out, got, *rest = comm(
+    args = [x, y, *stats, bias]
+    most = max(S, C) - 1
+    home = (jax.ShapeDtypeStruct((T, n, D), BF), ANY)
+    x, y, got, *rest = comm(
         kernel, S, C, number, "finish", args, [IN_VMEM] * len(args),
-        [(jax.ShapeDtypeStruct((T, n, D), BF), ANY), (jax.ShapeDtypeStruct((T, C, S, tall, 128), F32), ANY)],
+        [home, home, (jax.ShapeDtypeStruct((T, C, S, tall, 128), F32), ANY)],
         [
-            pltpu.VMEM((S, n, wide), BF), pltpu.VMEM((C, n, wide), BF), pltpu.VMEM((tall, D), F32),
-            DMA((S - 1,)), DMA((S - 1,)), DMA((C - 1,)), DMA((C - 1,)), DMA((S - 1,)), DMA((S - 1,)),
-            DMA, DMA, DMA((4,)), DMA((many,)), DMA((many,)), DMA, DMA,
+            pltpu.VMEM((S, n, wide), BF), pltpu.VMEM((C, n, wide), BF), pltpu.VMEM((C, n, wide), BF),
+            pltpu.VMEM((tall, D), F32), DMA((3, most)), DMA((3, most)), DMA((4,)),
+            DMA((2, S - 1, pieces)), DMA((2, S - 1, pieces)), DMA((2, pieces)), DMA((3,)), DMA((3,)),
+            DMA((many,)), DMA((many,)),
         ],
         riders,
     )
-    return [out.reshape(T * n, D), got] + rest
+    return [x.reshape(T * n, D), y.reshape(T * n, D), got] + rest
+
+
+def ordered(D, S, C):
+    return D // (S * C) % 128 == 0
 
 
 def turn_tables(rows):
@@ -819,20 +861,27 @@
                 bias_ref[:, lanes] += jnp.sum(value.astype(F32), axis=0, keepdims=True)
 
 
-def attend_back(S, C, number, q, k, v, o, do, lse, begin, riders):
+def attend_back(S, C, T, number, q, k, v, o, do, lse, begin, act, wd, riders):
     rows, wide = q.shape
+    K, D, n = act.shape[1], wd.shape[0], rows // (S * T)
 
     def kernel(ride, ins, outs, scratch):
-        greet(S, C, axes=ride.axes)
-        ride.start()
-        attend_back_work(ins, outs[0], outs[1], scratch)
+        _, _, row, col = plane(S)
+        greet(S, C, row + [col], other=True, axes=ride.axes)
+
+        def meanwhile():
+            ride.start()
+            attend_back_work(ins[2:], outs[0], outs[1], scratch[:4])
+
+        sum_over_plane(S, T, ins[0], ins[1], outs[2], scratch[4:], meanwhile)
         ride.wait()
 
-    args = [q, k, v, o, do, lse, *turn_tables(rows), begin]
+    args = [act.reshape(S * T, n, K), wd, q, k, v, o, do, lse, *turn_tables(rows), begin]
     return comm(
         kernel, S, C, number, "attend_back", args, [IN_VMEM] * len(args),
-        [(jax.ShapeDtypeStruct((rows, 3 * wide), BF), IN_VMEM), (jax.ShapeDtypeStruct((1, 3 * wide), F32), IN_VMEM)],
-        [pltpu.VMEM((wide, rows), BF)] + [pltpu.VMEM((rows, wide), F32)] * 3,
+        [(jax.ShapeDtypeStruct((rows, 3 * wide), BF), IN_VMEM), (jax.ShapeDtypeStruct((1, 3 * wide), F32), IN_VMEM),
+         (jax.ShapeDtypeStruct((n, D), F32), IN_VMEM)],
+        [pltpu.VMEM((wide, rows), BF)] + [pltpu.VMEM((rows, wide), F32)] * 3 + sum_scratch(S, n, D),
         riders,
     )
 
@@ -934,39 +983,46 @@
         mid, n2, cot = sum_norm_gather(S, C, T, 2, o, wo, own_tok, gains[1:], shifts[1:], [("ctx", cot)])
         cot, n2 = after(cot, n2)
         (gb,) = gather_columns(S, C, T, 4, cot)
-        gu = mm(n2, wg, 1, 0)
-        gate, up = gu[:, :fn], gu[:, fn:]
-        logistic = jax.nn.sigmoid(gate)
-        act = (gate * logistic * up).astype(BF)
+        gu, act = by_rows(
+            gates_kernel, "gates", [(True, n2), (False, wg)],
+            [jax.ShapeDtypeStruct((L, 2 * fn), F32), jax.ShapeDtypeStruct((L, fn), BF)],
+        )
         gw_down = mm(gb, act, 0, 0).astype(BF)
         wd, gw_down = after(wd, gw_down)
         gw_down = sum_ctx(gw_down)
 
-        got, dgu = sum_and_gates(S, C, T, 5, act, wd, gb, gu)
+        (dgu,) = by_rows(
+            gates_back_kernel, "gates_back", [(True, gb), (False, wd), (True, gu)],
+            [jax.ShapeDtypeStruct((L, 2 * fn), BF)],
+        )
         gw_gateup = mm(n2, dgu, 0, 0).astype(BF)
         dgu, gw_gateup = after(dgu, gw_gateup)
         gw_gateup = sum_ctx(gw_gateup)
-        out = parts((mid + got).astype(BF))
-        dmid, gb1, stats2, out = sum_back_gather(
-            S, C, T, 6, dgu, wg, mid, own(gb), gains[1:], [("shard", out)]
-        )
+        dmid, gb1, stats2 = sum_back_gather(S, C, T, 6, dgu, wg, mid, own(gb), gains[1:])
         gw_out = mm(gb1, o, 0, 0).astype(BF)
         gb1, gw_out = after(gb1, gw_out)
         gw_out = sum_ctx(gw_out)
         do = mm(gb1, wo, 1, 0).astype(BF)
-        dqkv, gbias, gw_gateup, gw_down, out = attend_back(
-            S, C, 11, q, k, v, o, do, lse, begin, [("shard", gw_gateup), ("shard", gw_down), ("ctx", out)]
+        dqkv, gbias, got, gw_down = attend_back(
+            S, C, T, 11, q, k, v, o, do, lse, begin, act, wd, [("shard", gw_down)]
         )
+        out = parts((mid + got).astype(BF))
         gw_qkv = mm(n1, dqkv, 0, 0).astype(BF)
         dqkv, gw_qkv = after(dqkv, gw_qkv)
         gw_qkv = sum_ctx(gw_qkv)
-        low, stats1, out = sum_back(S, C, T, 8, dqkv, wq, own_tok, dmid, gains[:1], [("shard", out)])
-        gtok, small, gw_qkv, gw_out, mate = finish(
-            S, C, T, 10, low, [stats1, stats2], gbias, [("shard", gw_qkv), ("shard", gw_out), ("tp", out)]
+        low, stats1, out, gw_gateup = sum_back(
+            S, C, T, 8, dqkv, wq, own_tok, dmid, gains[:1], [("shard", out), ("shard", gw_gateup)]
         )
-        gtok = unpermute(gtok).astype(F32)
-        out = jnp.where(c == 0, jnp.stack((out, mate)), jnp.stack((mate, out)))
-        out = unpermute(out.transpose(0, 2, 1, 3).reshape(R, D))
+        low, gw_gateup, gw_down = lax.optimization_barrier((low, gw_gateup, gw_down))
+        gw_gateup = gw_gateup.astype(F32).reshape(S, nb, 2, fn).transpose(1, 2, 0, 3).reshape(w_gateup.shape)
+        gw_down = gw_down.astype(F32).swapaxes(1, 2).reshape(w_down.shape)
+        low, gw_gateup, gw_down = lax.optimization_barrier((low, gw_gateup, gw_down))
+        gtok, out, small, gw_qkv, gw_out = finish(
+            S, C, T, 10, low, out, [stats1, stats2], gbias, [("shard", gw_qkv), ("shard", gw_out)]
+        )
+        if not ordered(D, S, C):
+            gtok, out = unpermute(gtok), unpermute(out)
+        gtok = gtok.astype(F32)
         norms = lax.dynamic_slice_in_dim(jnp.sum(small[..., :4, :], axis=(0, 1, 2)), (z * S + p) * nb % 128, nb, 1)
         gbias = lax.dynamic_index_in_dim(small, c, 0, keepdims=False)[:, :, 4 : 4 + 3 * hn // 128]
         gbias = jnp.sum(gbias, axis=0).reshape(S, 3, heads, S * C, nf)
@@ -979,8 +1035,8 @@
             gw_qkv.astype(F32).reshape(S, nb, 3, hn).transpose(1, 2, 0, 3).reshape(w_qkv.shape),
             gbias,
             gw_out.astype(F32).swapaxes(1, 2).reshape(w_out.shape),
-            gw_gateup.astype(F32).reshape(S, nb, 2, fn).transpose(1, 2, 0, 3).reshape(w_gateup.shape),
-            gw_down.astype(F32).swapaxes(1, 2).reshape(w_down.shape),
+            gw_gateup,
+            gw_down,
             jnp.stack((norms[0], norms[2]))[None],
             jnp.stack((norms[1], norms[3]))[None],
         )

time: 699 us -> 672 us (0.961)
  local copies, waits for them, and re-layouts: 81.3 us -> 51.3 us
  Pallas kernels: 484 us -> 505 us
  matrix products: 65.6 us -> 51.7 us
    pallas_call x0 -> x2, Pallas kernels: none -> 28.2 us  [by_rows(): pl.pallas_call(kernel, grid=(L // BLK,), in_specs=[spec(x.shape[1]) if ro...]
    dot_general x7 -> x6, matrix products: 65.6 us -> 51.7 us  [mm(): lax.dot_general(a, b, (((ca,), (cb,)), ((), ())), preferred_element_type=...]
    convert_element_type x4 -> x0, local copies, waits for them, and re-layouts: 13.7 us -> none  [the longest x3 11.3 us: body(): gtok = unpermute(gtok).astype(F32)]
    reduce_scatter x4, waiting for transfers between devices: 10.2 us -> 0.01 us  [sum_ctx(): g = lax.psum_scatter(g.astype(BF), 'ctx', scatter_dimension=0, tiled=True)]
    dot_general x1 -> x0, local copies, waits for them, and re-layouts: 9.37 us -> none  [mm(): lax.dot_general(a, b, (((ca,), (cb,)), ((), ())), preferred_element_type=...]
    unnamed x55 -> x61, local copies, waits for them, and re-layouts: 23.7 us -> 17.1 us
    pallas_call x9 -> x8, Pallas kernels: 464 us -> 462 us  [comm(): pl.pallas_call(body, out_shape=[shape for shape, _ in outs] + ride.shapes...]
  transfers between devices with their start and end apart: 7 -> 7, of which waited for: 3 -> 1; matrix products, arithmetic and copies ran while one was open for 18% -> 15% of each run, Pallas kernels for 58% -> 62%
where the time goes in v7:
time: 672 us; the launch traced here: 664 us
  Pallas kernels  505 us (75%)
  matrix products  51.7 us (8%)
  local copies, waits for them, and re-layouts  51.3 us (8%)
  other arithmetic  21.1 us (3%)
  waiting for transfers between devices  19.4 us (3%)
  between operations  15 us (2%)
    pallas_call x8, Pallas kernels, comm(): pl.pallas_call(body, out_shape=[shape for shape, _ in outs] + ride.shapes...  462 us
    dot_general x6, matrix products, mm(): lax.dot_general(a, b, (((ca,), (cb,)), ((), ())), preferred_element_type=...  51.7 us
    pallas_call x2, Pallas kernels, by_rows(): pl.pallas_call(kernel, grid=(L // BLK,), in_specs=[spec(x.shape[1]) if ro...  28.2 us
    all_gather x3, waiting for transfers between devices, over_ctx(): return lax.all_gather(w.reshape(S * nb, -1), 'ctx', axis=0, tiled=True)  18.6 us
    unnamed x61, local copies, waits for them, and re-layouts  17.1 us
    pallas_call x1, Pallas kernels, attend(): pl.pallas_call(attend_kernel, in_specs=[pl.BlockSpec(memory_space=pltpu.S...  15.4 us
  transfers between devices with their start and end apart: 7, of which 1 were waited for; matrix products, arithmetic and copies ran while one was open for 15% of the time, Pallas kernels for 62%

profile of v7, /device:TPU:9, one launch (start us, length us, event | category | flops | bytes accessed | tf_op | source)
XLA Modules:
  0.0 664.1 jit_solution(12492549553654278782)
XLA Ops:
  14.3 36.2 %exchange.1 = (f32[2,4,4,8,128]{4,3,2,1,0:T(8,128)}, bf16[4,192,512]{2,1,0:T(8,128)(2,1)}, bf16[4,192,512]{2,1,0:T(8,128)(2,1)}, bf16[4,128,768]{2,1,0:T(8,128)(2,1)}, bf16[4,128,256]{2,1,0:T(8,128)(2,1)}) custom-call(f32[4,4,8,128]{3,2,1,0:T(8,128)} %broadcast_in_dim.18.refs_0_, bf16[4,192,512]{2,1,0:T(8,128)(2,1)} %reshape.237.refs_1_, ...), custom_call_target="tpu_custom_call" | custom-call | bytes 120000000 | tf_op jit(solution)/shard_map/exchange/pallas_call | solution.py:108
  52.6 3.8 copy.105
  58.1 2.3 copy.107
  60.4 67.9 %gather_columns.2 = (bf16[4,2,192,2048]{3,2,1,0:T(8,128)(2,1)}, bf16[4,512,256]{2,1,0:T(8,128)(2,1)}, bf16[4,128,1408]{2,1,0:T(8,128)(2,1)}, bf16[4,128,704]{2,1,0:T(8,128)(2,1)}, bf16[4,192,512]{2,1,0:T(8,128)(2,1)}) custom-call(bf16[4,192,512]{2,1,0:T(8,128)(2,1)} %get-tuple-element.61.refs_0_, bf16[512,256]{1,0:T(8,128)(2,1)} %bitcast.156, ...), custom_call_target="tpu_custom_call" | custom-call | bytes 120000000 | tf_op jit(solution)/shard_map/gather_columns/pallas_call | solution.py:108
  129.1 3.8 convert_reduce_fusion
  133.7 1.8 fusion.1
  137.3 2.1 constant_dynamic-slice_fusion.1.refs_2_
  139.4 7.9 %add_convert_fusion = bf16[1536,2048]{1,0:T(8,128)(2,1)} fusion(f32[2048]{0:T(1024)S(1)} %get-tuple-element.151, f32[2048]{0:T(1024)S(1)} %get-tuple-element.148, f32[1536]{0:T(1024)S(1)} %rsqrt.12, f32[1536]{0:T(1024)S(1)} %div.25, bf16[4,2,192,2048]{3,2,1,0:T(8,128)(2,1)} %get-tuple-element.63), kind=kLoop, calls=%fused_computation.4 | loop fusion | flops 18874368 | bytes 12611584 | tf_op jit(solution)/shard_map/convert_element_type | solution.py:979
  147.4 10.1 %convolution_add_fusion.qkv_ref = f32[1536,768]{1,0:T(8,128)} fusion(bf16[1536,2048]{1,0:T(8,128)(2,1)} %add_convert_fusion, bf16[2048,768]{1,0:T(8,128)(2,1)} %all-gather.4.cloned.1.call-done.refs_1_, f32[768]{0:T(1024)S(1)} %add.91), kind=kOutput, calls=%fused_computation.6 | convolution fusion | flops 4833017856 | bytes 14158848 | tf_op jit(solution)/shard_map/dot_general | solution.py:26
  157.5 15.4 %attend.1 = (bf16[1536,256]{1,0:T(8,128)(2,1)S(1)}, bf16[1536,256]{1,0:T(8,128)(2,1)S(1)}, bf16[1536,256]{1,0:T(8,128)(2,1)S(1)}, bf16[1536,256]{1,0:T(8,128)(2,1)S(1)}, f32[4,1536]{1,0:T(4,128)S(1)}) custom-call(s32[3]{0:T(128)S(1)} %and_select_fusion.first_ref, f32[1536,768]{1,0:T(8,128)} %convolution_add_fusion.qkv_ref, f32[256,128]{1,0:T(8,128)S(1)} %copy-done.7, ...), custom_call_target="tpu_custom_call" | custom-call | tf_op jit(solution)/shard_map/attend/pallas_call | solution.py:781
  177.1 71.8 %sum_norm_gather.1 = (f32[192,2048]{1,0:T(8,128)}, bf16[8,192,2048]{2,1,0:T(8,128)(2,1)}, bf16[4,192,512]{2,1,0:T(8,128)(2,1)}) custom-call(bf16[8,192,256]{2,1,0:T(8,128)(2,1)} %bitcast.120, bf16[2048,256]{1,0:T(8,128)(2,1)} %bitcast.148, bf16[192,2048]{1,0:T(8,128)(2,1)} %constant_dynamic-slice_fusion.1.refs_2_, f32[1,2048]{1,0:T(1,128)} %bitcast.161, ...), custom_call_target="tpu_custom_call" | custom-call | bytes 120000000 | tf_op jit(solution)/shard_map/sum_norm_gather/pallas_call | solution.py:108
  248.9 32.2 %gather_columns.3 = bf16[4,2,192,2048]{3,2,1,0:T(8,128)(2,1)} custom-call(bf16[4,192,512]{2,1,0:T(8,128)(2,1)} %get-tuple-element.74.refs_0_), custom_call_target="tpu_custom_call" | custom-call | bytes 120000000 | tf_op jit(solution)/shard_map/gather_columns/pallas_call | solution.py:108
  281.1 15.8 %gates.1 = (f32[1536,1408]{1,0:T(8,128)}, bf16[1536,704]{1,0:T(8,128)(2,1)S(1)}) custom-call(bf16[1536,2048]{1,0:T(8,128)(2,1)} %bitcast.129, bf16[2048,1408]{1,0:T(8,128)(2,1)} %all-gather.6.cloned.1.call-done.wg_ref.refs_1_), custom_call_target="tpu_custom_call" | custom-call | tf_op jit(solution)/shard_map/gates/pallas_call | solution.py:425
  297.0 6.0 convolution_convert_fusion.2
  303.0 18.6 %all-gather.8.cloned.1.call-done.wd_ref.refs_1_ = bf16[2048,704]{1,0:T(8,128)(2,1)} async-done(((bf16[512,704]{1,0:T(8,128)(2,1)}), bf16[2048,704]{1,0:T(8,128)(2,1)}) %all-gather.8.cloned.1.call-update) | async-done | bytes 2883600 | tf_op jit(solution)/shard_map/all_gather | solution.py:932
  321.7 1.9 copy-done
  323.6 12.3 %gates_back.1 = bf16[1536,1408]{1,0:T(8,128)(2,1)} custom-call(bf16[1536,2048]{1,0:T(8,128)(2,1)} %bitcast.123, bf16[2048,704]{1,0:T(8,128)(2,1)S(1)} %copy-done, f32[1536,1408]{1,0:T(8,128)} %get-tuple-element.79.gu_ref), custom_call_target="tpu_custom_call" | custom-call | tf_op jit(solution)/shard_map/gates_back/pallas_call | solution.py:425
  335.9 15.0 %convolution_convert_fusion = bf16[2048,1408]{1,0:T(8,128)(2,1)} fusion(bf16[1536,2048]{1,0:T(8,128)(2,1)} %bitcast.130, bf16[1536,1408]{1,0:T(8,128)(2,1)} %gates_back.1), kind=kOutput, calls=%fused_computation.5 | convolution fusion | flops 8861253632 | bytes 16384000 | tf_op jit(solution)/shard_map/dot_general | solution.py:26
  350.9 2.1 constant_dynamic-slice_fusion.refs_3_
  353.0 79.6 %sum_back_gather.1 = (f32[192,2048]{1,0:T(8,128)}, bf16[8,192,2048]{2,1,0:T(8,128)(2,1)}, f32[2,2048]{1,0:T(2,128)}) custom-call(bf16[8,192,1408]{2,1,0:T(8,128)(2,1)} %bitcast.126, bf16[2048,1408]{1,0:T(8,128)(2,1)} %all-gather.6.cloned.1.call-done.wg_ref.refs_1_, f32[192,2048]{1,0:T(8,128)} %get-tuple-element.81.refs_2_, ...), custom_call_target="tpu_custom_call" | custom-call | bytes 120000000 | tf_op jit(solution)/shard_map/sum_back_gather/pallas_call | solution.py:108
  432.6 5.8 convolution_convert_fusion.4
  438.5 5.5 convolution_convert_fusion.3.refs_6_
  444.0 2.3 copy.112
  446.3 56.2 %attend_back.1 = (bf16[1536,768]{1,0:T(8,128)(2,1)}, f32[1,768]{1,0:T(1,128)}, f32[192,2048]{1,0:T(8,128)}, bf16[4,128,704]{2,1,0:T(8,128)(2,1)}) custom-call(bf16[8,192,704]{2,1,0:T(8,128)(2,1)} %bitcast.121, bf16[2048,704]{1,0:T(8,128)(2,1)} %all-gather.8.cloned.1.call-done.wd_ref.refs_1_, bf16[1536,256]{1,0:T(8,128)(2,1)} %copy-done.4, ...), custom_call_target="tpu_custom_call" | custom-call | bytes 120000000 | tf_op jit(solution)/shard_map/attend_back/pallas_call | solution.py:108
  502.5 9.3 %convolution_convert_fusion.1 = bf16[2048,768]{1,0:T(8,128)(2,1)} fusion(bf16[1536,2048]{1,0:T(8,128)(2,1)} %add_convert_fusion, bf16[1536,768]{1,0:T(8,128)(2,1)} %get-tuple-element.87), kind=kOutput, calls=%fused_computation.7 | convolution fusion | flops 4833411072 | bytes 11796480 | tf_op jit(solution)/shard_map/dot_general | solution.py:26
  513.0 59.5 %sum_back.1 = (bf16[192,2048]{1,0:T(8,128)(2,1)}, f32[2,2048]{1,0:T(2,128)}, bf16[4,192,512]{2,1,0:T(8,128)(2,1)}, bf16[4,128,1408]{2,1,0:T(8,128)(2,1)}) custom-call(bf16[8,192,768]{2,1,0:T(8,128)(2,1)} %bitcast.143, bf16[2048,768]{1,0:T(8,128)(2,1)} %all-gather.4.cloned.1.call-done.refs_1_, bf16[192,2048]{1,0:T(8,128)(2,1)} %constant_dynamic-slice_fusion.1.refs_2_, ...), custom_call_target="tpu_custom_call" | custom-call | bytes 120000000 | tf_op jit(solution)/shard_map/sum_back/pallas_call | solution.py:108
  572.5 3.2 copy.114
  575.7 2.1 copy.115
  579.1 3.0 copy.116
  582.1 3.3 copy.122
  585.4 58.5 %finish.1 = (bf16[2,192,2048]{2,1,0:T(8,128)(2,1)}, bf16[2,192,2048]{2,1,0:T(8,128)(2,1)}, f32[2,4,4,16,128]{4,3,2,1,0:T(8,128)}, bf16[4,128,768]{2,1,0:T(8,128)(2,1)}, bf16[4,128,256]{2,1,0:T(8,128)(2,1)}) custom-call(bf16[192,2048]{1,0:T(8,128)(2,1)} %get-tuple-element.97.refs_0_, bf16[4,192,512]{2,1,0:T(8,128)(2,1)} %get-tuple-element.98.refs_1_, ...), custom_call_target="tpu_custom_call" | custom-call | bytes 120000000 | tf_op jit(solution)/shard_map/finish/pallas_call | solution.py:108
  648.9 3.6 bitcast_convert_fusion
  (136 shorter events, 30.4 us)
Async XLA Ops:
  7.2 3.7 copy-start.24
  7.2 3.9 copy-start.27
  7.2 3.9 copy-start.19
  7.2 140.2 %all-gather.4.cloned.1.call-start = ((), (), s32[]{:S(2)}) async-start(), calls=%async_computation.4 | async-start | bytes 3932160 | tf_op jit(solution)/shard_map/all_gather | solution.py:932
  9.4 3.4 copy-start.22
  9.4 4.2 copy-start.25
  9.4 4.2 copy-start.26
  50.5 230.6 %all-gather.6.cloned.1.call-start = ((), (), s32[]{:S(2)}) async-start(), calls=%async_computation.5 | async-start | bytes 7208960 | tf_op jit(solution)/shard_map/all_gather | solution.py:932
  128.3 193.3 %all-gather.8.cloned.1.call-start = ((), (), s32[]{:S(2)}) async-start(), calls=%async_computation.6 | async-start | bytes 3932160 | tf_op jit(solution)/shard_map/all_gather | solution.py:932
  129.0 314.9 %reduce-scatter.5.cloned.1.call-start = ((), (), s32[]{:S(2)}) async-start(), calls=%async_computation.7 | async-start | bytes 3604480 | tf_op jit(solution)/shard_map/reduce_scatter | solution.py:935
  129.1 4.6 copy-start.13
  132.9 2.6 copy-start.23
  136.6 20.8 %copy-start.9 = (s32[1,1536]{1,0:T(1,128)}, s32[1,1536]{1,0:T(1,128)S(1)}, u32[]{:S(2)}) copy-start(s32[1,1536]{1,0:T(1,128)S(1)} %broadcast_in_dim.31.begin_ref.refs_12_) | copy-start | bytes 18436
  147.4 10.1 %copy-start.7 = (f32[256,128]{1,0:T(8,128)S(1)}, f32[256,128]{1,0:T(8,128)}, u32[]{:S(2)}) copy-start(f32[256,128]{1,0:T(8,128)} %constant.83.clone.cos_ref.refs_8_) | copy-start | bytes 393220
  147.4 10.1 %copy-start.8 = (f32[256,128]{1,0:T(8,128)S(1)}, f32[256,128]{1,0:T(8,128)}, u32[]{:S(2)}) copy-start(f32[256,128]{1,0:T(8,128)} %constant.84.clone.sin_ref.refs_9_) | copy-start | bytes 393220
  147.4 10.1 %copy-start.11 = (f32[6,128]{1,0:T(8,128)S(1)}, f32[6,128]{1,0:T(8,128)}, u32[]{:S(2)}) copy-start(f32[6,128]{1,0:T(8,128)} %constant.85.clone.cosf_ref.refs_10_) | copy-start | bytes 9220
  147.4 10.1 %copy-start.12 = (f32[6,128]{1,0:T(8,128)S(1)}, f32[6,128]{1,0:T(8,128)}, u32[]{:S(2)}) copy-start(f32[6,128]{1,0:T(8,128)} %constant.86.clone.sinf_ref.refs_11_) | copy-start | bytes 9220
  174.7 0.9 copy-start.5
  175.6 0.9 copy-start.6
  281.1 15.9 %copy-start.14 = (bf16[4,2,192,2048]{3,2,1,0:T(8,128)(2,1)S(1)}, bf16[4,2,192,2048]{3,2,1,0:T(8,128)(2,1)}, u32[]{:S(2)}) copy-start(bf16[4,2,192,2048]{3,2,1,0:T(8,128)(2,1)} %gather_columns.3) | copy-start | bytes 18874372
  297.0 6.0 copy-start.3
  321.6 191.4 %reduce-scatter.7.cloned.1.call-start = ((), (), s32[]{:S(2)}) async-start(), calls=%async_computation.8 | async-start | bytes 7208960 | tf_op jit(solution)/shard_map/reduce_scatter | solution.py:935
  321.7 1.9 copy-start
  350.9 234.5 %reduce-scatter.11.cloned.1.call-start = ((), (), s32[]{:S(2)}) async-start(), calls=%async_computation.10 | async-start | bytes 1310720 | tf_op jit(solution)/shard_map/reduce_scatter | solution.py:935
  353.0 79.6 %copy-start.2 = (bf16[1536,256]{1,0:T(8,128)(2,1)S(1)}, bf16[1536,256]{1,0:T(8,128)(2,1)}, u32[]{:S(2)}) copy-start(bf16[1536,256]{1,0:T(8,128)(2,1)} %copy-done.1) | copy-start | bytes 2359300
  432.6 5.8 copy-start.18
  438.4 147.0 %reduce-scatter.9.cloned.1.call-start = ((), (), s32[]{:S(2)}) async-start(), calls=%async_computation.9 | async-start | bytes 3932160 | tf_op jit(solution)/shard_map/reduce_scatter | solution.py:935
  502.5 9.4 %copy-start.15 = (f32[192,2048]{1,0:T(8,128)S(1)}, f32[192,2048]{1,0:T(8,128)}, u32[]{:S(2)}) copy-start(f32[192,2048]{1,0:T(8,128)} %get-tuple-element.81.refs_2_) | copy-start | bytes 4718596
  502.5 9.4 %copy-start.17 = (f32[192,2048]{1,0:T(8,128)S(1)}, f32[192,2048]{1,0:T(8,128)}, u32[]{:S(2)}) copy-start(f32[192,2048]{1,0:T(8,128)} %get-tuple-element.89) | copy-start | bytes 4718596
  575.7 2.1 copy-start.20
  647.2 5.2 copy-start.21
  648.9 7.0 %copy-start.16 = (bf16[2,192,2048]{2,1,0:T(8,128)(2,1)S(1)}, bf16[2,192,2048]{2,1,0:T(8,128)(2,1)}, u32[]{:S(2)}) copy-start(bf16[2,192,2048]{2,1,0:T(8,128)(2,1)} %get-tuple-element.104) | copy-start | bytes 4718596
  (3 other events, 2.4 us)
Sparse Core Ops, SparseCore 0:
  50.6 82.8 all-gather.3
  135.1 121.6 all-gather.5
  258.4 63.1 all-gather.7
  324.3 56.6 reduce-scatter.4
  383.2 102.7 reduce-scatter.6
  488.7 25.5 reduce-scatter.10
  517.3 60.4 reduce-scatter.8

commit v8 on v7

--- a/solution.py
+++ b/solution.py
@@ -399,6 +399,58 @@
         copy.wait_send()
 
 
+def project(S, C, T, number, tok, raw, gain, shift, bias):
+    L, D = tok.shape
+    _, parts, nb, wide = raw.shape
+    hn = wide // S
+    most = S - 1
+
+    def kernel(ride, ins, outs, scratch):
+        tok_ref, raw_ref, gain_ref, shift_ref, bias_ref = ins
+        n_ref, out_ref, w_ref = outs
+        send, recv, own = scratch
+        p, _, _ = here()
+        mates = [(p + k) % S for k in range(1, S)]
+        greet(S, C, mates)
+
+        def lanes(q):
+            return pl.ds(pl.multiple_of(q * hn, 128), hn)
+
+        copies = []
+        for part in range(parts):
+            dst = w_ref.at[:, p, :, pl.ds(part * hn, hn)]
+            for k, q in enumerate(mates):
+                copies.append(
+                    remote(raw_ref.at[:, part, :, lanes(q)], dst, send.at[k, part], recv.at[k, part], {"shard": q})
+                )
+            copies.append(pltpu.make_async_copy(raw_ref.at[:, part, :, lanes(p)], dst, own.at[part]))
+        for copy in copies:
+            copy.start()
+
+        def normed(r):
+            n_ref[r, :] = (norm_of(tok_ref[r, :].astype(F32))[0] * gain_ref[...] + shift_ref[...]).astype(BF)
+
+        row_blocks(L, normed)
+        for copy in copies:
+            copy.wait()
+        w = w_ref[...].reshape(D, parts * hn)
+
+        @pl.loop(0, L // BLK)
+        def _(i):
+            r = pl.ds(pl.multiple_of(i * BLK, BLK), BLK)
+            out_ref[r, :] = mm(n_ref[r, :], w, 1, 0) + bias_ref[...]
+
+    n, out, w = comm(
+        kernel, S, C, number, "project", [tok, raw, gain, shift, bias], [IN_VMEM] * 5,
+        [
+            (jax.ShapeDtypeStruct((L, D), BF), IN_VMEM), (jax.ShapeDtypeStruct((L, parts * hn), F32), IN_VMEM),
+            (jax.ShapeDtypeStruct((C, S, nb, parts * hn), BF), IN_VMEM),
+        ],
+        [DMA((most, parts)), DMA((most, parts)), DMA((parts,))],
+    )
+    return n, out, w.reshape(D, parts * hn)
+
+
 def gates_kernel(n2_ref, wg_ref, gu_ref, act_ref):
     both = mm(n2_ref[...], wg_ref[...], 1, 0)
     gu_ref[...] = both
@@ -565,8 +617,9 @@
     )
 
 
-def finish(S, C, T, number, x, y, stats, bias, riders):
+def finish(S, C, T, number, x, y, stats, bias, gateup, down, qkv, out):
     n, D = x.shape
+    fn, hn = down.shape[2], out.shape[2]
     wide, lines = D // S, bias.shape[1] // 128
     nb = D // (S * C)
     count = sum(z.shape[0] for z in stats)
@@ -575,9 +628,11 @@
     pieces = S if ordered(D, S, C) else 1
 
     def kernel(ride, ins, outs, scratch):
-        x_ref, y_ref, stat_refs, bias_ref = ins[0], ins[1], ins[2:-1], ins[-1]
-        x_out, y_out, got = outs
-        xbuf, xbuf2, ybuf2, tile, send, recv, own, psend, precv, pown, lsend, lrecv, tsend, trecv = scratch
+        x_ref, y_ref, stat_refs, bias_ref = ins[0], ins[1], ins[2:-5], ins[-5]
+        gateup_ref, down_ref, qkv_ref, o_ref = ins[-4:]
+        x_out, y_out, got, gateup_out, down_out, qkv_out, o_out = outs
+        xbuf, xbuf2, ybuf2, tile, send, recv, own, psend, precv, pown, lsend, lrecv, tsend, trecv = scratch[:14]
+        qkv_buf, o_buf, gsend, grecv, gown = scratch[14:]
         p, z, c = here()
         other = {"tp": 1 - c}
         everyone = [(i, j) for i in range(C) for j in range(S) if i or j]
@@ -626,7 +681,14 @@
 
         x_hop = turn_over(lambda q: x_ref.at[:, part(q)], xbuf.at[p], 0, S, p, "shard")
         y_hop = turn_over(lambda q: y_ref.at[q], ybuf2.at[z], 1, C, z, "ctx")
-        ride.start()
+        moves = []
+        for i, (src, dst) in enumerate(((qkv_ref, qkv_buf), (o_ref, o_buf))):
+            moves.append(pltpu.make_async_copy(src.at[p], dst.at[p], gown.at[i]))
+            for k in range(1, S):
+                q = (p + k) % S
+                moves.append(remote(src.at[q], dst.at[p], gsend.at[i, k - 1], grecv.at[i, k - 1], {"shard": q}))
+        for copy in moves:
+            copy.start()
         tile[...] = jnp.zeros_like(tile)
         at = 0
         for ref in stat_refs:
@@ -649,12 +711,23 @@
         for copy in x_hop:
             copy.wait()
         x_hop = turn_over(lambda q: xbuf.at[q], xbuf2.at[z], 2, C, z, "ctx")
+        for q in range(S):
+            down_out[q * fn : (q + 1) * fn, :] = down_ref[q].astype(F32).T
         for copy in y_hop:
             copy.wait()
         y_hop = arrive(ybuf2, y_out, 0)
         for copy in small:
             copy.wait()
         small_last = both(got, 0)
+        for i in range(2):
+            for q in range(S):
+                gateup_out[:, i, q * fn : (q + 1) * fn] = gateup_ref[q, :, i * fn : (i + 1) * fn].astype(F32)
+        for copy in moves:
+            copy.wait()
+        for q in range(S):
+            o_out[q * hn : (q + 1) * hn, :] = o_buf[q].astype(F32).T
+            for i in range(3):
+                qkv_out[i, :, q * hn : (q + 1) * hn] = qkv_buf[q, :, i * hn : (i + 1) * hn].astype(F32)
         for copy in x_hop:
             copy.wait()
         x_hop = arrive(xbuf2, x_out, 1)
@@ -667,21 +740,24 @@
         settle(got, 0, small_last)
         settle(y_out, 1, y_last)
         settle(x_out, 2, x_last)
-        ride.wait()
-
-    args = [x, y, *stats, bias]
+
+    args = [x, y, *stats, bias, gateup, down, qkv, out]
     most = max(S, C) - 1
     home = (jax.ShapeDtypeStruct((T, n, D), BF), ANY)
     x, y, got, *rest = comm(
         kernel, S, C, number, "finish", args, [IN_VMEM] * len(args),
-        [home, home, (jax.ShapeDtypeStruct((T, C, S, tall, 128), F32), ANY)],
+        [home, home, (jax.ShapeDtypeStruct((T, C, S, tall, 128), F32), ANY)]
+        + [
+            (jax.ShapeDtypeStruct(shape, F32), IN_VMEM)
+            for shape in ((nb, 2, S * fn), (S * fn, nb), (3, nb, S * hn), (S * hn, nb))
+        ],
         [
             pltpu.VMEM((S, n, wide), BF), pltpu.VMEM((C, n, wide), BF), pltpu.VMEM((C, n, wide), BF),
             pltpu.VMEM((tall, D), F32), DMA((3, most)), DMA((3, most)), DMA((4,)),
             DMA((2, S - 1, pieces)), DMA((2, S - 1, pieces)), DMA((2, pieces)), DMA((3,)), DMA((3,)),
             DMA((many,)), DMA((many,)),
+            pltpu.VMEM(qkv.shape, BF), pltpu.VMEM(out.shape, BF), DMA((2, S - 1)), DMA((2, S - 1)), DMA((2,)),
         ],
-        riders,
     )
     return [x.reshape(T * n, D), y.reshape(T * n, D), got] + rest
 
@@ -941,25 +1017,19 @@
         nf = HEAD // (S * C)
 
         tile = tiles_of((norm_gain[0].reshape(-1), norm_bias[0].reshape(-1), b_qkv[0].reshape(-1), lengths[0]), ())
-        small, _, tok, wq, wo = exchange(
+        raw = lax.all_gather(w_qkv[0].swapaxes(0, 1).reshape(3 * nb, -1), "ctx", axis=0, tiled=True)
+        small, _, tok, wo, wg, wd, cot = exchange(
             S, C, T, 0,
             [
-                ("shard", w_qkv[0].reshape(nb, 3, S, hn).transpose(2, 0, 1, 3).reshape(S, nb, 3 * hn)),
                 ("shard", w_out[0].reshape(S, hn, nb).swapaxes(1, 2)),
+                ("shard", w_gateup[0].reshape(nb, 2, S, fn).transpose(2, 0, 1, 3).reshape(S, nb, 2 * fn)),
+                ("shard", w_down[0].reshape(S, fn, nb).swapaxes(1, 2)),
+                ("shard", to_parts(half_of(cotangent))),
             ],
             jnp.broadcast_to(tile, (C, S, 8, 128)),
             to_parts(half_of(tokens)),
         )
-        wq = over_ctx(wq)
-        tok, wo, wg, wd, cot = gather_columns(
-            S, C, T, 1, tok,
-            [
-                ("all", wo.reshape(S * nb, hn)),
-                ("shard", w_gateup[0].reshape(nb, 2, S, fn).transpose(2, 0, 1, 3).reshape(S, nb, 2 * fn)),
-                ("shard", w_down[0].reshape(S, fn, nb).swapaxes(1, 2)),
-                ("shard", to_parts(half_of(cotangent))),
-            ],
-        )
+        tok, wo = gather_columns(S, C, T, 1, tok, [("all", wo.reshape(S * nb, hn))])
         wo, wg, wd = wo.reshape(D, hn), over_ctx(wg), over_ctx(wd)
 
         small = lax.dynamic_index_in_dim(small, c, 0, keepdims=False).reshape(C, S, 1024)
@@ -976,9 +1046,8 @@
         begin = doc_begins(lengths_row, L)
         begin = begin[None, :]
 
-        n1 = (norm_of(tok.astype(F32))[0] * gains[0] + shifts[0]).astype(BF)
+        n1, qkv, wq = project(S, C, T, 12, tok, raw.reshape(C, 3, nb, -1), gains[:1], shifts[:1], bias)
         own_tok = own(tok)
-        qkv = mm(n1, wq, 1, 0) + bias
         q, k, v, o, lse = attend(qkv, begin)
         mid, n2, cot = sum_norm_gather(S, C, T, 2, o, wo, own_tok, gains[1:], shifts[1:], [("ctx", cot)])
         cot, n2 = after(cot, n2)
@@ -1013,12 +1082,8 @@
         low, stats1, out, gw_gateup = sum_back(
             S, C, T, 8, dqkv, wq, own_tok, dmid, gains[:1], [("shard", out), ("shard", gw_gateup)]
         )
-        low, gw_gateup, gw_down = lax.optimization_barrier((low, gw_gateup, gw_down))
-        gw_gateup = gw_gateup.astype(F32).reshape(S, nb, 2, fn).transpose(1, 2, 0, 3).reshape(w_gateup.shape)
-        gw_down = gw_down.astype(F32).swapaxes(1, 2).reshape(w_down.shape)
-        low, gw_gateup, gw_down = lax.optimization_barrier((low, gw_gateup, gw_down))
-        gtok, out, small, gw_qkv, gw_out = finish(
-            S, C, T, 10, low, out, [stats1, stats2], gbias, [("shard", gw_qkv), ("shard", gw_out)]
+        gtok, out, small, gw_gateup, gw_down, gw_qkv, gw_out = finish(
+            S, C, T, 10, low, out, [stats1, stats2], gbias, gw_gateup, gw_down, gw_qkv, gw_out
         )
         if not ordered(D, S, C):
             gtok, out = unpermute(gtok), unpermute(out)
@@ -1032,11 +1097,11 @@
         return (
             out,
             gtok,
-            gw_qkv.astype(F32).reshape(S, nb, 3, hn).transpose(1, 2, 0, 3).reshape(w_qkv.shape),
+            gw_qkv.swapaxes(0, 1).reshape(w_qkv.shape),
             gbias,
-            gw_out.astype(F32).swapaxes(1, 2).reshape(w_out.shape),
-            gw_gateup,
-            gw_down,
+            gw_out.reshape(w_out.shape),
+            gw_gateup.reshape(w_gateup.shape),
+            gw_down.reshape(w_down.shape),
             jnp.stack((norms[0], norms[2]))[None],
             jnp.stack((norms[1], norms[3]))[None],
         )

time: 672 us -> 662 us (0.985)
  Pallas kernels: 505 us -> 547 us
  waiting for transfers between devices: 19.4 us -> 1.51 us
  other arithmetic: 21.1 us -> 7.69 us
  matrix products: 51.7 us -> 41.7 us
  local copies, waits for them, and re-layouts: 51.3 us -> 43.7 us
    pallas_call x8 -> x9, Pallas kernels: 462 us -> 499 us  [comm(): pl.pallas_call(body, out_shape=[shape for shape, _ in outs] + ride.shapes...]
    all_gather x3 -> x2, waiting for transfers between devices: 18.6 us -> 0.02 us  [over_ctx(): return lax.all_gather(w.reshape(S * nb, -1), 'ctx', axis=0, tiled=True)]
    reshape x7 -> x1, local copies, waits for them, and re-layouts: 11.9 us -> 0.72 us  [body(): bias = bias.transpose(2, 3, 1, 0, 4).reshape(1, 3 * hn)]
    dot_general x6 -> x5, matrix products: 51.7 us -> 41.7 us  [mm(): lax.dot_general(a, b, (((ca,), (cb,)), ((), ())), preferred_element_type=...]
    convert_element_type x1 -> x0, other arithmetic: 7.92 us -> none  [body(): n1 = (norm_of(tok.astype(F32))[0] * gains[0] + shifts[0]).astype(BF)]
    unnamed x61 -> x60, local copies, waits for them, and re-layouts: 17.1 us -> 18.4 us
  transfers between devices with their start and end apart: 7 -> 7, of which waited for: 1 -> 0; matrix products, arithmetic and copies ran while one was open for 15% -> 10% of each run, Pallas kernels for 62% -> 74%
where the time goes in v8:
time: 662 us; the launch traced here: 657 us
  Pallas kernels  547 us (83%)
  local copies, waits for them, and re-layouts  43.7 us (7%)
  matrix products  41.7 us (6%)
  between operations  14.8 us (2%)
  other arithmetic  7.69 us (1%)
    pallas_call x9, Pallas kernels, comm(): pl.pallas_call(body, out_shape=[shape for shape, _ in outs] + ride.shapes...  499 us
    dot_general x5, matrix products, mm(): lax.dot_general(a, b, (((ca,), (cb,)), ((), ())), preferred_element_type=...  41.7 us
    pallas_call x2, Pallas kernels, by_rows(): pl.pallas_call(kernel, grid=(L // BLK,), in_specs=[spec(x.shape[1]) if ro...  28 us
    pallas_call x1, Pallas kernels, attend(): pl.pallas_call(attend_kernel, in_specs=[pl.BlockSpec(memory_space=pltpu.S...  20.2 us
    unnamed x60, local copies, waits for them, and re-layouts  18.4 us
  transfers between devices with their start and end apart: 7, of which 0 were waited for; matrix products, arithmetic and copies ran while one was open for 10% of the time, Pallas kernels for 74%

profile of v8, /device:TPU:9, one launch (start us, length us, event | category | flops | bytes accessed | tf_op | source)
XLA Modules:
  0.0 657.4 jit_solution(4347175332841621672)
XLA Ops:
  8.0 1.5 constant_dynamic-slice_fusion.5
  10.3 1.2 reshape.187.refs_1_
  12.4 1.2 reshape.190.refs_5_
  13.8 3.8 copy.71
  17.7 1.5 copy.75.refs_3_
  19.3 2.3 copy.73
  23.2 58.1 %exchange.1 = (f32[2,4,4,8,128]{4,3,2,1,0:T(8,128)}, bf16[4,192,512]{2,1,0:T(8,128)(2,1)}, bf16[4,192,512]{2,1,0:T(8,128)(2,1)}, bf16[4,128,256]{2,1,0:T(8,128)(...) custom-call(f32[4,4,8,128]{3,2,1,0:T(8,128)} %broadcast_in_dim.27.refs_0_, ...), custom_call_target="tpu_custom_call" | custom-call | bytes 120000000 | tf_op jit(solution)/shard_map/exchange/pallas_call | solution.py:108
  84.7 35.0 %gather_columns.2 = (bf16[4,2,192,2048]{3,2,1,0:T(8,128)(2,1)}, bf16[4,512,256]{2,1,0:T(8,128)(2,1)}) custom-call(bf16[4,192,512]{2,1,0:T(8,128)(2,1)} %get-tuple-element.59.refs_0_, bf16[512,256]{1,0:T(8,128)(2,1)} %bitcast.145), custom_call_target="tpu_custom_call" | custom-call | bytes 120000000 | tf_op jit(solution)/shard_map/gather_columns/pallas_call | solution.py:108
  120.4 2.1 constant_dynamic-slice_fusion.1.refs_2_
  122.5 50.6 %project.1 = (bf16[1536,2048]{1,0:T(8,128)(2,1)}, f32[1536,768]{1,0:T(8,128)}, bf16[4,4,128,768]{3,2,1,0:T(8,128)(2,1)}) custom-call(bf16[1536,2048]{1,0:T(8,128)(2,1)} %bitcast.115, bf16[4,3,128,1024]{3,2,1,0:T(8,128)(2,1)} %bitcast.123, f32[1,2048]{1,0:T(1,128)} %bitcast.150, f32[1,2048]{1,0:T(1,128)} %bitcast.153, f32[1,768]{1,0:T(1,128)} %reshape.199.refs_4_), custom_call_target="tpu_custom_call" | custom-call | bytes 120000000 | tf_op jit(solution)/shard_map/project/pallas_call | solution.py:108
  173.2 20.2 %attend.1 = (bf16[1536,256]{1,0:T(8,128)(2,1)S(1)}, bf16[1536,256]{1,0:T(8,128)(2,1)S(1)}, bf16[1536,256]{1,0:T(8,128)(2,1)S(1)}, bf16[1536,256]{1,0:T(8,128)(2,1)S(1)}, f32[4,1536]{1,0:T(4,128)S(1)}) custom-call(s32[3]{0:T(128)S(1)} %and_select_fusion.first_ref, f32[1536,768]{1,0:T(8,128)} %get-tuple-element.62.qkv_ref, f32[256,128]{1,0:T(8,128)S(1)} %copy-done.7, ...), custom_call_target="tpu_custom_call" | custom-call | tf_op jit(solution)/shard_map/attend/pallas_call | solution.py:857
  197.6 67.3 %sum_norm_gather.1 = (f32[192,2048]{1,0:T(8,128)}, bf16[8,192,2048]{2,1,0:T(8,128)(2,1)}, bf16[4,192,512]{2,1,0:T(8,128)(2,1)}) custom-call(bf16[8,192,256]{2,1,0:T(8,128)(2,1)} %bitcast.108, bf16[2048,256]{1,0:T(8,128)(2,1)} %bitcast.136, bf16[192,2048]{1,0:T(8,128)(2,1)} %constant_dynamic-slice_fusion.1.refs_2_, f32[1,2048]{1,0:T(1,128)} %bitcast.148, ...), custom_call_target="tpu_custom_call" | custom-call | bytes 120000000 | tf_op jit(solution)/shard_map/sum_norm_gather/pallas_call | solution.py:108
  264.9 32.1 %gather_columns.3 = bf16[4,2,192,2048]{3,2,1,0:T(8,128)(2,1)} custom-call(bf16[4,192,512]{2,1,0:T(8,128)(2,1)} %get-tuple-element.72.refs_0_), custom_call_target="tpu_custom_call" | custom-call | bytes 120000000 | tf_op jit(solution)/shard_map/gather_columns/pallas_call | solution.py:108
  297.1 15.8 %gates.1 = (f32[1536,1408]{1,0:T(8,128)}, bf16[1536,704]{1,0:T(8,128)(2,1)S(1)}) custom-call(bf16[1536,2048]{1,0:T(8,128)(2,1)} %bitcast.116, bf16[2048,1408]{1,0:T(8,128)(2,1)} %all-gather.6.cloned.1.call-done.wg_ref.refs_1_), custom_call_target="tpu_custom_call" | custom-call | tf_op jit(solution)/shard_map/gates/pallas_call | solution.py:477
  312.9 6.0 convolution_convert_fusion.2
  319.4 1.9 copy-done
  321.3 12.2 %gates_back.1 = bf16[1536,1408]{1,0:T(8,128)(2,1)} custom-call(bf16[1536,2048]{1,0:T(8,128)(2,1)} %bitcast.110, bf16[2048,704]{1,0:T(8,128)(2,1)S(1)} %copy-done, f32[1536,1408]{1,0:T(8,128)} %get-tuple-element.77.gu_ref), custom_call_target="tpu_custom_call" | custom-call | tf_op jit(solution)/shard_map/gates_back/pallas_call | solution.py:477
  333.5 15.1 %convolution_convert_fusion = bf16[2048,1408]{1,0:T(8,128)(2,1)} fusion(bf16[1536,2048]{1,0:T(8,128)(2,1)} %bitcast.117, bf16[1536,1408]{1,0:T(8,128)(2,1)} %gates_back.1), kind=kOutput, calls=%fused_computation | convolution fusion | flops 8861253632 | bytes 16384000 | tf_op jit(solution)/shard_map/dot_general | solution.py:26
  348.6 2.1 constant_dynamic-slice_fusion.refs_3_
  350.7 79.3 %sum_back_gather.1 = (f32[192,2048]{1,0:T(8,128)}, bf16[8,192,2048]{2,1,0:T(8,128)(2,1)}, f32[2,2048]{1,0:T(2,128)}) custom-call(bf16[8,192,1408]{2,1,0:T(8,128)(2,1)} %bitcast.113, bf16[2048,1408]{1,0:T(8,128)(2,1)} %all-gather.6.cloned.1.call-done.wg_ref.refs_1_, f32[192,2048]{1,0:T(8,128)} %get-tuple-element.79.refs_2_, ...), custom_call_target="tpu_custom_call" | custom-call | bytes 120000000 | tf_op jit(solution)/shard_map/sum_back_gather/pallas_call | solution.py:108
  430.1 5.8 convolution_convert_fusion.4
  435.9 5.6 convolution_convert_fusion.3.refs_6_
  441.6 2.3 copy.78
  443.8 56.1 %attend_back.1 = (bf16[1536,768]{1,0:T(8,128)(2,1)}, f32[1,768]{1,0:T(1,128)}, f32[192,2048]{1,0:T(8,128)}, bf16[4,128,704]{2,1,0:T(8,128)(2,1)}) custom-call(bf16[8,192,704]{2,1,0:T(8,128)(2,1)} %bitcast.109, bf16[2048,704]{1,0:T(8,128)(2,1)} %all-gather.8.cloned.1.call-done.wd_ref.refs_1_, bf16[1536,256]{1,0:T(8,128)(2,1)} %copy-done.4, ...), custom_call_target="tpu_custom_call" | custom-call | bytes 120000000 | tf_op jit(solution)/shard_map/attend_back/pallas_call | solution.py:108
  499.9 9.2 %convolution_convert_fusion.1 = bf16[2048,768]{1,0:T(8,128)(2,1)} fusion(bf16[1536,2048]{1,0:T(8,128)(2,1)} %get-tuple-element.85, bf16[1536,768]{1,0:T(8,128)(2,1)} %get-tuple-element.86), kind=kOutput, calls=%fused_computation.1 | convolution fusion | flops 4833411072 | bytes 11796480 | tf_op jit(solution)/shard_map/dot_general | solution.py:26
  509.2 1.4 copy-done.14
  512.1 60.1 %sum_back.1 = (bf16[192,2048]{1,0:T(8,128)(2,1)}, f32[2,2048]{1,0:T(2,128)}, bf16[4,192,512]{2,1,0:T(8,128)(2,1)}, bf16[4,128,1408]{2,1,0:T(8,128)(2,1)}) custom-call(bf16[8,192,768]{2,1,0:T(8,128)(2,1)} %bitcast.129, bf16[2048,768]{1,0:T(8,128)(2,1)} %bitcast.124, bf16[192,2048]{1,0:T(8,128)(2,1)} %constant_dynamic-slice_fusion.1.refs_2_, ...), custom_call_target="tpu_custom_call" | custom-call | bytes 120000000 | tf_op jit(solution)/shard_map/sum_back/pallas_call | solution.py:108
  572.3 60.2 %finish.1 = (bf16[2,192,2048]{2,1,0:T(8,128)(2,1)}, bf16[2,192,2048]{2,1,0:T(8,128)(2,1)}, f32[2,4,4,16,128]{4,3,2,1,0:T(8,128)}, f32[128,2,2816]{2,1,0:T(2,128)...) custom-call(bf16[192,2048]{1,0:T(8,128)(2,1)} %get-tuple-element.91.refs_0_, ...), custom_call_target="tpu_custom_call" | custom-call | bytes 120000000 | tf_op jit(solution)/shard_map/finish/pallas_call | solution.py:108
  635.0 3.6 bitcast_convert_fusion
  641.2 1.2 maximum_bitcast_fusion.1
  642.4 1.2 maximum_bitcast_fusion
  646.8 1.6 copy.94
  (118 shorter events, 25.0 us)
Async XLA Ops:
  7.2 115.3 %all-gather.4.cloned.1.call-start = ((), (), s32[]{:S(2)}) async-start(), calls=%async_computation.4 | async-start | bytes 3932160 | tf_op jit(solution)/shard_map/all_gather | solution.py:1020
  7.9 289.2 %all-gather.6.cloned.1.call-start = ((), (), s32[]{:S(2)}) async-start(), calls=%async_computation.5 | async-start | bytes 7208960 | tf_op jit(solution)/shard_map/all_gather | solution.py:1008
  10.3 3.2 copy-start.23
  17.6 4.0 copy-start.22
  17.7 4.7 copy-start.26
  17.7 4.7 copy-start.24
  17.7 4.7 copy-start.25
  81.3 237.6 %all-gather.8.cloned.1.call-start = ((), (), s32[]{:S(2)}) async-start(), calls=%async_computation.6 | async-start | bytes 3932160 | tf_op jit(solution)/shard_map/all_gather | solution.py:1008
  82.1 359.5 %reduce-scatter.5.cloned.1.call-start = ((), (), s32[]{:S(2)}) async-start(), calls=%async_computation.7 | async-start | bytes 3604480 | tf_op jit(solution)/shard_map/reduce_scatter | solution.py:1011
  84.6 88.5 %copy-start.9 = (s32[1,1536]{1,0:T(1,128)}, s32[1,1536]{1,0:T(1,128)S(1)}, u32[]{:S(2)}) copy-start(s32[1,1536]{1,0:T(1,128)S(1)} %broadcast_in_dim.29.begin_ref.refs_12_) | copy-start | bytes 18436
  122.5 50.7 %copy-start.7 = (f32[256,128]{1,0:T(8,128)S(1)}, f32[256,128]{1,0:T(8,128)}, u32[]{:S(2)}) copy-start(f32[256,128]{1,0:T(8,128)} %constant.77.clone.cos_ref.refs_8_) | copy-start | bytes 393220
  122.5 50.7 %copy-start.8 = (f32[256,128]{1,0:T(8,128)S(1)}, f32[256,128]{1,0:T(8,128)}, u32[]{:S(2)}) copy-start(f32[256,128]{1,0:T(8,128)} %constant.78.clone.sin_ref.refs_9_) | copy-start | bytes 393220
  122.5 50.7 %copy-start.11 = (f32[6,128]{1,0:T(8,128)S(1)}, f32[6,128]{1,0:T(8,128)}, u32[]{:S(2)}) copy-start(f32[6,128]{1,0:T(8,128)} %constant.79.clone.cosf_ref.refs_10_) | copy-start | bytes 9220
  122.5 50.7 %copy-start.12 = (f32[6,128]{1,0:T(8,128)S(1)}, f32[6,128]{1,0:T(8,128)}, u32[]{:S(2)}) copy-start(f32[6,128]{1,0:T(8,128)} %constant.80.clone.sinf_ref.refs_11_) | copy-start | bytes 9220
  193.4 0.9 copy-start.1
  195.2 0.9 copy-start.5
  196.1 0.9 copy-start.6
  297.1 15.8 %copy-start.13 = (bf16[4,2,192,2048]{3,2,1,0:T(8,128)(2,1)S(1)}, bf16[4,2,192,2048]{3,2,1,0:T(8,128)(2,1)}, u32[]{:S(2)}) copy-start(bf16[4,2,192,2048]{3,2,1,0:T(8,128)(2,1)} %gather_columns.3) | copy-start | bytes 18874372
  312.9 6.0 copy-start.3
  319.0 193.2 %reduce-scatter.7.cloned.1.call-start = ((), (), s32[]{:S(2)}) async-start(), calls=%async_computation.8 | async-start | bytes 7208960 | tf_op jit(solution)/shard_map/reduce_scatter | solution.py:1011
  319.4 1.9 copy-start
  348.6 223.7 %reduce-scatter.11.cloned.1.call-start = ((), (), s32[]{:S(2)}) async-start(), calls=%async_computation.10 | async-start | bytes 1310720 | tf_op jit(solution)/shard_map/reduce_scatter | solution.py:1011
  350.7 79.3 %copy-start.2 = (bf16[1536,256]{1,0:T(8,128)(2,1)S(1)}, bf16[1536,256]{1,0:T(8,128)(2,1)}, u32[]{:S(2)}) copy-start(bf16[1536,256]{1,0:T(8,128)(2,1)} %copy-done.1) | copy-start | bytes 2359300
  430.1 5.8 copy-start.20
  435.9 136.4 %reduce-scatter.9.cloned.1.call-start = ((), (), s32[]{:S(2)}) async-start(), calls=%async_computation.9 | async-start | bytes 3932160 | tf_op jit(solution)/shard_map/reduce_scatter | solution.py:1011
  509.1 1.4 copy-start.14
  509.1 1.9 copy-start.18
  632.5 11.2 %copy-start.17 = (bf16[2,192,2048]{2,1,0:T(8,128)(2,1)S(1)}, bf16[2,192,2048]{2,1,0:T(8,128)(2,1)}, u32[]{:S(2)}) copy-start(bf16[2,192,2048]{2,1,0:T(8,128)(2,1)} %get-tuple-element.100) | copy-start | bytes 4718596
  635.0 9.8 %copy-start.16 = (f32[3,128,1024]{2,1,0:T(8,128)S(1)}, f32[3,128,1024]{2,1,0:T(8,128)}, u32[]{:S(2)}) copy-start(f32[3,128,1024]{2,1,0:T(8,128)} %get-tuple-element.102) | copy-start | bytes 4718596
  643.7 2.3 copy-start.21
  643.7 3.1 copy-start.15
  646.8 2.4 copy-start.19
  (2 other events, 1.5 us)
Sparse Core Ops, SparseCore 0:
  9.6 79.0 all-gather.3
  90.2 125.6 all-gather.5
  217.6 69.2 all-gather.7
  319.1 54.9 reduce-scatter.4
  376.3 102.7 reduce-scatter.6
  481.8 25.5 reduce-scatter.10
  510.4 60.4 reduce-scatter.8

commit v9 on v8

--- a/solution.py
+++ b/solution.py
@@ -189,7 +189,7 @@
     return [DMA((2 * count,)), DMA((2 * count,))]
 
 
-def spread(S, own, region, send, recv):
+def spread(S, own, region, send, recv, work=(None, None)):
     p, _, c = here()
     B = S // 2
     a, b, rows, col = plane(S)
@@ -228,12 +228,16 @@
         push(q, h, per + COL + h, other)
         return q
 
+    if work[0] is not None:
+        work[0]()
     for j in range(1, B):
         q = from_row(j, 0)
         push(q, 0, VIA_COL + j - 1, col)
     q = from_col(1)
     for j in range(1, B):
         push(q, 1, VIA_ROW + j - 1, rows[j - 1])
+    if work[1] is not None:
+        work[1]()
     for j in range(1, B):
         from_row(j, 1)
     from_col(0)
@@ -256,11 +260,13 @@
         copy.wait_send()
 
 
-def gather_columns(S, C, T, number, x, riders=()):
+def gather_columns(S, C, T, number, x, riders=(), extra=None):
     _, n, wide = x.shape
+    more, more_specs, more_outs, more_scratch, task = extra or ((), (), (), (), None)
 
     def kernel(ride, ins, outs, scratch):
-        (x_ref,), (out_ref,), (send, recv, own) = ins, outs, scratch
+        x_ref, out_ref = ins[0], outs[0]
+        send, recv, own = scratch[:3]
         p, _, c = here()
         _, _, rows, col = plane(S)
 
@@ -275,14 +281,18 @@
             copy.start()
         greet(S, C, rows + [col], other=True, axes=ride.axes)
         ride.start()
-        spread(S, lambda h: x_ref.at[pl.ds(h * (C // 2), C // 2)], region, send, recv)
+        work = [None, None]
+        if task is not None:
+            work = [functools.partial(task, ins[1:], outs[1:], scratch[3:], piece) for piece in range(2)]
+        spread(S, lambda h: x_ref.at[pl.ds(h * (C // 2), C // 2)], region, send, recv, work)
         for copy in local:
             copy.wait()
         ride.wait()
 
     out, *rest = comm(
-        kernel, S, C, number, "gather_columns", [x], [IN_VMEM],
-        [(jax.ShapeDtypeStruct((C, T, n, wide * S), x.dtype), ANY)], spread_sems(S) + [DMA((2,))], riders,
+        kernel, S, C, number, "gather_columns", [x, *more], [IN_VMEM, *more_specs],
+        [(jax.ShapeDtypeStruct((C, T, n, wide * S), x.dtype), ANY), *more_outs],
+        spread_sems(S) + [DMA((2,)), *more_scratch], riders,
     )
     return [out.reshape(C * T * n, wide * S)] + rest
 
@@ -399,7 +409,7 @@
         copy.wait_send()
 
 
-def project(S, C, T, number, tok, raw, gain, shift, bias):
+def project(S, C, T, number, tok, raw, gain, shift, bias, riders):
     L, D = tok.shape
     _, parts, nb, wide = raw.shape
     hn = wide // S
@@ -411,7 +421,7 @@
         send, recv, own = scratch
         p, _, _ = here()
         mates = [(p + k) % S for k in range(1, S)]
-        greet(S, C, mates)
+        greet(S, C, mates, axes=ride.axes)
 
         def lanes(q):
             return pl.ds(pl.multiple_of(q * hn, 128), hn)
@@ -426,6 +436,7 @@
             copies.append(pltpu.make_async_copy(raw_ref.at[:, part, :, lanes(p)], dst, own.at[part]))
         for copy in copies:
             copy.start()
+        ride.start()
 
         def normed(r):
             n_ref[r, :] = (norm_of(tok_ref[r, :].astype(F32))[0] * gain_ref[...] + shift_ref[...]).astype(BF)
@@ -440,15 +451,18 @@
             r = pl.ds(pl.multiple_of(i * BLK, BLK), BLK)
             out_ref[r, :] = mm(n_ref[r, :], w, 1, 0) + bias_ref[...]
 
-    n, out, w = comm(
+        ride.wait()
+
+    n, out, w, *rest = comm(
         kernel, S, C, number, "project", [tok, raw, gain, shift, bias], [IN_VMEM] * 5,
         [
             (jax.ShapeDtypeStruct((L, D), BF), IN_VMEM), (jax.ShapeDtypeStruct((L, parts * hn), F32), IN_VMEM),
             (jax.ShapeDtypeStruct((C, S, nb, parts * hn), BF), IN_VMEM),
         ],
         [DMA((most, parts)), DMA((most, parts)), DMA((parts,))],
-    )
-    return n, out, w.reshape(D, parts * hn)
+        riders,
+    )
+    return [n, out, w.reshape(D, parts * hn)] + rest
 
 
 def gates_kernel(n2_ref, wg_ref, gu_ref, act_ref):
@@ -470,17 +484,18 @@
 
 def by_rows(kernel, name, arrays, outs):
     L = outs[0].shape[0]
+    size = L // 2
 
     def spec(width):
-        return pl.BlockSpec((BLK, width), lambda i: (i, 0))
+        return pl.BlockSpec((size, width), lambda i: (i, 0))
 
     return pl.pallas_call(
         kernel,
-        grid=(L // BLK,),
+        grid=(L // size,),
         in_specs=[spec(x.shape[1]) if rows else pl.BlockSpec(x.shape, lambda i: (0, 0)) for rows, x in arrays],
         out_specs=[spec(x.shape[1]) for x in outs],
         out_shape=outs,
-        compiler_params=pltpu.CompilerParams(vmem_limit_bytes=48 << 20),
+        compiler_params=pltpu.CompilerParams(vmem_limit_bytes=60 << 20),
         name=name,
     )(*[x for _, x in arrays])
 
@@ -489,6 +504,13 @@
     @pl.loop(0, n // ROWS)
     def _(i):
         work(pl.ds(pl.multiple_of(i * ROWS, ROWS), ROWS))
+
+
+def own_rows(T, x_ref, row_ref, sem):
+    p, _, c = here()
+    copy = pltpu.make_async_copy(x_ref.at[p * T + c], row_ref, sem)
+    copy.start()
+    return copy
 
 
 def norm_of(v):
@@ -527,13 +549,15 @@
     D, n = w.shape[0], L // (S * T)
 
     def kernel(ride, ins, outs, scratch):
-        x_ref, w_ref, res_ref, gain_ref, shift_ref = ins
+        x_ref, w_ref, all_ref, gain_ref, shift_ref = ins
         v_ref, out_ref = outs
-        acc, low, send, recv, own = scratch[:5]
+        acc, low, send, recv, own, res_ref, sem = scratch[:7]
         _, _, rows, col = plane(S)
+        rest = own_rows(T, all_ref, res_ref, sem)
         greet(S, C, rows + [col], other=True, axes=ride.axes)
         ride.start()
-        sum_over_plane(S, T, x_ref, w_ref, acc, scratch[5:])
+        sum_over_plane(S, T, x_ref, w_ref, acc, scratch[7:])
+        rest.wait()
 
         def work(r):
             v = res_ref[r, :].astype(F32) + acc[r, :]
@@ -545,9 +569,11 @@
         ride.wait()
 
     v, out, *rest = comm(
-        kernel, S, C, number, "sum_norm_gather", [x.reshape(S * T, n, K), w, residual, gain, shift], [IN_VMEM] * 5,
+        kernel, S, C, number, "sum_norm_gather", [x.reshape(S * T, n, K), w, residual.reshape(S * T, n, D), gain, shift],
+        [IN_VMEM, IN_VMEM, ANY, IN_VMEM, IN_VMEM],
         [(jax.ShapeDtypeStruct((n, D), F32), IN_VMEM), (jax.ShapeDtypeStruct((S * T, n, D), BF), ANY)],
-        [pltpu.VMEM((n, D), F32), pltpu.VMEM((n, D), BF)] + spread_sems(S) + [DMA] + sum_scratch(S, n, D),
+        [pltpu.VMEM((n, D), F32), pltpu.VMEM((n, D), BF)] + spread_sems(S)
+        + [DMA, pltpu.VMEM((n, D), BF), DMA] + sum_scratch(S, n, D),
         riders,
     )
     return [v, out.reshape(L, D)] + rest
@@ -558,13 +584,15 @@
     D, n = w.shape[0], L // (S * T)
 
     def kernel(ride, ins, outs, scratch):
-        x_ref, w_ref, in_ref, res_ref, gain_ref = ins
+        x_ref, w_ref, in_ref, all_ref, gain_ref = ins
         v_ref, out_ref, stats = outs
-        acc, low, send, recv, own = scratch[:5]
+        acc, low, send, recv, own, res_ref, sem = scratch[:7]
         _, _, rows, col = plane(S)
+        rest = own_rows(T, all_ref, res_ref, sem)
         greet(S, C, rows + [col], other=True, axes=ride.axes)
         ride.start()
-        sum_over_plane(S, T, x_ref, w_ref, acc, scratch[5:])
+        sum_over_plane(S, T, x_ref, w_ref, acc, scratch[7:])
+        rest.wait()
         stats[...] = jnp.zeros_like(stats)
 
         def work(r):
@@ -577,12 +605,14 @@
         ride.wait()
 
     g, out, stats, *rest = comm(
-        kernel, S, C, number, "sum_back_gather", [x.reshape(S * T, n, K), w, v, residual, gain], [IN_VMEM] * 5,
+        kernel, S, C, number, "sum_back_gather", [x.reshape(S * T, n, K), w, v, residual.reshape(S * T, n, D), gain],
+        [IN_VMEM, IN_VMEM, IN_VMEM, ANY, IN_VMEM],
         [
             (jax.ShapeDtypeStruct((n, D), F32), IN_VMEM), (jax.ShapeDtypeStruct((S * T, n, D), BF), ANY),
             (jax.ShapeDtypeStruct((2, D), F32), IN_VMEM),
         ],
-        [pltpu.VMEM((n, D), F32), pltpu.VMEM((n, D), BF)] + spread_sems(S) + [DMA] + sum_scratch(S, n, D),
+        [pltpu.VMEM((n, D), F32), pltpu.VMEM((n, D), BF)] + spread_sems(S)
+        + [DMA, pltpu.VMEM((n, D), BF), DMA] + sum_scratch(S, n, D),
         riders,
     )
     return [g, out.reshape(L, D), stats] + rest
@@ -593,13 +623,15 @@
     D, n = w.shape[0], L // (S * T)
 
     def kernel(ride, ins, outs, scratch):
-        x_ref, w_ref, in_ref, res_ref, gain_ref = ins
+        x_ref, w_ref, all_ref, res_ref, gain_ref = ins
         low, stats = outs
-        acc = scratch[0]
+        acc, in_ref, sem = scratch[:3]
         _, _, rows, col = plane(S)
+        rest = own_rows(T, all_ref, in_ref, sem)
         greet(S, C, rows + [col], other=True, axes=ride.axes)
         ride.start()
-        sum_over_plane(S, T, x_ref, w_ref, acc, scratch[1:])
+        sum_over_plane(S, T, x_ref, w_ref, acc, scratch[3:])
+        rest.wait()
         stats[...] = jnp.zeros_like(stats)
 
         def work(r):
@@ -610,9 +642,10 @@
         ride.wait()
 
     return comm(
-        kernel, S, C, number, "sum_back", [x.reshape(S * T, n, K), w, v, residual, gain], [IN_VMEM] * 5,
+        kernel, S, C, number, "sum_back", [x.reshape(S * T, n, K), w, v.reshape(S * T, n, D), residual, gain],
+        [IN_VMEM, IN_VMEM, ANY, IN_VMEM, IN_VMEM],
         [(jax.ShapeDtypeStruct((n, D), BF), IN_VMEM), (jax.ShapeDtypeStruct((2, D), F32), IN_VMEM)],
-        [pltpu.VMEM((n, D), F32)] + sum_scratch(S, n, D),
+        [pltpu.VMEM((n, D), F32), pltpu.VMEM((n, D), BF), DMA] + sum_scratch(S, n, D),
         riders,
     )
 
@@ -630,9 +663,9 @@
     def kernel(ride, ins, outs, scratch):
         x_ref, y_ref, stat_refs, bias_ref = ins[0], ins[1], ins[2:-5], ins[-5]
         gateup_ref, down_ref, qkv_ref, o_ref = ins[-4:]
-        x_out, y_out, got, gateup_out, down_out, qkv_out, o_out = outs
+        x_out, y_out, norm_out, bias_out, gateup_out, down_out, qkv_out, o_out = outs
         xbuf, xbuf2, ybuf2, tile, send, recv, own, psend, precv, pown, lsend, lrecv, tsend, trecv = scratch[:14]
-        qkv_buf, o_buf, gsend, grecv, gown = scratch[14:]
+        qkv_buf, o_buf, gsend, grecv, gown, got = scratch[14:]
         p, z, c = here()
         other = {"tp": 1 - c}
         everyone = [(i, j) for i in range(C) for j in range(S) if i or j]
@@ -690,10 +723,10 @@
         for copy in moves:
             copy.start()
         tile[...] = jnp.zeros_like(tile)
-        at = 0
-        for ref in stat_refs:
-            tile[at : at + ref.shape[0], :] = ref[...]
-            at += ref.shape[0]
+        at = count
+        for i, ref in enumerate(stat_refs):
+            for j in range(2):
+                tile[j * len(stat_refs) + i : j * len(stat_refs) + i + 1, :] = ref[j : j + 1, :]
         for k in range(lines):
             for block in range(D // 128):
                 tile[at + k : at + k + 1, pl.ds(block * 128, 128)] = bias_ref[:, pl.ds(k * 128, 128)]
@@ -719,6 +752,7 @@
         for copy in small:
             copy.wait()
         small_last = both(got, 0)
+        bias_out[...] = jnp.sum(got[c, :, :, count : count + lines, :], axis=0)
         for i in range(2):
             for q in range(S):
                 gateup_out[:, i, q * fn : (q + 1) * fn] = gateup_ref[q, :, i * fn : (i + 1) * fn].astype(F32)
@@ -738,18 +772,19 @@
             copy.wait()
         x_last = both(x_out, 2)
         settle(got, 0, small_last)
+        norm_out[...] = jnp.sum(got[:, :, :, :count, :], axis=(0, 1, 2))
         settle(y_out, 1, y_last)
         settle(x_out, 2, x_last)
 
     args = [x, y, *stats, bias, gateup, down, qkv, out]
     most = max(S, C) - 1
     home = (jax.ShapeDtypeStruct((T, n, D), BF), ANY)
-    x, y, got, *rest = comm(
+    x, y, *rest = comm(
         kernel, S, C, number, "finish", args, [IN_VMEM] * len(args),
-        [home, home, (jax.ShapeDtypeStruct((T, C, S, tall, 128), F32), ANY)]
+        [home, home]
         + [
             (jax.ShapeDtypeStruct(shape, F32), IN_VMEM)
-            for shape in ((nb, 2, S * fn), (S * fn, nb), (3, nb, S * hn), (S * hn, nb))
+            for shape in ((count, 128), (S, lines, 128), (nb, 2, S * fn), (S * fn, nb), (3, nb, S * hn), (S * hn, nb))
         ],
         [
             pltpu.VMEM((S, n, wide), BF), pltpu.VMEM((C, n, wide), BF), pltpu.VMEM((C, n, wide), BF),
@@ -757,9 +792,10 @@
             DMA((2, S - 1, pieces)), DMA((2, S - 1, pieces)), DMA((2, pieces)), DMA((3,)), DMA((3,)),
             DMA((many,)), DMA((many,)),
             pltpu.VMEM(qkv.shape, BF), pltpu.VMEM(out.shape, BF), DMA((2, S - 1)), DMA((2, S - 1)), DMA((2,)),
+            pltpu.VMEM((T, C, S, tall, 128), F32),
         ],
     )
-    return [x.reshape(T * n, D), y.reshape(T * n, D), got] + rest
+    return [x.reshape(T * n, D), y.reshape(T * n, D)] + rest
 
 
 def ordered(D, S, C):
@@ -793,10 +829,10 @@
     return next(size for size in (512, 256) if rows % size == 0)
 
 
-def attend_kernel(
-    first_ref, qkv_ref, cos_ref, sin_ref, cosf_ref, sinf_ref, begin_ref,
-    qo_ref, ko_ref, vo_ref, o_ref, lse_ref, vt_ref,
-):
+def attend_work(ins, outs, scratch, piece):
+    qkv_ref, cos_ref, sin_ref, cosf_ref, sinf_ref, begin_ref = ins
+    qo_ref, ko_ref, vo_ref, o_ref, lse_ref = outs
+    (vt_ref,) = scratch
     rows, wide = qo_ref.shape
     pairs, size = wide // 128, block_of(rows)
     tables = (cos_ref, sin_ref, cosf_ref, sinf_ref)
@@ -804,18 +840,22 @@
     key_at = lax.broadcasted_iota(jnp.int32, (size, size), 0)
     query_at = lax.broadcasted_iota(jnp.int32, (1, size), 1)
 
-    @pl.loop(0, rows // BLK)
-    def _(i):
-        r = pl.ds(pl.multiple_of(i * BLK, BLK), BLK)
-        for t in range(pairs):
-            w = pl.ds(t * 128, 128)
-            q, k, v = (qkv_ref[r, pl.ds(part * wide + t * 128, 128)] for part in range(3))
-            qo_ref[r, w] = turn(q, i, tables, 1.0).astype(BF) * jnp.asarray(HEAD**-0.5, BF)
-            ko_ref[r, w] = turn(k, i, tables, 1.0).astype(BF)
-            vo_ref[r, w] = v.astype(BF)
-            vt_ref[w, r] = v.T.astype(BF)
-
-    @pl.loop(0, rows // size)
+    if piece == 0:
+
+        @pl.loop(0, rows // BLK)
+        def _(i):
+            r = pl.ds(pl.multiple_of(i * BLK, BLK), BLK)
+            for t in range(pairs):
+                w = pl.ds(t * 128, 128)
+                q, k, v = (qkv_ref[r, pl.ds(part * wide + t * 128, 128)] for part in range(3))
+                qo_ref[r, w] = turn(q, i, tables, 1.0).astype(BF) * jnp.asarray(HEAD**-0.5, BF)
+                ko_ref[r, w] = turn(k, i, tables, 1.0).astype(BF)
+                vo_ref[r, w] = v.astype(BF)
+                vt_ref[w, r] = v.T.astype(BF)
+
+    last = rows // size - 1
+
+    @pl.loop(0 if piece == 0 else last, last if piece == 0 else last + 1)
     def _(i):
         r = pl.ds(pl.multiple_of(i * size, size), size)
         qs = sum((two_heads(qo_ref[r, pl.ds(t * 128, 128)], left) for t in range(pairs)), [])
@@ -840,7 +880,7 @@
         start = (
             jnp.full((1, size), NEG, F32), jnp.zeros((1, size), F32), jnp.zeros((HEAD, size), F32)
         )
-        done = lax.fori_loop(first_ref[i], i + 1, step, (start,) * (2 * pairs))
+        done = lax.fori_loop(0, i + 1, step, (start,) * (2 * pairs))
         for t in range(pairs):
             both = []
             for h in (2 * t, 2 * t + 1):
@@ -850,19 +890,15 @@
             o_ref[r, pl.ds(t * 128, 128)] = jnp.concatenate(both, axis=0).T.astype(BF)
 
 
-def attend(qkv, begin):
+def attend(S, C, T, number, qkv, begin, x):
     rows, wide = qkv.shape[0], qkv.shape[1] // 3
-    size = block_of(rows)
     half = jax.ShapeDtypeStruct((rows, wide), BF)
-    return pl.pallas_call(
-        attend_kernel,
-        in_specs=[pl.BlockSpec(memory_space=pltpu.SMEM)] + [IN_VMEM] * 6,
-        out_specs=[IN_VMEM] * 5,
-        out_shape=[half] * 4 + [jax.ShapeDtypeStruct((wide // HEAD, rows), F32)],
-        scratch_shapes=[pltpu.VMEM((wide, rows), BF)],
-        compiler_params=pltpu.CompilerParams(vmem_limit_bytes=48 << 20),
-        name="attend",
-    )(begin[0, ::size] // size, qkv, *turn_tables(rows), begin)
+    args = [qkv, *turn_tables(rows), begin]
+    outs = [half] * 4 + [jax.ShapeDtypeStruct((wide // HEAD, rows), F32)]
+    return gather_columns(
+        S, C, T, number, x, (),
+        (args, [IN_VMEM] * len(args), [(shape, IN_VMEM) for shape in outs], [pltpu.VMEM((wide, rows), BF)], attend_work),
+    )
 
 
 def attend_back_work(ins, out_ref, bias_ref, scratch):
@@ -995,9 +1031,6 @@
         def unpermute(x):
             return x.reshape(x.shape[0], C, S, nb).swapaxes(1, 2).reshape(x.shape)
 
-        def own(x):
-            return lax.dynamic_slice_in_dim(x, (p * T + c) * n, n, 0)
-
         def half_of(x):
             return lax.dynamic_slice_in_dim(x, c * n, n, 0)
 
@@ -1029,8 +1062,8 @@
             jnp.broadcast_to(tile, (C, S, 8, 128)),
             to_parts(half_of(tokens)),
         )
-        tok, wo = gather_columns(S, C, T, 1, tok, [("all", wo.reshape(S * nb, hn))])
-        wo, wg, wd = wo.reshape(D, hn), over_ctx(wg), over_ctx(wd)
+        (tok,) = gather_columns(S, C, T, 1, tok)
+        wg, wd = over_ctx(wg), over_ctx(wd)
 
         small = lax.dynamic_index_in_dim(small, c, 0, keepdims=False).reshape(C, S, 1024)
         norms = small[:, :, : 4 * nb].reshape(C * S, 4, nb).swapaxes(0, 1).reshape(4, D)
@@ -1046,12 +1079,13 @@
         begin = doc_begins(lengths_row, L)
         begin = begin[None, :]
 
-        n1, qkv, wq = project(S, C, T, 12, tok, raw.reshape(C, 3, nb, -1), gains[:1], shifts[:1], bias)
-        own_tok = own(tok)
-        q, k, v, o, lse = attend(qkv, begin)
-        mid, n2, cot = sum_norm_gather(S, C, T, 2, o, wo, own_tok, gains[1:], shifts[1:], [("ctx", cot)])
-        cot, n2 = after(cot, n2)
-        (gb,) = gather_columns(S, C, T, 4, cot)
+        n1, qkv, wq, cot, wo = project(
+            S, C, T, 12, tok, raw.reshape(C, 3, nb, -1), gains[:1], shifts[:1], bias,
+            [("ctx", cot), ("all", wo.reshape(S * nb, hn))],
+        )
+        wo = wo.reshape(D, hn)
+        gb, q, k, v, o, lse = attend(S, C, T, 4, qkv, begin, cot)
+        mid, n2 = sum_norm_gather(S, C, T, 2, o, wo, tok, gains[1:], shifts[1:])
         gu, act = by_rows(
             gates_kernel, "gates", [(True, n2), (False, wg)],
             [jax.ShapeDtypeStruct((L, 2 * fn), F32), jax.ShapeDtypeStruct((L, fn), BF)],
@@ -1067,7 +1101,7 @@
         gw_gateup = mm(n2, dgu, 0, 0).astype(BF)
         dgu, gw_gateup = after(dgu, gw_gateup)
         gw_gateup = sum_ctx(gw_gateup)
-        dmid, gb1, stats2 = sum_back_gather(S, C, T, 6, dgu, wg, mid, own(gb), gains[1:])
+        dmid, gb1, stats2 = sum_back_gather(S, C, T, 6, dgu, wg, mid, gb, gains[1:])
         gw_out = mm(gb1, o, 0, 0).astype(BF)
         gb1, gw_out = after(gb1, gw_out)
         gw_out = sum_ctx(gw_out)
@@ -1080,17 +1114,16 @@
         dqkv, gw_qkv = after(dqkv, gw_qkv)
         gw_qkv = sum_ctx(gw_qkv)
         low, stats1, out, gw_gateup = sum_back(
-            S, C, T, 8, dqkv, wq, own_tok, dmid, gains[:1], [("shard", out), ("shard", gw_gateup)]
+            S, C, T, 8, dqkv, wq, tok, dmid, gains[:1], [("shard", out), ("shard", gw_gateup)]
         )
-        gtok, out, small, gw_gateup, gw_down, gw_qkv, gw_out = finish(
+        gtok, out, norms, gbias, gw_gateup, gw_down, gw_qkv, gw_out = finish(
             S, C, T, 10, low, out, [stats1, stats2], gbias, gw_gateup, gw_down, gw_qkv, gw_out
         )
         if not ordered(D, S, C):
             gtok, out = unpermute(gtok), unpermute(out)
         gtok = gtok.astype(F32)
-        norms = lax.dynamic_slice_in_dim(jnp.sum(small[..., :4, :], axis=(0, 1, 2)), (z * S + p) * nb % 128, nb, 1)
-        gbias = lax.dynamic_index_in_dim(small, c, 0, keepdims=False)[:, :, 4 : 4 + 3 * hn // 128]
-        gbias = jnp.sum(gbias, axis=0).reshape(S, 3, heads, S * C, nf)
+        norms = lax.dynamic_slice_in_dim(norms, (z * S + p) * nb % 128, nb, 1) if nb % 128 else norms
+        gbias = gbias.reshape(S, 3, heads, S * C, nf)
         gbias = lax.dynamic_index_in_dim(gbias, p * C + z, 3, keepdims=False)
         gbias = gbias.swapaxes(0, 1).reshape(b_qkv.shape)
 
@@ -1102,8 +1135,8 @@
             gw_out.reshape(w_out.shape),
             gw_gateup.reshape(w_gateup.shape),
             gw_down.reshape(w_down.shape),
-            jnp.stack((norms[0], norms[2]))[None],
-            jnp.stack((norms[1], norms[3]))[None],
+            norms[None, :2],
+            norms[None, 2:],
         )
 
     return body

time: 662 us -> 689 us (1.041)
  Pallas kernels: 547 us -> 581 us
  local copies, waits for them, and re-layouts: 43.7 us -> 33 us
    pallas_call x9, Pallas kernels: 499 us -> 553 us  [comm(): pl.pallas_call(body, out_shape=[shape for shape, _ in outs] + ride.shapes...]
    pallas_call x3 -> x2, Pallas kernels: 48.2 us -> 28.6 us  [by_rows(): pl.pallas_call(kernel, grid=(L // size,), in_specs=[spec(x.shape[1]) if r...]
    unnamed x60 -> x32, local copies, waits for them, and re-layouts: 18.4 us -> 10.4 us
  transfers between devices with their start and end apart: 7 -> 7, of which waited for: 0 -> 1; matrix products, arithmetic and copies ran while one was open for 10% -> 10% of each run, Pallas kernels for 74% -> 76%
where the time goes in v9:
time: 689 us; the launch traced here: 684 us
  Pallas kernels  581 us (84%)
  matrix products  45.2 us (7%)
  local copies, waits for them, and re-layouts  33 us (5%)
  between operations  15 us (2%)
    pallas_call x9, Pallas kernels, comm(): pl.pallas_call(body, out_shape=[shape for shape, _ in outs] + ride.shapes...  553 us
    dot_general x5, matrix products, mm(): lax.dot_general(a, b, (((ca,), (cb,)), ((), ())), preferred_element_type=...  45.2 us
    pallas_call x2, Pallas kernels, by_rows(): pl.pallas_call(kernel, grid=(L // size,), in_specs=[spec(x.shape[1]) if r...  28.6 us
  transfers between devices with their start and end apart: 7, of which 1 were waited for; matrix products, arithmetic and copies ran while one was open for 10% of the time, Pallas kernels for 76%

profile of v9, /device:TPU:9, one launch (start us, length us, event | category | flops | bytes accessed | tf_op | source)
XLA Modules:
  0.0 684.1 jit_solution(10558406028777052446)
XLA Ops:
  8.9 1.8 copy.58
  10.7 2.3 copy.61
  12.9 1.9 copy.59
  14.9 1.5 copy.63.refs_3_
  16.5 1.5 constant_dynamic-slice_fusion.3
  18.9 1.2 reshape.190.refs_5_
  20.9 1.2 reshape.187.refs_1_
  22.8 58.1 %exchange.1 = (f32[2,4,4,8,128]{4,3,2,1,0:T(8,128)}, bf16[4,192,512]{2,1,0:T(8,128)(2,1)}, bf16[4,192,512]{2,1,0:T(8,128)(2,1)}, bf16[4,128,256]{2,1,0:T(8,128)(...) custom-call(f32[4,4,8,128]{3,2,1,0:T(8,128)} %broadcast_in_dim.27.refs_0_, ...), custom_call_target="tpu_custom_call" | custom-call | bytes 120000000 | tf_op jit(solution)/shard_map/exchange/pallas_call | solution.py:108
  84.7 32.8 %gather_columns.2 = bf16[4,2,192,2048]{3,2,1,0:T(8,128)(2,1)} custom-call(bf16[4,192,512]{2,1,0:T(8,128)(2,1)} %get-tuple-element.57.refs_0_), custom_call_target="tpu_custom_call" | custom-call | bytes 120000000 | tf_op jit(solution)/shard_map/gather_columns/pallas_call | solution.py:108
  118.1 104.4 %project.1 = (bf16[1536,2048]{1,0:T(8,128)(2,1)}, f32[1536,768]{1,0:T(8,128)}, bf16[4,4,128,768]{3,2,1,0:T(8,128)(2,1)}, bf16[4,192,512]{2,1,0:T(8,128)(2,1)}, bf16[4,512,256]{2,1,0:T(8,128)(2,1)}) custom-call(bf16[1536,2048]{1,0:T(8,128)(2,1)} %bitcast.100, bf16[4,3,128,1024]{3,2,1,0:T(8,128)(2,1)} %bitcast.115, f32[1,2048]{1,0:T(1,128)} %bitcast.141, ...), custom_call_target="tpu_custom_call" | custom-call | bytes 120000000 | tf_op jit(solution)/shard_map/project/pallas_call | solution.py:108
  222.5 35.3 %gather_columns.3 = (bf16[4,2,192,2048]{3,2,1,0:T(8,128)(2,1)}, bf16[1536,256]{1,0:T(8,128)(2,1)}, bf16[1536,256]{1,0:T(8,128)(2,1)}, bf16[1536,256]{1,0:T(8,128...) custom-call(bf16[4,192,512]{2,1,0:T(8,128)(2,1)} %get-tuple-element.61.refs_0_, ...), custom_call_target="tpu_custom_call" | custom-call | bytes 120000000 | tf_op jit(solution)/shard_map/gather_columns/pallas_call | solution.py:108
  257.8 67.2 %sum_norm_gather.1 = (f32[192,2048]{1,0:T(8,128)}, bf16[8,192,2048]{2,1,0:T(8,128)(2,1)}) custom-call(bf16[8,192,256]{2,1,0:T(8,128)(2,1)} %bitcast.119, bf16[2048,256]{1,0:T(8,128)(2,1)} %bitcast.129, bf16[8,192,2048]{2,1,0:T(8,128)(2,1)} %bitcast.101, f32[1,2048]{1,0:T(1,128)} %bitcast.143, f32[1,2048]{1,0:T(1,128)} %bitcast.146), custom_call_target="tpu_custom_call" | custom-call | bytes 120000000 | tf_op jit(solution)/shard_map/sum_norm_gather/pallas_call | solution.py:108
  325.1 16.5 %gates.1 = (f32[1536,1408]{1,0:T(8,128)}, bf16[1536,704]{1,0:T(8,128)(2,1)}) custom-call(bf16[1536,2048]{1,0:T(8,128)(2,1)} %bitcast.107, bf16[2048,1408]{1,0:T(8,128)(2,1)} %all-gather.6.cloned.1.call-done.wg_ref.refs_1_), custom_call_target="tpu_custom_call" | custom-call | tf_op jit(solution)/shard_map/gates/pallas_call | solution.py:492
  341.6 9.8 %convolution_convert_fusion.2 = bf16[2048,704]{0,1:T(8,128)(2,1)} fusion(bf16[1536,2048]{1,0:T(8,128)(2,1)} %bitcast.103, bf16[1536,704]{1,0:T(8,128)(2,1)} %get-tuple-element.67), kind=kOutput, calls=%fused_computation.2 | convolution fusion | flops 4430626816 | bytes 11337728 | tf_op jit(solution)/shard_map/dot_general | solution.py:26
  351.5 12.0 %gates_back.1 = bf16[1536,1408]{1,0:T(8,128)(2,1)} custom-call(bf16[1536,2048]{1,0:T(8,128)(2,1)} %bitcast.104, bf16[2048,704]{1,0:T(8,128)(2,1)} %all-gather.8.cloned.1.call-done.wd_ref.refs_1_, f32[1536,1408]{1,0:T(8,128)} %get-tuple-element.74.gu_ref), custom_call_target="tpu_custom_call" | custom-call | tf_op jit(solution)/shard_map/gates_back/pallas_call | solution.py:492
  363.5 15.0 %convolution_convert_fusion = bf16[2048,1408]{1,0:T(8,128)(2,1)} fusion(bf16[1536,2048]{1,0:T(8,128)(2,1)} %bitcast.108, bf16[1536,1408]{1,0:T(8,128)(2,1)} %gates_back.1), kind=kOutput, calls=%fused_computation | convolution fusion | flops 8861253632 | bytes 16384000 | tf_op jit(solution)/shard_map/dot_general | solution.py:26
  378.6 79.2 %sum_back_gather.1 = (f32[192,2048]{1,0:T(8,128)}, bf16[8,192,2048]{2,1,0:T(8,128)(2,1)}, f32[2,2048]{1,0:T(2,128)}) custom-call(bf16[8,192,1408]{2,1,0:T(8,128)(2,1)} %bitcast.106, bf16[2048,1408]{1,0:T(8,128)(2,1)} %all-gather.6.cloned.1.call-done.wg_ref.refs_1_, f32[192,2048]{1,0:T(8,128)} %get-tuple-element.76.refs_2_, bf16[8,192,2048]{2,1,0:T(8,128)(2,1)} %bitcast.105, ...), custom_call_target="tpu_custom_call" | custom-call | bytes 120000000 | tf_op jit(solution)/shard_map/sum_back_gather/pallas_call | solution.py:108
  457.9 5.8 convolution_convert_fusion.4
  463.7 5.5 convolution_convert_fusion.3.refs_6_
  469.2 2.3 copy.66
  471.5 56.1 %attend_back.1 = (bf16[1536,768]{1,0:T(8,128)(2,1)}, f32[1,768]{1,0:T(1,128)}, f32[192,2048]{1,0:T(8,128)}, bf16[4,128,704]{2,1,0:T(8,128)(2,1)}) custom-call(bf16[8,192,704]{2,1,0:T(8,128)(2,1)} %bitcast.122, bf16[2048,704]{1,0:T(8,128)(2,1)} %all-gather.8.cloned.1.call-done.wd_ref.refs_1_, bf16[1536,256]{1,0:T(8,128)(2,1)} %get-tuple-element.71.refs_2_, ...), custom_call_target="tpu_custom_call" | custom-call | bytes 120000000 | tf_op jit(solution)/shard_map/attend_back/pallas_call | solution.py:108
  527.6 9.2 %convolution_convert_fusion.1 = bf16[2048,768]{1,0:T(8,128)(2,1)} fusion(bf16[1536,2048]{1,0:T(8,128)(2,1)} %get-tuple-element.82, bf16[1536,768]{1,0:T(8,128)(2,1)} %get-tuple-element.83), kind=kOutput, calls=%fused_computation.1 | convolution fusion | flops 4833411072 | bytes 11796480 | tf_op jit(solution)/shard_map/dot_general | solution.py:26
  536.8 1.4 copy-done
  539.8 59.5 %sum_back.1 = (bf16[192,2048]{1,0:T(8,128)(2,1)}, f32[2,2048]{1,0:T(2,128)}, bf16[4,192,512]{2,1,0:T(8,128)(2,1)}, bf16[4,128,1408]{2,1,0:T(8,128)(2,1)}) custom-call(bf16[8,192,768]{2,1,0:T(8,128)(2,1)} %bitcast.121, bf16[2048,768]{1,0:T(8,128)(2,1)} %bitcast.112, bf16[8,192,2048]{2,1,0:T(8,128)(2,1)} %bitcast.102, f32[192,2048]{1,0:T(8,128)} %get-tuple-element.85.refs_3_, ...), custom_call_target="tpu_custom_call" | custom-call | bytes 120000000 | tf_op jit(solution)/shard_map/sum_back/pallas_call | solution.py:108
  599.4 3.9 reduce-scatter.9.cloned.1.call-done
  603.3 59.9 %finish.1 = (bf16[2,192,2048]{2,1,0:T(8,128)(2,1)}, bf16[2,192,2048]{2,1,0:T(8,128)(2,1)}, f32[4,128]{1,0:T(4,128)}, f32[4,6,128]{2,1,0:T(8,128)}, f32[128,2,281...) custom-call(bf16[192,2048]{1,0:T(8,128)(2,1)} %get-tuple-element.88.refs_0_, ...), custom_call_target="tpu_custom_call" | custom-call | bytes 120000000 | tf_op jit(solution)/shard_map/finish/pallas_call | solution.py:108
  663.2 1.4 slice_bitcast_fusion
  664.6 1.1 reshape.218
  666.6 3.6 bitcast_convert_fusion
  670.1 1.1 copy.79
  671.3 1.1 copy.80
  673.3 1.6 copy.82
  (80 shorter events, 13.9 us)
Async XLA Ops:
  7.2 5.7 copy-start.6
  7.2 110.9 %all-gather.4.cloned.1.call-start = ((), (), s32[]{:S(2)}) async-start(), calls=%async_computation.4 | async-start | bytes 3932160 | tf_op jit(solution)/shard_map/all_gather | solution.py:1053
  7.9 317.2 %all-gather.6.cloned.1.call-start = ((), (), s32[]{:S(2)}) async-start(), calls=%async_computation.5 | async-start | bytes 7208960 | tf_op jit(solution)/shard_map/all_gather | solution.py:1041
  18.8 3.3 copy-start.12
  18.9 3.3 copy-start.10
  18.9 3.3 copy-start.11
  81.0 270.4 %all-gather.8.cloned.1.call-start = ((), (), s32[]{:S(2)}) async-start(), calls=%async_computation.6 | async-start | bytes 3932160 | tf_op jit(solution)/shard_map/all_gather | solution.py:1041
  81.7 387.4 %reduce-scatter.5.cloned.1.call-start = ((), (), s32[]{:S(2)}) async-start(), calls=%async_computation.7 | async-start | bytes 3604480 | tf_op jit(solution)/shard_map/reduce_scatter | solution.py:1044
  351.4 188.4 %reduce-scatter.7.cloned.1.call-start = ((), (), s32[]{:S(2)}) async-start(), calls=%async_computation.8 | async-start | bytes 7208960 | tf_op jit(solution)/shard_map/reduce_scatter | solution.py:1044
  378.6 220.8 %reduce-scatter.11.cloned.1.call-start = ((), (), s32[]{:S(2)}) async-start(), calls=%async_computation.10 | async-start | bytes 1310720 | tf_op jit(solution)/shard_map/reduce_scatter | solution.py:1044
  378.6 79.2 %copy-start.1 = (bf16[1536,256]{1,0:T(8,128)(2,1)S(1)}, bf16[1536,256]{1,0:T(8,128)(2,1)}, u32[]{:S(2)}) copy-start(bf16[1536,256]{1,0:T(8,128)(2,1)} %get-tuple-element.63.refs_5_) | copy-start | bytes 2359300
  457.9 5.8 copy-start.8
  463.6 139.6 %reduce-scatter.9.cloned.1.call-start = ((), (), s32[]{:S(2)}) async-start(), calls=%async_computation.9 | async-start | bytes 3932160 | tf_op jit(solution)/shard_map/reduce_scatter | solution.py:1044
  536.8 1.4 copy-start
  536.8 1.9 copy-start.5
  663.2 6.9 %copy-start.4 = (bf16[2,192,2048]{2,1,0:T(8,128)(2,1)S(1)}, bf16[2,192,2048]{2,1,0:T(8,128)(2,1)}, u32[]{:S(2)}) copy-start(bf16[2,192,2048]{2,1,0:T(8,128)(2,1)} %get-tuple-element.97) | copy-start | bytes 4718596
  666.6 4.7 copy-start.3
  670.1 2.3 copy-start.9
  670.1 3.1 copy-start.2
  673.3 2.4 copy-start.7
Sparse Core Ops, SparseCore 0:
  9.6 79.0 all-gather.3
  90.2 143.8 all-gather.5
  235.7 63.2 all-gather.7
  351.6 54.7 reduce-scatter.4
  408.6 102.7 reduce-scatter.6
  514.1 25.5 reduce-scatter.10
  542.7 60.5 reduce-scatter.8

commit v10 on v9

--- a/solution.py
+++ b/solution.py
@@ -279,6 +279,8 @@
         ]
         for copy in local:
             copy.start()
+        if task is not None:
+            task(ins[1:], outs[1:], scratch[3:], None)
         greet(S, C, rows + [col], other=True, axes=ride.axes)
         ride.start()
         work = [None, None]
@@ -383,7 +385,7 @@
         remote(ref, ref, send, recv, other).wait_recv()
 
     if meanwhile is not None:
-        meanwhile()
+        meanwhile(0)
     total = mine[B, top, :].astype(F32)
     for j in range(1, B):
         came(row1.at[j - 1, 1], rsend.at[j - 1, 1], rrecv.at[j - 1, 1])
@@ -394,6 +396,8 @@
         came(col1.at[j], csend.at[j], crecv.at[j])
         to_row[j - 1] = (mine[j, low, :].astype(F32) + col1[j].astype(F32)).astype(BF)
         push(to_row.at[j - 1], row2.at[j - 1], fsend.at[j], frecv.at[j], rows[j - 1])
+    if meanwhile is not None:
+        meanwhile(1)
     came(col1.at[0], csend.at[0], crecv.at[0])
     upper, lower = out_ref[top, :], out_ref[low, :] + col1[0].astype(F32)
     for j in range(1, B):
@@ -409,7 +413,7 @@
         copy.wait_send()
 
 
-def project(S, C, T, number, tok, raw, gain, shift, bias, riders):
+def project(S, C, T, number, tok, raw, gain, shift, bias):
     L, D = tok.shape
     _, parts, nb, wide = raw.shape
     hn = wide // S
@@ -421,7 +425,7 @@
         send, recv, own = scratch
         p, _, _ = here()
         mates = [(p + k) % S for k in range(1, S)]
-        greet(S, C, mates, axes=ride.axes)
+        greet(S, C, mates)
 
         def lanes(q):
             return pl.ds(pl.multiple_of(q * hn, 128), hn)
@@ -436,7 +440,6 @@
             copies.append(pltpu.make_async_copy(raw_ref.at[:, part, :, lanes(p)], dst, own.at[part]))
         for copy in copies:
             copy.start()
-        ride.start()
 
         def normed(r):
             n_ref[r, :] = (norm_of(tok_ref[r, :].astype(F32))[0] * gain_ref[...] + shift_ref[...]).astype(BF)
@@ -451,26 +454,15 @@
             r = pl.ds(pl.multiple_of(i * BLK, BLK), BLK)
             out_ref[r, :] = mm(n_ref[r, :], w, 1, 0) + bias_ref[...]
 
-        ride.wait()
-
-    n, out, w, *rest = comm(
+    n, out, w = comm(
         kernel, S, C, number, "project", [tok, raw, gain, shift, bias], [IN_VMEM] * 5,
         [
             (jax.ShapeDtypeStruct((L, D), BF), IN_VMEM), (jax.ShapeDtypeStruct((L, parts * hn), F32), IN_VMEM),
             (jax.ShapeDtypeStruct((C, S, nb, parts * hn), BF), IN_VMEM),
         ],
         [DMA((most, parts)), DMA((most, parts)), DMA((parts,))],
-        riders,
-    )
-    return [n, out, w.reshape(D, parts * hn)] + rest
-
-
-def gates_kernel(n2_ref, wg_ref, gu_ref, act_ref):
-    both = mm(n2_ref[...], wg_ref[...], 1, 0)
-    gu_ref[...] = both
-    width = act_ref.shape[1]
-    gate, up = both[:, :width], both[:, width:]
-    act_ref[...] = (gate * jax.nn.sigmoid(gate) * up).astype(BF)
+    )
+    return n, out, w.reshape(D, parts * hn)
 
 
 def gates_back_kernel(gb_ref, wd_ref, gu_ref, dgu_ref):
@@ -482,20 +474,49 @@
     dgu_ref[...] = jnp.concatenate((dgate, dact * gate * s), axis=1).astype(BF)
 
 
+def gates_work(ins, outs, scratch, piece):
+    gu_ref, act_ref = outs
+    n2_ref, wg_ref, sems = scratch
+    if piece != 1:
+        for i, (x, y) in enumerate(zip(ins, (n2_ref, wg_ref))):
+            copy = pltpu.make_async_copy(x, y, sems.at[i])
+            copy.wait() if piece == 0 else copy.start()
+    if piece is None:
+        return
+    (rows, width), half = act_ref.shape, act_ref.shape[0] // BLK // 2
+
+    @pl.loop(piece * half, piece * half + half)
+    def _(i):
+        r = pl.ds(pl.multiple_of(i * BLK, BLK), BLK)
+        both = mm(n2_ref[r, :], wg_ref[...], 1, 0)
+        gu_ref[r, :] = both
+        gate, up = both[:, :width], both[:, width:]
+        act_ref[r, :] = (gate * jax.nn.sigmoid(gate) * up).astype(BF)
+
+
+def gates(S, C, T, number, n2, wg, x):
+    L, width = n2.shape[0], wg.shape[1] // 2
+    outs = [jax.ShapeDtypeStruct((L, 2 * width), F32), jax.ShapeDtypeStruct((L, width), BF)]
+    return gather_columns(
+        S, C, T, number, x, (),
+        ([n2, wg], [ANY, ANY], [(shape, IN_VMEM) for shape in outs],
+         [pltpu.VMEM(n2.shape, BF), pltpu.VMEM(wg.shape, BF), DMA((2,))], gates_work),
+    )
+
+
 def by_rows(kernel, name, arrays, outs):
     L = outs[0].shape[0]
-    size = L // 2
 
     def spec(width):
-        return pl.BlockSpec((size, width), lambda i: (i, 0))
+        return pl.BlockSpec((BLK, width), lambda i: (i, 0))
 
     return pl.pallas_call(
         kernel,
-        grid=(L // size,),
+        grid=(L // BLK,),
         in_specs=[spec(x.shape[1]) if rows else pl.BlockSpec(x.shape, lambda i: (0, 0)) for rows, x in arrays],
         out_specs=[spec(x.shape[1]) for x in outs],
         out_shape=outs,
-        compiler_params=pltpu.CompilerParams(vmem_limit_bytes=60 << 20),
+        compiler_params=pltpu.CompilerParams(vmem_limit_bytes=48 << 20),
         name=name,
     )(*[x for _, x in arrays])
 
@@ -829,10 +850,10 @@
     return next(size for size in (512, 256) if rows % size == 0)
 
 
-def attend_work(ins, outs, scratch, piece):
-    qkv_ref, cos_ref, sin_ref, cosf_ref, sinf_ref, begin_ref = ins
-    qo_ref, ko_ref, vo_ref, o_ref, lse_ref = outs
-    (vt_ref,) = scratch
+def attend_kernel(
+    first_ref, qkv_ref, cos_ref, sin_ref, cosf_ref, sinf_ref, begin_ref,
+    qo_ref, ko_ref, vo_ref, o_ref, lse_ref, vt_ref,
+):
     rows, wide = qo_ref.shape
     pairs, size = wide // 128, block_of(rows)
     tables = (cos_ref, sin_ref, cosf_ref, sinf_ref)
@@ -840,22 +861,18 @@
     key_at = lax.broadcasted_iota(jnp.int32, (size, size), 0)
     query_at = lax.broadcasted_iota(jnp.int32, (1, size), 1)
 
-    if piece == 0:
-
-        @pl.loop(0, rows // BLK)
-        def _(i):
-            r = pl.ds(pl.multiple_of(i * BLK, BLK), BLK)
-            for t in range(pairs):
-                w = pl.ds(t * 128, 128)
-                q, k, v = (qkv_ref[r, pl.ds(part * wide + t * 128, 128)] for part in range(3))
-                qo_ref[r, w] = turn(q, i, tables, 1.0).astype(BF) * jnp.asarray(HEAD**-0.5, BF)
-                ko_ref[r, w] = turn(k, i, tables, 1.0).astype(BF)
-                vo_ref[r, w] = v.astype(BF)
-                vt_ref[w, r] = v.T.astype(BF)
-
-    last = rows // size - 1
-
-    @pl.loop(0 if piece == 0 else last, last if piece == 0 else last + 1)
+    @pl.loop(0, rows // BLK)
+    def _(i):
+        r = pl.ds(pl.multiple_of(i * BLK, BLK), BLK)
+        for t in range(pairs):
+            w = pl.ds(t * 128, 128)
+            q, k, v = (qkv_ref[r, pl.ds(part * wide + t * 128, 128)] for part in range(3))
+            qo_ref[r, w] = turn(q, i, tables, 1.0).astype(BF) * jnp.asarray(HEAD**-0.5, BF)
+            ko_ref[r, w] = turn(k, i, tables, 1.0).astype(BF)
+            vo_ref[r, w] = v.astype(BF)
+            vt_ref[w, r] = v.T.astype(BF)
+
+    @pl.loop(0, rows // size)
     def _(i):
         r = pl.ds(pl.multiple_of(i * size, size), size)
         qs = sum((two_heads(qo_ref[r, pl.ds(t * 128, 128)], left) for t in range(pairs)), [])
@@ -880,7 +897,7 @@
         start = (
             jnp.full((1, size), NEG, F32), jnp.zeros((1, size), F32), jnp.zeros((HEAD, size), F32)
         )
-        done = lax.fori_loop(0, i + 1, step, (start,) * (2 * pairs))
+        done = lax.fori_loop(first_ref[i], i + 1, step, (start,) * (2 * pairs))
         for t in range(pairs):
             both = []
             for h in (2 * t, 2 * t + 1):
@@ -890,18 +907,22 @@
             o_ref[r, pl.ds(t * 128, 128)] = jnp.concatenate(both, axis=0).T.astype(BF)
 
 
-def attend(S, C, T, number, qkv, begin, x):
+def attend(qkv, begin):
     rows, wide = qkv.shape[0], qkv.shape[1] // 3
+    size = block_of(rows)
     half = jax.ShapeDtypeStruct((rows, wide), BF)
-    args = [qkv, *turn_tables(rows), begin]
-    outs = [half] * 4 + [jax.ShapeDtypeStruct((wide // HEAD, rows), F32)]
-    return gather_columns(
-        S, C, T, number, x, (),
-        (args, [IN_VMEM] * len(args), [(shape, IN_VMEM) for shape in outs], [pltpu.VMEM((wide, rows), BF)], attend_work),
-    )
-
-
-def attend_back_work(ins, out_ref, bias_ref, scratch):
+    return pl.pallas_call(
+        attend_kernel,
+        in_specs=[pl.BlockSpec(memory_space=pltpu.SMEM)] + [IN_VMEM] * 6,
+        out_specs=[IN_VMEM] * 5,
+        out_shape=[half] * 4 + [jax.ShapeDtypeStruct((wide // HEAD, rows), F32)],
+        scratch_shapes=[pltpu.VMEM((wide, rows), BF)],
+        compiler_params=pltpu.CompilerParams(vmem_limit_bytes=48 << 20),
+        name="attend",
+    )(begin[0, ::size] // size, qkv, *turn_tables(rows), begin)
+
+
+def attend_back_work(ins, out_ref, bias_ref, scratch, piece):
     q_ref, k_ref, v_ref, o_ref, do_ref, lse_ref, cos_ref, sin_ref, cosf_ref, sinf_ref, begin_ref = ins
     kt_ref, dq_ref, dk_ref, dv_ref = scratch
     rows, wide = q_ref.shape
@@ -911,8 +932,10 @@
     key_at = lax.broadcasted_iota(jnp.int32, (size, size), 0)
     query_at = lax.broadcasted_iota(jnp.int32, (1, size), 1)
 
-    @pl.loop(0, rows // BLK)
-    def _(i):
+    last = rows // size - 1
+    first, stop = (0, last) if piece == 0 else (last, last + 1)
+
+    def prepare(i):
         r = pl.ds(pl.multiple_of(i * BLK, BLK), BLK)
         for t in range(pairs):
             w = pl.ds(t * 128, 128)
@@ -920,7 +943,10 @@
             dk_ref[r, w] = jnp.zeros((BLK, 128), F32)
             dv_ref[r, w] = jnp.zeros((BLK, 128), F32)
 
-    @pl.loop(0, rows // size)
+    if piece == 0:
+        pl.loop(0, rows // BLK)(prepare)
+
+    @pl.loop(first, stop)
     def _(i):
         r = pl.ds(pl.multiple_of(i * size, size), size)
         qs, dos, deltas, lses = [], [], [], []
@@ -959,6 +985,8 @@
             both = jnp.concatenate(done[2 * t : 2 * t + 2], axis=0)
             dq_ref[r, pl.ds(t * 128, 128)] = both.T * (HEAD**-0.5)
 
+    if piece == 0:
+        return
     bias_ref[...] = jnp.zeros_like(bias_ref)
 
     @pl.loop(0, rows // BLK)
@@ -981,9 +1009,10 @@
         _, _, row, col = plane(S)
         greet(S, C, row + [col], other=True, axes=ride.axes)
 
-        def meanwhile():
-            ride.start()
-            attend_back_work(ins[2:], outs[0], outs[1], scratch[:4])
+        def meanwhile(piece):
+            if piece == 0:
+                ride.start()
+            attend_back_work(ins[2:], outs[0], outs[1], scratch[:4], piece)
 
         sum_over_plane(S, T, ins[0], ins[1], outs[2], scratch[4:], meanwhile)
         ride.wait()
@@ -1062,8 +1091,8 @@
             jnp.broadcast_to(tile, (C, S, 8, 128)),
             to_parts(half_of(tokens)),
         )
-        (tok,) = gather_columns(S, C, T, 1, tok)
-        wg, wd = over_ctx(wg), over_ctx(wd)
+        tok, wo = gather_columns(S, C, T, 1, tok, [("all", wo.reshape(S * nb, hn))])
+        wo, wg, wd = wo.reshape(D, hn), over_ctx(wg), over_ctx(wd)
 
         small = lax.dynamic_index_in_dim(small, c, 0, keepdims=False).reshape(C, S, 1024)
         norms = small[:, :, : 4 * nb].reshape(C * S, 4, nb).swapaxes(0, 1).reshape(4, D)
@@ -1079,17 +1108,10 @@
         begin = doc_begins(lengths_row, L)
         begin = begin[None, :]
 
-        n1, qkv, wq, cot, wo = project(
-            S, C, T, 12, tok, raw.reshape(C, 3, nb, -1), gains[:1], shifts[:1], bias,
-            [("ctx", cot), ("all", wo.reshape(S * nb, hn))],
-        )
-        wo = wo.reshape(D, hn)
-        gb, q, k, v, o, lse = attend(S, C, T, 4, qkv, begin, cot)
-        mid, n2 = sum_norm_gather(S, C, T, 2, o, wo, tok, gains[1:], shifts[1:])
-        gu, act = by_rows(
-            gates_kernel, "gates", [(True, n2), (False, wg)],
-            [jax.ShapeDtypeStruct((L, 2 * fn), F32), jax.ShapeDtypeStruct((L, fn), BF)],
-        )
+        n1, qkv, wq = project(S, C, T, 12, tok, raw.reshape(C, 3, nb, -1), gains[:1], shifts[:1], bias)
+        q, k, v, o, lse = attend(qkv, begin)
+        mid, n2, cot = sum_norm_gather(S, C, T, 2, o, wo, tok, gains[1:], shifts[1:], [("ctx", cot)])
+        gb, gu, act = gates(S, C, T, 4, n2, wg, cot)
         gw_down = mm(gb, act, 0, 0).astype(BF)
         wd, gw_down = after(wd, gw_down)
         gw_down = sum_ctx(gw_down)
@@ -1104,10 +1126,10 @@
         dmid, gb1, stats2 = sum_back_gather(S, C, T, 6, dgu, wg, mid, gb, gains[1:])
         gw_out = mm(gb1, o, 0, 0).astype(BF)
         gb1, gw_out = after(gb1, gw_out)
-        gw_out = sum_ctx(gw_out)
         do = mm(gb1, wo, 1, 0).astype(BF)
-        dqkv, gbias, got, gw_down = attend_back(
-            S, C, T, 11, q, k, v, o, do, lse, begin, act, wd, [("shard", gw_down)]
+        dqkv, gbias, got, gw_down, gw_out = attend_back(
+            S, C, T, 11, q, k, v, o, do, lse, begin, act, wd,
+            [("shard", gw_down), ("ctx", gw_out.reshape(C, S * nb, hn))],
         )
         out = parts((mid + got).astype(BF))
         gw_qkv = mm(n1, dqkv, 0, 0).astype(BF)
@@ -1117,7 +1139,8 @@
             S, C, T, 8, dqkv, wq, tok, dmid, gains[:1], [("shard", out), ("shard", gw_gateup)]
         )
         gtok, out, norms, gbias, gw_gateup, gw_down, gw_qkv, gw_out = finish(
-            S, C, T, 10, low, out, [stats1, stats2], gbias, gw_gateup, gw_down, gw_qkv, gw_out
+            S, C, T, 10, low, out, [stats1, stats2], gbias, gw_gateup, gw_down, gw_qkv,
+            jnp.sum(gw_out.astype(F32), axis=0).astype(BF).reshape(S, nb, hn),
         )
         if not ordered(D, S, C):
             gtok, out = unpermute(gtok), unpermute(out)

time: 689 us -> 651 us (0.945)
  Pallas kernels: 581 us -> 544 us
    pallas_call x9, Pallas kernels: 553 us -> 511 us  [comm(): pl.pallas_call(body, out_shape=[shape for shape, _ in outs] + ride.shapes...]
    unnamed x32 -> x58, local copies, waits for them, and re-layouts: 10.4 us -> 16.4 us
  transfers between devices with their start and end apart: 7 -> 6, of which waited for: 1 -> 0; matrix products, arithmetic and copies ran while one was open for 10% -> 10% of each run, Pallas kernels for 76% -> 75%
where the time goes in v10:
time: 651 us; the launch traced here: 647 us
  Pallas kernels  544 us (84%)
  matrix products  41.4 us (6%)
  local copies, waits for them, and re-layouts  38.5 us (6%)
  between operations  14.7 us (2%)
    pallas_call x9, Pallas kernels, comm(): pl.pallas_call(body, out_shape=[shape for shape, _ in outs] + ride.shapes...  511 us
    dot_general x5, matrix products, mm(): lax.dot_general(a, b, (((ca,), (cb,)), ((), ())), preferred_element_type=...  41.4 us
    pallas_call x1, Pallas kernels, attend(): pl.pallas_call(attend_kernel, in_specs=[pl.BlockSpec(memory_space=pltpu.S...  20.3 us
    unnamed x58, local copies, waits for them, and re-layouts  16.4 us
  transfers between devices with their start and end apart: 6, of which 0 were waited for; matrix products, arithmetic and copies ran while one was open for 10% of the time, Pallas kernels for 75%

profile of v10, /device:TPU:9, one launch (start us, length us, event | category | flops | bytes accessed | tf_op | source)
XLA Modules:
  0.0 646.8 jit_solution(11437235588473368333)
XLA Ops:
  8.9 1.8 copy.58
  10.7 2.3 copy.61
  12.9 1.9 copy.59
  14.9 1.5 copy.63.refs_3_
  16.5 1.5 constant_dynamic-slice_fusion.3
  18.9 1.2 reshape.193.refs_5_
  20.9 1.2 reshape.190.refs_1_
  22.8 58.1 %exchange.1 = (f32[2,4,4,8,128]{4,3,2,1,0:T(8,128)}, bf16[4,192,512]{2,1,0:T(8,128)(2,1)}, bf16[4,192,512]{2,1,0:T(8,128)(2,1)}, bf16[4,128,256]{2,1,0:T(8,128)(...) custom-call(f32[4,4,8,128]{3,2,1,0:T(8,128)} %broadcast_in_dim.27.refs_0_, ...), custom_call_target="tpu_custom_call" | custom-call | bytes 120000000 | tf_op jit(solution)/shard_map/exchange/pallas_call | solution.py:108
  84.7 35.1 %gather_columns.2 = (bf16[4,2,192,2048]{3,2,1,0:T(8,128)(2,1)}, bf16[4,512,256]{2,1,0:T(8,128)(2,1)}) custom-call(bf16[4,192,512]{2,1,0:T(8,128)(2,1)} %get-tuple-element.60.refs_0_, bf16[512,256]{1,0:T(8,128)(2,1)} %bitcast.148), custom_call_target="tpu_custom_call" | custom-call | bytes 120000000 | tf_op jit(solution)/shard_map/gather_columns/pallas_call | solution.py:108
  120.5 50.6 %project.1 = (bf16[1536,2048]{1,0:T(8,128)(2,1)}, f32[1536,768]{1,0:T(8,128)}, bf16[4,4,128,768]{3,2,1,0:T(8,128)(2,1)}) custom-call(bf16[1536,2048]{1,0:T(8,128)(2,1)} %bitcast.110, bf16[4,3,128,1024]{3,2,1,0:T(8,128)(2,1)} %bitcast.126, f32[1,2048]{1,0:T(1,128)} %bitcast.151, f32[1,2048]{1,0:T(1,128)} %bitcast.156, f32[1,768]{1,0:T(1,128)} %reshape.202.refs_4_), custom_call_target="tpu_custom_call" | custom-call | bytes 120000000 | tf_op jit(solution)/shard_map/project/pallas_call | solution.py:108
  171.1 20.3 %attend.1 = (bf16[1536,256]{1,0:T(8,128)(2,1)S(1)}, bf16[1536,256]{1,0:T(8,128)(2,1)S(1)}, bf16[1536,256]{1,0:T(8,128)(2,1)S(1)}, bf16[1536,256]{1,0:T(8,128)(2,1)S(1)}, f32[4,1536]{1,0:T(4,128)S(1)}) custom-call(s32[3]{0:T(128)S(1)} %and_select_fusion.first_ref, f32[1536,768]{1,0:T(8,128)} %get-tuple-element.63.qkv_ref, f32[256,128]{1,0:T(8,128)S(1)} %copy-done.7, ...), custom_call_target="tpu_custom_call" | custom-call | tf_op jit(solution)/shard_map/attend/pallas_call | solution.py:914
  195.5 67.9 %sum_norm_gather.1 = (f32[192,2048]{1,0:T(8,128)}, bf16[8,192,2048]{2,1,0:T(8,128)(2,1)}, bf16[4,192,512]{2,1,0:T(8,128)(2,1)}) custom-call(bf16[8,192,256]{2,1,0:T(8,128)(2,1)} %bitcast.109, bf16[2048,256]{1,0:T(8,128)(2,1)} %bitcast.137, bf16[8,192,2048]{2,1,0:T(8,128)(2,1)} %bitcast.111, f32[1,2048]{1,0:T(1,128)} %bitcast.153, f32[1,2048]{1,0:T(1,128)} %bitcast.155, ...), custom_call_target="tpu_custom_call" | custom-call | bytes 120000000 | tf_op jit(solution)/shard_map/sum_norm_gather/pallas_call | solution.py:108
  263.4 36.3 %gather_columns.3 = (bf16[4,2,192,2048]{3,2,1,0:T(8,128)(2,1)}, f32[1536,1408]{1,0:T(8,128)}, bf16[1536,704]{1,0:T(8,128)(2,1)}) custom-call(bf16[4,192,512]{2,1,0:T(8,128)(2,1)} %get-tuple-element.67.refs_0_, bf16[1536,2048]{1,0:T(8,128)(2,1)} %bitcast.117, bf16[2048,1408]{1,0:T(8,128)(2,1)} %all-gather.6.cloned.1.call-done.refs_2_.refs_1_), custom_call_target="tpu_custom_call" | custom-call | bytes 120000000 | tf_op jit(solution)/shard_map/gather_columns/pallas_call | solution.py:108
  299.7 9.8 %convolution_convert_fusion.2 = bf16[2048,704]{0,1:T(8,128)(2,1)} fusion(bf16[1536,2048]{1,0:T(8,128)(2,1)} %bitcast.113, bf16[1536,704]{1,0:T(8,128)(2,1)} %get-tuple-element.70), kind=kOutput, calls=%fused_computation.2 | convolution fusion | flops 4430626816 | bytes 11337728 | tf_op jit(solution)/shard_map/dot_general | solution.py:26
  309.6 1.9 copy-done
  311.5 12.6 %gates_back.1 = bf16[1536,1408]{1,0:T(8,128)(2,1)} custom-call(bf16[1536,2048]{1,0:T(8,128)(2,1)} %bitcast.114, bf16[2048,704]{1,0:T(8,128)(2,1)S(1)} %copy-done, f32[1536,1408]{1,0:T(8,128)} %get-tuple-element.77.gu_ref), custom_call_target="tpu_custom_call" | custom-call | tf_op jit(solution)/shard_map/gates_back/pallas_call | solution.py:513
  324.1 13.8 %convolution_convert_fusion = bf16[2048,1408]{1,0:T(8,128)(2,1)} fusion(bf16[1536,2048]{1,0:T(8,128)(2,1)S(1)} %bitcast.118, bf16[1536,1408]{1,0:T(8,128)(2,1)} %gates_back.1), kind=kOutput, calls=%fused_computation | convolution fusion | flops 8861253632 | bytes 16384000 | tf_op jit(solution)/shard_map/dot_general | solution.py:26
  338.0 79.1 %sum_back_gather.1 = (f32[192,2048]{1,0:T(8,128)}, bf16[8,192,2048]{2,1,0:T(8,128)(2,1)}, f32[2,2048]{1,0:T(2,128)}) custom-call(bf16[8,192,1408]{2,1,0:T(8,128)(2,1)} %bitcast.116, bf16[2048,1408]{1,0:T(8,128)(2,1)} %all-gather.6.cloned.1.call-done.refs_2_.refs_1_, f32[192,2048]{1,0:T(8,128)} %get-tuple-element.79.refs_2_, bf16[8,192,2048]{2,1,0:T(8,128)(2,1)} %bitcast.115, ...), custom_call_target="tpu_custom_call" | custom-call | bytes 120000000 | tf_op jit(solution)/shard_map/sum_back_gather/pallas_call | solution.py:108
  417.1 5.9 convolution_convert_fusion.4
  423.0 2.8 convolution_convert_fusion.3.refs_6_
  425.8 2.3 copy.66
  428.0 63.8 %attend_back.1 = (bf16[1536,768]{1,0:T(8,128)(2,1)}, f32[1,768]{1,0:T(1,128)}, f32[192,2048]{1,0:T(8,128)}, bf16[4,128,704]{2,1,0:T(8,128)(2,1)}, bf16[4,512,256]{2,1,0:T(8,128)(2,1)}) custom-call(bf16[8,192,704]{2,1,0:T(8,128)(2,1)} %bitcast.131, bf16[2048,704]{1,0:T(8,128)(2,1)} %all-gather.8.cloned.1.call-done.wd_ref.refs_1_, ...), custom_call_target="tpu_custom_call" | custom-call | bytes 120000000 | tf_op jit(solution)/shard_map/attend_back/pallas_call | solution.py:108
  491.8 9.2 %convolution_convert_fusion.1 = bf16[2048,768]{1,0:T(8,128)(2,1)} fusion(bf16[1536,2048]{1,0:T(8,128)(2,1)} %get-tuple-element.86, bf16[1536,768]{1,0:T(8,128)(2,1)} %get-tuple-element.87), kind=kOutput, calls=%fused_computation.1 | convolution fusion | flops 4833411072 | bytes 11796480 | tf_op jit(solution)/shard_map/dot_general | solution.py:26
  501.0 1.4 copy-done.13
  504.0 2.1 reduce_sum.22
  506.2 60.4 %sum_back.1 = (bf16[192,2048]{1,0:T(8,128)(2,1)}, f32[2,2048]{1,0:T(2,128)}, bf16[4,192,512]{2,1,0:T(8,128)(2,1)}, bf16[4,128,1408]{2,1,0:T(8,128)(2,1)}) custom-call(bf16[8,192,768]{2,1,0:T(8,128)(2,1)} %bitcast.130, bf16[2048,768]{1,0:T(8,128)(2,1)} %bitcast.122, bf16[8,192,2048]{2,1,0:T(8,128)(2,1)} %bitcast.112, f32[192,2048]{1,0:T(8,128)} %get-tuple-element.89.refs_3_, ...), custom_call_target="tpu_custom_call" | custom-call | bytes 120000000 | tf_op jit(solution)/shard_map/sum_back/pallas_call | solution.py:108
  566.6 59.6 %finish.1 = (bf16[2,192,2048]{2,1,0:T(8,128)(2,1)}, bf16[2,192,2048]{2,1,0:T(8,128)(2,1)}, f32[4,128]{1,0:T(4,128)}, f32[4,6,128]{2,1,0:T(8,128)}, f32[128,2,281...) custom-call(bf16[192,2048]{1,0:T(8,128)(2,1)} %get-tuple-element.92.refs_0_, ...), custom_call_target="tpu_custom_call" | custom-call | bytes 120000000 | tf_op jit(solution)/shard_map/finish/pallas_call | solution.py:108
  626.2 1.4 slice_bitcast_fusion
  629.6 3.6 bitcast_convert_fusion
  633.1 1.1 copy.79
  634.3 1.1 copy.80
  636.3 1.6 copy.82
  (106 shorter events, 19.2 us)
Async XLA Ops:
  7.2 5.7 copy-start.18
  7.2 113.3 %all-gather.4.cloned.1.call-start = ((), (), s32[]{:S(2)}) async-start(), calls=%async_computation.3 | async-start | bytes 3932160 | tf_op jit(solution)/shard_map/all_gather | solution.py:1082
  7.9 255.5 %all-gather.6.cloned.1.call-start = ((), (), s32[]{:S(2)}) async-start(), calls=%async_computation.4 | async-start | bytes 7208960 | tf_op jit(solution)/shard_map/all_gather | solution.py:1070
  18.8 3.3 copy-start.25
  18.9 3.3 copy-start.22
  18.9 3.3 copy-start.23
  81.0 228.5 %all-gather.8.cloned.1.call-start = ((), (), s32[]{:S(2)}) async-start(), calls=%async_computation.5 | async-start | bytes 3932160 | tf_op jit(solution)/shard_map/all_gather | solution.py:1070
  81.7 344.0 %reduce-scatter.4.cloned.1.call-start = ((), (), s32[]{:S(2)}) async-start(), calls=%async_computation.6 | async-start | bytes 3604480 | tf_op jit(solution)/shard_map/reduce_scatter | solution.py:1073
  83.6 87.5 %copy-start.8 = (s32[1,1536]{1,0:T(1,128)}, s32[1,1536]{1,0:T(1,128)S(1)}, u32[]{:S(2)}) copy-start(s32[1,1536]{1,0:T(1,128)S(1)} %broadcast_in_dim.29.begin_ref.refs_12_) | copy-start | bytes 18436
  120.5 50.6 %copy-start.6 = (f32[256,128]{1,0:T(8,128)S(1)}, f32[256,128]{1,0:T(8,128)}, u32[]{:S(2)}) copy-start(f32[256,128]{1,0:T(8,128)} %constant.67.clone.sin_ref.refs_9_) | copy-start | bytes 393220
  120.5 50.6 %copy-start.7 = (f32[256,128]{1,0:T(8,128)S(1)}, f32[256,128]{1,0:T(8,128)}, u32[]{:S(2)}) copy-start(f32[256,128]{1,0:T(8,128)} %constant.66.clone.cos_ref.refs_8_) | copy-start | bytes 393220
  120.5 50.6 %copy-start.10 = (f32[6,128]{1,0:T(8,128)S(1)}, f32[6,128]{1,0:T(8,128)}, u32[]{:S(2)}) copy-start(f32[6,128]{1,0:T(8,128)} %constant.69.clone.sinf_ref.refs_11_) | copy-start | bytes 9220
  120.5 50.6 %copy-start.11 = (f32[6,128]{1,0:T(8,128)S(1)}, f32[6,128]{1,0:T(8,128)}, u32[]{:S(2)}) copy-start(f32[6,128]{1,0:T(8,128)} %constant.68.clone.cosf_ref.refs_10_) | copy-start | bytes 9220
  191.4 0.9 copy-start.1
  192.3 0.9 copy-start.3
  193.2 0.9 copy-start.4
  194.1 0.9 copy-start.5
  194.9 0.6 copy-start.9
  309.5 196.6 %reduce-scatter.6.cloned.1.call-start = ((), (), s32[]{:S(2)}) async-start(), calls=%async_computation.7 | async-start | bytes 7208960 | tf_op jit(solution)/shard_map/reduce_scatter | solution.py:1073
  309.6 1.9 copy-start
  311.5 12.6 %copy-start.12 = (bf16[8,192,2048]{2,1,0:T(8,128)(2,1)S(1)}, bf16[8,192,2048]{2,1,0:T(8,128)(2,1)}, u32[]{:S(2)}) copy-start(bf16[8,192,2048]{2,1,0:T(8,128)(2,1)} %get-tuple-element.68) | copy-start | bytes 18874372
  337.9 228.7 %reduce-scatter.8.cloned.1.call-start = ((), (), s32[]{:S(2)}) async-start(), calls=%async_computation.8 | async-start | bytes 3932160 | tf_op jit(solution)/shard_map/reduce_scatter | solution.py:1073
  338.0 79.1 %copy-start.2 = (bf16[1536,256]{1,0:T(8,128)(2,1)S(1)}, bf16[1536,256]{1,0:T(8,128)(2,1)}, u32[]{:S(2)}) copy-start(bf16[1536,256]{1,0:T(8,128)(2,1)} %copy-done.1) | copy-start | bytes 2359300
  417.1 5.9 copy-start.20
  417.1 5.9 copy-start.24
  501.0 1.4 copy-start.13
  501.0 1.9 copy-start.17
  626.2 6.9 %copy-start.16 = (bf16[2,192,2048]{2,1,0:T(8,128)(2,1)S(1)}, bf16[2,192,2048]{2,1,0:T(8,128)(2,1)}, u32[]{:S(2)}) copy-start(bf16[2,192,2048]{2,1,0:T(8,128)(2,1)} %get-tuple-element.101) | copy-start | bytes 4718596
  629.6 4.7 copy-start.15
  633.1 2.3 copy-start.21
  633.1 3.1 copy-start.14
  636.2 2.4 copy-start.19
Sparse Core Ops, SparseCore 0:
  9.6 79.0 all-gather.3
  90.2 126.8 all-gather.5
  218.8 70.1 all-gather.7
  309.7 53.8 reduce-scatter.3
  365.7 123.3 reduce-scatter.5
  501.2 59.6 reduce-scatter.7

commit v11 on v10

--- a/solution.py
+++ b/solution.py
@@ -1,4 +1,5 @@
 import functools
+import math
 
 import jax
 import jax.numpy as jnp
@@ -93,8 +94,17 @@
     pl.semaphore_wait(barrier, len(peers))
 
 
+def in_vmem(shape, dtype):
+    *lead, tall, wide = (1, 1) + tuple(shape)
+    tile = 32 // np.dtype(dtype).itemsize
+    return math.prod(lead) * -(-tall // tile) * tile * -(-wide // 128) * 128 * np.dtype(dtype).itemsize
+
+
 def comm(kernel, S, C, number, name, args, in_specs, outs, scratch, riders=()):
     ride = Riders(S, C, riders)
+    held = [x for x, spec in zip(args, in_specs) if spec is IN_VMEM] + [x for x, spec in outs if spec is IN_VMEM]
+    held += ride.arrays + [x for x in scratch if getattr(x, "memory_space", None) == pltpu.VMEM]
+    room = sum(in_vmem(x.shape, x.dtype) for x in held) + (10 << 20)
     na, nr, no, ns = len(args), len(ride.axes), len(outs), len(scratch)
 
     def body(*refs):
@@ -112,7 +122,7 @@
         out_specs=[spec for _, spec in outs] + [ANY] * nr,
         scratch_shapes=list(scratch) + ride.scratch,
         compiler_params=pltpu.CompilerParams(
-            collective_id=number, has_side_effects=True, vmem_limit_bytes=56 << 20
+            collective_id=number, has_side_effects=True, vmem_limit_bytes=min(room, 60 << 20)
         ),
         cost_estimate=pl.CostEstimate(flops=0, bytes_accessed=120_000_000, transcendentals=0),
         name=name,
@@ -341,18 +351,14 @@
     def to_other(e):
         return remote(away.at[e], sib.at[e], asend.at[e], arecv.at[e], other)
 
-    def first(i, _):
-        e = S - 1 - i
-
+    def for_other(e):
         def store(w, value):
             away[e, :, w] = value.astype(BF)
 
         product(e, 1 - c, store)
         to_other(e).start()
-        return 0
-
-    lax.fori_loop(0, S, first, 0)
-
+
+    for_other(S - 1)
     top, low = pl.ds(0, half), pl.ds(half, half)
     started = []
 
@@ -362,6 +368,8 @@
         started.append(copy)
 
     for e in range(S - 1, -1, -1):
+        if e:
+            for_other(e - 1)
         to_other(e).wait()
 
         def store(w, value):
@@ -777,18 +785,18 @@
         for i in range(2):
             for q in range(S):
                 gateup_out[:, i, q * fn : (q + 1) * fn] = gateup_ref[q, :, i * fn : (i + 1) * fn].astype(F32)
+        for copy in x_hop:
+            copy.wait()
+        x_hop = arrive(xbuf2, x_out, 1)
+        for copy in y_hop:
+            copy.wait()
+        y_last = both(y_out, 1)
         for copy in moves:
             copy.wait()
         for q in range(S):
             o_out[q * hn : (q + 1) * hn, :] = o_buf[q].astype(F32).T
             for i in range(3):
                 qkv_out[i, :, q * hn : (q + 1) * hn] = qkv_buf[q, :, i * hn : (i + 1) * hn].astype(F32)
-        for copy in x_hop:
-            copy.wait()
-        x_hop = arrive(xbuf2, x_out, 1)
-        for copy in y_hop:
-            copy.wait()
-        y_last = both(y_out, 1)
         for copy in x_hop:
             copy.wait()
         x_last = both(x_out, 2)

time: 651 us -> 703 us (1.080)
  local copies, waits for them, and re-layouts: 38.5 us -> 115 us
  Pallas kernels: 544 us -> 522 us
    unnamed x58 -> x172, local copies, waits for them, and re-layouts: 16.4 us -> 88.4 us
    pallas_call x9, Pallas kernels: 511 us -> 489 us  [comm(): pl.pallas_call(body, out_shape=[shape for shape, _ in outs] + ride.shapes...]
  transfers between devices with their start and end apart: 6 -> 6, of which waited for: 0 -> 0; matrix products, arithmetic and copies ran while one was open for 10% -> 10% of each run, Pallas kernels for 75% -> 67%
where the time goes in v11:
time: 703 us; the launch traced here: 699 us
  Pallas kernels  522 us (74%)
  local copies, waits for them, and re-layouts  115 us (16%)
  matrix products  38.6 us (5%)
  between operations  14.8 us (2%)
    pallas_call x9, Pallas kernels, comm(): pl.pallas_call(body, out_shape=[shape for shape, _ in outs] + ride.shapes...  489 us
    unnamed x172, local copies, waits for them, and re-layouts  88.4 us
    dot_general x5, matrix products, mm(): lax.dot_general(a, b, (((ca,), (cb,)), ((), ())), preferred_element_type=...  38.6 us
    pallas_call x1, Pallas kernels, attend(): pl.pallas_call(attend_kernel, in_specs=[pl.BlockSpec(memory_space=pltpu.S...  20.1 us
  transfers between devices with their start and end apart: 6, of which 0 were waited for; matrix products, arithmetic and copies ran while one was open for 10% of the time, Pallas kernels for 67%

profile of v11, /device:TPU:9, one launch (start us, length us, event | category | flops | bytes accessed | tf_op | source)
XLA Modules:
  0.0 698.6 jit_solution(296292805568547701)
XLA Ops:
  11.3 3.8 copy.59
  18.2 2.8 constant_dynamic-slice_fusion.3
  21.0 2.3 reshape.192
  26.2 3.0 reshape.189
  29.2 2.3 copy.57
  31.5 2.3 reshape.190.refs_1_
  35.1 54.1 %exchange.1 = (f32[2,4,4,8,128]{4,3,2,1,0:T(8,128)S(1)}, bf16[4,192,512]{2,1,0:T(8,128)(2,1)}, bf16[4,192,512]{2,1,0:T(8,128)(2,1)S(1)}, bf16[4,128,256]{2,1,0:T...) custom-call(f32[4,4,8,128]{3,2,1,0:T(8,128)S(1)} %broadcast_in_dim.2, ...), custom_call_target="tpu_custom_call" | custom-call | bytes 120000000 | tf_op jit(solution)/shard_map/exchange/pallas_call | solution.py:118
  96.1 50.2 %gather_columns.2 = (bf16[4,2,192,2048]{3,2,1,0:T(8,128)(2,1)S(1)}, bf16[4,512,256]{2,1,0:T(8,128)(2,1)S(1)}) custom-call(bf16[4,192,512]{2,1,0:T(8,128)(2,1)S(1)} %copy-done.55, bf16[512,256]{1,0:T(8,128)(2,1)S(1)} %bitcast.142), custom_call_target="tpu_custom_call" | custom-call | bytes 120000000 | tf_op jit(solution)/shard_map/gather_columns/pallas_call | solution.py:118
  146.2 2.6 copy-done
  151.5 41.3 %project.1 = (bf16[1536,2048]{1,0:T(8,128)(2,1)S(1)}, f32[1536,768]{1,0:T(8,128)S(1)}, bf16[4,4,128,768]{3,2,1,0:T(8,128)(2,1)S(1)}) custom-call(bf16[1536,2048]{1,0:T(8,128)(2,1)} %bitcast.109, bf16[4,3,128,1024]{3,2,1,0:T(8,128)(2,1)S(1)} %bitcast.124, f32[1,2048]{1,0:T(1,128)S(1)} %bitcast.143, f32[1,2048]{1,0:T(1,128)S(1)} %bitcast.148, ...), custom_call_target="tpu_custom_call" | custom-call | bytes 120000000 | tf_op jit(solution)/shard_map/project/pallas_call | solution.py:118
  196.7 2.7 copy-done.76
  199.4 20.1 %attend.1 = (bf16[1536,256]{1,0:T(8,128)(2,1)S(1)}, bf16[1536,256]{1,0:T(8,128)(2,1)S(1)}, bf16[1536,256]{1,0:T(8,128)(2,1)S(1)}, bf16[1536,256]{1,0:T(8,128)(2,1)S(1)}, f32[4,1536]{1,0:T(4,128)S(1)}) custom-call(s32[3]{0:T(128)S(1)} %and_select_fusion.first_ref, f32[1536,768]{1,0:T(8,128)} %copy-done.10, f32[256,128]{1,0:T(8,128)S(1)} %copy-done.57, ...), custom_call_target="tpu_custom_call" | custom-call | tf_op jit(solution)/shard_map/attend/pallas_call | solution.py:922
  224.0 70.4 %sum_norm_gather.1 = (f32[192,2048]{1,0:T(8,128)S(1)}, bf16[8,192,2048]{2,1,0:T(8,128)(2,1)S(1)}, bf16[4,192,512]{2,1,0:T(8,128)(2,1)S(1)}) custom-call(bf16[8,192,256]{2,1,0:T(8,128)(2,1)S(1)} %bitcast.122, bf16[2048,256]{1,0:T(8,128)(2,1)S(1)} %bitcast.134, bf16[8,192,2048]{2,1,0:T(8,128)(2,1)S(1)} %bitcast.112, f32[1,2048]{1,0:T(1,128)S(1)} %bitcast.145, ...), custom_call_target="tpu_custom_call" | custom-call | bytes 120000000 | tf_op jit(solution)/shard_map/sum_norm_gather/pallas_call | solution.py:118
  294.4 2.6 copy-done.7
  297.9 2.6 copy-done.3
  300.5 2.8 copy-done.8
  304.5 34.8 %gather_columns.3 = (bf16[4,2,192,2048]{3,2,1,0:T(8,128)(2,1)S(1)}, f32[1536,1408]{1,0:T(8,128)}, bf16[1536,704]{1,0:T(8,128)(2,1)S(1)}) custom-call(bf16[4,192,512]{2,1,0:T(8,128)(2,1)S(1)} %copy-done.52, bf16[1536,2048]{1,0:T(8,128)(2,1)S(1)} %bitcast.118, bf16[2048,1408]{1,0:T(8,128)(2,1)S(1)} %copy-done.3), custom_call_target="tpu_custom_call" | custom-call | bytes 120000000 | tf_op jit(solution)/shard_map/gather_columns/pallas_call | solution.py:118
  339.3 2.6 copy-done.2
  342.7 6.2 convolution_convert_fusion.2
  350.8 12.6 %gates_back.1 = bf16[1536,1408]{1,0:T(8,128)(2,1)} custom-call(bf16[1536,2048]{1,0:T(8,128)(2,1)} %bitcast.115, bf16[2048,704]{1,0:T(8,128)(2,1)S(1)} %copy-done.6, f32[1536,1408]{1,0:T(8,128)} %get-tuple-element.77.gu_ref), custom_call_target="tpu_custom_call" | custom-call | tf_op jit(solution)/shard_map/gates_back/pallas_call | solution.py:521
  363.4 13.8 %convolution_convert_fusion = bf16[2048,1408]{1,0:T(8,128)(2,1)} fusion(bf16[1536,2048]{1,0:T(8,128)(2,1)S(1)} %bitcast.119, bf16[1536,1408]{1,0:T(8,128)(2,1)} %gates_back.1), kind=kOutput, calls=%fused_computation | convolution fusion | flops 8861253632 | bytes 16384000 | tf_op jit(solution)/shard_map/dot_general | solution.py:27
  377.3 2.6 copy-done.4
  379.9 2.3 copy-done.5
  382.2 70.5 %sum_back_gather.1 = (f32[192,2048]{1,0:T(8,128)S(1)}, bf16[8,192,2048]{2,1,0:T(8,128)(2,1)}, f32[2,2048]{1,0:T(2,128)S(1)}) custom-call(bf16[8,192,1408]{2,1,0:T(8,128)(2,1)S(1)} %bitcast.117, bf16[2048,1408]{1,0:T(8,128)(2,1)S(1)} %copy-done.4, f32[192,2048]{1,0:T(8,128)S(1)} %get-tuple-element.79.refs_2_, bf16[8,192,2048]{2,1,0:T(8,128)(2,1)} %bitcast.116, ...), custom_call_target="tpu_custom_call" | custom-call | bytes 120000000 | tf_op jit(solution)/shard_map/sum_back_gather/pallas_call | solution.py:118
  452.7 6.3 convolution_convert_fusion.4
  459.0 2.7 convolution_convert_fusion.3.refs_6_
  471.9 58.3 %attend_back.1 = (bf16[1536,768]{1,0:T(8,128)(2,1)S(1)}, f32[1,768]{1,0:T(1,128)S(1)}, f32[192,2048]{1,0:T(8,128)S(1)}, bf16[4,128,704]{2,1,0:T(8,128)(2,1)S(1)}, bf16[4,512,256]{2,1,0:T(8,128)(2,1)S(1)}) custom-call(bf16[8,192,704]{2,1,0:T(8,128)(2,1)} %bitcast.128, bf16[2048,704]{1,0:T(8,128)(2,1)} %all-gather.8.cloned.1.call-done.wd_ref.refs_1_, ...), custom_call_target="tpu_custom_call" | custom-call | bytes 120000000 | tf_op jit(solution)/shard_map/attend_back/pallas_call | solution.py:118
  533.3 9.7 %convolution_convert_fusion.1 = bf16[2048,768]{1,0:T(8,128)(2,1)} fusion(bf16[1536,2048]{1,0:T(8,128)(2,1)} %copy-done.76, bf16[1536,768]{1,0:T(8,128)(2,1)S(1)} %get-tuple-element.87), kind=kOutput, calls=%fused_computation.1 | convolution fusion | flops 4833411072 | bytes 11796480 | tf_op jit(solution)/shard_map/dot_general | solution.py:27
  548.0 2.8 copy-done.1
  555.7 55.1 %sum_back.1 = (bf16[192,2048]{1,0:T(8,128)(2,1)S(1)}, f32[2,2048]{1,0:T(2,128)S(1)}, bf16[4,192,512]{2,1,0:T(8,128)(2,1)S(1)}, bf16[4,128,1408]{2,1,0:T(8,128)(2,1)S(1)}) custom-call(bf16[8,192,768]{2,1,0:T(8,128)(2,1)S(1)} %bitcast.127, bf16[2048,768]{1,0:T(8,128)(2,1)S(1)} %bitcast.121, bf16[8,192,2048]{2,1,0:T(8,128)(2,1)S(1)} %bitcast.113, ...), custom_call_target="tpu_custom_call" | custom-call | bytes 120000000 | tf_op jit(solution)/shard_map/sum_back/pallas_call | solution.py:118
  619.6 54.6 %finish.1 = (bf16[2,192,2048]{2,1,0:T(8,128)(2,1)S(1)}, bf16[2,192,2048]{2,1,0:T(8,128)(2,1)S(1)}, f32[4,128]{1,0:T(4,128)S(1)}, f32[4,6,128]{2,1,0:T(8,128)S(1)...) custom-call(bf16[192,2048]{1,0:T(8,128)(2,1)S(1)} %copy-done.47, ...), custom_call_target="tpu_custom_call" | custom-call | bytes 120000000 | tf_op jit(solution)/shard_map/finish/pallas_call | solution.py:118
  681.4 3.6 bitcast_convert_fusion
  (221 shorter events, 79.2 us)
Async XLA Ops:
  7.2 142.3 %all-gather.4.cloned.1.call-start = ((), (), s32[]{:S(2)}) async-start(), calls=%async_computation.3 | async-start | bytes 3932160 | tf_op jit(solution)/shard_map/all_gather | solution.py:1090
  7.9 290.0 %all-gather.6.cloned.1.call-start = ((), (), s32[]{:S(2)}) async-start(), calls=%async_computation.4 | async-start | bytes 7208960 | tf_op jit(solution)/shard_map/all_gather | solution.py:1078
  24.5 9.4 %copy-start.80 = (s32[1,3]{1,0:T(1,128)S(1)}, s32[1,3]{1,0:T(1,128)}, u32[]{:S(2)}) copy-start(s32[1,3]{1,0:T(1,128)} %param.19) | copy-start | bytes 40
  24.5 9.4 %copy-start.77 = (bf16[1,2,128]{2,1,0:T(2,128)(2,1)S(1)}, bf16[1,2,128]{2,1,0:T(2,128)(2,1)}, u32[]{:S(2)}) copy-start(bf16[1,2,128]{2,1,0:T(2,128)(2,1)} %param.26) | copy-start | bytes 1540
  24.5 9.4 %copy-start.78 = (bf16[1,2,128]{2,1,0:T(2,128)(2,1)S(1)}, bf16[1,2,128]{2,1,0:T(2,128)(2,1)}, u32[]{:S(2)}) copy-start(bf16[1,2,128]{2,1,0:T(2,128)(2,1)} %param.25) | copy-start | bytes 1540
  93.7 255.1 %all-gather.8.cloned.1.call-start = ((), (), s32[]{:S(2)}) async-start(), calls=%async_computation.5 | async-start | bytes 3932160 | tf_op jit(solution)/shard_map/all_gather | solution.py:1078
  94.4 367.3 %reduce-scatter.4.cloned.1.call-start = ((), (), s32[]{:S(2)}) async-start(), calls=%async_computation.6 | async-start | bytes 3604480 | tf_op jit(solution)/shard_map/reduce_scatter | solution.py:1081
  95.5 103.9 %copy-start.63 = (s32[1,1536]{1,0:T(1,128)}, s32[1,1536]{1,0:T(1,128)S(1)}, u32[]{:S(2)}) copy-start(s32[1,1536]{1,0:T(1,128)S(1)} %broadcast_in_dim.29.begin_ref.refs_12_) | copy-start | bytes 18436
  149.4 73.4 %slice-start = ((s8[6291456]{0:T(1024)(128)(4,1)}), s8[4194304]{0:T(1024)(128)(4,1)S(1)}, s32[]{:S(2)}) async-start(s8[6291456]{0:T(1024)(128)(4,1)} %bitcast.110), calls=%async_computation.9 | async-start | bytes 8388608
  151.5 47.8 %copy-start.56 = (f32[256,128]{1,0:T(8,128)S(1)}, f32[256,128]{1,0:T(8,128)}, u32[]{:S(2)}) copy-start(f32[256,128]{1,0:T(8,128)} %constant.67.clone.sin_ref.refs_9_) | copy-start | bytes 393220
  151.5 47.8 %copy-start.57 = (f32[256,128]{1,0:T(8,128)S(1)}, f32[256,128]{1,0:T(8,128)}, u32[]{:S(2)}) copy-start(f32[256,128]{1,0:T(8,128)} %constant.66.clone.cos_ref.refs_8_) | copy-start | bytes 393220
  151.5 47.8 %copy-start.70 = (f32[6,128]{1,0:T(8,128)S(1)}, f32[6,128]{1,0:T(8,128)}, u32[]{:S(2)}) copy-start(f32[6,128]{1,0:T(8,128)} %constant.69.clone.sinf_ref.refs_11_) | copy-start | bytes 9220
  151.5 47.9 %copy-start.72 = (f32[6,128]{1,0:T(8,128)S(1)}, f32[6,128]{1,0:T(8,128)}, u32[]{:S(2)}) copy-start(f32[6,128]{1,0:T(8,128)} %constant.68.clone.cosf_ref.refs_10_) | copy-start | bytes 9220
  151.5 71.3 %slice-start.1 = ((s8[6291456]{0:T(1024)(128)(4,1)}), s8[2097152]{0:T(1024)(128)(4,1)S(1)}, s32[]{:S(2)}) async-start(s8[6291456]{0:T(1024)(128)(4,1)} %bitcast.110), calls=%async_computation.10 | async-start | bytes 4194304
  196.7 2.7 copy-start.76
  199.3 23.5 %copy-start.65 = (f32[1,16,128]{2,1,0:T(8,128)S(1)}, f32[1,16,128]{2,1,0:T(8,128)}, u32[]{:S(2)}) copy-start(f32[1,16,128]{2,1,0:T(8,128)} %get-tuple-element.109) | copy-start | bytes 24580
  300.5 2.8 copy-start.8
  339.3 2.6 copy-start.2
  339.3 3.3 copy-start.17
  348.9 198.8 %reduce-scatter.6.cloned.1.call-start = ((), (), s32[]{:S(2)}) async-start(), calls=%async_computation.7 | async-start | bytes 7208960 | tf_op jit(solution)/shard_map/reduce_scatter | solution.py:1081
  350.8 12.6 %copy-start.9 = (bf16[8,192,2048]{2,1,0:T(8,128)(2,1)S(1)}, bf16[8,192,2048]{2,1,0:T(8,128)(2,1)}, u32[]{:S(2)}) copy-start(bf16[8,192,2048]{2,1,0:T(8,128)(2,1)} %copy-done.7) | copy-start | bytes 18874372
  377.2 236.5 %reduce-scatter.8.cloned.1.call-start = ((), (), s32[]{:S(2)}) async-start(), calls=%async_computation.8 | async-start | bytes 3932160 | tf_op jit(solution)/shard_map/reduce_scatter | solution.py:1081
  377.2 2.6 copy-start.4
  452.7 6.3 copy-start.18
  452.7 6.3 copy-start.68
  452.7 6.3 copy-start.79
  459.0 4.1 copy-start.64
  547.9 2.8 copy-start.1
  555.7 58.0 %copy-start.69 = (f32[2,2048]{1,0:T(2,128)S(1)}, f32[2,2048]{1,0:T(2,128)}, u32[]{:S(2)}) copy-start(f32[2,2048]{1,0:T(2,128)} %copy-done.68) | copy-start | bytes 49156
  555.7 58.0 %copy-start.75 = (f32[1,768]{1,0:T(1,128)S(1)}, f32[1,768]{1,0:T(1,128)}, u32[]{:S(2)}) copy-start(f32[1,768]{1,0:T(1,128)} %copy-done.74) | copy-start | bytes 9220
  681.4 3.6 copy-start.23
  681.4 4.7 copy-start.21
  (57 other events, 76.0 us)
Sparse Core Ops, SparseCore 0:
  9.6 79.0 all-gather.3
  93.8 120.2 all-gather.5
  215.7 77.7 all-gather.7
  349.0 54.9 reduce-scatter.3
  406.2 121.6 reduce-scatter.5
  544.5 59.5 reduce-scatter.7

commit v12 on v11

--- a/solution.py
+++ b/solution.py
@@ -1,5 +1,4 @@
 import functools
-import math
 
 import jax
 import jax.numpy as jnp
@@ -94,17 +93,8 @@
     pl.semaphore_wait(barrier, len(peers))
 
 
-def in_vmem(shape, dtype):
-    *lead, tall, wide = (1, 1) + tuple(shape)
-    tile = 32 // np.dtype(dtype).itemsize
-    return math.prod(lead) * -(-tall // tile) * tile * -(-wide // 128) * 128 * np.dtype(dtype).itemsize
-
-
 def comm(kernel, S, C, number, name, args, in_specs, outs, scratch, riders=()):
     ride = Riders(S, C, riders)
-    held = [x for x, spec in zip(args, in_specs) if spec is IN_VMEM] + [x for x, spec in outs if spec is IN_VMEM]
-    held += ride.arrays + [x for x in scratch if getattr(x, "memory_space", None) == pltpu.VMEM]
-    room = sum(in_vmem(x.shape, x.dtype) for x in held) + (10 << 20)
     na, nr, no, ns = len(args), len(ride.axes), len(outs), len(scratch)
 
     def body(*refs):
@@ -122,7 +112,7 @@
         out_specs=[spec for _, spec in outs] + [ANY] * nr,
         scratch_shapes=list(scratch) + ride.scratch,
         compiler_params=pltpu.CompilerParams(
-            collective_id=number, has_side_effects=True, vmem_limit_bytes=min(room, 60 << 20)
+            collective_id=number, has_side_effects=True, vmem_limit_bytes=62 << 20
         ),
         cost_estimate=pl.CostEstimate(flops=0, bytes_accessed=120_000_000, transcendentals=0),
         name=name,
@@ -524,7 +514,7 @@
         in_specs=[spec(x.shape[1]) if rows else pl.BlockSpec(x.shape, lambda i: (0, 0)) for rows, x in arrays],
         out_specs=[spec(x.shape[1]) for x in outs],
         out_shape=outs,
-        compiler_params=pltpu.CompilerParams(vmem_limit_bytes=48 << 20),
+        compiler_params=pltpu.CompilerParams(vmem_limit_bytes=62 << 20),
         name=name,
     )(*[x for _, x in arrays])
 
@@ -925,7 +915,7 @@
         out_specs=[IN_VMEM] * 5,
         out_shape=[half] * 4 + [jax.ShapeDtypeStruct((wide // HEAD, rows), F32)],
         scratch_shapes=[pltpu.VMEM((wide, rows), BF)],
-        compiler_params=pltpu.CompilerParams(vmem_limit_bytes=48 << 20),
+        compiler_params=pltpu.CompilerParams(vmem_limit_bytes=62 << 20),
         name="attend",
     )(begin[0, ::size] // size, qkv, *turn_tables(rows), begin)
 

time: 703 us -> 649 us (0.923)
  local copies, waits for them, and re-layouts: 115 us -> 32.4 us
  Pallas kernels: 522 us -> 546 us
    unnamed x172 -> x36, local copies, waits for them, and re-layouts: 88.4 us -> 10.4 us
    pallas_call x9, Pallas kernels: 489 us -> 516 us  [comm(): pl.pallas_call(body, out_shape=[shape for shape, _ in outs] + ride.shapes...]
  transfers between devices with their start and end apart: 6 -> 6, of which waited for: 0 -> 0; matrix products, arithmetic and copies ran while one was open for 10% -> 10% of each run, Pallas kernels for 67% -> 75%
where the time goes in v12:
time: 649 us; the launch traced here: 645 us
  Pallas kernels  546 us (84%)
  matrix products  42.6 us (7%)
  local copies, waits for them, and re-layouts  32.4 us (5%)
  between operations  14.6 us (2%)
  other arithmetic  6.78 us (1%)
    pallas_call x9, Pallas kernels, comm(): pl.pallas_call(body, out_shape=[shape for shape, _ in outs] + ride.shapes...  516 us
    dot_general x5, matrix products, mm(): lax.dot_general(a, b, (((ca,), (cb,)), ((), ())), preferred_element_type=...  42.6 us
    pallas_call x1, Pallas kernels, attend(): pl.pallas_call(attend_kernel, in_specs=[pl.BlockSpec(memory_space=pltpu.S...  17 us
    pallas_call x1, Pallas kernels, by_rows(): pl.pallas_call(kernel, grid=(L // BLK,), in_specs=[spec(x.shape[1]) if ro...  13.2 us
  transfers between devices with their start and end apart: 6, of which 0 were waited for; matrix products, arithmetic and copies ran while one was open for 10% of the time, Pallas kernels for 75%

profile of v12, /device:TPU:9, one launch (start us, length us, event | category | flops | bytes accessed | tf_op | source)
XLA Modules:
  0.0 645.0 jit_solution(3324251677517495066)
XLA Ops:
  8.9 1.8 copy.58
  10.7 2.3 copy.61
  12.9 1.9 copy.59
  14.9 1.5 copy.63.refs_3_
  16.5 1.5 constant_dynamic-slice_fusion.3
  18.9 1.2 reshape.193.refs_5_
  20.9 1.2 reshape.190.refs_1_
  22.8 58.2 %exchange.1 = (f32[2,4,4,8,128]{4,3,2,1,0:T(8,128)}, bf16[4,192,512]{2,1,0:T(8,128)(2,1)}, bf16[4,192,512]{2,1,0:T(8,128)(2,1)}, bf16[4,128,256]{2,1,0:T(8,128)(...) custom-call(f32[4,4,8,128]{3,2,1,0:T(8,128)} %broadcast_in_dim.27.refs_0_, ...), custom_call_target="tpu_custom_call" | custom-call | bytes 120000000 | tf_op jit(solution)/shard_map/exchange/pallas_call | solution.py:108
  84.8 35.1 %gather_columns.2 = (bf16[4,2,192,2048]{3,2,1,0:T(8,128)(2,1)}, bf16[4,512,256]{2,1,0:T(8,128)(2,1)}) custom-call(bf16[4,192,512]{2,1,0:T(8,128)(2,1)} %get-tuple-element.60.refs_0_, bf16[512,256]{1,0:T(8,128)(2,1)} %bitcast.148), custom_call_target="tpu_custom_call" | custom-call | bytes 120000000 | tf_op jit(solution)/shard_map/gather_columns/pallas_call | solution.py:108
  121.0 50.4 %project.1 = (bf16[1536,2048]{1,0:T(8,128)(2,1)}, f32[1536,768]{1,0:T(8,128)}, bf16[4,4,128,768]{3,2,1,0:T(8,128)(2,1)}) custom-call(bf16[1536,2048]{1,0:T(8,128)(2,1)} %bitcast.109, bf16[4,3,128,1024]{3,2,1,0:T(8,128)(2,1)} %bitcast.126, f32[1,2048]{1,0:T(1,128)} %bitcast.151, f32[1,2048]{1,0:T(1,128)} %bitcast.156, f32[1,768]{1,0:T(1,128)} %reshape.202.refs_4_), custom_call_target="tpu_custom_call" | custom-call | bytes 120000000 | tf_op jit(solution)/shard_map/project/pallas_call | solution.py:108
  171.5 17.0 %attend.1 = (bf16[1536,256]{1,0:T(8,128)(2,1)}, bf16[1536,256]{1,0:T(8,128)(2,1)}, bf16[1536,256]{1,0:T(8,128)(2,1)}, bf16[1536,256]{1,0:T(8,128)(2,1)}, f32[4,1536]{1,0:T(4,128)}) custom-call(s32[3]{0:T(128)} %and_select_fusion.first_ref, f32[1536,768]{1,0:T(8,128)} %get-tuple-element.63.qkv_ref, f32[256,128]{1,0:T(8,128)} %constant.66.clone.cos_ref.refs_8_, ...), custom_call_target="tpu_custom_call" | custom-call | tf_op jit(solution)/shard_map/attend/pallas_call | solution.py:912
  188.5 73.1 %sum_norm_gather.1 = (f32[192,2048]{1,0:T(8,128)}, bf16[8,192,2048]{2,1,0:T(8,128)(2,1)}, bf16[4,192,512]{2,1,0:T(8,128)(2,1)}) custom-call(bf16[8,192,256]{2,1,0:T(8,128)(2,1)} %bitcast.122, bf16[2048,256]{1,0:T(8,128)(2,1)} %bitcast.137, bf16[8,192,2048]{2,1,0:T(8,128)(2,1)} %bitcast.110, f32[1,2048]{1,0:T(1,128)} %bitcast.153, f32[1,2048]{1,0:T(1,128)} %bitcast.155, ...), custom_call_target="tpu_custom_call" | custom-call | bytes 120000000 | tf_op jit(solution)/shard_map/sum_norm_gather/pallas_call | solution.py:108
  261.6 36.2 %gather_columns.3 = (bf16[4,2,192,2048]{3,2,1,0:T(8,128)(2,1)}, f32[1536,1408]{1,0:T(8,128)}, bf16[1536,704]{1,0:T(8,128)(2,1)}) custom-call(bf16[4,192,512]{2,1,0:T(8,128)(2,1)} %get-tuple-element.67.refs_0_, bf16[1536,2048]{1,0:T(8,128)(2,1)} %bitcast.116, bf16[2048,1408]{1,0:T(8,128)(2,1)} %all-gather.6.cloned.1.call-done.refs_2_.refs_1_), custom_call_target="tpu_custom_call" | custom-call | bytes 120000000 | tf_op jit(solution)/shard_map/gather_columns/pallas_call | solution.py:108
  297.8 9.8 %convolution_convert_fusion.2 = bf16[2048,704]{0,1:T(8,128)(2,1)} fusion(bf16[1536,2048]{1,0:T(8,128)(2,1)} %bitcast.112, bf16[1536,704]{1,0:T(8,128)(2,1)} %get-tuple-element.70), kind=kOutput, calls=%fused_computation.2 | convolution fusion | flops 4430626816 | bytes 11337728 | tf_op jit(solution)/shard_map/dot_general | solution.py:26
  307.7 13.2 %gates_back.1 = bf16[1536,1408]{1,0:T(8,128)(2,1)} custom-call(bf16[1536,2048]{1,0:T(8,128)(2,1)} %bitcast.113, bf16[2048,704]{1,0:T(8,128)(2,1)} %all-gather.8.cloned.1.call-done.wd_ref.refs_1_, f32[1536,1408]{1,0:T(8,128)} %get-tuple-element.77.gu_ref), custom_call_target="tpu_custom_call" | custom-call | tf_op jit(solution)/shard_map/gates_back/pallas_call | solution.py:511
  320.8 15.0 %convolution_convert_fusion = bf16[2048,1408]{1,0:T(8,128)(2,1)} fusion(bf16[1536,2048]{1,0:T(8,128)(2,1)} %bitcast.117, bf16[1536,1408]{1,0:T(8,128)(2,1)} %gates_back.1), kind=kOutput, calls=%fused_computation | convolution fusion | flops 8861253632 | bytes 16384000 | tf_op jit(solution)/shard_map/dot_general | solution.py:26
  335.9 76.3 %sum_back_gather.1 = (f32[192,2048]{1,0:T(8,128)}, bf16[8,192,2048]{2,1,0:T(8,128)(2,1)}, f32[2,2048]{1,0:T(2,128)}) custom-call(bf16[8,192,1408]{2,1,0:T(8,128)(2,1)} %bitcast.115, bf16[2048,1408]{1,0:T(8,128)(2,1)} %all-gather.6.cloned.1.call-done.refs_2_.refs_1_, f32[192,2048]{1,0:T(8,128)} %get-tuple-element.79.refs_2_, bf16[8,192,2048]{2,1,0:T(8,128)(2,1)} %bitcast.114, ...), custom_call_target="tpu_custom_call" | custom-call | bytes 120000000 | tf_op jit(solution)/shard_map/sum_back_gather/pallas_call | solution.py:108
  412.3 5.8 convolution_convert_fusion.4
  418.1 2.8 convolution_convert_fusion.3.refs_6_
  420.9 2.3 copy.66
  423.2 67.0 %attend_back.1 = (bf16[1536,768]{1,0:T(8,128)(2,1)}, f32[1,768]{1,0:T(1,128)}, f32[192,2048]{1,0:T(8,128)}, bf16[4,128,704]{2,1,0:T(8,128)(2,1)}, bf16[4,512,256]{2,1,0:T(8,128)(2,1)}) custom-call(bf16[8,192,704]{2,1,0:T(8,128)(2,1)} %bitcast.131, bf16[2048,704]{1,0:T(8,128)(2,1)} %all-gather.8.cloned.1.call-done.wd_ref.refs_1_, ...), custom_call_target="tpu_custom_call" | custom-call | bytes 120000000 | tf_op jit(solution)/shard_map/attend_back/pallas_call | solution.py:108
  490.2 9.2 %convolution_convert_fusion.1 = bf16[2048,768]{1,0:T(8,128)(2,1)} fusion(bf16[1536,2048]{1,0:T(8,128)(2,1)} %get-tuple-element.86, bf16[1536,768]{1,0:T(8,128)(2,1)} %get-tuple-element.87), kind=kOutput, calls=%fused_computation.1 | convolution fusion | flops 4833411072 | bytes 11796480 | tf_op jit(solution)/shard_map/dot_general | solution.py:26
  499.4 1.4 copy-done
  502.4 2.1 reduce_sum.22
  504.5 60.2 %sum_back.1 = (bf16[192,2048]{1,0:T(8,128)(2,1)}, f32[2,2048]{1,0:T(2,128)}, bf16[4,192,512]{2,1,0:T(8,128)(2,1)}, bf16[4,128,1408]{2,1,0:T(8,128)(2,1)}) custom-call(bf16[8,192,768]{2,1,0:T(8,128)(2,1)} %bitcast.130, bf16[2048,768]{1,0:T(8,128)(2,1)} %bitcast.121, bf16[8,192,2048]{2,1,0:T(8,128)(2,1)} %bitcast.111, f32[192,2048]{1,0:T(8,128)} %get-tuple-element.89.refs_3_, ...), custom_call_target="tpu_custom_call" | custom-call | bytes 120000000 | tf_op jit(solution)/shard_map/sum_back/pallas_call | solution.py:108
  564.8 59.6 %finish.1 = (bf16[2,192,2048]{2,1,0:T(8,128)(2,1)}, bf16[2,192,2048]{2,1,0:T(8,128)(2,1)}, f32[4,128]{1,0:T(4,128)}, f32[4,6,128]{2,1,0:T(8,128)}, f32[128,2,281...) custom-call(bf16[192,2048]{1,0:T(8,128)(2,1)} %get-tuple-element.92.refs_0_, ...), custom_call_target="tpu_custom_call" | custom-call | bytes 120000000 | tf_op jit(solution)/shard_map/finish/pallas_call | solution.py:108
  624.4 1.4 slice_bitcast_fusion
  625.8 1.1 reshape.222
  627.8 3.6 bitcast_convert_fusion
  631.3 1.1 copy.79
  632.5 1.1 copy.80
  634.5 1.6 copy.82
  (84 shorter events, 14.4 us)
Async XLA Ops:
  7.2 5.7 copy-start.6
  7.2 113.8 %all-gather.4.cloned.1.call-start = ((), (), s32[]{:S(2)}) async-start(), calls=%async_computation.3 | async-start | bytes 3932160 | tf_op jit(solution)/shard_map/all_gather | solution.py:1080
  7.9 253.7 %all-gather.6.cloned.1.call-start = ((), (), s32[]{:S(2)}) async-start(), calls=%async_computation.4 | async-start | bytes 7208960 | tf_op jit(solution)/shard_map/all_gather | solution.py:1068
  18.8 3.3 copy-start.14
  18.9 3.3 copy-start.11
  18.9 3.3 copy-start.12
  81.0 226.6 %all-gather.8.cloned.1.call-start = ((), (), s32[]{:S(2)}) async-start(), calls=%async_computation.5 | async-start | bytes 3932160 | tf_op jit(solution)/shard_map/all_gather | solution.py:1068
  81.8 339.1 %reduce-scatter.4.cloned.1.call-start = ((), (), s32[]{:S(2)}) async-start(), calls=%async_computation.6 | async-start | bytes 3604480 | tf_op jit(solution)/shard_map/reduce_scatter | solution.py:1071
  83.6 87.8 %copy-start.10 = (s32[1,1536]{1,0:T(1,128)}, s32[1,1536]{1,0:T(1,128)S(1)}, u32[]{:S(2)}) copy-start(s32[1,1536]{1,0:T(1,128)S(1)} %broadcast_in_dim.29.begin_ref.refs_12_) | copy-start | bytes 18436
  307.6 196.9 %reduce-scatter.6.cloned.1.call-start = ((), (), s32[]{:S(2)}) async-start(), calls=%async_computation.7 | async-start | bytes 7208960 | tf_op jit(solution)/shard_map/reduce_scatter | solution.py:1071
  335.9 228.9 %reduce-scatter.8.cloned.1.call-start = ((), (), s32[]{:S(2)}) async-start(), calls=%async_computation.8 | async-start | bytes 3932160 | tf_op jit(solution)/shard_map/reduce_scatter | solution.py:1071
  335.9 76.3 %copy-start.1 = (bf16[1536,256]{1,0:T(8,128)(2,1)S(1)}, bf16[1536,256]{1,0:T(8,128)(2,1)}, u32[]{:S(2)}) copy-start(bf16[1536,256]{1,0:T(8,128)(2,1)} %get-tuple-element.64.refs_5_) | copy-start | bytes 2359300
  412.3 5.8 copy-start.8
  412.3 5.8 copy-start.13
  499.4 1.4 copy-start
  499.4 1.9 copy-start.5
  624.4 6.9 %copy-start.4 = (bf16[2,192,2048]{2,1,0:T(8,128)(2,1)S(1)}, bf16[2,192,2048]{2,1,0:T(8,128)(2,1)}, u32[]{:S(2)}) copy-start(bf16[2,192,2048]{2,1,0:T(8,128)(2,1)} %get-tuple-element.101) | copy-start | bytes 4718596
  627.8 4.7 copy-start.3
  631.3 2.3 copy-start.9
  631.3 3.1 copy-start.2
  634.5 2.4 copy-start.7
Sparse Core Ops, SparseCore 0:
  9.6 79.0 all-gather.3
  90.2 133.2 all-gather.5
  225.2 63.8 all-gather.7
  307.8 54.0 reduce-scatter.3
  364.0 123.7 reduce-scatter.5
  499.5 59.4 reduce-scatter.7

commit v13 on v12

--- a/solution.py
+++ b/solution.py
@@ -119,30 +119,51 @@
     )(*args, *ride.arrays)
 
 
-def exchange(S, C, T, number, riders, tiles, rows=None):
+def exchange(S, C, T, number, riders, tiles, rows, beside, turned):
+    R, D = rows.shape
+    n, wide, nb = R // T, D // S, D // (S * C)
+    pieces = S if ordered(D, S, C) else 1
+    p, z, c = here()
+    if pieces == 1:
+        rows, beside = (
+            lax.dynamic_slice_in_dim(x, c * n, n, 0).reshape(n, S, C, nb).transpose(2, 0, 1, 3).reshape(S, n, wide)
+            for x in (rows, beside)
+        )
+    heights = [x.shape[0] // S for x in turned]
+
     def kernel(ride, ins, outs, scratch):
-        tile, got = ins[0], outs[0]
-        send, recv, bsend, brecv, own = scratch[:5]
+        tile, x_ref, y_ref, *raws = ins
+        got, x_buf, x_out, y_out, *turns = outs
+        send, recv, bsend, brecv, own, hsend, hrecv, hown, zsend, zrecv, zown, wsend, wrecv, wown, *stages = scratch
         p, z, c = here()
+        mates = [(p + k) % S for k in range(1, S)]
         everyone = [(i, j) for i in range(C) for j in range(S) if i or j]
+        peers = [{"shard": (p + j) % S, "ctx": (z + i) % C} for i, j in everyone]
         barrier = pltpu.get_barrier_semaphore()
-        peers = [{"shard": (p + j) % S, "ctx": (z + i) % C} for i, j in everyone] + [{"tp": 1 - c}]
-        for where in peers:
+        for where in peers + [{"tp": 1 - c}]:
             pl.semaphore_signal(barrier, inc=1, device_id=where, device_id_type=MESH)
-        pl.semaphore_wait(barrier, len(peers))
-
-        def turn_over(source, target, k, axis, size, me):
-            ssem, rsem, local = scratch[5:]
-            hop = [pltpu.make_async_copy(source.at[me], target.at[me], local.at[k])]
-            for j in range(1, size):
-                q = (me + j) % size
-                hop.append(remote(source.at[q], target.at[me], ssem.at[k, j - 1], rsem.at[k, j - 1], {axis: q}))
+        pl.semaphore_wait(barrier, len(peers) + 1)
+
+        def columns(ref, q, i):
+            if pieces == 1:
+                return ref.at[q]
+            lanes = pl.ds(pl.multiple_of((i * C + q) * nb, 128), nb)
+            return ref.at[pl.ds(pl.multiple_of(c * n, 16), n), lanes]
+
+        def first_hop(ref, out, at):
+            hop = []
+            for i in range(pieces):
+                dst = out.at[p, :, pl.ds(i * (wide // pieces), wide // pieces)]
+                hop.append(pltpu.make_async_copy(columns(ref, p, i), dst, hown.at[at, i]))
+                for k, q in enumerate(mates):
+                    hop.append(
+                        remote(columns(ref, q, i), dst, hsend.at[at, k, i], hrecv.at[at, k, i], {"shard": q})
+                    )
             for copy in hop:
                 copy.start()
             return hop
 
-        if rows is not None:
-            first = turn_over(ins[1], outs[1], 0, "shard", S, p)
+        x_hop = first_hop(x_ref, x_buf, 0)
         local = pltpu.make_async_copy(tile.at[z, p], got.at[c, z, p], own)
         local.start()
         copies = []
@@ -151,10 +172,24 @@
             copies.append(remote(tile.at[g, q], got.at[c, z, p], send.at[at], recv.at[at], where))
             copies[-1].start()
         ride.start()
-        if rows is not None:
-            for copy in first:
-                copy.wait()
-            second = turn_over(outs[1], outs[2], 1, "ctx", C, z)
+        y_hop = first_hop(y_ref, y_out, 1)
+        moves = []
+        for m, (raw, stage, out, height) in enumerate(zip(raws, stages, turns, heights)):
+            for q in range(S):
+                stage[q] = raw[q * height : (q + 1) * height, :].astype(F32).T.astype(BF)
+            moves.append(pltpu.make_async_copy(stage.at[p], out.at[p], wown.at[m]))
+            for k, q in enumerate(mates):
+                moves.append(remote(stage.at[q], out.at[p], wsend.at[m, k], wrecv.at[m, k], {"shard": q}))
+            for copy in moves[-S:]:
+                copy.start()
+        for copy in x_hop:
+            copy.wait()
+        line = [pltpu.make_async_copy(x_buf.at[z], x_out.at[z], zown)]
+        for k in range(1, C):
+            g = (z + k) % C
+            line.append(remote(x_buf.at[g], x_out.at[z], zsend.at[k - 1], zrecv.at[k - 1], {"ctx": g}))
+        for copy in line:
+            copy.start()
         local.wait()
         for copy in copies:
             copy.wait()
@@ -162,19 +197,25 @@
         back.start()
         back.wait_send()
         remote(got.at[1 - c], got.at[1 - c], bsend, brecv, {"tp": 1 - c}).wait_recv()
-        if rows is not None:
-            for copy in second:
-                copy.wait()
+        for copy in line + y_hop + moves:
+            copy.wait()
         ride.wait()
 
-    count, most = C * S - 1, max(S, C) - 1
-    args, outs = [tiles], [(jax.ShapeDtypeStruct((T,) + tiles.shape, tiles.dtype), ANY)]
-    scratch = [DMA((count,)), DMA((count,)), DMA, DMA, DMA]
-    if rows is not None:
-        args.append(rows)
-        outs += [(jax.ShapeDtypeStruct(rows.shape, rows.dtype), IN_VMEM)] * 2
-        scratch += [DMA((2, most)), DMA((2, most)), DMA((2,))]
-    return comm(kernel, S, C, number, "exchange", args, [IN_VMEM] * len(args), outs, scratch, riders)
+    count, m = C * S - 1, len(turned)
+    part = jax.ShapeDtypeStruct((S, n, wide), rows.dtype)
+    return comm(
+        kernel, S, C, number, "exchange", [tiles, rows, beside, *turned],
+        [IN_VMEM, ANY, ANY] + [IN_VMEM] * m,
+        [(jax.ShapeDtypeStruct((T,) + tiles.shape, tiles.dtype), ANY), (part, IN_VMEM), (part, IN_VMEM), (part, ANY)]
+        + [(jax.ShapeDtypeStruct((S, nb, height), BF), ANY) for height in heights],
+        [
+            DMA((count,)), DMA((count,)), DMA, DMA, DMA,
+            DMA((2, S - 1, pieces)), DMA((2, S - 1, pieces)), DMA((2, pieces)),
+            DMA((C - 1,)), DMA((C - 1,)), DMA, DMA((m, S - 1)), DMA((m, S - 1)), DMA((m,)),
+        ]
+        + [pltpu.VMEM((S, nb, height), BF) for height in heights],
+        riders,
+    )
 
 
 def plane(S):
@@ -1049,17 +1090,11 @@
         nb = D // (S * C)
         L = R * C
 
-        def to_parts(x):
-            return x.reshape(n, S, C, nb).transpose(2, 0, 1, 3).reshape(S, n, D // S)
-
         def parts(x):
             return x.reshape(n, S, D // S).swapaxes(0, 1)
 
         def unpermute(x):
             return x.reshape(x.shape[0], C, S, nb).swapaxes(1, 2).reshape(x.shape)
-
-        def half_of(x):
-            return lax.dynamic_slice_in_dim(x, c * n, n, 0)
 
         def after(x, y):
             return lax.optimization_barrier((x, y))
@@ -1078,16 +1113,13 @@
 
         tile = tiles_of((norm_gain[0].reshape(-1), norm_bias[0].reshape(-1), b_qkv[0].reshape(-1), lengths[0]), ())
         raw = lax.all_gather(w_qkv[0].swapaxes(0, 1).reshape(3 * nb, -1), "ctx", axis=0, tiled=True)
-        small, _, tok, wo, wg, wd, cot = exchange(
+        small, _, tok, cot, wo, wd, wg = exchange(
             S, C, T, 0,
-            [
-                ("shard", w_out[0].reshape(S, hn, nb).swapaxes(1, 2)),
-                ("shard", w_gateup[0].reshape(nb, 2, S, fn).transpose(2, 0, 1, 3).reshape(S, nb, 2 * fn)),
-                ("shard", w_down[0].reshape(S, fn, nb).swapaxes(1, 2)),
-                ("shard", to_parts(half_of(cotangent))),
-            ],
+            [("shard", w_gateup[0].reshape(nb, 2, S, fn).transpose(2, 0, 1, 3).reshape(S, nb, 2 * fn))],
             jnp.broadcast_to(tile, (C, S, 8, 128)),
-            to_parts(half_of(tokens)),
+            tokens,
+            cotangent,
+            [w_out[0], w_down[0]],
         )
         tok, wo = gather_columns(S, C, T, 1, tok, [("all", wo.reshape(S * nb, hn))])
         wo, wg, wd = wo.reshape(D, hn), over_ctx(wg), over_ctx(wd)
@@ -1124,10 +1156,10 @@
         dmid, gb1, stats2 = sum_back_gather(S, C, T, 6, dgu, wg, mid, gb, gains[1:])
         gw_out = mm(gb1, o, 0, 0).astype(BF)
         gb1, gw_out = after(gb1, gw_out)
+        gw_out = sum_ctx(gw_out)
         do = mm(gb1, wo, 1, 0).astype(BF)
-        dqkv, gbias, got, gw_down, gw_out = attend_back(
-            S, C, T, 11, q, k, v, o, do, lse, begin, act, wd,
-            [("shard", gw_down), ("ctx", gw_out.reshape(C, S * nb, hn))],
+        dqkv, gbias, got, gw_down = attend_back(
+            S, C, T, 11, q, k, v, o, do, lse, begin, act, wd, [("shard", gw_down)]
         )
         out = parts((mid + got).astype(BF))
         gw_qkv = mm(n1, dqkv, 0, 0).astype(BF)
@@ -1137,8 +1169,7 @@
             S, C, T, 8, dqkv, wq, tok, dmid, gains[:1], [("shard", out), ("shard", gw_gateup)]
         )
         gtok, out, norms, gbias, gw_gateup, gw_down, gw_qkv, gw_out = finish(
-            S, C, T, 10, low, out, [stats1, stats2], gbias, gw_gateup, gw_down, gw_qkv,
-            jnp.sum(gw_out.astype(F32), axis=0).astype(BF).reshape(S, nb, hn),
+            S, C, T, 10, low, out, [stats1, stats2], gbias, gw_gateup, gw_down, gw_qkv, gw_out
         )
         if not ordered(D, S, C):
             gtok, out = unpermute(gtok), unpermute(out)

time: 649 us -> 637 us (0.982)
  Pallas kernels: 546 us -> 528 us
  waiting for transfers between devices: 1.48 us -> 15.3 us
  local copies, waits for them, and re-layouts: 32.4 us -> 24.7 us
    pallas_call x9, Pallas kernels: 516 us -> 493 us  [comm(): pl.pallas_call(body, out_shape=[shape for shape, _ in outs] + ride.shapes...]
    reduce_scatter x3 -> x4, waiting for transfers between devices: 0.02 us -> 13.9 us  [sum_ctx(): g = lax.psum_scatter(g.astype(BF), 'ctx', scatter_dimension=0, tiled=True)]
  transfers between devices with their start and end apart: 6 -> 7, of which waited for: 0 -> 1; matrix products, arithmetic and copies ran while one was open for 10% -> 9% of each run, Pallas kernels for 75% -> 74%
where the time goes in v13:
time: 637 us; the launch traced here: 634 us
  Pallas kernels  528 us (83%)
  matrix products  45.7 us (7%)
  local copies, waits for them, and re-layouts  24.7 us (4%)
  waiting for transfers between devices  15.3 us (2%)
  between operations  14.7 us (2%)
    pallas_call x9, Pallas kernels, comm(): pl.pallas_call(body, out_shape=[shape for shape, _ in outs] + ride.shapes...  493 us
    dot_general x5, matrix products, mm(): lax.dot_general(a, b, (((ca,), (cb,)), ((), ())), preferred_element_type=...  45.7 us
    pallas_call x1, Pallas kernels, attend(): pl.pallas_call(attend_kernel, in_specs=[pl.BlockSpec(memory_space=pltpu.S...  21.8 us
    reduce_scatter x4, waiting for transfers between devices, sum_ctx(): g = lax.psum_scatter(g.astype(BF), 'ctx', scatter_dimension=0, tiled=True)  13.9 us
    pallas_call x1, Pallas kernels, by_rows(): pl.pallas_call(kernel, grid=(L // BLK,), in_specs=[spec(x.shape[1]) if ro...  13.2 us
  transfers between devices with their start and end apart: 7, of which 1 were waited for; matrix products, arithmetic and copies ran while one was open for 9% of the time, Pallas kernels for 74%

profile of v13, /device:TPU:9, one launch (start us, length us, event | category | flops | bytes accessed | tf_op | source)
XLA Modules:
  0.0 634.0 jit_solution(15764951479923777814)
XLA Ops:
  8.8 3.8 copy.49
  12.8 1.5 copy.51.refs_5_
  15.1 56.6 %exchange.1 = (f32[2,4,4,8,128]{4,3,2,1,0:T(8,128)}, bf16[4,192,512]{2,1,0:T(8,128)(2,1)}, bf16[4,192,512]{2,1,0:T(8,128)(2,1)}, bf16[4,192,512]{2,1,0:T(8,128)(...) custom-call(f32[4,4,8,128]{3,2,1,0:T(8,128)} %broadcast_in_dim.27.refs_0_, ...), custom_call_target="tpu_custom_call" | custom-call | bytes 120000000 | tf_op jit(solution)/shard_map/exchange/pallas_call | solution.py:108
  72.8 0.8 constant_dynamic-slice_fusion.2
  75.2 38.7 %gather_columns.2 = (bf16[4,2,192,2048]{3,2,1,0:T(8,128)(2,1)}, bf16[4,512,256]{2,1,0:T(8,128)(2,1)}) custom-call(bf16[4,192,512]{2,1,0:T(8,128)(2,1)} %get-tuple-element.59.refs_0_, bf16[512,256]{1,0:T(8,128)(2,1)} %bitcast.138), custom_call_target="tpu_custom_call" | custom-call | bytes 120000000 | tf_op jit(solution)/shard_map/gather_columns/pallas_call | solution.py:108
  115.1 50.6 %project.1 = (bf16[1536,2048]{1,0:T(8,128)(2,1)}, f32[1536,768]{1,0:T(8,128)}, bf16[4,4,128,768]{3,2,1,0:T(8,128)(2,1)}) custom-call(bf16[1536,2048]{1,0:T(8,128)(2,1)} %bitcast.104, bf16[4,3,128,1024]{3,2,1,0:T(8,128)(2,1)} %bitcast.117, f32[1,2048]{1,0:T(1,128)} %bitcast.141, f32[1,2048]{1,0:T(1,128)} %bitcast.146, f32[1,768]{1,0:T(1,128)} %reshape.183.refs_4_), custom_call_target="tpu_custom_call" | custom-call | bytes 120000000 | tf_op jit(solution)/shard_map/project/pallas_call | solution.py:108
  165.7 21.8 %attend.1 = (bf16[1536,256]{1,0:T(8,128)(2,1)}, bf16[1536,256]{1,0:T(8,128)(2,1)}, bf16[1536,256]{1,0:T(8,128)(2,1)}, bf16[1536,256]{1,0:T(8,128)(2,1)}, f32[4,1536]{1,0:T(4,128)}) custom-call(s32[3]{0:T(128)} %and_select_fusion.first_ref, f32[1536,768]{1,0:T(8,128)} %get-tuple-element.62.qkv_ref, f32[256,128]{1,0:T(8,128)} %constant.59.clone.cos_ref.refs_8_, ...), custom_call_target="tpu_custom_call" | custom-call | tf_op jit(solution)/shard_map/attend/pallas_call | solution.py:953
  187.5 68.6 %sum_norm_gather.1 = (f32[192,2048]{1,0:T(8,128)}, bf16[8,192,2048]{2,1,0:T(8,128)(2,1)}, bf16[4,192,512]{2,1,0:T(8,128)(2,1)}) custom-call(bf16[8,192,256]{2,1,0:T(8,128)(2,1)} %bitcast.119, bf16[2048,256]{1,0:T(8,128)(2,1)} %bitcast.129, bf16[8,192,2048]{2,1,0:T(8,128)(2,1)} %bitcast.105, f32[1,2048]{1,0:T(1,128)} %bitcast.143, f32[1,2048]{1,0:T(1,128)} %bitcast.145, ...), custom_call_target="tpu_custom_call" | custom-call | bytes 120000000 | tf_op jit(solution)/shard_map/sum_norm_gather/pallas_call | solution.py:108
  256.1 36.2 %gather_columns.3 = (bf16[4,2,192,2048]{3,2,1,0:T(8,128)(2,1)}, f32[1536,1408]{1,0:T(8,128)}, bf16[1536,704]{1,0:T(8,128)(2,1)}) custom-call(bf16[4,192,512]{2,1,0:T(8,128)(2,1)} %get-tuple-element.66.refs_0_, bf16[1536,2048]{1,0:T(8,128)(2,1)} %bitcast.111, bf16[2048,1408]{1,0:T(8,128)(2,1)} %all-gather.6.cloned.1.call-done.refs_2_.refs_1_), custom_call_target="tpu_custom_call" | custom-call | bytes 120000000 | tf_op jit(solution)/shard_map/gather_columns/pallas_call | solution.py:108
  292.3 9.8 %convolution_convert_fusion.2 = bf16[2048,704]{0,1:T(8,128)(2,1)} fusion(bf16[1536,2048]{1,0:T(8,128)(2,1)} %bitcast.107, bf16[1536,704]{1,0:T(8,128)(2,1)} %get-tuple-element.69), kind=kOutput, calls=%fused_computation.2 | convolution fusion | flops 4430626816 | bytes 11337728 | tf_op jit(solution)/shard_map/dot_general | solution.py:26
  302.2 13.2 %gates_back.1 = bf16[1536,1408]{1,0:T(8,128)(2,1)} custom-call(bf16[1536,2048]{1,0:T(8,128)(2,1)} %bitcast.108, bf16[2048,704]{1,0:T(8,128)(2,1)} %all-gather.8.cloned.1.call-done.wd_ref.refs_1_, f32[1536,1408]{1,0:T(8,128)} %get-tuple-element.76.gu_ref), custom_call_target="tpu_custom_call" | custom-call | tf_op jit(solution)/shard_map/gates_back/pallas_call | solution.py:552
  315.3 15.0 %convolution_convert_fusion = bf16[2048,1408]{1,0:T(8,128)(2,1)} fusion(bf16[1536,2048]{1,0:T(8,128)(2,1)} %bitcast.112, bf16[1536,1408]{1,0:T(8,128)(2,1)} %gates_back.1), kind=kOutput, calls=%fused_computation | convolution fusion | flops 8861253632 | bytes 16384000 | tf_op jit(solution)/shard_map/dot_general | solution.py:26
  330.4 74.9 %sum_back_gather.1 = (f32[192,2048]{1,0:T(8,128)}, bf16[8,192,2048]{2,1,0:T(8,128)(2,1)}, f32[2,2048]{1,0:T(2,128)}) custom-call(bf16[8,192,1408]{2,1,0:T(8,128)(2,1)} %bitcast.110, bf16[2048,1408]{1,0:T(8,128)(2,1)} %all-gather.6.cloned.1.call-done.refs_2_.refs_1_, f32[192,2048]{1,0:T(8,128)} %get-tuple-element.78.refs_2_, bf16[8,192,2048]{2,1,0:T(8,128)(2,1)} %bitcast.109, ...), custom_call_target="tpu_custom_call" | custom-call | bytes 120000000 | tf_op jit(solution)/shard_map/sum_back_gather/pallas_call | solution.py:108
  405.4 5.8 convolution_convert_fusion.4
  411.2 5.6 convolution_convert_fusion.3.refs_6_
  416.9 2.3 copy.54
  419.1 49.5 %attend_back.1 = (bf16[1536,768]{1,0:T(8,128)(2,1)}, f32[1,768]{1,0:T(1,128)}, f32[192,2048]{1,0:T(8,128)}, bf16[4,128,704]{2,1,0:T(8,128)(2,1)}) custom-call(bf16[8,192,704]{2,1,0:T(8,128)(2,1)} %bitcast.123, bf16[2048,704]{1,0:T(8,128)(2,1)} %all-gather.8.cloned.1.call-done.wd_ref.refs_1_, bf16[1536,256]{1,0:T(8,128)(2,1)} %get-tuple-element.73.refs_2_, ...), custom_call_target="tpu_custom_call" | custom-call | bytes 120000000 | tf_op jit(solution)/shard_map/attend_back/pallas_call | solution.py:108
  468.6 9.6 %convolution_convert_fusion.1 = bf16[2048,768]{1,0:T(8,128)(2,1)} fusion(bf16[1536,2048]{1,0:T(8,128)(2,1)} %get-tuple-element.84, bf16[1536,768]{1,0:T(8,128)(2,1)} %get-tuple-element.85), kind=kOutput, calls=%fused_computation.1 | convolution fusion | flops 4833411072 | bytes 11796480 | tf_op jit(solution)/shard_map/dot_general | solution.py:26
  478.2 1.4 copy-done
  480.3 0.9 copy.60
  481.2 58.1 %sum_back.1 = (bf16[192,2048]{1,0:T(8,128)(2,1)}, f32[2,2048]{1,0:T(2,128)}, bf16[4,192,512]{2,1,0:T(8,128)(2,1)}, bf16[4,128,1408]{2,1,0:T(8,128)(2,1)}) custom-call(bf16[8,192,768]{2,1,0:T(8,128)(2,1)} %bitcast.122, bf16[2048,768]{1,0:T(8,128)(2,1)} %bitcast.116, bf16[8,192,2048]{2,1,0:T(8,128)(2,1)} %bitcast.106, f32[192,2048]{1,0:T(8,128)} %get-tuple-element.87.refs_3_, ...), custom_call_target="tpu_custom_call" | custom-call | bytes 120000000 | tf_op jit(solution)/shard_map/sum_back/pallas_call | solution.py:108
  539.4 13.8 %reduce-scatter.9.cloned.1.call-done = bf16[512,768]{1,0:T(8,128)(2,1)} async-done(((bf16[2048,768]{1,0:T(8,128)(2,1)}), bf16[512,768]{1,0:T(8,128)(2,1)}) %reduce-scatter.9.cloned.1.call-update) | async-done | bytes 786448 | tf_op jit(solution)/shard_map/reduce_scatter | solution.py:1106
  553.2 60.1 %finish.1 = (bf16[2,192,2048]{2,1,0:T(8,128)(2,1)}, bf16[2,192,2048]{2,1,0:T(8,128)(2,1)}, f32[4,128]{1,0:T(4,128)}, f32[4,6,128]{2,1,0:T(8,128)}, f32[128,2,281...) custom-call(bf16[192,2048]{1,0:T(8,128)(2,1)} %get-tuple-element.90.refs_0_, ...), custom_call_target="tpu_custom_call" | custom-call | bytes 120000000 | tf_op jit(solution)/shard_map/finish/pallas_call | solution.py:108
  613.3 1.4 slice_bitcast_fusion
  614.7 1.1 reshape.202
  616.7 3.6 bitcast_convert_fusion
  620.2 1.1 copy.67
  621.4 1.1 copy.68
  622.5 0.8 copy.69
  623.4 1.6 copy.70
  624.9 0.8 copy-done.6
  625.8 1.1 copy.71
  (73 shorter events, 8.0 us)
Async XLA Ops:
  7.2 107.9 %all-gather.4.cloned.1.call-start = ((), (), s32[]{:S(2)}) async-start(), calls=%async_computation.4 | async-start | bytes 3932160 | tf_op jit(solution)/shard_map/all_gather | solution.py:1115
  7.9 248.2 %all-gather.6.cloned.1.call-start = ((), (), s32[]{:S(2)}) async-start(), calls=%async_computation.5 | async-start | bytes 7208960 | tf_op jit(solution)/shard_map/all_gather | solution.py:1103
  12.7 1.7 copy-start.12
  12.7 1.7 copy-start.10
  12.7 1.7 copy-start.11
  71.7 230.4 %all-gather.8.cloned.1.call-start = ((), (), s32[]{:S(2)}) async-start(), calls=%async_computation.6 | async-start | bytes 3932160 | tf_op jit(solution)/shard_map/all_gather | solution.py:1103
  72.4 344.4 %reduce-scatter.5.cloned.1.call-start = ((), (), s32[]{:S(2)}) async-start(), calls=%async_computation.7 | async-start | bytes 3604480 | tf_op jit(solution)/shard_map/reduce_scatter | solution.py:1106
  74.0 91.6 %copy-start.9 = (s32[1,1536]{1,0:T(1,128)}, s32[1,1536]{1,0:T(1,128)S(1)}, u32[]{:S(2)}) copy-start(s32[1,1536]{1,0:T(1,128)S(1)} %broadcast_in_dim.29.begin_ref.refs_12_) | copy-start | bytes 18436
  302.1 179.1 %reduce-scatter.7.cloned.1.call-start = ((), (), s32[]{:S(2)}) async-start(), calls=%async_computation.8 | async-start | bytes 7208960 | tf_op jit(solution)/shard_map/reduce_scatter | solution.py:1106
  330.4 209.0 %reduce-scatter.11.cloned.1.call-start = ((), (), s32[]{:S(2)}) async-start(), calls=%async_computation.10 | async-start | bytes 1310720 | tf_op jit(solution)/shard_map/reduce_scatter | solution.py:1106
  330.4 74.9 %copy-start.1 = (bf16[1536,256]{1,0:T(8,128)(2,1)S(1)}, bf16[1536,256]{1,0:T(8,128)(2,1)}, u32[]{:S(2)}) copy-start(bf16[1536,256]{1,0:T(8,128)(2,1)} %get-tuple-element.63.refs_5_) | copy-start | bytes 2359300
  405.4 5.8 copy-start.7
  411.2 142.1 %reduce-scatter.9.cloned.1.call-start = ((), (), s32[]{:S(2)}) async-start(), calls=%async_computation.9 | async-start | bytes 3932160 | tf_op jit(solution)/shard_map/reduce_scatter | solution.py:1106
  478.2 1.4 copy-start
  478.2 1.9 copy-start.5
  613.3 6.9 %copy-start.4 = (bf16[2,192,2048]{2,1,0:T(8,128)(2,1)S(1)}, bf16[2,192,2048]{2,1,0:T(8,128)(2,1)}, u32[]{:S(2)}) copy-start(bf16[2,192,2048]{2,1,0:T(8,128)(2,1)} %get-tuple-element.99) | copy-start | bytes 4718596
  616.7 4.7 copy-start.3
  620.2 2.3 copy-start.8
  620.2 3.1 copy-start.2
  623.4 2.4 copy-start.6
Sparse Core Ops, SparseCore 0:
  9.6 94.0 all-gather.3
  105.3 123.7 all-gather.5
  230.7 63.2 all-gather.7
  302.2 54.0 reduce-scatter.4
  358.5 102.7 reduce-scatter.6
  464.0 25.5 reduce-scatter.10
  492.6 60.5 reduce-scatter.8

commit v14 on v13

--- a/solution.py
+++ b/solution.py
@@ -133,7 +133,7 @@
 
     def kernel(ride, ins, outs, scratch):
         tile, x_ref, y_ref, *raws = ins
-        got, x_buf, x_out, y_out, *turns = outs
+        got, x_buf, x_out, y_buf, y_out, *turns = outs
         send, recv, bsend, brecv, own, hsend, hrecv, hown, zsend, zrecv, zown, wsend, wrecv, wown, *stages = scratch
         p, z, c = here()
         mates = [(p + k) % S for k in range(1, S)]
@@ -164,6 +164,7 @@
             return hop
 
         x_hop = first_hop(x_ref, x_buf, 0)
+        y_hop = first_hop(y_ref, y_buf, 1)
         local = pltpu.make_async_copy(tile.at[z, p], got.at[c, z, p], own)
         local.start()
         copies = []
@@ -172,7 +173,6 @@
             copies.append(remote(tile.at[g, q], got.at[c, z, p], send.at[at], recv.at[at], where))
             copies[-1].start()
         ride.start()
-        y_hop = first_hop(y_ref, y_out, 1)
         moves = []
         for m, (raw, stage, out, height) in enumerate(zip(raws, stages, turns, heights)):
             for q in range(S):
@@ -182,14 +182,19 @@
                 moves.append(remote(stage.at[q], out.at[p], wsend.at[m, k], wrecv.at[m, k], {"shard": q}))
             for copy in moves[-S:]:
                 copy.start()
-        for copy in x_hop:
-            copy.wait()
-        line = [pltpu.make_async_copy(x_buf.at[z], x_out.at[z], zown)]
-        for k in range(1, C):
-            g = (z + k) % C
-            line.append(remote(x_buf.at[g], x_out.at[z], zsend.at[k - 1], zrecv.at[k - 1], {"ctx": g}))
-        for copy in line:
-            copy.start()
+        def second_hop(hop, buf, out, at):
+            for copy in hop:
+                copy.wait()
+            line = [pltpu.make_async_copy(buf.at[z], out.at[z], zown.at[at])]
+            for k in range(1, C):
+                g = (z + k) % C
+                line.append(remote(buf.at[g], out.at[z], zsend.at[at, k - 1], zrecv.at[at, k - 1], {"ctx": g}))
+            for copy in line:
+                copy.start()
+            return line
+
+        line = second_hop(x_hop, x_buf, x_out, 0)
+        line += second_hop(y_hop, y_buf, y_out, 1)
         local.wait()
         for copy in copies:
             copy.wait()
@@ -197,7 +202,7 @@
         back.start()
         back.wait_send()
         remote(got.at[1 - c], got.at[1 - c], bsend, brecv, {"tp": 1 - c}).wait_recv()
-        for copy in line + y_hop + moves:
+        for copy in line + moves:
             copy.wait()
         ride.wait()
 
@@ -206,12 +211,13 @@
     return comm(
         kernel, S, C, number, "exchange", [tiles, rows, beside, *turned],
         [IN_VMEM, ANY, ANY] + [IN_VMEM] * m,
-        [(jax.ShapeDtypeStruct((T,) + tiles.shape, tiles.dtype), ANY), (part, IN_VMEM), (part, IN_VMEM), (part, ANY)]
+        [(jax.ShapeDtypeStruct((T,) + tiles.shape, tiles.dtype), ANY), (part, IN_VMEM), (part, IN_VMEM), (part, IN_VMEM),
+         (part, IN_VMEM)]
         + [(jax.ShapeDtypeStruct((S, nb, height), BF), ANY) for height in heights],
         [
             DMA((count,)), DMA((count,)), DMA, DMA, DMA,
             DMA((2, S - 1, pieces)), DMA((2, S - 1, pieces)), DMA((2, pieces)),
-            DMA((C - 1,)), DMA((C - 1,)), DMA, DMA((m, S - 1)), DMA((m, S - 1)), DMA((m,)),
+            DMA((2, C - 1)), DMA((2, C - 1)), DMA((2,)), DMA((m, S - 1)), DMA((m, S - 1)), DMA((m,)),
         ]
         + [pltpu.VMEM((S, nb, height), BF) for height in heights],
         riders,
@@ -710,9 +716,9 @@
     )
 
 
-def finish(S, C, T, number, x, y, stats, bias, gateup, down, qkv, out):
+def finish(S, C, T, number, x, y, stats, bias, qkv, out):
     n, D = x.shape
-    fn, hn = down.shape[2], out.shape[2]
+    hn = out.shape[2]
     wide, lines = D // S, bias.shape[1] // 128
     nb = D // (S * C)
     count = sum(z.shape[0] for z in stats)
@@ -721,9 +727,9 @@
     pieces = S if ordered(D, S, C) else 1
 
     def kernel(ride, ins, outs, scratch):
-        x_ref, y_ref, stat_refs, bias_ref = ins[0], ins[1], ins[2:-5], ins[-5]
-        gateup_ref, down_ref, qkv_ref, o_ref = ins[-4:]
-        x_out, y_out, norm_out, bias_out, gateup_out, down_out, qkv_out, o_out = outs
+        x_ref, y_ref, stat_refs, bias_ref = ins[0], ins[1], ins[2:-3], ins[-3]
+        qkv_ref, o_ref = ins[-2:]
+        x_out, y_out, norm_out, bias_out, qkv_out, o_out = outs
         xbuf, xbuf2, ybuf2, tile, send, recv, own, psend, precv, pown, lsend, lrecv, tsend, trecv = scratch[:14]
         qkv_buf, o_buf, gsend, grecv, gown, got = scratch[14:]
         p, z, c = here()
@@ -804,8 +810,6 @@
         for copy in x_hop:
             copy.wait()
         x_hop = turn_over(lambda q: xbuf.at[q], xbuf2.at[z], 2, C, z, "ctx")
-        for q in range(S):
-            down_out[q * fn : (q + 1) * fn, :] = down_ref[q].astype(F32).T
         for copy in y_hop:
             copy.wait()
         y_hop = arrive(ybuf2, y_out, 0)
@@ -813,9 +817,6 @@
             copy.wait()
         small_last = both(got, 0)
         bias_out[...] = jnp.sum(got[c, :, :, count : count + lines, :], axis=0)
-        for i in range(2):
-            for q in range(S):
-                gateup_out[:, i, q * fn : (q + 1) * fn] = gateup_ref[q, :, i * fn : (i + 1) * fn].astype(F32)
         for copy in x_hop:
             copy.wait()
         x_hop = arrive(xbuf2, x_out, 1)
@@ -836,7 +837,7 @@
         settle(y_out, 1, y_last)
         settle(x_out, 2, x_last)
 
-    args = [x, y, *stats, bias, gateup, down, qkv, out]
+    args = [x, y, *stats, bias, qkv, out]
     most = max(S, C) - 1
     home = (jax.ShapeDtypeStruct((T, n, D), BF), ANY)
     x, y, *rest = comm(
@@ -844,7 +845,7 @@
         [home, home]
         + [
             (jax.ShapeDtypeStruct(shape, F32), IN_VMEM)
-            for shape in ((count, 128), (S, lines, 128), (nb, 2, S * fn), (S * fn, nb), (3, nb, S * hn), (S * hn, nb))
+            for shape in ((count, 128), (S, lines, 128), (3, nb, S * hn), (S * hn, nb))
         ],
         [
             pltpu.VMEM((S, n, wide), BF), pltpu.VMEM((C, n, wide), BF), pltpu.VMEM((C, n, wide), BF),
@@ -856,6 +857,26 @@
         ],
     )
     return [x.reshape(T * n, D), y.reshape(T * n, D)] + rest
+
+
+def final_kernel(gateup_ref, down_ref, gateup_out, down_out):
+    S, _, fn = down_ref.shape
+    for q in range(S):
+        down_out[q * fn : (q + 1) * fn, :] = down_ref[q].astype(F32).T
+        for i in range(2):
+            gateup_out[:, i, q * fn : (q + 1) * fn] = gateup_ref[q, :, i * fn : (i + 1) * fn].astype(F32)
+
+
+def final(gateup, down):
+    S, nb, fn = down.shape
+    return pl.pallas_call(
+        final_kernel,
+        in_specs=[IN_VMEM] * 2,
+        out_specs=[IN_VMEM] * 2,
+        out_shape=[jax.ShapeDtypeStruct((nb, 2, S * fn), F32), jax.ShapeDtypeStruct((S * fn, nb), F32)],
+        compiler_params=pltpu.CompilerParams(vmem_limit_bytes=62 << 20),
+        name="final",
+    )(gateup, down)
 
 
 def ordered(D, S, C):
@@ -1113,7 +1134,7 @@
 
         tile = tiles_of((norm_gain[0].reshape(-1), norm_bias[0].reshape(-1), b_qkv[0].reshape(-1), lengths[0]), ())
         raw = lax.all_gather(w_qkv[0].swapaxes(0, 1).reshape(3 * nb, -1), "ctx", axis=0, tiled=True)
-        small, _, tok, cot, wo, wd, wg = exchange(
+        small, _, tok, _, cot, wo, wd, wg = exchange(
             S, C, T, 0,
             [("shard", w_gateup[0].reshape(nb, 2, S, fn).transpose(2, 0, 1, 3).reshape(S, nb, 2 * fn))],
             jnp.broadcast_to(tile, (C, S, 8, 128)),
@@ -1140,7 +1161,7 @@
 
         n1, qkv, wq = project(S, C, T, 12, tok, raw.reshape(C, 3, nb, -1), gains[:1], shifts[:1], bias)
         q, k, v, o, lse = attend(qkv, begin)
-        mid, n2, cot = sum_norm_gather(S, C, T, 2, o, wo, tok, gains[1:], shifts[1:], [("ctx", cot)])
+        mid, n2 = sum_norm_gather(S, C, T, 2, o, wo, tok, gains[1:], shifts[1:])
         gb, gu, act = gates(S, C, T, 4, n2, wg, cot)
         gw_down = mm(gb, act, 0, 0).astype(BF)
         wd, gw_down = after(wd, gw_down)
@@ -1168,8 +1189,9 @@
         low, stats1, out, gw_gateup = sum_back(
             S, C, T, 8, dqkv, wq, tok, dmid, gains[:1], [("shard", out), ("shard", gw_gateup)]
         )
-        gtok, out, norms, gbias, gw_gateup, gw_down, gw_qkv, gw_out = finish(
-            S, C, T, 10, low, out, [stats1, stats2], gbias, gw_gateup, gw_down, gw_qkv, gw_out
+        low, gw_gateup, gw_down = lax.optimization_barrier((low, *final(gw_gateup, gw_down)))
+        gtok, out, norms, gbias, gw_qkv, gw_out = finish(
+            S, C, T, 10, low, out, [stats1, stats2], gbias, gw_qkv, gw_out
         )
         if not ordered(D, S, C):
             gtok, out = unpermute(gtok), unpermute(out)

time: 637 us -> 675 us (1.060)
  Pallas kernels: 528 us -> 572 us
    pallas_call x9, Pallas kernels: 493 us -> 538 us  [comm(): pl.pallas_call(body, out_shape=[shape for shape, _ in outs] + ride.shapes...]
  transfers between devices with their start and end apart: 7 -> 7, of which waited for: 1 -> 1; matrix products, arithmetic and copies ran while one was open for 9% -> 9% of each run, Pallas kernels for 74% -> 76%
where the time goes in v14:
time: 675 us; the launch traced here: 671 us
  Pallas kernels  572 us (85%)
  matrix products  45.6 us (7%)
  local copies, waits for them, and re-layouts  21.2 us (3%)
  between operations  14.7 us (2%)
  waiting for transfers between devices  13 us (2%)
    pallas_call x9, Pallas kernels, comm(): pl.pallas_call(body, out_shape=[shape for shape, _ in outs] + ride.shapes...  538 us
    dot_general x5, matrix products, mm(): lax.dot_general(a, b, (((ca,), (cb,)), ((), ())), preferred_element_type=...  45.6 us
    pallas_call x1, Pallas kernels, attend(): pl.pallas_call(attend_kernel, in_specs=[pl.BlockSpec(memory_space=pltpu.S...  17 us
  transfers between devices with their start and end apart: 7, of which 1 were waited for; matrix products, arithmetic and copies ran while one was open for 9% of the time, Pallas kernels for 76%

profile of v14, /device:TPU:9, one launch (start us, length us, event | category | flops | bytes accessed | tf_op | source)
XLA Modules:
  0.0 671.4 jit_solution(7914712560222388308)
XLA Ops:
  8.0 0.8 copy.48
  8.8 3.8 copy.49
  12.8 1.5 copy.51.refs_5_
  15.1 91.7 %exchange.1 = (f32[2,4,4,8,128]{4,3,2,1,0:T(8,128)}, bf16[4,192,512]{2,1,0:T(8,128)(2,1)}, bf16[4,192,512]{2,1,0:T(8,128)(2,1)}, bf16[4,192,512]{2,1,0:T(8,128)(...) custom-call(f32[4,4,8,128]{3,2,1,0:T(8,128)} %broadcast_in_dim.27.re, ...), custom_call_target="tpu_custom_call" | custom-call | bytes 120000000 | tf_op jit(solution)/shard_map/exchange/pallas_call | solution.py:108
  107.9 0.8 constant_dynamic-slice_fusion.2
  109.6 0.7 reshape.183.refs_4_
  110.3 50.4 %gather_columns.2 = (bf16[4,2,192,2048]{3,2,1,0:T(8,128)(2,1)}, bf16[4,512,256]{2,1,0:T(8,128)(2,1)}) custom-call(bf16[4,192,512]{2,1,0:T(8,128)(2,1)} %get-tuple-element.62.refs_0_, bf16[512,256]{1,0:T(8,128)(2,1)} %bitcast.135), custom_call_target="tpu_custom_call" | custom-call | bytes 120000000 | tf_op jit(solution)/shard_map/gather_columns/pallas_call | solution.py:108
  161.8 44.0 %project.1 = (bf16[1536,2048]{1,0:T(8,128)(2,1)}, f32[1536,768]{1,0:T(8,128)}, bf16[4,4,128,768]{3,2,1,0:T(8,128)(2,1)}) custom-call(bf16[1536,2048]{1,0:T(8,128)(2,1)} %bitcast.104, bf16[4,3,128,1024]{3,2,1,0:T(8,128)(2,1)} %bitcast.117, f32[1,2048]{1,0:T(1,128)} %bitcast.139, f32[1,2048]{1,0:T(1,128)} %bitcast.144, f32[1,768]{1,0:T(1,128)} %reshape.183.refs_4_), custom_call_target="tpu_custom_call" | custom-call | bytes 120000000 | tf_op jit(solution)/shard_map/project/pallas_call | solution.py:108
  205.8 17.0 %attend.1 = (bf16[1536,256]{1,0:T(8,128)(2,1)}, bf16[1536,256]{1,0:T(8,128)(2,1)}, bf16[1536,256]{1,0:T(8,128)(2,1)}, bf16[1536,256]{1,0:T(8,128)(2,1)}, f32[4,1536]{1,0:T(4,128)}) custom-call(s32[3]{0:T(128)} %and_select_fusion.first_ref, f32[1536,768]{1,0:T(8,128)} %get-tuple-element.65.qkv_ref, f32[256,128]{1,0:T(8,128)} %constant.59.clone.cos_ref.refs_8_, ...), custom_call_target="tpu_custom_call" | custom-call | tf_op jit(solution)/shard_map/attend/pallas_call | solution.py:974
  222.8 73.9 %sum_norm_gather.1 = (f32[192,2048]{1,0:T(8,128)}, bf16[8,192,2048]{2,1,0:T(8,128)(2,1)}) custom-call(bf16[8,192,256]{2,1,0:T(8,128)(2,1)} %bitcast.120, bf16[2048,256]{1,0:T(8,128)(2,1)} %bitcast.127, bf16[8,192,2048]{2,1,0:T(8,128)(2,1)} %bitcast.105, f32[1,2048]{1,0:T(1,128)} %bitcast.141, f32[1,2048]{1,0:T(1,128)} %bitcast.143), custom_call_target="tpu_custom_call" | custom-call | bytes 120000000 | tf_op jit(solution)/shard_map/sum_norm_gather/pallas_call | solution.py:108
  296.8 36.2 %gather_columns.3 = (bf16[4,2,192,2048]{3,2,1,0:T(8,128)(2,1)}, f32[1536,1408]{1,0:T(8,128)}, bf16[1536,704]{1,0:T(8,128)(2,1)}) custom-call(bf16[4,192,512]{2,1,0:T(8,128)(2,1)} %get-tuple-element.60.refs_0_, bf16[1536,2048]{1,0:T(8,128)(2,1)} %bitcast.111, bf16[2048,1408]{1,0:T(8,128)(2,1)} %all-gather.6.cloned.1.call-done.refs_2_.refs_1_), custom_call_target="tpu_custom_call" | custom-call | bytes 120000000 | tf_op jit(solution)/shard_map/gather_columns/pallas_call | solution.py:108
  332.9 9.8 %convolution_convert_fusion.2 = bf16[2048,704]{0,1:T(8,128)(2,1)} fusion(bf16[1536,2048]{1,0:T(8,128)(2,1)} %bitcast.107, bf16[1536,704]{1,0:T(8,128)(2,1)} %get-tuple-element.70), kind=kOutput, calls=%fused_computation.2 | convolution fusion | flops 4430626816 | bytes 11337728 | tf_op jit(solution)/shard_map/dot_general | solution.py:26
  342.8 12.7 %gates_back.1 = bf16[1536,1408]{1,0:T(8,128)(2,1)} custom-call(bf16[1536,2048]{1,0:T(8,128)(2,1)} %bitcast.108, bf16[2048,704]{1,0:T(8,128)(2,1)} %all-gather.8.cloned.1.call-done.wd_ref.refs_1_, f32[1536,1408]{1,0:T(8,128)} %get-tuple-element.77.gu_ref), custom_call_target="tpu_custom_call" | custom-call | tf_op jit(solution)/shard_map/gates_back/pallas_call | solution.py:558
  355.5 15.0 %convolution_convert_fusion = bf16[2048,1408]{1,0:T(8,128)(2,1)} fusion(bf16[1536,2048]{1,0:T(8,128)(2,1)} %bitcast.112, bf16[1536,1408]{1,0:T(8,128)(2,1)} %gates_back.1), kind=kOutput, calls=%fused_computation | convolution fusion | flops 8861253632 | bytes 16384000 | tf_op jit(solution)/shard_map/dot_general | solution.py:26
  370.6 75.7 %sum_back_gather.1 = (f32[192,2048]{1,0:T(8,128)}, bf16[8,192,2048]{2,1,0:T(8,128)(2,1)}, f32[2,2048]{1,0:T(2,128)}) custom-call(bf16[8,192,1408]{2,1,0:T(8,128)(2,1)} %bitcast.110, bf16[2048,1408]{1,0:T(8,128)(2,1)} %all-gather.6.cloned.1.call-done.refs_2_.refs_1_, f32[192,2048]{1,0:T(8,128)} %get-tuple-element.79.refs_2_, bf16[8,192,2048]{2,1,0:T(8,128)(2,1)} %bitcast.109, ...), custom_call_target="tpu_custom_call" | custom-call | bytes 120000000 | tf_op jit(solution)/shard_map/sum_back_gather/pallas_call | solution.py:108
  446.3 5.9 convolution_convert_fusion.4
  452.3 5.5 convolution_convert_fusion.3.refs_6_
  457.8 2.3 copy.54
  460.1 48.6 %attend_back.1 = (bf16[1536,768]{1,0:T(8,128)(2,1)}, f32[1,768]{1,0:T(1,128)}, f32[192,2048]{1,0:T(8,128)}, bf16[4,128,704]{2,1,0:T(8,128)(2,1)}) custom-call(bf16[8,192,704]{2,1,0:T(8,128)(2,1)} %bitcast.122, bf16[2048,704]{1,0:T(8,128)(2,1)} %all-gather.8.cloned.1.call-done.wd_ref.refs_1_, bf16[1536,256]{1,0:T(8,128)(2,1)} %get-tuple-element.74.refs_2_, ...), custom_call_target="tpu_custom_call" | custom-call | bytes 120000000 | tf_op jit(solution)/shard_map/attend_back/pallas_call | solution.py:108
  508.7 9.4 %convolution_convert_fusion.1 = bf16[2048,768]{1,0:T(8,128)(2,1)} fusion(bf16[1536,2048]{1,0:T(8,128)(2,1)} %get-tuple-element.85, bf16[1536,768]{1,0:T(8,128)(2,1)} %get-tuple-element.86), kind=kOutput, calls=%fused_computation.1 | convolution fusion | flops 4833411072 | bytes 11796480 | tf_op jit(solution)/shard_map/dot_general | solution.py:26
  518.2 1.4 copy-done
  520.2 0.9 copy.60
  521.1 59.3 %sum_back.1 = (bf16[192,2048]{1,0:T(8,128)(2,1)}, f32[2,2048]{1,0:T(2,128)}, bf16[4,192,512]{2,1,0:T(8,128)(2,1)}, bf16[4,128,1408]{2,1,0:T(8,128)(2,1)}) custom-call(bf16[8,192,768]{2,1,0:T(8,128)(2,1)} %bitcast.121, bf16[2048,768]{1,0:T(8,128)(2,1)} %bitcast.116, bf16[8,192,2048]{2,1,0:T(8,128)(2,1)} %bitcast.106, f32[192,2048]{1,0:T(8,128)} %get-tuple-element.88.refs_3_, ...), custom_call_target="tpu_custom_call" | custom-call | bytes 120000000 | tf_op jit(solution)/shard_map/sum_back/pallas_call | solution.py:108
  580.4 4.2 final.1
  584.6 11.5 %reduce-scatter.9.cloned.1.call-done = bf16[512,768]{1,0:T(8,128)(2,1)} async-done(((bf16[2048,768]{1,0:T(8,128)(2,1)}), bf16[512,768]{1,0:T(8,128)(2,1)}) %reduce-scatter.9.cloned.1.call-update) | async-done | bytes 786448 | tf_op jit(solution)/shard_map/reduce_scatter | solution.py:1127
  596.1 58.1 %finish.1 = (bf16[2,192,2048]{2,1,0:T(8,128)(2,1)}, bf16[2,192,2048]{2,1,0:T(8,128)(2,1)}, f32[4,128]{1,0:T(4,128)}, f32[4,6,128]{2,1,0:T(8,128)}, f32[3,128,1024]{2,1,0:T(8,128)}, /*index=5*/f32[1024,128]{1,0:T(8,128)}) custom-call(bf16[192,2048]{1,0:T(8,128)(2,1)} %get-tuple-element.96.refs_0_, bf16[4,192,512]{2,1,0:T(8,128)(2,1)} %get-tuple-element.97.refs_1_, ...), custom_call_target="tpu_custom_call" | custom-call | bytes 120000000 | tf_op jit(solution)/shard_map/finish/pallas_call | solution.py:108
  654.3 1.4 slice_bitcast_fusion
  655.6 1.1 reshape.202
  657.6 3.6 bitcast_convert_fusion
  661.2 1.1 copy.65
  662.4 1.1 copy.66
  663.5 0.8 copy.67
  (68 shorter events, 6.5 us)
Async XLA Ops:
  7.2 154.6 %all-gather.4.cloned.1.call-start = ((), (), s32[]{:S(2)}) async-start(), calls=%async_computation.4 | async-start | bytes 3932160 | tf_op jit(solution)/shard_map/all_gather | solution.py:1136
  7.9 288.9 %all-gather.6.cloned.1.call-start = ((), (), s32[]{:S(2)}) async-start(), calls=%async_computation.5 | async-start | bytes 7208960 | tf_op jit(solution)/shard_map/all_gather | solution.py:1124
  12.7 1.7 copy-start.10
  12.7 1.7 copy-start.8
  12.7 1.7 copy-start.9
  106.8 235.9 %all-gather.8.cloned.1.call-start = ((), (), s32[]{:S(2)}) async-start(), calls=%async_computation.6 | async-start | bytes 3932160 | tf_op jit(solution)/shard_map/all_gather | solution.py:1124
  107.5 350.3 %reduce-scatter.5.cloned.1.call-start = ((), (), s32[]{:S(2)}) async-start(), calls=%async_computation.7 | async-start | bytes 3604480 | tf_op jit(solution)/shard_map/reduce_scatter | solution.py:1127
  109.1 96.7 %copy-start.7 = (s32[1,1536]{1,0:T(1,128)}, s32[1,1536]{1,0:T(1,128)S(1)}, u32[]{:S(2)}) copy-start(s32[1,1536]{1,0:T(1,128)S(1)} %broadcast_in_dim.29.begin_ref.refs_12_) | copy-start | bytes 18436
  342.7 178.4 %reduce-scatter.7.cloned.1.call-start = ((), (), s32[]{:S(2)}) async-start(), calls=%async_computation.8 | async-start | bytes 7208960 | tf_op jit(solution)/shard_map/reduce_scatter | solution.py:1127
  370.6 214.1 %reduce-scatter.11.cloned.1.call-start = ((), (), s32[]{:S(2)}) async-start(), calls=%async_computation.10 | async-start | bytes 1310720 | tf_op jit(solution)/shard_map/reduce_scatter | solution.py:1127
  370.6 75.7 %copy-start.1 = (bf16[1536,256]{1,0:T(8,128)(2,1)S(1)}, bf16[1536,256]{1,0:T(8,128)(2,1)}, u32[]{:S(2)}) copy-start(bf16[1536,256]{1,0:T(8,128)(2,1)} %get-tuple-element.66.refs_5_) | copy-start | bytes 2359300
  446.3 6.0 copy-start.5
  452.2 143.9 %reduce-scatter.9.cloned.1.call-start = ((), (), s32[]{:S(2)}) async-start(), calls=%async_computation.9 | async-start | bytes 3932160 | tf_op jit(solution)/shard_map/reduce_scatter | solution.py:1127
  518.1 1.4 copy-start
  518.1 1.9 copy-start.4
  654.3 6.9 %copy-start.3 = (bf16[2,192,2048]{2,1,0:T(8,128)(2,1)S(1)}, bf16[2,192,2048]{2,1,0:T(8,128)(2,1)}, u32[]{:S(2)}) copy-start(bf16[2,192,2048]{2,1,0:T(8,128)(2,1)} %get-tuple-element.103) | copy-start | bytes 4718596
  657.6 4.7 copy-start.2
  661.2 2.3 copy-start.6
Sparse Core Ops, SparseCore 0:
  9.6 95.7 all-gather.3
  107.0 121.6 all-gather.5
  230.3 61.7 all-gather.7
  342.9 56.3 reduce-scatter.4
  401.5 102.7 reduce-scatter.6
  507.0 25.5 reduce-scatter.10
  535.6 60.4 reduce-scatter.8

commit v15 on v14

--- a/solution.py
+++ b/solution.py
@@ -133,7 +133,7 @@
 
     def kernel(ride, ins, outs, scratch):
         tile, x_ref, y_ref, *raws = ins
-        got, x_buf, x_out, y_buf, y_out, *turns = outs
+        got, x_buf, x_out, y_out, *turns = outs
         send, recv, bsend, brecv, own, hsend, hrecv, hown, zsend, zrecv, zown, wsend, wrecv, wown, *stages = scratch
         p, z, c = here()
         mates = [(p + k) % S for k in range(1, S)]
@@ -164,7 +164,6 @@
             return hop
 
         x_hop = first_hop(x_ref, x_buf, 0)
-        y_hop = first_hop(y_ref, y_buf, 1)
         local = pltpu.make_async_copy(tile.at[z, p], got.at[c, z, p], own)
         local.start()
         copies = []
@@ -173,6 +172,7 @@
             copies.append(remote(tile.at[g, q], got.at[c, z, p], send.at[at], recv.at[at], where))
             copies[-1].start()
         ride.start()
+        y_hop = first_hop(y_ref, y_out, 1)
         moves = []
         for m, (raw, stage, out, height) in enumerate(zip(raws, stages, turns, heights)):
             for q in range(S):
@@ -182,19 +182,14 @@
                 moves.append(remote(stage.at[q], out.at[p], wsend.at[m, k], wrecv.at[m, k], {"shard": q}))
             for copy in moves[-S:]:
                 copy.start()
-        def second_hop(hop, buf, out, at):
-            for copy in hop:
-                copy.wait()
-            line = [pltpu.make_async_copy(buf.at[z], out.at[z], zown.at[at])]
-            for k in range(1, C):
-                g = (z + k) % C
-                line.append(remote(buf.at[g], out.at[z], zsend.at[at, k - 1], zrecv.at[at, k - 1], {"ctx": g}))
-            for copy in line:
-                copy.start()
-            return line
-
-        line = second_hop(x_hop, x_buf, x_out, 0)
-        line += second_hop(y_hop, y_buf, y_out, 1)
+        for copy in x_hop:
+            copy.wait()
+        line = [pltpu.make_async_copy(x_buf.at[z], x_out.at[z], zown)]
+        for k in range(1, C):
+            g = (z + k) % C
+            line.append(remote(x_buf.at[g], x_out.at[z], zsend.at[k - 1], zrecv.at[k - 1], {"ctx": g}))
+        for copy in line:
+            copy.start()
         local.wait()
         for copy in copies:
             copy.wait()
@@ -202,7 +197,7 @@
         back.start()
         back.wait_send()
         remote(got.at[1 - c], got.at[1 - c], bsend, brecv, {"tp": 1 - c}).wait_recv()
-        for copy in line + moves:
+        for copy in line + y_hop + moves:
             copy.wait()
         ride.wait()
 
@@ -211,13 +206,12 @@
     return comm(
         kernel, S, C, number, "exchange", [tiles, rows, beside, *turned],
         [IN_VMEM, ANY, ANY] + [IN_VMEM] * m,
-        [(jax.ShapeDtypeStruct((T,) + tiles.shape, tiles.dtype), ANY), (part, IN_VMEM), (part, IN_VMEM), (part, IN_VMEM),
-         (part, IN_VMEM)]
+        [(jax.ShapeDtypeStruct((T,) + tiles.shape, tiles.dtype), ANY), (part, IN_VMEM), (part, IN_VMEM), (part, ANY)]
         + [(jax.ShapeDtypeStruct((S, nb, height), BF), ANY) for height in heights],
         [
             DMA((count,)), DMA((count,)), DMA, DMA, DMA,
             DMA((2, S - 1, pieces)), DMA((2, S - 1, pieces)), DMA((2, pieces)),
-            DMA((2, C - 1)), DMA((2, C - 1)), DMA((2,)), DMA((m, S - 1)), DMA((m, S - 1)), DMA((m,)),
+            DMA((C - 1,)), DMA((C - 1,)), DMA, DMA((m, S - 1)), DMA((m, S - 1)), DMA((m,)),
         ]
         + [pltpu.VMEM((S, nb, height), BF) for height in heights],
         riders,
@@ -1134,7 +1128,7 @@
 
         tile = tiles_of((norm_gain[0].reshape(-1), norm_bias[0].reshape(-1), b_qkv[0].reshape(-1), lengths[0]), ())
         raw = lax.all_gather(w_qkv[0].swapaxes(0, 1).reshape(3 * nb, -1), "ctx", axis=0, tiled=True)
-        small, _, tok, _, cot, wo, wd, wg = exchange(
+        small, _, tok, cot, wo, wd, wg = exchange(
             S, C, T, 0,
             [("shard", w_gateup[0].reshape(nb, 2, S, fn).transpose(2, 0, 1, 3).reshape(S, nb, 2 * fn))],
             jnp.broadcast_to(tile, (C, S, 8, 128)),
@@ -1161,7 +1155,7 @@
 
         n1, qkv, wq = project(S, C, T, 12, tok, raw.reshape(C, 3, nb, -1), gains[:1], shifts[:1], bias)
         q, k, v, o, lse = attend(qkv, begin)
-        mid, n2 = sum_norm_gather(S, C, T, 2, o, wo, tok, gains[1:], shifts[1:])
+        mid, n2, cot = sum_norm_gather(S, C, T, 2, o, wo, tok, gains[1:], shifts[1:], [("ctx", cot)])
         gb, gu, act = gates(S, C, T, 4, n2, wg, cot)
         gw_down = mm(gb, act, 0, 0).astype(BF)
         wd, gw_down = after(wd, gw_down)

time: 675 us -> 636 us (0.942)
  Pallas kernels: 572 us -> 536 us
    pallas_call x9, Pallas kernels: 538 us -> 502 us  [comm(): pl.pallas_call(body, out_shape=[shape for shape, _ in outs] + ride.shapes...]
where the time goes in v15:
time: 636 us; the launch traced here: 633 us
  Pallas kernels  536 us (84%)
  matrix products  45.7 us (7%)
  local copies, waits for them, and re-layouts  21.2 us (3%)
  between operations  14.7 us (2%)
  waiting for transfers between devices  9.37 us (1%)
    pallas_call x9, Pallas kernels, comm(): pl.pallas_call(body, out_shape=[shape for shape, _ in outs] + ride.shapes...  502 us
    dot_general x5, matrix products, mm(): lax.dot_general(a, b, (((ca,), (cb,)), ((), ())), preferred_element_type=...  45.7 us
    pallas_call x1, Pallas kernels, attend(): pl.pallas_call(attend_kernel, in_specs=[pl.BlockSpec(memory_space=pltpu.S...  17 us
    pallas_call x1, Pallas kernels, by_rows(): pl.pallas_call(kernel, grid=(L // BLK,), in_specs=[spec(x.shape[1]) if ro...  13.2 us
  transfers between devices with their start and end apart: 7, of which 1 were waited for; matrix products, arithmetic and copies ran while one was open for 9% of the time, Pallas kernels for 76%

profile of v15, /device:TPU:9, one launch (start us, length us, event | category | flops | bytes accessed | tf_op | source)
XLA Modules:
  0.0 632.5 jit_solution(6480435504884186190)
XLA Ops:
  8.0 0.8 copy.48
  8.8 3.8 copy.49
  12.8 1.5 copy.51.refs_5_
  15.1 56.6 %exchange.1 = (f32[2,4,4,8,128]{4,3,2,1,0:T(8,128)}, bf16[4,192,512]{2,1,0:T(8,128)(2,1)}, bf16[4,192,512]{2,1,0:T(8,128)(2,1)}, bf16[4,192,512]{2,1,0:T(8,128)(...) custom-call(f32[4,4,8,128]{3,2,1,0:T(8,128)} %broadcast_in_dim.27.refs_0_, ...), custom_call_target="tpu_custom_call" | custom-call | bytes 120000000 | tf_op jit(solution)/shard_map/exchange/pallas_call | solution.py:108
  72.8 0.8 constant_dynamic-slice_fusion.2
  74.5 0.7 reshape.183.refs_4_
  75.2 38.7 %gather_columns.2 = (bf16[4,2,192,2048]{3,2,1,0:T(8,128)(2,1)}, bf16[4,512,256]{2,1,0:T(8,128)(2,1)}) custom-call(bf16[4,192,512]{2,1,0:T(8,128)(2,1)} %get-tuple-element.62.refs_0_, bf16[512,256]{1,0:T(8,128)(2,1)} %bitcast.135), custom_call_target="tpu_custom_call" | custom-call | bytes 120000000 | tf_op jit(solution)/shard_map/gather_columns/pallas_call | solution.py:108
  115.1 50.6 %project.1 = (bf16[1536,2048]{1,0:T(8,128)(2,1)}, f32[1536,768]{1,0:T(8,128)}, bf16[4,4,128,768]{3,2,1,0:T(8,128)(2,1)}) custom-call(bf16[1536,2048]{1,0:T(8,128)(2,1)} %bitcast.104, bf16[4,3,128,1024]{3,2,1,0:T(8,128)(2,1)} %bitcast.117, f32[1,2048]{1,0:T(1,128)} %bitcast.139, f32[1,2048]{1,0:T(1,128)} %bitcast.144, f32[1,768]{1,0:T(1,128)} %reshape.183.refs_4_), custom_call_target="tpu_custom_call" | custom-call | bytes 120000000 | tf_op jit(solution)/shard_map/project/pallas_call | solution.py:108
  165.7 17.0 %attend.1 = (bf16[1536,256]{1,0:T(8,128)(2,1)}, bf16[1536,256]{1,0:T(8,128)(2,1)}, bf16[1536,256]{1,0:T(8,128)(2,1)}, bf16[1536,256]{1,0:T(8,128)(2,1)}, f32[4,1536]{1,0:T(4,128)}) custom-call(s32[3]{0:T(128)} %and_select_fusion.first_ref, f32[1536,768]{1,0:T(8,128)} %get-tuple-element.65.qkv_ref, f32[256,128]{1,0:T(8,128)} %constant.59.clone.cos_ref.refs_8_, ...), custom_call_target="tpu_custom_call" | custom-call | tf_op jit(solution)/shard_map/attend/pallas_call | solution.py:968
  182.7 77.8 %sum_norm_gather.1 = (f32[192,2048]{1,0:T(8,128)}, bf16[8,192,2048]{2,1,0:T(8,128)(2,1)}, bf16[4,192,512]{2,1,0:T(8,128)(2,1)}) custom-call(bf16[8,192,256]{2,1,0:T(8,128)(2,1)} %bitcast.119, bf16[2048,256]{1,0:T(8,128)(2,1)} %bitcast.127, bf16[8,192,2048]{2,1,0:T(8,128)(2,1)} %bitcast.105, f32[1,2048]{1,0:T(1,128)} %bitcast.141, f32[1,2048]{1,0:T(1,128)} %bitcast.143, ...), custom_call_target="tpu_custom_call" | custom-call | bytes 120000000 | tf_op jit(solution)/shard_map/sum_norm_gather/pallas_call | solution.py:108
  260.6 36.3 %gather_columns.3 = (bf16[4,2,192,2048]{3,2,1,0:T(8,128)(2,1)}, f32[1536,1408]{1,0:T(8,128)}, bf16[1536,704]{1,0:T(8,128)(2,1)}) custom-call(bf16[4,192,512]{2,1,0:T(8,128)(2,1)} %get-tuple-element.69.refs_0_, bf16[1536,2048]{1,0:T(8,128)(2,1)} %bitcast.111, bf16[2048,1408]{1,0:T(8,128)(2,1)} %all-gather.6.cloned.1.call-done.refs_2_.refs_1_), custom_call_target="tpu_custom_call" | custom-call | bytes 120000000 | tf_op jit(solution)/shard_map/gather_columns/pallas_call | solution.py:108
  296.8 9.8 %convolution_convert_fusion.2 = bf16[2048,704]{0,1:T(8,128)(2,1)} fusion(bf16[1536,2048]{1,0:T(8,128)(2,1)} %bitcast.107, bf16[1536,704]{1,0:T(8,128)(2,1)} %get-tuple-element.72), kind=kOutput, calls=%fused_computation.2 | convolution fusion | flops 4430626816 | bytes 11337728 | tf_op jit(solution)/shard_map/dot_general | solution.py:26
  306.7 13.2 %gates_back.1 = bf16[1536,1408]{1,0:T(8,128)(2,1)} custom-call(bf16[1536,2048]{1,0:T(8,128)(2,1)} %bitcast.108, bf16[2048,704]{1,0:T(8,128)(2,1)} %all-gather.8.cloned.1.call-done.wd_ref.refs_1_, f32[1536,1408]{1,0:T(8,128)} %get-tuple-element.79.gu_ref), custom_call_target="tpu_custom_call" | custom-call | tf_op jit(solution)/shard_map/gates_back/pallas_call | solution.py:552
  319.8 15.0 %convolution_convert_fusion = bf16[2048,1408]{1,0:T(8,128)(2,1)} fusion(bf16[1536,2048]{1,0:T(8,128)(2,1)} %bitcast.112, bf16[1536,1408]{1,0:T(8,128)(2,1)} %gates_back.1), kind=kOutput, calls=%fused_computation | convolution fusion | flops 8861253632 | bytes 16384000 | tf_op jit(solution)/shard_map/dot_general | solution.py:26
  335.0 75.8 %sum_back_gather.1 = (f32[192,2048]{1,0:T(8,128)}, bf16[8,192,2048]{2,1,0:T(8,128)(2,1)}, f32[2,2048]{1,0:T(2,128)}) custom-call(bf16[8,192,1408]{2,1,0:T(8,128)(2,1)} %bitcast.110, bf16[2048,1408]{1,0:T(8,128)(2,1)} %all-gather.6.cloned.1.call-done.refs_2_.refs_1_, f32[192,2048]{1,0:T(8,128)} %get-tuple-element.81.refs_2_, bf16[8,192,2048]{2,1,0:T(8,128)(2,1)} %bitcast.109, ...), custom_call_target="tpu_custom_call" | custom-call | bytes 120000000 | tf_op jit(solution)/shard_map/sum_back_gather/pallas_call | solution.py:108
  410.8 5.8 convolution_convert_fusion.4
  416.7 5.5 convolution_convert_fusion.3.refs_6_
  422.2 2.3 copy.54
  424.5 48.5 %attend_back.1 = (bf16[1536,768]{1,0:T(8,128)(2,1)}, f32[1,768]{1,0:T(1,128)}, f32[192,2048]{1,0:T(8,128)}, bf16[4,128,704]{2,1,0:T(8,128)(2,1)}) custom-call(bf16[8,192,704]{2,1,0:T(8,128)(2,1)} %bitcast.122, bf16[2048,704]{1,0:T(8,128)(2,1)} %all-gather.8.cloned.1.call-done.wd_ref.refs_1_, bf16[1536,256]{1,0:T(8,128)(2,1)} %get-tuple-element.76.refs_2_, ...), custom_call_target="tpu_custom_call" | custom-call | bytes 120000000 | tf_op jit(solution)/shard_map/attend_back/pallas_call | solution.py:108
  473.0 9.6 %convolution_convert_fusion.1 = bf16[2048,768]{1,0:T(8,128)(2,1)} fusion(bf16[1536,2048]{1,0:T(8,128)(2,1)} %get-tuple-element.87, bf16[1536,768]{1,0:T(8,128)(2,1)} %get-tuple-element.88), kind=kOutput, calls=%fused_computation.1 | convolution fusion | flops 4833411072 | bytes 11796480 | tf_op jit(solution)/shard_map/dot_general | solution.py:26
  482.6 1.4 copy-done
  484.7 0.9 copy.60
  485.6 59.6 %sum_back.1 = (bf16[192,2048]{1,0:T(8,128)(2,1)}, f32[2,2048]{1,0:T(2,128)}, bf16[4,192,512]{2,1,0:T(8,128)(2,1)}, bf16[4,128,1408]{2,1,0:T(8,128)(2,1)}) custom-call(bf16[8,192,768]{2,1,0:T(8,128)(2,1)} %bitcast.121, bf16[2048,768]{1,0:T(8,128)(2,1)} %bitcast.116, bf16[8,192,2048]{2,1,0:T(8,128)(2,1)} %bitcast.106, f32[192,2048]{1,0:T(8,128)} %get-tuple-element.90.refs_3_, ...), custom_call_target="tpu_custom_call" | custom-call | bytes 120000000 | tf_op jit(solution)/shard_map/sum_back/pallas_call | solution.py:108
  545.2 4.2 final.1
  549.4 7.9 %reduce-scatter.9.cloned.1.call-done = bf16[512,768]{1,0:T(8,128)(2,1)} async-done(((bf16[2048,768]{1,0:T(8,128)(2,1)}), bf16[512,768]{1,0:T(8,128)(2,1)}) %reduce-scatter.9.cloned.1.call-update) | async-done | bytes 786448 | tf_op jit(solution)/shard_map/reduce_scatter | solution.py:1121
  557.3 58.1 %finish.1 = (bf16[2,192,2048]{2,1,0:T(8,128)(2,1)}, bf16[2,192,2048]{2,1,0:T(8,128)(2,1)}, f32[4,128]{1,0:T(4,128)}, f32[4,6,128]{2,1,0:T(8,128)}, f32[3,128,1024]{2,1,0:T(8,128)}, /*index=5*/f32[1024,128]{1,0:T(8,128)}) custom-call(bf16[192,2048]{1,0:T(8,128)(2,1)} %get-tuple-element.98.refs_0_, bf16[4,192,512]{2,1,0:T(8,128)(2,1)} %get-tuple-element.99.refs_1_, ...), custom_call_target="tpu_custom_call" | custom-call | bytes 120000000 | tf_op jit(solution)/shard_map/finish/pallas_call | solution.py:108
  615.4 1.4 slice_bitcast_fusion
  616.8 1.1 reshape.202
  618.8 3.6 bitcast_convert_fusion
  622.3 1.1 copy.65
  623.5 1.1 copy.66
  624.6 0.8 copy.67
  (68 shorter events, 6.5 us)
Async XLA Ops:
  7.2 107.9 %all-gather.4.cloned.1.call-start = ((), (), s32[]{:S(2)}) async-start(), calls=%async_computation.4 | async-start | bytes 3932160 | tf_op jit(solution)/shard_map/all_gather | solution.py:1130
  7.9 252.7 %all-gather.6.cloned.1.call-start = ((), (), s32[]{:S(2)}) async-start(), calls=%async_computation.5 | async-start | bytes 7208960 | tf_op jit(solution)/shard_map/all_gather | solution.py:1118
  12.7 1.7 copy-start.10
  12.7 1.7 copy-start.8
  12.7 1.7 copy-start.9
  71.7 234.9 %all-gather.8.cloned.1.call-start = ((), (), s32[]{:S(2)}) async-start(), calls=%async_computation.6 | async-start | bytes 3932160 | tf_op jit(solution)/shard_map/all_gather | solution.py:1118
  72.4 349.8 %reduce-scatter.5.cloned.1.call-start = ((), (), s32[]{:S(2)}) async-start(), calls=%async_computation.7 | async-start | bytes 3604480 | tf_op jit(solution)/shard_map/reduce_scatter | solution.py:1121
  74.0 91.6 %copy-start.7 = (s32[1,1536]{1,0:T(1,128)}, s32[1,1536]{1,0:T(1,128)S(1)}, u32[]{:S(2)}) copy-start(s32[1,1536]{1,0:T(1,128)S(1)} %broadcast_in_dim.29.begin_ref.refs_12_) | copy-start | bytes 18436
  306.6 179.0 %reduce-scatter.7.cloned.1.call-start = ((), (), s32[]{:S(2)}) async-start(), calls=%async_computation.8 | async-start | bytes 7208960 | tf_op jit(solution)/shard_map/reduce_scatter | solution.py:1121
  334.9 214.5 %reduce-scatter.11.cloned.1.call-start = ((), (), s32[]{:S(2)}) async-start(), calls=%async_computation.10 | async-start | bytes 1310720 | tf_op jit(solution)/shard_map/reduce_scatter | solution.py:1121
  335.0 75.9 %copy-start.1 = (bf16[1536,256]{1,0:T(8,128)(2,1)S(1)}, bf16[1536,256]{1,0:T(8,128)(2,1)}, u32[]{:S(2)}) copy-start(bf16[1536,256]{1,0:T(8,128)(2,1)} %get-tuple-element.66.refs_5_) | copy-start | bytes 2359300
  410.8 5.8 copy-start.5
  416.6 140.7 %reduce-scatter.9.cloned.1.call-start = ((), (), s32[]{:S(2)}) async-start(), calls=%async_computation.9 | async-start | bytes 3932160 | tf_op jit(solution)/shard_map/reduce_scatter | solution.py:1121
  482.6 1.4 copy-start
  482.6 1.9 copy-start.4
  615.4 6.9 %copy-start.3 = (bf16[2,192,2048]{2,1,0:T(8,128)(2,1)S(1)}, bf16[2,192,2048]{2,1,0:T(8,128)(2,1)}, u32[]{:S(2)}) copy-start(bf16[2,192,2048]{2,1,0:T(8,128)(2,1)} %get-tuple-element.105) | copy-start | bytes 4718596
  618.8 4.7 copy-start.2
  622.3 2.3 copy-start.6
Sparse Core Ops, SparseCore 0:
  9.6 94.0 all-gather.3
  105.3 123.6 all-gather.5
  230.5 63.4 all-gather.7
  306.8 53.6 reduce-scatter.4
  362.6 102.7 reduce-scatter.6
  468.1 25.6 reduce-scatter.10
  496.7 60.5 reduce-scatter.8

commit v16 on v15

--- a/solution.py
+++ b/solution.py
@@ -93,7 +93,7 @@
     pl.semaphore_wait(barrier, len(peers))
 
 
-def comm(kernel, S, C, number, name, args, in_specs, outs, scratch, riders=()):
+def comm(kernel, S, C, number, name, args, in_specs, outs, scratch, riders=(), room=62):
     ride = Riders(S, C, riders)
     na, nr, no, ns = len(args), len(ride.axes), len(outs), len(scratch)
 
@@ -112,7 +112,7 @@
         out_specs=[spec for _, spec in outs] + [ANY] * nr,
         scratch_shapes=list(scratch) + ride.scratch,
         compiler_params=pltpu.CompilerParams(
-            collective_id=number, has_side_effects=True, vmem_limit_bytes=62 << 20
+            collective_id=number, has_side_effects=True, vmem_limit_bytes=room << 20
         ),
         cost_estimate=pl.CostEstimate(flops=0, bytes_accessed=120_000_000, transcendentals=0),
         name=name,
@@ -301,7 +301,7 @@
         copy.wait_send()
 
 
-def gather_columns(S, C, T, number, x, riders=(), extra=None):
+def gather_columns(S, C, T, number, x, riders=(), extra=None, room=62):
     _, n, wide = x.shape
     more, more_specs, more_outs, more_scratch, task = extra or ((), (), (), (), None)
 
@@ -335,7 +335,7 @@
     out, *rest = comm(
         kernel, S, C, number, "gather_columns", [x, *more], [IN_VMEM, *more_specs],
         [(jax.ShapeDtypeStruct((C, T, n, wide * S), x.dtype), ANY), *more_outs],
-        spread_sems(S) + [DMA((2,)), *more_scratch], riders,
+        spread_sems(S) + [DMA((2,)), *more_scratch], riders, room,
     )
     return [out.reshape(C * T * n, wide * S)] + rest
 
@@ -540,6 +540,7 @@
         S, C, T, number, x, (),
         ([n2, wg], [ANY, ANY], [(shape, IN_VMEM) for shape in outs],
          [pltpu.VMEM(n2.shape, BF), pltpu.VMEM(wg.shape, BF), DMA((2,))], gates_work),
+        50,
     )
 
 
@@ -1136,7 +1137,8 @@
             cotangent,
             [w_out[0], w_down[0]],
         )
-        tok, wo = gather_columns(S, C, T, 1, tok, [("all", wo.reshape(S * nb, hn))])
+        tok, wo, cot = gather_columns(S, C, T, 1, tok, [("all", wo.reshape(S * nb, hn)), ("ctx", cot)])
+        wg, wd, tok = lax.optimization_barrier((wg, wd, tok))
         wo, wg, wd = wo.reshape(D, hn), over_ctx(wg), over_ctx(wd)
 
         small = lax.dynamic_index_in_dim(small, c, 0, keepdims=False).reshape(C, S, 1024)
@@ -1155,7 +1157,7 @@
 
         n1, qkv, wq = project(S, C, T, 12, tok, raw.reshape(C, 3, nb, -1), gains[:1], shifts[:1], bias)
         q, k, v, o, lse = attend(qkv, begin)
-        mid, n2, cot = sum_norm_gather(S, C, T, 2, o, wo, tok, gains[1:], shifts[1:], [("ctx", cot)])
+        mid, n2 = sum_norm_gather(S, C, T, 2, o, wo, tok, gains[1:], shifts[1:])
         gb, gu, act = gates(S, C, T, 4, n2, wg, cot)
         gw_down = mm(gb, act, 0, 0).astype(BF)
         wd, gw_down = after(wd, gw_down)

time: 636 us -> 646 us (1.016)
  transfers between devices with their start and end apart: 7 -> 7, of which waited for: 1 -> 1; matrix products, arithmetic and copies ran while one was open for 9% -> 9% of each run, Pallas kernels for 76% -> 75%
where the time goes in v16:
time: 646 us; the launch traced here: 644 us
  Pallas kernels  542 us (84%)
  matrix products  45.4 us (7%)
  local copies, waits for them, and re-layouts  21.7 us (3%)
  between operations  14.7 us (2%)
  waiting for transfers between devices  14.4 us (2%)
    pallas_call x9, Pallas kernels, comm(): pl.pallas_call(body, out_shape=[shape for shape, _ in outs] + ride.shapes...  508 us
    dot_general x5, matrix products, mm(): lax.dot_general(a, b, (((ca,), (cb,)), ((), ())), preferred_element_type=...  45.4 us
    pallas_call x1, Pallas kernels, attend(): pl.pallas_call(attend_kernel, in_specs=[pl.BlockSpec(memory_space=pltpu.S...  17 us
    reduce_scatter x4, waiting for transfers between devices, sum_ctx(): g = lax.psum_scatter(g.astype(BF), 'ctx', scatter_dimension=0, tiled=True)  13 us
  transfers between devices with their start and end apart: 7, of which 1 were waited for; matrix products, arithmetic and copies ran while one was open for 9% of the time, Pallas kernels for 75%

profile of v16, /device:TPU:9, one launch (start us, length us, event | category | flops | bytes accessed | tf_op | source)
XLA Modules:
  0.0 643.8 jit_solution(14230055721124224641)
XLA Ops:
  8.0 0.8 copy.48
  8.8 3.8 copy.49
  12.8 1.5 copy.51.refs_5_
  15.1 56.6 %exchange.1 = (f32[2,4,4,8,128]{4,3,2,1,0:T(8,128)}, bf16[4,192,512]{2,1,0:T(8,128)(2,1)}, bf16[4,192,512]{2,1,0:T(8,128)(2,1)}, bf16[4,192,512]{2,1,0:T(8,128)(...) custom-call(f32[4,4,8,128]{3,2,1,0:T(8,128)} %broadcast_in_dim.27.refs_0_, ...), custom_call_target="tpu_custom_call" | custom-call | bytes 120000000 | tf_op jit(solution)/shard_map/exchange/pallas_call | solution.py:108
  71.7 58.3 %gather_columns.2 = (bf16[4,2,192,2048]{3,2,1,0:T(8,128)(2,1)}, bf16[4,512,256]{2,1,0:T(8,128)(2,1)}, bf16[4,192,512]{2,1,0:T(8,128)(2,1)}) custom-call(bf16[4,192,512]{2,1,0:T(8,128)(2,1)} %get-tuple-element.64.refs_0_, bf16[512,256]{1,0:T(8,128)(2,1)} %bitcast.135, bf16[4,192,512]{2,1,0:T(8,128)(2,1)} %get-tuple-element.66.refs_2_), custom_call_target="tpu_custom_call" | custom-call | bytes 120000000 | tf_op jit(solution)/shard_map/gather_columns/pallas_call | solution.py:108
  131.7 0.7 reshape.187.refs_4_
  133.6 50.7 %project.1 = (bf16[1536,2048]{1,0:T(8,128)(2,1)}, f32[1536,768]{1,0:T(8,128)}, bf16[4,4,128,768]{3,2,1,0:T(8,128)(2,1)}) custom-call(bf16[1536,2048]{1,0:T(8,128)(2,1)} %bitcast.105, bf16[4,3,128,1024]{3,2,1,0:T(8,128)(2,1)} %bitcast.118, f32[1,2048]{1,0:T(1,128)} %bitcast.139, f32[1,2048]{1,0:T(1,128)} %bitcast.144, f32[1,768]{1,0:T(1,128)} %reshape.187.refs_4_), custom_call_target="tpu_custom_call" | custom-call | bytes 120000000 | tf_op jit(solution)/shard_map/project/pallas_call | solution.py:108
  184.3 17.0 %attend.1 = (bf16[1536,256]{1,0:T(8,128)(2,1)}, bf16[1536,256]{1,0:T(8,128)(2,1)}, bf16[1536,256]{1,0:T(8,128)(2,1)}, bf16[1536,256]{1,0:T(8,128)(2,1)}, f32[4,1536]{1,0:T(4,128)}) custom-call(s32[3]{0:T(128)} %and_select_fusion.first_ref, f32[1536,768]{1,0:T(8,128)} %get-tuple-element.73.qkv_ref, f32[256,128]{1,0:T(8,128)} %constant.59.clone.cos_ref.refs_8_, ...), custom_call_target="tpu_custom_call" | custom-call | tf_op jit(solution)/shard_map/attend/pallas_call | solution.py:969
  201.3 67.8 %sum_norm_gather.1 = (f32[192,2048]{1,0:T(8,128)}, bf16[8,192,2048]{2,1,0:T(8,128)(2,1)}) custom-call(bf16[8,192,256]{2,1,0:T(8,128)(2,1)} %bitcast.121, bf16[2048,256]{1,0:T(8,128)(2,1)} %bitcast.127, bf16[8,192,2048]{2,1,0:T(8,128)(2,1)} %bitcast.106, f32[1,2048]{1,0:T(1,128)} %bitcast.141, f32[1,2048]{1,0:T(1,128)} %bitcast.143), custom_call_target="tpu_custom_call" | custom-call | bytes 120000000 | tf_op jit(solution)/shard_map/sum_norm_gather/pallas_call | solution.py:108
  269.2 34.4 %gather_columns.3 = (bf16[4,2,192,2048]{3,2,1,0:T(8,128)(2,1)}, f32[1536,1408]{1,0:T(8,128)}, bf16[1536,704]{1,0:T(8,128)(2,1)S(1)}) custom-call(bf16[4,192,512]{2,1,0:T(8,128)(2,1)S(1)} %copy-done.1, bf16[1536,2048]{1,0:T(8,128)(2,1)} %bitcast.112, bf16[2048,1408]{1,0:T(8,128)(2,1)} %all-gather.6.cloned.1.call-done.refs_2_.refs_1_), custom_call_target="tpu_custom_call" | custom-call | bytes 120000000 | tf_op jit(solution)/shard_map/gather_columns/pallas_call | solution.py:108
  303.6 1.4 copy-done
  305.0 9.6 %convolution_convert_fusion.2 = bf16[2048,704]{0,1:T(8,128)(2,1)} fusion(bf16[1536,2048]{1,0:T(8,128)(2,1)} %bitcast.108, bf16[1536,704]{1,0:T(8,128)(2,1)S(1)} %get-tuple-element.78), kind=kOutput, calls=%fused_computation.2 | convolution fusion | flops 4430626816 | bytes 11337728 | tf_op jit(solution)/shard_map/dot_general | solution.py:26
  314.7 12.8 %gates_back.1 = bf16[1536,1408]{1,0:T(8,128)(2,1)} custom-call(bf16[1536,2048]{1,0:T(8,128)(2,1)} %bitcast.109, bf16[2048,704]{1,0:T(8,128)(2,1)} %all-gather.8.cloned.1.call-done.wd_ref.refs_1_, f32[1536,1408]{1,0:T(8,128)} %get-tuple-element.85.gu_ref), custom_call_target="tpu_custom_call" | custom-call | tf_op jit(solution)/shard_map/gates_back/pallas_call | solution.py:553
  327.5 15.1 %convolution_convert_fusion = bf16[2048,1408]{1,0:T(8,128)(2,1)} fusion(bf16[1536,2048]{1,0:T(8,128)(2,1)} %bitcast.113, bf16[1536,1408]{1,0:T(8,128)(2,1)} %gates_back.1), kind=kOutput, calls=%fused_computation | convolution fusion | flops 8861253632 | bytes 16384000 | tf_op jit(solution)/shard_map/dot_general | solution.py:26
  342.6 75.1 %sum_back_gather.1 = (f32[192,2048]{1,0:T(8,128)}, bf16[8,192,2048]{2,1,0:T(8,128)(2,1)}, f32[2,2048]{1,0:T(2,128)}) custom-call(bf16[8,192,1408]{2,1,0:T(8,128)(2,1)} %bitcast.111, bf16[2048,1408]{1,0:T(8,128)(2,1)} %all-gather.6.cloned.1.call-done.refs_2_.refs_1_, f32[192,2048]{1,0:T(8,128)} %get-tuple-element.87.refs_2_, bf16[8,192,2048]{2,1,0:T(8,128)(2,1)} %bitcast.110, ...), custom_call_target="tpu_custom_call" | custom-call | bytes 120000000 | tf_op jit(solution)/shard_map/sum_back_gather/pallas_call | solution.py:108
  417.8 5.8 convolution_convert_fusion.4
  423.9 5.5 convolution_convert_fusion.3.refs_6_
  429.4 2.3 copy.54
  431.7 48.4 %attend_back.1 = (bf16[1536,768]{1,0:T(8,128)(2,1)}, f32[1,768]{1,0:T(1,128)}, f32[192,2048]{1,0:T(8,128)}, bf16[4,128,704]{2,1,0:T(8,128)(2,1)}) custom-call(bf16[8,192,704]{2,1,0:T(8,128)(2,1)} %bitcast.104, bf16[2048,704]{1,0:T(8,128)(2,1)} %all-gather.8.cloned.1.call-done.wd_ref.refs_1_, bf16[1536,256]{1,0:T(8,128)(2,1)} %get-tuple-element.82.refs_2_, ...), custom_call_target="tpu_custom_call" | custom-call | bytes 120000000 | tf_op jit(solution)/shard_map/attend_back/pallas_call | solution.py:108
  480.1 9.4 %convolution_convert_fusion.1 = bf16[2048,768]{1,0:T(8,128)(2,1)} fusion(bf16[1536,2048]{1,0:T(8,128)(2,1)} %get-tuple-element.93, bf16[1536,768]{1,0:T(8,128)(2,1)} %get-tuple-element.94), kind=kOutput, calls=%fused_computation.1 | convolution fusion | flops 4833411072 | bytes 11796480 | tf_op jit(solution)/shard_map/dot_general | solution.py:26
  489.5 1.4 copy-done.2
  491.5 0.9 copy.60
  492.5 58.9 %sum_back.1 = (bf16[192,2048]{1,0:T(8,128)(2,1)}, f32[2,2048]{1,0:T(2,128)}, bf16[4,192,512]{2,1,0:T(8,128)(2,1)}, bf16[4,128,1408]{2,1,0:T(8,128)(2,1)}) custom-call(bf16[8,192,768]{2,1,0:T(8,128)(2,1)} %bitcast.122, bf16[2048,768]{1,0:T(8,128)(2,1)} %bitcast.117, bf16[8,192,2048]{2,1,0:T(8,128)(2,1)} %bitcast.107, f32[192,2048]{1,0:T(8,128)} %get-tuple-element.96.refs_3_, ...), custom_call_target="tpu_custom_call" | custom-call | bytes 120000000 | tf_op jit(solution)/shard_map/sum_back/pallas_call | solution.py:108
  551.3 4.2 final.1
  555.5 13.0 %reduce-scatter.9.cloned.1.call-done = bf16[512,768]{1,0:T(8,128)(2,1)} async-done(((bf16[2048,768]{1,0:T(8,128)(2,1)}), bf16[512,768]{1,0:T(8,128)(2,1)}) %reduce-scatter.9.cloned.1.call-update) | async-done | bytes 786448 | tf_op jit(solution)/shard_map/reduce_scatter | solution.py:1122
  568.5 58.2 %finish.1 = (bf16[2,192,2048]{2,1,0:T(8,128)(2,1)}, bf16[2,192,2048]{2,1,0:T(8,128)(2,1)}, f32[4,128]{1,0:T(4,128)}, f32[4,6,128]{2,1,0:T(8,128)}, f32[3,128,1024]{2,1,0:T(8,128)}, /*index=5*/f32[1024,128]{1,0:T(8,128)}) custom-call(bf16[192,2048]{1,0:T(8,128)(2,1)} %get-tuple-element.104.refs_0_, bf16[4,192,512]{2,1,0:T(8,128)(2,1)} %get-tuple-element.105.refs_1_, ...), custom_call_target="tpu_custom_call" | custom-call | bytes 120000000 | tf_op jit(solution)/shard_map/finish/pallas_call | solution.py:108
  626.7 1.4 slice_bitcast_fusion
  628.0 1.1 reshape.207
  630.0 3.6 bitcast_convert_fusion
  633.6 1.1 copy.65
  634.7 1.1 copy.66
  635.9 0.8 copy.67
  (74 shorter events, 6.4 us)
Async XLA Ops:
  7.2 126.4 %all-gather.4.cloned.1.call-start = ((), (), s32[]{:S(2)}) async-start(), calls=%async_computation.4 | async-start | bytes 3932160 | tf_op jit(solution)/shard_map/all_gather | solution.py:1131
  7.9 261.3 %all-gather.6.cloned.1.call-start = ((), (), s32[]{:S(2)}) async-start(), calls=%async_computation.5 | async-start | bytes 7208960 | tf_op jit(solution)/shard_map/all_gather | solution.py:1119
  12.7 1.7 copy-start.13
  12.7 1.7 copy-start.11
  12.7 1.7 copy-start.12
  71.7 59.1 %copy-start.10 = (f32[2,4,4,8,128]{4,3,2,1,0:T(8,128)S(1)}, f32[2,4,4,8,128]{4,3,2,1,0:T(8,128)}, u32[]{:S(2)}) copy-start(f32[2,4,4,8,128]{4,3,2,1,0:T(8,128)} %get-tuple-element.68) | copy-start | bytes 393220
  130.0 184.6 %all-gather.8.cloned.1.call-start = ((), (), s32[]{:S(2)}) async-start(), calls=%async_computation.6 | async-start | bytes 3932160 | tf_op jit(solution)/shard_map/all_gather | solution.py:1119
  130.8 298.6 %reduce-scatter.5.cloned.1.call-start = ((), (), s32[]{:S(2)}) async-start(), calls=%async_computation.7 | async-start | bytes 3604480 | tf_op jit(solution)/shard_map/reduce_scatter | solution.py:1122
  131.3 53.0 %copy-start.9 = (s32[1,1536]{1,0:T(1,128)}, s32[1,1536]{1,0:T(1,128)S(1)}, u32[]{:S(2)}) copy-start(s32[1,1536]{1,0:T(1,128)S(1)} %broadcast_in_dim.29.begin_ref.refs_12_) | copy-start | bytes 18436
  201.3 67.9 %copy-start.1 = (bf16[4,192,512]{2,1,0:T(8,128)(2,1)S(1)}, bf16[4,192,512]{2,1,0:T(8,128)(2,1)}, u32[]{:S(2)}) copy-start(bf16[4,192,512]{2,1,0:T(8,128)(2,1)} %get-tuple-element.67.refs_0_) | copy-start | bytes 2359300
  303.6 1.4 copy-start
  314.6 177.8 %reduce-scatter.7.cloned.1.call-start = ((), (), s32[]{:S(2)}) async-start(), calls=%async_computation.8 | async-start | bytes 7208960 | tf_op jit(solution)/shard_map/reduce_scatter | solution.py:1122
  342.6 213.0 %reduce-scatter.11.cloned.1.call-start = ((), (), s32[]{:S(2)}) async-start(), calls=%async_computation.10 | async-start | bytes 1310720 | tf_op jit(solution)/shard_map/reduce_scatter | solution.py:1122
  342.6 75.2 %copy-start.3 = (bf16[1536,256]{1,0:T(8,128)(2,1)S(1)}, bf16[1536,256]{1,0:T(8,128)(2,1)}, u32[]{:S(2)}) copy-start(bf16[1536,256]{1,0:T(8,128)(2,1)} %get-tuple-element.74.refs_5_) | copy-start | bytes 2359300
  417.8 6.1 copy-start.7
  423.7 144.8 %reduce-scatter.9.cloned.1.call-start = ((), (), s32[]{:S(2)}) async-start(), calls=%async_computation.9 | async-start | bytes 3932160 | tf_op jit(solution)/shard_map/reduce_scatter | solution.py:1122
  489.4 1.4 copy-start.2
  489.4 1.9 copy-start.6
  626.7 6.9 %copy-start.5 = (bf16[2,192,2048]{2,1,0:T(8,128)(2,1)S(1)}, bf16[2,192,2048]{2,1,0:T(8,128)(2,1)}, u32[]{:S(2)}) copy-start(bf16[2,192,2048]{2,1,0:T(8,128)(2,1)} %get-tuple-element.111) | copy-start | bytes 4718596
  630.0 4.7 copy-start.4
  633.6 2.3 copy-start.8
Sparse Core Ops, SparseCore 0:
  9.6 97.7 all-gather.3
  130.2 104.2 all-gather.5
  236.0 62.0 all-gather.7
  314.8 56.8 reduce-scatter.4
  373.8 102.7 reduce-scatter.6
  479.3 25.5 reduce-scatter.10
  507.9 60.4 reduce-scatter.8
